TPU v7x, 32 devices: a whole 2x2x4 slice. The times are simulated.
32 devices in a mesh: seq: 8 (over z, x), head: 4 (over y, core).
Axes of the slice: x: 2, y: 2, z: 4, core: 2. Of those that a mesh axis runs over, the one named last changes fastest.
Arguments:
- queries: bfloat16 [2048, 2048], P('seq', 'head'), may hold values from -6 to 6
- keys: bfloat16 [2048, 1024], P('seq', 'head'), may hold values from -5 to 5
- values: bfloat16 [2048, 1024], P('seq', 'head'), may hold values from -6 to 6
- out_weight: bfloat16 [2048, 5376], P('head'), may hold values from -0.125 to 0.125
- out_grad: bfloat16 [2048, 5376], P(('seq', 'head')), may hold values from -6 to 6
Outputs:
- projected: bfloat16 [2048, 5376], P(('seq', 'head'))
- query_gradient: bfloat16 [2048, 2048], P('seq', 'head')
- key_gradient: bfloat16 [2048, 1024], P('seq', 'head')
- value_gradient: bfloat16 [2048, 1024], P('seq', 'head')
All inputs are finite; a program needn't handle non-finite values.
Results may differ from a plain program's by a relative error of at most 0.018.
Values may be sent and summed in bfloat16 or wider, within the bound.
No kernel may reach another device: no remote copies, remote signals or barrier semaphores. Data moves between devices by JAX's collectives and lax.ppermute only.
A program may use at most 64 MiB of HBM per device.

v0:
```python
import jax
import jax.numpy as jnp
from jax import lax
from jax.sharding import PartitionSpec as P

HEAD_SIZE = 128
WIN = 1024


LOGIT_SCALE = 168.0 ** (-0.5)


def passed_along(value, axis, steps):
    count = lax.axis_size(axis)
    first, last = (max(0, -steps), min(count, count - steps))
    return lax.ppermute(value, axis, [(source, source + steps) for source in range(first, last)])


def shortened(shard):
    return jax.tree.map(lambda a: a.astype(jnp.bfloat16) if a.dtype == jnp.float32 else a, shard)


def head_scores(query_mat, key_mat, kv_heads):
    query_head_rows = query_mat.reshape(query_mat.shape[0], kv_heads, -1, HEAD_SIZE)
    key_head_rows = key_mat.reshape(key_mat.shape[0], kv_heads, HEAD_SIZE)
    return (
        jnp.einsum(
            "pfbo,vfo->fbpv", query_head_rows, key_head_rows, preferred_element_type=jnp.float32
        )
        * LOGIT_SCALE
    )


def per_device(queries, keys, values, out_weight, out_grad):
    tok_rows = queries.shape[0]
    kv_heads = keys.shape[1] // HEAD_SIZE
    reach_blocks = (WIN + tok_rows - 2) // tok_rows
    seq_index = lax.axis_index("seq")
    earlier_blocks = []
    for distance in range(reach_blocks):
        earlier_blocks.append(passed_along((keys, values), "seq", distance + 1))
    earlier_blocks = earlier_blocks[::-1]
    key_all = jnp.concatenate([pair[0] for pair in earlier_blocks] + [keys], 0)
    value_all = jnp.concatenate([pair[1] for pair in earlier_blocks] + [values], 0)
    window_behind = reach_blocks * tok_rows
    window_rows = key_all.shape[0]
    key_head_rows = key_all.reshape(window_rows, kv_heads, HEAD_SIZE)
    value_head_rows = value_all.reshape(window_rows, kv_heads, HEAD_SIZE)
    query_head_rows = queries.reshape(tok_rows, kv_heads, -1, HEAD_SIZE)
    logit_scores = head_scores(queries, key_all, kv_heads)
    query_pos = jnp.arange(tok_rows, dtype=jnp.int32)[:, None] + window_behind
    key_pos = jnp.arange(window_rows, dtype=jnp.int32)[None, :]
    gap = query_pos - key_pos
    key_global = seq_index * tok_rows - window_behind + key_pos
    allowed = (gap >= 0) & (gap < WIN) & (key_global >= 0)
    logit_scores = jnp.where(allowed, logit_scores, -jnp.inf)
    row_max = jnp.max(logit_scores, axis=-1, keepdims=True)
    log_total = row_max + jnp.log(jnp.sum(jnp.exp(logit_scores - row_max), axis=-1, keepdims=True))
    attention_prob = jnp.exp(logit_scores - log_total).astype(jnp.bfloat16)
    attended_rows = jnp.einsum(
        "ebml,leh->mebh", attention_prob, value_head_rows, preferred_element_type=jnp.float32
    ).astype(jnp.bfloat16)
    attended_flat = attended_rows.reshape(tok_rows, -1)
    projected = lax.psum_scatter(
        jnp.dot(attended_flat, out_weight, preferred_element_type=jnp.float32).astype(jnp.bfloat16),
        "head",
        scatter_dimension=0,
        tiled=True,
    )
    attended_gradient = lax.dot_general(
        lax.all_gather(out_grad, "head", axis=0, tiled=True),
        out_weight,
        (((1,), (1,)), ((), ())),
        preferred_element_type=jnp.float32,
    ).astype(jnp.bfloat16)
    gradient_heads = attended_gradient.reshape(tok_rows, kv_heads, -1, HEAD_SIZE)
    row_delta = jnp.sum(
        gradient_heads.astype(jnp.float32) * attended_rows.astype(jnp.float32), axis=-1
    ).transpose(1, 2, 0)[..., None]
    prob_gradient = jnp.einsum(
        "pfbo,vfo->fbpv", gradient_heads, value_head_rows, preferred_element_type=jnp.float32
    )
    score_gradient = (attention_prob.astype(jnp.float32) * (prob_gradient - row_delta)).astype(
        jnp.bfloat16
    )
    query_gradient = (
        jnp.einsum(
            "ebml,leh->mebh", score_gradient, key_head_rows, preferred_element_type=jnp.float32
        )
        * LOGIT_SCALE
    )
    query_gradient = query_gradient.reshape(tok_rows, -1).astype(jnp.bfloat16)
    key_terms = (
        jnp.einsum(
            "cqiz,icqf->zcf", score_gradient, query_head_rows, preferred_element_type=jnp.float32
        )
        * LOGIT_SCALE
    )
    value_terms = jnp.einsum(
        "cqiz,icqf->zcf", attention_prob, gradient_heads, preferred_element_type=jnp.float32
    )
    key_gradient = key_terms[window_behind:]
    value_gradient = value_terms[window_behind:]
    for distance in range(reach_blocks):
        lower = (reach_blocks - (distance + 1)) * tok_rows
        key_back, value_back = passed_along(
            shortened((key_terms[lower : lower + tok_rows], value_terms[lower : lower + tok_rows])),
            "seq",
            -(distance + 1),
        )
        key_gradient = key_gradient + key_back
        value_gradient = value_gradient + value_back
    key_gradient = key_gradient.reshape(tok_rows, -1).astype(jnp.bfloat16)
    value_gradient = value_gradient.reshape(tok_rows, -1).astype(jnp.bfloat16)
    return (projected, query_gradient, key_gradient, value_gradient)


def solution(mesh):
    return jax.shard_map(
        per_device,
        mesh=mesh,
        in_specs=(
            P("seq", "head"),
            P("seq", "head"),
            P("seq", "head"),
            P("head", None),
            P(("seq", "head"), None),
        ),
        out_specs=(P(("seq", "head"), None), P("seq", "head"), P("seq", "head"), P("seq", "head")),
        check_vma=False,
    )
```

profile of v0, /device:TPU:0, one launch (start us, length us, event | category | flops | bytes accessed | tf_op | source)
XLA Modules:
  0.0 114.5 jit_solution(4000072810786523243)
XLA Ops:
  7.2 0.0 copy-start.4
  7.2 0.0 all-gather.2.cloned.1.call-start
  7.2 0.7 all-gather.2.cloned.1.call-update
  7.9 0.0 reduce-scatter.2.cloned.1.call-start
  8.0 1.0 copy.24
  9.0 5.9 %collective-permute-start.4 = (bf16[256,256]{0,1:T(8,128)(2,1)S(1)}, bf16[256,256]{0,1:T(8,128)(2,1)S(1)}, u32[]{:S(2)}, u32[]{:S(2)}) collective-permute-start(bf16[256,256]{0,1:T(8,128)(2,1)S(1)} %copy.24), channel_id=1, source_target_pairs={{0,16},{4,20},{8,24},{12,28},{1,17},{5,21},{9,25},{13,29},{2,18},{... | collective-permute-start | bytes 393224 | tf_op jit(solution)/shard_map/ppermute | solution.py:16
  14.9 4.4 %collective-permute-start.5 = (bf16[256,256]{0,1:T(8,128)(2,1)S(1)}, bf16[256,256]{0,1:T(8,128)(2,1)S(1)}, u32[]{:S(2)}, u32[]{:S(2)}) collective-permute-start(bf16[256,256]{0,1:T(8,128)(2,1)S(1)} %copy.24), channel_id=1, source_target_pairs={{0,12},{4,16},{8,20},{12,24},{16,28},{1,13},{5,17},{9,21},{13,25},... | collective-permute-start | bytes 393224 | tf_op jit(solution)/shard_map/ppermute | solution.py:16
  19.3 1.3 %collective-permute-start.6 = (bf16[256,256]{0,1:T(8,128)(2,1)S(1)}, bf16[256,256]{0,1:T(8,128)(2,1)S(1)}, u32[]{:S(2)}, u32[]{:S(2)}) collective-permute-start(bf16[256,256]{0,1:T(8,128)(2,1)S(1)} %copy.24), channel_id=1, source_target_pairs={{0,8},{4,12},{8,16},{12,20},{16,24},{20,28},{1,9},{5,13},{9,17},{1... | collective-permute-start | bytes 393224 | tf_op jit(solution)/shard_map/ppermute | solution.py:16
  20.6 1.9 %collective-permute-start = (bf16[256,256]{1,0:T(8,128)(2,1)}, bf16[256,256]{1,0:T(8,128)(2,1)S(1)}, u32[]{:S(2)}, u32[]{:S(2)}) collective-permute-start(bf16[256,256]{1,0:T(8,128)(2,1)} %param.7), channel_id=1, source_target_pairs={{0,16},{4,20},{8,24},{12,28},{1,17},{5,21},{9,25},{13,29},{2,18},{... | collective-permute-start | bytes 393224 | tf_op jit(solution)/shard_map/ppermute | solution.py:16
  22.6 1.9 %collective-permute-start.1 = (bf16[256,256]{1,0:T(8,128)(2,1)}, bf16[256,256]{1,0:T(8,128)(2,1)S(1)}, u32[]{:S(2)}, u32[]{:S(2)}) collective-permute-start(bf16[256,256]{1,0:T(8,128)(2,1)} %param.7), channel_id=1, source_target_pairs={{0,12},{4,16},{8,20},{12,24},{16,28},{1,13},{5,17},{9,21},{13,25},... | collective-permute-start | bytes 393224 | tf_op jit(solution)/shard_map/ppermute | solution.py:16
  24.5 0.4 fusion.7
  24.9 1.1 copy.57
  26.0 0.0 copy-start.2
  26.0 2.9 %collective-permute-done = bf16[256,256]{1,0:T(8,128)(2,1)S(1)} collective-permute-done((bf16[256,256]{1,0:T(8,128)(2,1)}, bf16[256,256]{1,0:T(8,128)(2,1)S(1)}, u32[]{:S(2)}, u32[]{:S(2)}) %collective-permute-start) | collective-permute-done | bytes 131104 | tf_op jit(solution)/shard_map/ppermute | solution.py:16
  28.9 6.4 %collective-permute-start.2 = (bf16[256,256]{1,0:T(8,128)(2,1)}, bf16[256,256]{1,0:T(8,128)(2,1)S(1)}, u32[]{:S(2)}, u32[]{:S(2)}) collective-permute-start(bf16[256,256]{1,0:T(8,128)(2,1)} %param.7), channel_id=1, source_target_pairs={{0,8},{4,12},{8,16},{12,20},{16,24},{20,28},{1,9},{5,13},{9,17},{1... | collective-permute-start | bytes 393224 | tf_op jit(solution)/shard_map/ppermute | solution.py:16
  35.3 0.0 collective-permute-done.1
  35.3 9.0 %collective-permute-start.3 = (bf16[256,256]{1,0:T(8,128)(2,1)}, bf16[256,256]{1,0:T(8,128)(2,1)S(1)}, u32[]{:S(2)}, u32[]{:S(2)}) collective-permute-start(bf16[256,256]{1,0:T(8,128)(2,1)} %param.7), channel_id=1, source_target_pairs={{0,4},{4,8},{8,12},{12,16},{16,20},{20,24},{24,28},{1,5},{5,9},{9,... | collective-permute-start | bytes 393224 | tf_op jit(solution)/shard_map/ppermute | solution.py:16
  44.3 0.0 collective-permute-done.2
  44.4 3.9 %collective-permute-start.7 = (bf16[256,256]{0,1:T(8,128)(2,1)S(1)}, bf16[256,256]{0,1:T(8,128)(2,1)S(1)}, u32[]{:S(2)}, u32[]{:S(2)}) collective-permute-start(bf16[256,256]{0,1:T(8,128)(2,1)S(1)} %copy.24), channel_id=1, source_target_pairs={{0,4},{4,8},{8,12},{12,16},{16,20},{20,24},{24,28},{1,5},{5,9},{9,... | collective-permute-start | bytes 393224 | tf_op jit(solution)/shard_map/ppermute | solution.py:16
  48.3 0.0 collective-permute-done.3
  48.3 0.0 copy-done.4
  48.4 0.0 collective-permute-done.4
  48.4 0.0 collective-permute-done.5
  48.4 0.2 copy.23
  48.7 0.0 collective-permute-done.6
  48.7 2.1 %collective-permute-done.7 = bf16[256,256]{0,1:T(8,128)(2,1)S(1)} collective-permute-done((bf16[256,256]{0,1:T(8,128)(2,1)S(1)}, bf16[256,256]{0,1:T(8,128)(2,1)S(1)}, u32[]{:S(2)}, u32[]{:S(2)}) %collective-permute-start.7) | collective-permute-done | bytes 131104 | tf_op jit(solution)/shard_map/ppermute | solution.py:16
  50.8 0.0 copy-start
  50.8 1.0 fusion.19
  51.9 0.7 exponential_reduce_fusion
  52.6 0.8 exponential_convert_fusion
  53.4 0.0 all-gather.2.cloned.1.call-done
  53.4 5.7 %convolution_convert_fusion.2 = bf16[256,512]{1,0:T(8,128)(2,1)} fusion(bf16[256,5376]{1,0:T(8,128)(2,1)} %all-gather.2.cloned.1.call-done, bf16[512,5376]{1,0:T(8,128)(2,1)} %param.8), kind=kOutput, calls=%fused_computation.19 | convolution fusion | flops 1409417216 | bytes 8519680 | tf_op jit(solution)/shard_map/dot_general | solution.py:70
  59.1 1.1 copy.32
  60.2 0.5 multiply_reduce_fusion
  60.7 5.7 %convolution_convert_fusion = bf16[256,5376]{1,0:T(8,128)(2,1)} fusion(bf16[256,512]{0,1:T(8,128)(2,1)S(1)} %bitcast.75, bf16[512,5376]{1,0:T(8,128)(2,1)} %param.8), kind=kOutput, calls=%fused_computation | convolution fusion | flops 1410662400 | bytes 8519680 | tf_op jit(solution)/shard_map/dot_general | solution.py:65
  66.5 0.0 reduce-scatter.2.cloned.1.call-update
  66.5 2.0 %fusion.21 = (bf16[1280,2,128]{0,2,1:T(8,128)(2,1)S(1)}, f32[1280,2,128]{0,2,1:T(8,128)}) fusion(bf16[256,2,2,128]{0,3,2,1:T(8,128)(2,1)S(1)} %bitcast.69, bf16[2,2,256,1280]{2,3,1,0:T(8,128)(2,1)S(1)} %exponential_convert_fusion), kind=kOutput, calls=%fused_computation.48 | convolution fusion | flops 335872000 | bytes 4849664 | tf_op jit(solution)/shard_map/cqiz,icqf->zcf/dot_general | solution.py:99
  68.5 0.8 fusion.17
  69.3 1.3 %collective-permute-start.12 = (bf16[256,2,128]{0,2,1:T(8,128)(2,1)}, bf16[256,2,128]{0,2,1:T(8,128)(2,1)}, u32[]{:S(2)}, u32[]{:S(2)}) collective-permute-start(bf16[256,2,128]{0,2,1:T(8,128)(2,1)} %get-tuple-element.12), channel_id=1, source_target_pairs={{4,0},{8,4},{12,8},{16,12},{20,16},{24,20},{28,24},{5,1},{9,5},{13... | collective-permute-start | bytes 393224 | tf_op jit(solution)/shard_map/ppermute | solution.py:16
  70.6 1.3 %collective-permute-start.13 = (bf16[256,2,128]{0,2,1:T(8,128)(2,1)}, bf16[256,2,128]{0,2,1:T(8,128)(2,1)}, u32[]{:S(2)}, u32[]{:S(2)}) collective-permute-start(bf16[256,2,128]{0,2,1:T(8,128)(2,1)} %get-tuple-element.15), channel_id=1, source_target_pairs={{8,0},{12,4},{16,8},{20,12},{24,16},{28,20},{9,1},{13,5},{17,9},{2... | collective-permute-start | bytes 393224 | tf_op jit(solution)/shard_map/ppermute | solution.py:16
  71.9 1.3 %collective-permute-start.14 = (bf16[256,2,128]{0,2,1:T(8,128)(2,1)}, bf16[256,2,128]{0,2,1:T(8,128)(2,1)}, u32[]{:S(2)}, u32[]{:S(2)}) collective-permute-start(bf16[256,2,128]{0,2,1:T(8,128)(2,1)} %get-tuple-element.14), channel_id=1, source_target_pairs={{12,0},{16,4},{20,8},{24,12},{28,16},{13,1},{17,5},{21,9},{25,13},... | collective-permute-start | bytes 393224 | tf_op jit(solution)/shard_map/ppermute | solution.py:16
  73.2 1.3 %collective-permute-start.15 = (bf16[256,2,128]{0,2,1:T(8,128)(2,1)}, bf16[256,2,128]{0,2,1:T(8,128)(2,1)}, u32[]{:S(2)}, u32[]{:S(2)}) collective-permute-start(bf16[256,2,128]{0,2,1:T(8,128)(2,1)} %get-tuple-element.13), channel_id=1, source_target_pairs={{16,0},{20,4},{24,8},{28,12},{17,1},{21,5},{25,9},{29,13},{18,2},{... | collective-permute-start | bytes 393224 | tf_op jit(solution)/shard_map/ppermute | solution.py:16
  74.5 0.9 fusion.1
  75.4 0.2 copy-done.1
  75.6 0.5 fusion.8
  76.2 0.4 copy-done.3
  76.6 1.0 fusion.20
  77.7 1.3 %collective-permute-start.10 = (bf16[256,2,128]{0,2,1:T(8,128)(2,1)S(1)}, bf16[256,2,128]{0,2,1:T(8,128)(2,1)S(1)}, u32[]{:S(2)}, u32[]{:S(2)}) collective-permute-start(bf16[256,2,128]{0,2,1:T(8,128)(2,1)S(1)} %get-tuple-element.18), channel_id=1, source_target_pairs={{12,0},{16,4},{20,8},{24,12},{28,16},{13,1},{17,5},{21,9},{25,13},... | collective-permute-start | bytes 393224 | tf_op jit(solution)/shard_map/ppermute | solution.py:16
  79.0 0.8 copy.39
  79.8 0.0 collective-permute-done.12
  79.8 1.3 %collective-permute-start.11 = (bf16[256,2,128]{0,2,1:T(8,128)(2,1)S(1)}, bf16[256,2,128]{0,2,1:T(8,128)(2,1)S(1)}, u32[]{:S(2)}, u32[]{:S(2)}) collective-permute-start(bf16[256,2,128]{0,2,1:T(8,128)(2,1)S(1)} %get-tuple-element.17), channel_id=1, source_target_pairs={{16,0},{20,4},{24,8},{28,12},{17,1},{21,5},{25,9},{29,13},{18,2},{... | collective-permute-start | bytes 393224 | tf_op jit(solution)/shard_map/ppermute | solution.py:16
  81.1 0.1 collective-permute-done.13
  81.2 1.3 %collective-permute-start.8 = (bf16[256,2,128]{0,2,1:T(8,128)(2,1)S(1)}, bf16[256,2,128]{0,2,1:T(8,128)(2,1)S(1)}, u32[]{:S(2)}, u32[]{:S(2)}) collective-permute-start(bf16[256,2,128]{0,2,1:T(8,128)(2,1)S(1)} %get-tuple-element.16), channel_id=1, source_target_pairs={{4,0},{8,4},{12,8},{16,12},{20,16},{24,20},{28,24},{5,1},{9,5},{13... | collective-permute-start | bytes 393224 | tf_op jit(solution)/shard_map/ppermute | solution.py:16
  82.5 1.3 %collective-permute-done.14 = bf16[256,2,128]{0,2,1:T(8,128)(2,1)} collective-permute-done((bf16[256,2,128]{0,2,1:T(8,128)(2,1)}, bf16[256,2,128]{0,2,1:T(8,128)(2,1)}, u32[]{:S(2)}, u32[]{:S(2)}) %collective-permute-start.14) | collective-permute-done | bytes 131104 | tf_op jit(solution)/shard_map/ppermute | solution.py:16
  83.8 1.3 %collective-permute-start.9 = (bf16[256,2,128]{0,2,1:T(8,128)(2,1)S(1)}, bf16[256,2,128]{0,2,1:T(8,128)(2,1)S(1)}, u32[]{:S(2)}, u32[]{:S(2)}) collective-permute-start(bf16[256,2,128]{0,2,1:T(8,128)(2,1)S(1)} %get-tuple-element.19), channel_id=1, source_target_pairs={{8,0},{12,4},{16,8},{20,12},{24,16},{28,20},{9,1},{13,5},{17,9},{2... | collective-permute-start | bytes 393224 | tf_op jit(solution)/shard_map/ppermute | solution.py:16
  85.1 16.0 %collective-permute-done.15 = bf16[256,2,128]{0,2,1:T(8,128)(2,1)} collective-permute-done((bf16[256,2,128]{0,2,1:T(8,128)(2,1)}, bf16[256,2,128]{0,2,1:T(8,128)(2,1)}, u32[]{:S(2)}, u32[]{:S(2)}) %collective-permute-start.15) | collective-permute-done | bytes 131104 | tf_op jit(solution)/shard_map/ppermute | solution.py:16
  101.1 1.3 %fusion.12 = bf16[256,2,128]{0,2,1:T(8,128)(2,1)S(1)} fusion(f32[1280,2,128]{0,2,1:T(8,128)} %get-tuple-element.27, bf16[256,2,128]{0,2,1:T(8,128)(2,1)} %collective-permute-done.15, bf16[256,2,128]{0,2,1:T(8,128)(2,1)} %collective-permute-done.14, bf16[256,2,128]{0,2,1:T(8,128)(2,1)} %collective-permute-done.13, bf16[256,2,128]{0,2,1:T(8,128)(2,1)} %collective-permute-done.12), kind=kLoop, calls=%fused_computation.25 | loop fusion | flops 589824 | bytes 917504 | tf_op jit(solution)/shard_map/convert_element_type | solution.py:114
  102.3 0.8 copy.41
  103.1 0.0 collective-permute-done.10
  103.1 3.4 %collective-permute-done.11 = bf16[256,2,128]{0,2,1:T(8,128)(2,1)S(1)} collective-permute-done((bf16[256,2,128]{0,2,1:T(8,128)(2,1)S(1)}, bf16[256,2,128]{0,2,1:T(8,128)(2,1)S(1)}, u32[]{:S(2)}, u32[]{:S(2)}) %collective-permute-start.11) | collective-permute-done | bytes 131104 | tf_op jit(solution)/shard_map/ppermute | solution.py:16
  106.5 0.0 collective-permute-done.8
  106.5 0.2 collective-permute-done.9
  106.8 0.1 fusion.16
  106.9 0.8 copy.40
  (19 shorter events, 0.2 us)
Async XLA Ops:
  7.2 41.2 %copy-start.4 = (bf16[256,256]{1,0:T(8,128)(2,1)S(1)}, bf16[256,256]{1,0:T(8,128)(2,1)}, u32[]{:S(2)}) copy-start(bf16[256,256]{1,0:T(8,128)(2,1)} %param.7) | copy-start | bytes 393220
  7.2 46.2 %all-gather.2.cloned.1.call-start = ((), (), s32[]{:S(2)}) async-start(), calls=%async_computation.2 | async-start | bytes 3440640 | tf_op jit(solution)/shard_map/all_gather | solution.py:71
  7.9 99.7 %reduce-scatter.2.cloned.1.call-start = ((), (), s32[]{:S(2)}) async-start(), calls=%async_computation.1 | async-start | bytes 3440640 | tf_op jit(solution)/shard_map/reduce_scatter | solution.py:64
  9.0 39.4 %collective-permute-start.4 = (bf16[256,256]{0,1:T(8,128)(2,1)S(1)}, bf16[256,256]{0,1:T(8,128)(2,1)S(1)}, u32[]{:S(2)}, u32[]{:S(2)}) collective-permute-start(bf16[256,256]{0,1:T(8,128)(2,1)S(1)} %copy.24), channel_id=1, source_target_pairs={{0,16},{4,20},{8,24},{12,28},{1,17},{5,21},{9,25},{13,29},{2,18},{... | collective-permute-start | bytes 393224 | tf_op jit(solution)/shard_map/ppermute | solution.py:16
  14.9 33.5 %collective-permute-start.5 = (bf16[256,256]{0,1:T(8,128)(2,1)S(1)}, bf16[256,256]{0,1:T(8,128)(2,1)S(1)}, u32[]{:S(2)}, u32[]{:S(2)}) collective-permute-start(bf16[256,256]{0,1:T(8,128)(2,1)S(1)} %copy.24), channel_id=1, source_target_pairs={{0,12},{4,16},{8,20},{12,24},{16,28},{1,13},{5,17},{9,21},{13,25},... | collective-permute-start | bytes 393224 | tf_op jit(solution)/shard_map/ppermute | solution.py:16
  19.3 29.3 %collective-permute-start.6 = (bf16[256,256]{0,1:T(8,128)(2,1)S(1)}, bf16[256,256]{0,1:T(8,128)(2,1)S(1)}, u32[]{:S(2)}, u32[]{:S(2)}) collective-permute-start(bf16[256,256]{0,1:T(8,128)(2,1)S(1)} %copy.24), channel_id=1, source_target_pairs={{0,8},{4,12},{8,16},{12,20},{16,24},{20,28},{1,9},{5,13},{9,17},{1... | collective-permute-start | bytes 393224 | tf_op jit(solution)/shard_map/ppermute | solution.py:16
  20.6 8.3 %collective-permute-start = (bf16[256,256]{1,0:T(8,128)(2,1)}, bf16[256,256]{1,0:T(8,128)(2,1)S(1)}, u32[]{:S(2)}, u32[]{:S(2)}) collective-permute-start(bf16[256,256]{1,0:T(8,128)(2,1)} %param.7), channel_id=1, source_target_pairs={{0,16},{4,20},{8,24},{12,28},{1,17},{5,21},{9,25},{13,29},{2,18},{... | collective-permute-start | bytes 393224 | tf_op jit(solution)/shard_map/ppermute | solution.py:16
  22.6 12.8 %collective-permute-start.1 = (bf16[256,256]{1,0:T(8,128)(2,1)}, bf16[256,256]{1,0:T(8,128)(2,1)S(1)}, u32[]{:S(2)}, u32[]{:S(2)}) collective-permute-start(bf16[256,256]{1,0:T(8,128)(2,1)} %param.7), channel_id=1, source_target_pairs={{0,12},{4,16},{8,20},{12,24},{16,28},{1,13},{5,17},{9,21},{13,25},... | collective-permute-start | bytes 393224 | tf_op jit(solution)/shard_map/ppermute | solution.py:16
  26.0 25.8 %copy-start.2 = (bf16[256,512]{0,1:T(8,128)(2,1)}, bf16[256,512]{0,1:T(8,128)(2,1)S(1)}, u32[]{:S(2)}) copy-start(bf16[256,512]{0,1:T(8,128)(2,1)S(1)} %copy.57) | copy-start | bytes 786436
  28.9 15.4 %collective-permute-start.2 = (bf16[256,256]{1,0:T(8,128)(2,1)}, bf16[256,256]{1,0:T(8,128)(2,1)S(1)}, u32[]{:S(2)}, u32[]{:S(2)}) collective-permute-start(bf16[256,256]{1,0:T(8,128)(2,1)} %param.7), channel_id=1, source_target_pairs={{0,8},{4,12},{8,16},{12,20},{16,24},{20,28},{1,9},{5,13},{9,17},{1... | collective-permute-start | bytes 393224 | tf_op jit(solution)/shard_map/ppermute | solution.py:16
  35.3 13.0 %collective-permute-start.3 = (bf16[256,256]{1,0:T(8,128)(2,1)}, bf16[256,256]{1,0:T(8,128)(2,1)S(1)}, u32[]{:S(2)}, u32[]{:S(2)}) collective-permute-start(bf16[256,256]{1,0:T(8,128)(2,1)} %param.7), channel_id=1, source_target_pairs={{0,4},{4,8},{8,12},{12,16},{16,20},{20,24},{24,28},{1,5},{5,9},{9,... | collective-permute-start | bytes 393224 | tf_op jit(solution)/shard_map/ppermute | solution.py:16
  44.4 6.4 %collective-permute-start.7 = (bf16[256,256]{0,1:T(8,128)(2,1)S(1)}, bf16[256,256]{0,1:T(8,128)(2,1)S(1)}, u32[]{:S(2)}, u32[]{:S(2)}) collective-permute-start(bf16[256,256]{0,1:T(8,128)(2,1)S(1)} %copy.24), channel_id=1, source_target_pairs={{0,4},{4,8},{8,12},{12,16},{16,20},{20,24},{24,28},{1,5},{5,9},{9,... | collective-permute-start | bytes 393224 | tf_op jit(solution)/shard_map/ppermute | solution.py:16
  50.8 1.0 copy-start
  69.3 10.5 %collective-permute-start.12 = (bf16[256,2,128]{0,2,1:T(8,128)(2,1)}, bf16[256,2,128]{0,2,1:T(8,128)(2,1)}, u32[]{:S(2)}, u32[]{:S(2)}) collective-permute-start(bf16[256,2,128]{0,2,1:T(8,128)(2,1)} %get-tuple-element.12), channel_id=1, source_target_pairs={{4,0},{8,4},{12,8},{16,12},{20,16},{24,20},{28,24},{5,1},{9,5},{13... | collective-permute-start | bytes 393224 | tf_op jit(solution)/shard_map/ppermute | solution.py:16
  70.6 10.6 %collective-permute-start.13 = (bf16[256,2,128]{0,2,1:T(8,128)(2,1)}, bf16[256,2,128]{0,2,1:T(8,128)(2,1)}, u32[]{:S(2)}, u32[]{:S(2)}) collective-permute-start(bf16[256,2,128]{0,2,1:T(8,128)(2,1)} %get-tuple-element.15), channel_id=1, source_target_pairs={{8,0},{12,4},{16,8},{20,12},{24,16},{28,20},{9,1},{13,5},{17,9},{2... | collective-permute-start | bytes 393224 | tf_op jit(solution)/shard_map/ppermute | solution.py:16
  71.9 11.9 %collective-permute-start.14 = (bf16[256,2,128]{0,2,1:T(8,128)(2,1)}, bf16[256,2,128]{0,2,1:T(8,128)(2,1)}, u32[]{:S(2)}, u32[]{:S(2)}) collective-permute-start(bf16[256,2,128]{0,2,1:T(8,128)(2,1)} %get-tuple-element.14), channel_id=1, source_target_pairs={{12,0},{16,4},{20,8},{24,12},{28,16},{13,1},{17,5},{21,9},{25,13},... | collective-permute-start | bytes 393224 | tf_op jit(solution)/shard_map/ppermute | solution.py:16
  73.2 27.9 %collective-permute-start.15 = (bf16[256,2,128]{0,2,1:T(8,128)(2,1)}, bf16[256,2,128]{0,2,1:T(8,128)(2,1)}, u32[]{:S(2)}, u32[]{:S(2)}) collective-permute-start(bf16[256,2,128]{0,2,1:T(8,128)(2,1)} %get-tuple-element.13), channel_id=1, source_target_pairs={{16,0},{20,4},{24,8},{28,12},{17,1},{21,5},{25,9},{29,13},{18,2},{... | collective-permute-start | bytes 393224 | tf_op jit(solution)/shard_map/ppermute | solution.py:16
  74.5 1.1 copy-start.1
  75.6 1.0 copy-start.3
  77.7 25.4 %collective-permute-start.10 = (bf16[256,2,128]{0,2,1:T(8,128)(2,1)S(1)}, bf16[256,2,128]{0,2,1:T(8,128)(2,1)S(1)}, u32[]{:S(2)}, u32[]{:S(2)}) collective-permute-start(bf16[256,2,128]{0,2,1:T(8,128)(2,1)S(1)} %get-tuple-element.18), channel_id=1, source_target_pairs={{12,0},{16,4},{20,8},{24,12},{28,16},{13,1},{17,5},{21,9},{25,13},... | collective-permute-start | bytes 393224 | tf_op jit(solution)/shard_map/ppermute | solution.py:16
  79.8 26.7 %collective-permute-start.11 = (bf16[256,2,128]{0,2,1:T(8,128)(2,1)S(1)}, bf16[256,2,128]{0,2,1:T(8,128)(2,1)S(1)}, u32[]{:S(2)}, u32[]{:S(2)}) collective-permute-start(bf16[256,2,128]{0,2,1:T(8,128)(2,1)S(1)} %get-tuple-element.17), channel_id=1, source_target_pairs={{16,0},{20,4},{24,8},{28,12},{17,1},{21,5},{25,9},{29,13},{18,2},{... | collective-permute-start | bytes 393224 | tf_op jit(solution)/shard_map/ppermute | solution.py:16
  81.2 25.3 %collective-permute-start.8 = (bf16[256,2,128]{0,2,1:T(8,128)(2,1)S(1)}, bf16[256,2,128]{0,2,1:T(8,128)(2,1)S(1)}, u32[]{:S(2)}, u32[]{:S(2)}) collective-permute-start(bf16[256,2,128]{0,2,1:T(8,128)(2,1)S(1)} %get-tuple-element.16), channel_id=1, source_target_pairs={{4,0},{8,4},{12,8},{16,12},{20,16},{24,20},{28,24},{5,1},{9,5},{13... | collective-permute-start | bytes 393224 | tf_op jit(solution)/shard_map/ppermute | solution.py:16
  83.8 23.0 %collective-permute-start.9 = (bf16[256,2,128]{0,2,1:T(8,128)(2,1)S(1)}, bf16[256,2,128]{0,2,1:T(8,128)(2,1)S(1)}, u32[]{:S(2)}, u32[]{:S(2)}) collective-permute-start(bf16[256,2,128]{0,2,1:T(8,128)(2,1)S(1)} %get-tuple-element.19), channel_id=1, source_target_pairs={{8,0},{12,4},{16,8},{20,12},{24,16},{28,20},{9,1},{13,5},{17,9},{2... | collective-permute-start | bytes 393224 | tf_op jit(solution)/shard_map/ppermute | solution.py:16
Sparse Core Ops, SparseCore 0:
  9.6 28.9 all-gather.1
  66.6 38.2 reduce-scatter.1
where the time goes:
time: 116 us; the launch traced here: 114 us
  starting transfers between devices  45.1 us (39%)
  waiting for transfers between devices  26.8 us (23%)
  matrix products  17.5 us (15%)
  between operations  14.5 us (12%)
  local copies, waits for them, and re-layouts  7.38 us (6%)
  other arithmetic  3.2 us (3%)
    ppermute x16, starting transfers between devices, passed_along(): lax.ppermute(value, axis, [(source, source + steps) for source in range(f...  45.1 us
    ppermute x16, waiting for transfers between devices, passed_along(): lax.ppermute(value, axis, [(source, source + steps) for source in range(f...  26.1 us
    dot_general x1, matrix products, per_device(): jnp.dot(attended_flat, out_weight, preferred_element_type=jnp.float32)  5.75 us
    dot_general x1, matrix products, per_device(): lax.dot_general(lax.all_gather(out_grad, 'head', axis=0, tiled=True), out...  5.72 us
    unnamed x22, local copies, waits for them, and re-layouts  4.13 us
  transfers between devices with their start and end apart: 18, of which 7 were waited for; matrix products, arithmetic and copies ran while one was open for 12% of the time, Pallas kernels for 0%

commit v1 on v0

v1 whole, which is shorter than its diff:
```python
import jax
import jax.numpy as jnp
from jax import lax
from jax.experimental import pallas as pl
from jax.experimental.pallas import tpu as pltpu
from jax.sharding import PartitionSpec as P

HEAD_SIZE = 128
WIN = 1024
LOGIT_SCALE = 168.0 ** (-0.5)
LOG2E = 1.4426950408889634
NEG = -1e30
F32 = jnp.float32
BF16 = jnp.bfloat16
VMEM = pl.BlockSpec(memory_space=pltpu.VMEM)


def dot(a, b, ca, cb):
    return lax.dot_general(a, b, (((ca,), (cb,)), ((), ())), preferred_element_type=F32)


def shifted(value, steps):
    count = lax.axis_size("seq")
    first, last = (max(0, -steps), min(count, count - steps))
    return lax.ppermute(value, "seq", [(i, i + steps) for i in range(first, last)])


def swapped(value, axis, bit):
    count = lax.axis_size(axis)
    return lax.ppermute(value, axis, [(i, i ^ bit) for i in range(count)])


def to_parity(value, parity):
    count = lax.axis_size("seq")
    return lax.ppermute(value, "seq", [(i ^ 1, i) for i in range(parity, count, 2)])


def group_rows(group, head, size):
    return pl.ds(pl.multiple_of(jnp.bitwise_xor(group, head) * size, size), size)


def stacked(mat, kv_head):
    low = 2 * kv_head * HEAD_SIZE
    return jnp.concatenate([mat[:, low : low + HEAD_SIZE], mat[:, low + HEAD_SIZE : low + 2 * HEAD_SIZE]], 0)


def forward_kernel(q_ref, k_ref, v_ref, r1_ref, r2_ref, x1_ref, p0_ref, x2_ref, o_ref, p_ref):
    seq, head = lax.axis_index("seq"), lax.axis_index("head")
    odd = lax.rem(seq, 2) == 1
    tok = q_ref.shape[0]
    kv_heads = k_ref.shape[1] // HEAD_SIZE
    kv_cols = k_ref.shape[1]
    size = tok // 4
    q_rel = jnp.concatenate([q_ref[group_rows(g, head, size), :] for g in range(4)], 0)
    key_pos = lax.broadcasted_iota(jnp.int32, (tok, 2 * tok), 0)
    lane = lax.broadcasted_iota(jnp.int32, (tok, 2 * tok), 1)
    query_pos = jnp.bitwise_xor(jnp.bitwise_and(lane, tok - 1), head * size)
    causal = query_pos >= key_pos
    near = jnp.where(seq >= 2, 0.0, NEG).astype(F32)
    far = jnp.where(seq >= 4, 0.0, NEG).astype(F32)
    mixed = jnp.where(jnp.logical_or(odd, seq >= 4), 0.0, NEG).astype(F32)
    biases = [None, near, far, near, mixed]
    scale = LOGIT_SCALE * LOG2E
    for g in range(kv_heads):
        kc = slice(g * HEAD_SIZE, (g + 1) * HEAD_SIZE)
        vc = slice(kv_cols + g * HEAD_SIZE, kv_cols + (g + 1) * HEAD_SIZE)
        qg = stacked(q_rel, g)
        key_blocks = [k_ref[:, kc], r1_ref[:, kc], r2_ref[:, kc], x1_ref[:, kc], jnp.where(odd, p0_ref[:, kc], x2_ref[:, kc])]
        value_blocks = [v_ref[:, kc], r1_ref[:, vc], r2_ref[:, vc], x1_ref[:, vc], jnp.where(odd, p0_ref[:, vc], x2_ref[:, vc])]
        scores = [dot(kb, qg, 1, 1) for kb in key_blocks]
        scores[0] = jnp.where(causal, scores[0], NEG)
        scores[2] = jnp.where(causal, NEG, scores[2])
        tops = [jnp.max(sb, axis=0, keepdims=True) for sb in scores]
        tops = [t if b is None else t + b for t, b in zip(tops, biases)]
        top = tops[0]
        for t in tops[1:]:
            top = jnp.maximum(top, t)
        top = top * scale
        probs = [jnp.exp2(sb * scale - (top if b is None else top - b)) for sb, b in zip(scores, biases)]
        total = sum(jnp.sum(pb, axis=0, keepdims=True) for pb in probs)
        inv = 1.0 / total
        out = jnp.zeros((HEAD_SIZE, 2 * tok), F32)
        for b in range(5):
            pb = (probs[b] * inv).astype(BF16)
            p_ref[g, b] = pb
            out = out + dot(value_blocks[b], pb, 0, 0)
        out = out.T.astype(BF16)
        low = 2 * g * HEAD_SIZE
        o_ref[:, low : low + HEAD_SIZE] = out[:tok]
        o_ref[:, low + HEAD_SIZE : low + 2 * HEAD_SIZE] = out[tok:]


def backward_kernel(q_ref, k_ref, v_ref, r1_ref, r2_ref, x1_ref, p0_ref, x2_ref, p_ref, o_ref, d0_ref, d1_ref,
                    dq_ref, town_ref, t1_ref, t2_ref, tx_ref, tz_ref):
    seq, head = lax.axis_index("seq"), lax.axis_index("head")
    odd = lax.rem(seq, 2) == 1
    tok = q_ref.shape[0]
    kv_cols = k_ref.shape[1]
    kv_heads = kv_cols // HEAD_SIZE
    size = tok // 4
    q_rel = jnp.concatenate([q_ref[group_rows(g, head, size), :] for g in range(4)], 0)
    do_rel = jnp.concatenate([d0_ref[...], d1_ref[...]], 0)
    o_rel = o_ref[...]
    outs = [town_ref, t1_ref, t2_ref, tx_ref, tz_ref]
    for g in range(kv_heads):
        kc = slice(g * HEAD_SIZE, (g + 1) * HEAD_SIZE)
        vc = slice(kv_cols + g * HEAD_SIZE, kv_cols + (g + 1) * HEAD_SIZE)
        qg, dg, og = stacked(q_rel, g), stacked(do_rel, g), stacked(o_rel, g)
        key_blocks = [k_ref[:, kc], r1_ref[:, kc], r2_ref[:, kc], x1_ref[:, kc], jnp.where(odd, p0_ref[:, kc], x2_ref[:, kc])]
        value_blocks = [v_ref[:, kc], r1_ref[:, vc], r2_ref[:, vc], x1_ref[:, vc], jnp.where(odd, p0_ref[:, vc], x2_ref[:, vc])]
        delta = jnp.sum((dg.astype(F32) * og.astype(F32)).T, axis=0, keepdims=True)
        dq = jnp.zeros((HEAD_SIZE, 2 * tok), F32)
        for b in range(5):
            pb = p_ref[g, b]
            dp = dot(value_blocks[b], dg, 1, 1)
            ds = (pb.astype(F32) * (dp - delta)).astype(BF16)
            outs[b][:, vc] = dot(pb, dg, 1, 0).astype(outs[b].dtype)
            outs[b][:, kc] = (dot(ds, qg, 1, 0) * LOGIT_SCALE).astype(outs[b].dtype)
            dq = dq + dot(key_blocks[b], ds, 0, 0)
        dq = (dq * LOGIT_SCALE).T.astype(BF16)
        low = 2 * g * HEAD_SIZE
        for r in range(4):
            rows = group_rows(r, head, size)
            dq_ref[rows, low : low + HEAD_SIZE] = dq[r * size : (r + 1) * size]
            dq_ref[rows, low + HEAD_SIZE : low + 2 * HEAD_SIZE] = dq[tok + r * size : tok + (r + 1) * size]


def per_device(queries, keys, values, out_weight, out_grad):
    tok, q_cols = queries.shape
    kv_cols = keys.shape[1]
    kv_heads = kv_cols // HEAD_SIZE
    odd = lax.rem(lax.axis_index("seq"), 2) == 1
    params = pltpu.CompilerParams(vmem_limit_bytes=32 << 20)

    og_y = swapped(out_grad, "head", 2)
    own_kv = jnp.concatenate([keys, values], 1)
    r1 = shifted(own_kv, 2)
    p0 = to_parity(own_kv, 1)
    og_c = swapped(out_grad, "head", 1)
    r2 = shifted(r1, 2)
    x1 = swapped(r1, "seq", 1)
    x2 = to_parity(r2, 0)
    og_yc = swapped(og_y, "head", 1)

    attended, probs = pl.pallas_call(
        forward_kernel,
        out_shape=(
            jax.ShapeDtypeStruct((tok, q_cols), BF16),
            jax.ShapeDtypeStruct((kv_heads, 5, tok, 2 * tok), BF16),
        ),
        in_specs=[VMEM] * 8,
        out_specs=(VMEM, VMEM),
        compiler_params=params,
        name="attend",
    )(queries, keys, values, r1, r2, x1, p0, x2)

    half, size = tok // 2, tok // 4
    far_part = jnp.dot(attended[half:], out_weight, preferred_element_type=F32).astype(BF16)
    sent = swapped(far_part[size:], "head", 1)
    far_sum = (far_part[:size].astype(F32) + sent.astype(F32)).astype(BF16)
    near_part = jnp.dot(attended[:half], out_weight, preferred_element_type=F32).astype(BF16)
    from_y = swapped(far_sum, "head", 2)
    from_core = swapped(near_part[size:], "head", 1)
    projected = (near_part[:size].astype(F32) + from_core.astype(F32) + from_y.astype(F32)).astype(BF16)

    def back(rows):
        return dot(rows, out_weight, 1, 1).astype(BF16)

    near_grad = back(jnp.concatenate([out_grad, og_c], 0))
    far_grad = back(jnp.concatenate([og_y, og_yc], 0))

    block = jax.ShapeDtypeStruct((tok, 2 * kv_cols), BF16)
    query_gradient, t_own, t_1, t_2, t_x, t_z = pl.pallas_call(
        backward_kernel,
        out_shape=(
            jax.ShapeDtypeStruct((tok, q_cols), BF16),
            jax.ShapeDtypeStruct((tok, 2 * kv_cols), F32),
            block, block, block, block,
        ),
        in_specs=[VMEM] * 12,
        out_specs=(VMEM,) * 6,
        compiler_params=params,
        name="attend_grad",
    )(queries, keys, values, r1, r2, x1, p0, x2, probs, attended, near_grad, far_grad)

    def wide(a):
        return a.astype(F32)

    g = swapped(t_z, "seq", 1)
    zero = jnp.zeros_like(g)
    c1 = shifted((wide(t_2) + wide(jnp.where(odd, g, zero))).astype(BF16), -2)
    d1 = swapped(t_x, "seq", 1)
    e1 = shifted((wide(t_1) + wide(c1) + wide(d1)).astype(BF16), -2)
    own = (t_own + wide(e1) + wide(jnp.where(odd, zero, g))).astype(BF16)
    return (projected, query_gradient, own[:, :kv_cols], own[:, kv_cols:])


def solution(mesh):
    return jax.shard_map(
        per_device,
        mesh=mesh,
        in_specs=(
            P("seq", "head"),
            P("seq", "head"),
            P("seq", "head"),
            P("head", None),
            P(("seq", "head"), None),
        ),
        out_specs=(P(("seq", "head"), None), P("seq", "head"), P("seq", "head"), P("seq", "head")),
        check_vma=False,
    )
```

time: 116 us -> 79.2 us (0.68); the launches traced: 114 us -> 78.9 us
  starting transfers between devices: 45.1 us -> 22 us
  between operations: 14.5 us -> 0.88 us
  waiting for transfers between devices: 26.8 us -> 37.2 us
  matrix products: 17.5 us -> 8.34 us
  Pallas kernels: 0 us -> 6.28 us
  local copies, waits for them, and re-layouts: 7.38 us -> 2.66 us
  other arithmetic: 3.2 us -> 1.58 us
    ppermute x16 -> x15, starting transfers between devices: 45.1 us -> 22 us  [the longest x4 10.5 us: shifted(): lax.ppermute(value, 'seq', [(i, i + steps) for i in range(first, last)])]
    ppermute x16 -> x15, waiting for transfers between devices: 26.1 us -> 37.2 us  [the longest x4 17.7 us: shifted(): lax.ppermute(value, 'seq', [(i, i + steps) for i in range(first, last)])]
    dot_general x8 -> x4, matrix products: 17.5 us -> 8.34 us  [the longest x2 6.53 us: dot(): lax.dot_general(a, b, (((ca,), (cb,)), ((), ())), preferred_element_type=...]
    pallas_call x0 -> x2, Pallas kernels: none -> 6.28 us  [the longest x1 3.38 us: per_device(): pl.pallas_call(backward_kernel, out_shape=(jax.ShapeDtypeStruct((tok, q_c...]
    unnamed x22 -> x9, local copies, waits for them, and re-layouts: 4.13 us -> 0.94 us
  transfers between devices with their start and end apart: 18 -> 15, of which waited for: 7 -> 9; matrix products, arithmetic and copies ran while one was open for 12% -> 12% of each run, Pallas kernels for 0% -> 4%
where the time goes in v1:
time: 79.2 us; the launch traced here: 78.9 us
  waiting for transfers between devices  37.2 us (47%)
  starting transfers between devices  22 us (28%)
  matrix products  8.34 us (11%)
  Pallas kernels  6.28 us (8%)
  local copies, waits for them, and re-layouts  2.66 us (3%)
  other arithmetic  1.58 us (2%)
  between operations  0.88 us (1%)
    ppermute x4, waiting for transfers between devices, shifted(): lax.ppermute(value, 'seq', [(i, i + steps) for i in range(first, last)])  17.7 us
    ppermute x9, waiting for transfers between devices, swapped(): return lax.ppermute(value, axis, [(i, i ^ bit) for i in range(count)])  17.1 us
    ppermute x4, starting transfers between devices, shifted(): lax.ppermute(value, 'seq', [(i, i + steps) for i in range(first, last)])  10.5 us
    ppermute x9, starting transfers between devices, swapped(): return lax.ppermute(value, axis, [(i, i ^ bit) for i in range(count)])  6.83 us
    dot_general x2, matrix products, dot(): lax.dot_general(a, b, (((ca,), (cb,)), ((), ())), preferred_element_type=...  6.53 us
    ppermute x2, starting transfers between devices, to_parity(): lax.ppermute(value, 'seq', [(i ^ 1, i) for i in range(parity, count, 2)])  4.69 us
    pallas_call x1, Pallas kernels, per_device(): pl.pallas_call(backward_kernel, out_shape=(jax.ShapeDtypeStruct((tok, q_c...  3.38 us
    pallas_call x1, Pallas kernels, per_device(): pl.pallas_call(forward_kernel, out_shape=(jax.ShapeDtypeStruct((tok, q_co...  2.9 us
  transfers between devices with their start and end apart: 15, of which 9 were waited for; matrix products, arithmetic and copies ran while one was open for 12% of the time, Pallas kernels for 4%

profile of v1, /device:TPU:0, one launch (start us, length us, event | category | flops | bytes accessed | tf_op | source)
XLA Modules:
  0.0 78.9 jit_solution(17623797032402421990)
XLA Ops:
  0.6 3.0 %collective-permute-start.9 = (bf16[64,5376]{1,0:T(8,128)(2,1)}, bf16[64,5376]{1,0:T(8,128)(2,1)S(1)}, u32[]{:S(2)}, u32[]{:S(2)}) collective-permute-start(bf16[64,5376]{1,0:T(8,128)(2,1)} %param.9), channel_id=1, source_target_pairs={{0,2},{1,3},{2,0},{3,1},{4,6},{5,7},{6,4},{7,5},{8,10},{9,11},{10,... | collective-permute-start | bytes 2064392 | tf_op jit(solution)/shard_map/ppermute | solution.py:30
  3.7 0.0 collective-permute-start.8
  3.7 0.9 %constant_dynamic-update-slice_fusion.1 = bf16[256,512]{1,0:T(8,128)(2,1)S(1)} fusion(bf16[256,256]{1,0:T(8,128)(2,1)} %k_ref.3), kind=kLoop, calls=%fused_computation.20 | loop fusion | bytes 262144
  4.6 0.9 %constant_dynamic-update-slice_fusion = bf16[256,512]{1,0:T(8,128)(2,1)S(1)} fusion(bf16[256,512]{1,0:T(8,128)(2,1)S(1)} %constant_dynamic-update-slice_fusion.1, bf16[256,256]{1,0:T(8,128)(2,1)} %v_ref.3), kind=kLoop, calls=%fused_computation.19 | loop fusion | bytes 262144 | tf_op jit(solution)/shard_map/concatenate | solution.py:136
  5.5 3.5 %collective-permute-start = (bf16[256,512]{1,0:T(8,128)(2,1)S(1)}, bf16[256,512]{1,0:T(8,128)(2,1)S(1)}, u32[]{:S(2)}, u32[]{:S(2)}) collective-permute-start(bf16[256,512]{1,0:T(8,128)(2,1)S(1)} %constant_dynamic-update-slice_fusion), channel_id=1, source_target_pairs={{0,8},{4,12},{8,16},{12,20},{16,24},{20,28},{1,9},{5,13},{9,17},{1... | collective-permute-start | bytes 786440 | tf_op jit(solution)/shard_map/ppermute | solution.py:25
  9.0 6.2 %collective-permute-done.r1_ref = bf16[256,512]{1,0:T(8,128)(2,1)S(1)} collective-permute-done((bf16[256,512]{1,0:T(8,128)(2,1)S(1)}, bf16[256,512]{1,0:T(8,128)(2,1)S(1)}, u32[]{:S(2)}, u32[]{:S(2)}) %collective-permute-start) | collective-permute-done | bytes 262176 | tf_op jit(solution)/shard_map/ppermute | solution.py:25
  15.2 4.4 %collective-permute-start.1 = (bf16[256,512]{1,0:T(8,128)(2,1)S(1)}, bf16[256,512]{1,0:T(8,128)(2,1)S(1)}, u32[]{:S(2)}, u32[]{:S(2)}) collective-permute-start(bf16[256,512]{1,0:T(8,128)(2,1)S(1)} %collective-permute-done.r1_ref), channel_id=1, source_target_pairs={{0,8},{4,12},{8,16},{12,20},{16,24},{20,28},{1,9},{5,13},{9,17},{1... | collective-permute-start | bytes 786440 | tf_op jit(solution)/shard_map/ppermute | solution.py:25
  19.6 0.0 collective-permute-done.9
  19.6 0.1 collective-permute-start.10
  19.7 3.4 %collective-permute-start.3 = (bf16[256,512]{1,0:T(8,128)(2,1)S(1)}, bf16[256,512]{1,0:T(8,128)(2,1)S(1)}, u32[]{:S(2)}, u32[]{:S(2)}) collective-permute-start(bf16[256,512]{1,0:T(8,128)(2,1)S(1)} %constant_dynamic-update-slice_fusion), channel_id=1, source_target_pairs={{0,4},{8,12},{16,20},{24,28},{1,5},{9,13},{17,21},{25,29},{2,6},{1... | collective-permute-start | bytes 786440 | tf_op jit(solution)/shard_map/ppermute | solution.py:35
  23.1 0.0 copy-start
  23.1 0.0 copy-start.1
  23.1 0.0 copy-start.2
  23.2 0.0 copy-start.3
  23.2 0.1 collective-permute-start.2
  23.2 1.8 %collective-permute-done.1.r2_ref = bf16[256,512]{1,0:T(8,128)(2,1)S(1)} collective-permute-done((bf16[256,512]{1,0:T(8,128)(2,1)S(1)}, bf16[256,512]{1,0:T(8,128)(2,1)S(1)}, u32[]{:S(2)}, u32[]{:S(2)}) %collective-permute-start.1) | collective-permute-done | bytes 262176 | tf_op jit(solution)/shard_map/ppermute | solution.py:25
  25.0 1.3 %collective-permute-start.4 = (bf16[256,512]{1,0:T(8,128)(2,1)S(1)}, bf16[256,512]{1,0:T(8,128)(2,1)S(1)}, u32[]{:S(2)}, u32[]{:S(2)}) collective-permute-start(bf16[256,512]{1,0:T(8,128)(2,1)S(1)} %collective-permute-done.1.r2_ref), channel_id=1, source_target_pairs={{4,0},{12,8},{20,16},{28,24},{5,1},{13,9},{21,17},{29,25},{6,2},{1... | collective-permute-start | bytes 786440 | tf_op jit(solution)/shard_map/ppermute | solution.py:35
  26.3 0.0 collective-permute-done.8
  26.3 4.7 %fusion.11.d0_ref = bf16[128,512]{1,0:T(8,128)(2,1)S(1)} fusion(bf16[512,5376]{1,0:T(8,128)(2,1)} %param.8, bf16[64,5376]{1,0:T(8,128)(2,1)S(1)} %collective-permute-done.8, bf16[64,5376]{1,0:T(8,128)(2,1)} %param.9), kind=kOutput, calls=%fused_computation.13 | convolution fusion | flops 707461120 | bytes 7012352 | tf_op jit(solution)/shard_map/dot_general | solution.py:19
  31.0 0.0 collective-permute-done.3.p0_ref
  31.0 3.9 %collective-permute-done.2.x1_ref = bf16[256,512]{1,0:T(8,128)(2,1)S(1)} collective-permute-done((bf16[256,512]{1,0:T(8,128)(2,1)S(1)}, bf16[256,512]{1,0:T(8,128)(2,1)S(1)}, u32[]{:S(2)}, u32[]{:S(2)}) %collective-permute-start.2) | collective-permute-done | bytes 262176 | tf_op jit(solution)/shard_map/ppermute | solution.py:30
  34.9 2.4 %collective-permute-done.4.x2_ref = bf16[256,512]{1,0:T(8,128)(2,1)S(1)} collective-permute-done((bf16[256,512]{1,0:T(8,128)(2,1)S(1)}, bf16[256,512]{1,0:T(8,128)(2,1)S(1)}, u32[]{:S(2)}, u32[]{:S(2)}) %collective-permute-start.4) | collective-permute-done | bytes 262176 | tf_op jit(solution)/shard_map/ppermute | solution.py:35
  37.3 0.0 copy-done
  37.3 0.0 copy-done.1
  37.3 0.0 copy-done.2
  37.3 2.9 %attend.1 = (bf16[256,512]{1,0:T(8,128)(2,1)S(1)}, bf16[2,5,256,512]{3,2,1,0:T(8,128)(2,1)S(1)}) custom-call(bf16[256,512]{1,0:T(8,128)(2,1)S(1)} %copy-done.2, bf16[256,256]{1,0:T(8,128)(2,1)S(1)} %copy-done, bf16[256,256]{1,0:T(8,128)(2,1)S(1)} %copy-done.1, bf16[256,512]{1,0:T(8,128)(2,1)S(1)} %collective-permute-done.r1_ref, ...), custom_call_target="tpu_custom_call" | custom-call | tf_op jit(solution)/shard_map/attend/pallas_call | solution.py:145
  40.2 0.0 collective-permute-done.10
  40.2 0.0 copy-done.3
  40.2 1.9 %fusion.8.d1_ref = bf16[128,512]{1,0:T(8,128)(2,1)S(1)} fusion(bf16[512,5376]{1,0:T(8,128)(2,1)S(1)} %copy-done.3, bf16[64,5376]{1,0:T(8,128)(2,1)S(1)} %collective-permute-done.10, bf16[64,5376]{1,0:T(8,128)(2,1)S(1)} %collective-permute-done.9), kind=kOutput, calls=%fused_computation.12 | convolution fusion | flops 707461120 | bytes 7012352 | tf_op jit(solution)/shard_map/dot_general | solution.py:19
  42.1 3.4 %attend_grad.1 = (bf16[256,512]{1,0:T(8,128)(2,1)}, f32[256,512]{1,0:T(8,128)S(1)}, bf16[256,512]{1,0:T(8,128)(2,1)S(1)}, bf16[256,512]{1,0:T(8,128)(2,1)S(1)}, ...) custom-call(bf16[256,512]{1,0:T(8,128)(2,1)S(1)} %copy-done.2, bf16[256,256]{1,0:T(8,128)(2,1)S(1)} %copy-done, ...), custom_call_target="tpu_custom_call" | custom-call | tf_op jit(solution)/shard_map/attend_grad/pallas_call | solution.py:173
  45.5 0.1 collective-permute-start.11
  45.6 0.9 %convolution_convert_fusion = bf16[128,5376]{1,0:T(8,128)(2,1)S(1)} fusion(bf16[512,5376]{1,0:T(8,128)(2,1)S(1)} %copy-done.3, bf16[256,512]{1,0:T(8,128)(2,1)S(1)} %get-tuple-element.12.o_ref), kind=kOutput, calls=%fused_computation | convolution fusion | flops 705331200 | bytes 7012352 | tf_op jit(solution)/shard_map/dot_general | solution.py:158
  46.6 0.1 collective-permute-start.6
  46.6 2.0 %collective-permute-start.13 = (bf16[256,512]{1,0:T(8,128)(2,1)S(1)}, bf16[256,512]{1,0:T(8,128)(2,1)S(1)}, u32[]{:S(2)}, u32[]{:S(2)}) collective-permute-start(bf16[256,512]{1,0:T(8,128)(2,1)S(1)} %get-tuple-element.19), channel_id=1, source_target_pairs={{0,4},{4,0},{8,12},{12,8},{16,20},{20,16},{24,28},{28,24},{1,5},{5... | collective-permute-start | bytes 786440 | tf_op jit(solution)/shard_map/ppermute | solution.py:30
  48.6 6.1 %collective-permute-done.11 = bf16[256,512]{1,0:T(8,128)(2,1)S(1)} collective-permute-done((bf16[256,512]{1,0:T(8,128)(2,1)S(1)}, bf16[256,512]{1,0:T(8,128)(2,1)S(1)}, u32[]{:S(2)}, u32[]{:S(2)}) %collective-permute-start.11) | collective-permute-done | bytes 262176 | tf_op jit(solution)/shard_map/ppermute | solution.py:30
  54.7 0.1 add_convert_fusion.4
  54.8 1.3 %collective-permute-start.12 = (bf16[256,512]{1,0:T(8,128)(2,1)S(1)}, bf16[256,512]{1,0:T(8,128)(2,1)S(1)}, u32[]{:S(2)}, u32[]{:S(2)}) collective-permute-start(bf16[256,512]{1,0:T(8,128)(2,1)S(1)} %add_convert_fusion.4), channel_id=1, source_target_pairs={{8,0},{12,4},{16,8},{20,12},{24,16},{28,20},{9,1},{13,5},{17,9},{2... | collective-permute-start | bytes 786440 | tf_op jit(solution)/shard_map/ppermute | solution.py:25
  56.1 0.9 %convolution_convert_fusion.1 = bf16[128,5376]{1,0:T(8,128)(2,1)S(1)} fusion(bf16[512,5376]{1,0:T(8,128)(2,1)S(1)} %copy-done.3, bf16[256,512]{1,0:T(8,128)(2,1)S(1)} %get-tuple-element.12.o_ref), kind=kOutput, calls=%fused_computation.1 | convolution fusion | flops 705331200 | bytes 7012352 | tf_op jit(solution)/shard_map/dot_general | solution.py:161
  57.1 0.1 collective-permute-start.5
  57.1 1.5 %collective-permute-done.13 = bf16[256,512]{1,0:T(8,128)(2,1)S(1)} collective-permute-done((bf16[256,512]{1,0:T(8,128)(2,1)S(1)}, bf16[256,512]{1,0:T(8,128)(2,1)S(1)}, u32[]{:S(2)}, u32[]{:S(2)}) %collective-permute-start.13) | collective-permute-done | bytes 262176 | tf_op jit(solution)/shard_map/ppermute | solution.py:30
  58.7 4.4 %collective-permute-done.12 = bf16[256,512]{1,0:T(8,128)(2,1)S(1)} collective-permute-done((bf16[256,512]{1,0:T(8,128)(2,1)S(1)}, bf16[256,512]{1,0:T(8,128)(2,1)S(1)}, u32[]{:S(2)}, u32[]{:S(2)}) %collective-permute-start.12) | collective-permute-done | bytes 262176 | tf_op jit(solution)/shard_map/ppermute | solution.py:25
  63.1 0.1 add_convert_fusion.3
  63.2 1.3 %collective-permute-start.14 = (bf16[256,512]{1,0:T(8,128)(2,1)S(1)}, bf16[256,512]{1,0:T(8,128)(2,1)S(1)}, u32[]{:S(2)}, u32[]{:S(2)}) collective-permute-start(bf16[256,512]{1,0:T(8,128)(2,1)S(1)} %add_convert_fusion.3), channel_id=1, source_target_pairs={{8,0},{12,4},{16,8},{20,12},{24,16},{28,20},{9,1},{13,5},{17,9},{2... | collective-permute-start | bytes 786440 | tf_op jit(solution)/shard_map/ppermute | solution.py:25
  64.5 0.0 collective-permute-done.6
  64.5 0.2 add_convert_fusion.1
  64.6 1.4 %collective-permute-start.7 = (bf16[64,5376]{1,0:T(8,128)(2,1)S(1)}, bf16[64,5376]{1,0:T(8,128)(2,1)S(1)}, u32[]{:S(2)}, u32[]{:S(2)}) collective-permute-start(bf16[64,5376]{1,0:T(8,128)(2,1)S(1)} %add_convert_fusion.1), channel_id=1, source_target_pairs={{0,2},{1,3},{2,0},{3,1},{4,6},{5,7},{6,4},{7,5},{8,10},{9,11},{10,... | collective-permute-start | bytes 2064392 | tf_op jit(solution)/shard_map/ppermute | solution.py:30
  66.1 5.4 %collective-permute-done.14 = bf16[256,512]{1,0:T(8,128)(2,1)S(1)} collective-permute-done((bf16[256,512]{1,0:T(8,128)(2,1)S(1)}, bf16[256,512]{1,0:T(8,128)(2,1)S(1)}, u32[]{:S(2)}, u32[]{:S(2)}) %collective-permute-start.14) | collective-permute-done | bytes 262176 | tf_op jit(solution)/shard_map/ppermute | solution.py:25
  71.4 0.1 add_convert_fusion.2
  71.5 0.7 fusion.18
  72.3 0.0 collective-permute-done.5
  72.3 5.5 %collective-permute-done.7 = bf16[64,5376]{1,0:T(8,128)(2,1)S(1)} collective-permute-done((bf16[64,5376]{1,0:T(8,128)(2,1)S(1)}, bf16[64,5376]{1,0:T(8,128)(2,1)S(1)}, u32[]{:S(2)}, u32[]{:S(2)}) %collective-permute-start.7) | collective-permute-done | bytes 688160 | tf_op jit(solution)/shard_map/ppermute | solution.py:30
  77.8 1.1 %add_convert_fusion = bf16[64,5376]{1,0:T(8,128)(2,1)} fusion(bf16[64,5376]{1,0:T(8,128)(2,1)S(1)} %collective-permute-done.7, bf16[64,5376]{1,0:T(8,128)(2,1)S(1)} %collective-permute-done.5, bf16[128,5376]{1,0:T(8,128)(2,1)S(1)} %convolution_convert_fusion.1), kind=kLoop, calls=%fused_computation.10 | loop fusion | flops 2064384 | bytes 2752512 | tf_op jit(solution)/shard_map/convert_element_type | solution.py:164
  (2 shorter events, 0.1 us)
Async XLA Ops:
  0.6 19.0 %collective-permute-start.9 = (bf16[64,5376]{1,0:T(8,128)(2,1)}, bf16[64,5376]{1,0:T(8,128)(2,1)S(1)}, u32[]{:S(2)}, u32[]{:S(2)}) collective-permute-start(bf16[64,5376]{1,0:T(8,128)(2,1)} %param.9), channel_id=1, source_target_pairs={{0,2},{1,3},{2,0},{3,1},{4,6},{5,7},{6,4},{7,5},{8,10},{9,11},{10,... | collective-permute-start | bytes 2064392 | tf_op jit(solution)/shard_map/ppermute | solution.py:30
  3.7 22.7 %collective-permute-start.8 = (bf16[64,5376]{1,0:T(8,128)(2,1)}, bf16[64,5376]{1,0:T(8,128)(2,1)S(1)}, u32[]{:S(2)}, u32[]{:S(2)}) collective-permute-start(bf16[64,5376]{1,0:T(8,128)(2,1)} %param.9), channel_id=1, source_target_pairs={{0,1},{1,0},{2,3},{3,2},{4,5},{5,4},{6,7},{7,6},{8,9},{9,8},{10,11... | collective-permute-start | bytes 2064392 | tf_op jit(solution)/shard_map/ppermute | solution.py:30
  5.5 9.7 %collective-permute-start = (bf16[256,512]{1,0:T(8,128)(2,1)S(1)}, bf16[256,512]{1,0:T(8,128)(2,1)S(1)}, u32[]{:S(2)}, u32[]{:S(2)}) collective-permute-start(bf16[256,512]{1,0:T(8,128)(2,1)S(1)} %constant_dynamic-update-slice_fusion), channel_id=1, source_target_pairs={{0,8},{4,12},{8,16},{12,20},{16,24},{20,28},{1,9},{5,13},{9,17},{1... | collective-permute-start | bytes 786440 | tf_op jit(solution)/shard_map/ppermute | solution.py:25
  15.2 9.8 %collective-permute-start.1 = (bf16[256,512]{1,0:T(8,128)(2,1)S(1)}, bf16[256,512]{1,0:T(8,128)(2,1)S(1)}, u32[]{:S(2)}, u32[]{:S(2)}) collective-permute-start(bf16[256,512]{1,0:T(8,128)(2,1)S(1)} %collective-permute-done.r1_ref), channel_id=1, source_target_pairs={{0,8},{4,12},{8,16},{12,20},{16,24},{20,28},{1,9},{5,13},{9,17},{1... | collective-permute-start | bytes 786440 | tf_op jit(solution)/shard_map/ppermute | solution.py:25
  19.6 20.6 %collective-permute-start.10 = (bf16[64,5376]{1,0:T(8,128)(2,1)S(1)}, bf16[64,5376]{1,0:T(8,128)(2,1)S(1)}, u32[]{:S(2)}, u32[]{:S(2)}) collective-permute-start(bf16[64,5376]{1,0:T(8,128)(2,1)S(1)} %collective-permute-done.9), channel_id=1, source_target_pairs={{0,1},{1,0},{2,3},{3,2},{4,5},{5,4},{6,7},{7,6},{8,9},{9,8},{10,11... | collective-permute-start | bytes 2064392 | tf_op jit(solution)/shard_map/ppermute | solution.py:30
  19.7 11.3 %collective-permute-start.3 = (bf16[256,512]{1,0:T(8,128)(2,1)S(1)}, bf16[256,512]{1,0:T(8,128)(2,1)S(1)}, u32[]{:S(2)}, u32[]{:S(2)}) collective-permute-start(bf16[256,512]{1,0:T(8,128)(2,1)S(1)} %constant_dynamic-update-slice_fusion), channel_id=1, source_target_pairs={{0,4},{8,12},{16,20},{24,28},{1,5},{9,13},{17,21},{25,29},{2,6},{1... | collective-permute-start | bytes 786440 | tf_op jit(solution)/shard_map/ppermute | solution.py:35
  23.1 14.2 %copy-start = (bf16[256,256]{1,0:T(8,128)(2,1)S(1)}, bf16[256,256]{1,0:T(8,128)(2,1)}, u32[]{:S(2)}) copy-start(bf16[256,256]{1,0:T(8,128)(2,1)} %k_ref.3) | copy-start | bytes 393220
  23.1 14.1 %copy-start.1 = (bf16[256,256]{1,0:T(8,128)(2,1)S(1)}, bf16[256,256]{1,0:T(8,128)(2,1)}, u32[]{:S(2)}) copy-start(bf16[256,256]{1,0:T(8,128)(2,1)} %v_ref.3) | copy-start | bytes 393220
  23.1 14.1 %copy-start.2 = (bf16[256,512]{1,0:T(8,128)(2,1)S(1)}, bf16[256,512]{1,0:T(8,128)(2,1)}, u32[]{:S(2)}) copy-start(bf16[256,512]{1,0:T(8,128)(2,1)} %q_ref.3) | copy-start | bytes 786436
  23.2 17.0 %copy-start.3 = (bf16[512,5376]{1,0:T(8,128)(2,1)S(1)}, bf16[512,5376]{1,0:T(8,128)(2,1)}, u32[]{:S(2)}) copy-start(bf16[512,5376]{1,0:T(8,128)(2,1)} %param.8) | copy-start | bytes 16515076
  23.2 11.7 %collective-permute-start.2 = (bf16[256,512]{1,0:T(8,128)(2,1)S(1)}, bf16[256,512]{1,0:T(8,128)(2,1)S(1)}, u32[]{:S(2)}, u32[]{:S(2)}) collective-permute-start(bf16[256,512]{1,0:T(8,128)(2,1)S(1)} %collective-permute-done.r1_ref), channel_id=1, source_target_pairs={{0,4},{4,0},{8,12},{12,8},{16,20},{20,16},{24,28},{28,24},{1,5},{5... | collective-permute-start | bytes 786440 | tf_op jit(solution)/shard_map/ppermute | solution.py:30
  25.0 12.2 %collective-permute-start.4 = (bf16[256,512]{1,0:T(8,128)(2,1)S(1)}, bf16[256,512]{1,0:T(8,128)(2,1)S(1)}, u32[]{:S(2)}, u32[]{:S(2)}) collective-permute-start(bf16[256,512]{1,0:T(8,128)(2,1)S(1)} %collective-permute-done.1.r2_ref), channel_id=1, source_target_pairs={{4,0},{12,8},{20,16},{28,24},{5,1},{13,9},{21,17},{29,25},{6,2},{1... | collective-permute-start | bytes 786440 | tf_op jit(solution)/shard_map/ppermute | solution.py:35
  45.5 9.2 %collective-permute-start.11 = (bf16[256,512]{1,0:T(8,128)(2,1)S(1)}, bf16[256,512]{1,0:T(8,128)(2,1)S(1)}, u32[]{:S(2)}, u32[]{:S(2)}) collective-permute-start(bf16[256,512]{1,0:T(8,128)(2,1)S(1)} %get-tuple-element.18), channel_id=1, source_target_pairs={{0,4},{4,0},{8,12},{12,8},{16,20},{20,16},{24,28},{28,24},{1,5},{5... | collective-permute-start | bytes 786440 | tf_op jit(solution)/shard_map/ppermute | solution.py:30
  46.6 17.9 %collective-permute-start.6 = (bf16[64,5376]{1,0:T(8,128)(2,1)S(1)}, bf16[64,5376]{1,0:T(8,128)(2,1)S(1)}, u32[]{:S(2)}, u32[]{:S(2)}) collective-permute-start(bf16[64,5376]{1,0:T(8,128)(2,1)S(1)} %slice.35), channel_id=1, source_target_pairs={{0,1},{1,0},{2,3},{3,2},{4,5},{5,4},{6,7},{7,6},{8,9},{9,8},{10,11... | collective-permute-start | bytes 2064392 | tf_op jit(solution)/shard_map/ppermute | solution.py:30
  46.6 12.0 %collective-permute-start.13 = (bf16[256,512]{1,0:T(8,128)(2,1)S(1)}, bf16[256,512]{1,0:T(8,128)(2,1)S(1)}, u32[]{:S(2)}, u32[]{:S(2)}) collective-permute-start(bf16[256,512]{1,0:T(8,128)(2,1)S(1)} %get-tuple-element.19), channel_id=1, source_target_pairs={{0,4},{4,0},{8,12},{12,8},{16,20},{20,16},{24,28},{28,24},{1,5},{5... | collective-permute-start | bytes 786440 | tf_op jit(solution)/shard_map/ppermute | solution.py:30
  54.8 8.3 %collective-permute-start.12 = (bf16[256,512]{1,0:T(8,128)(2,1)S(1)}, bf16[256,512]{1,0:T(8,128)(2,1)S(1)}, u32[]{:S(2)}, u32[]{:S(2)}) collective-permute-start(bf16[256,512]{1,0:T(8,128)(2,1)S(1)} %add_convert_fusion.4), channel_id=1, source_target_pairs={{8,0},{12,4},{16,8},{20,12},{24,16},{28,20},{9,1},{13,5},{17,9},{2... | collective-permute-start | bytes 786440 | tf_op jit(solution)/shard_map/ppermute | solution.py:25
  57.1 15.2 %collective-permute-start.5 = (bf16[64,5376]{1,0:T(8,128)(2,1)S(1)}, bf16[64,5376]{1,0:T(8,128)(2,1)S(1)}, u32[]{:S(2)}, u32[]{:S(2)}) collective-permute-start(bf16[64,5376]{1,0:T(8,128)(2,1)S(1)} %slice.33), channel_id=1, source_target_pairs={{0,1},{1,0},{2,3},{3,2},{4,5},{5,4},{6,7},{7,6},{8,9},{9,8},{10,11... | collective-permute-start | bytes 2064392 | tf_op jit(solution)/shard_map/ppermute | solution.py:30
  63.2 8.3 %collective-permute-start.14 = (bf16[256,512]{1,0:T(8,128)(2,1)S(1)}, bf16[256,512]{1,0:T(8,128)(2,1)S(1)}, u32[]{:S(2)}, u32[]{:S(2)}) collective-permute-start(bf16[256,512]{1,0:T(8,128)(2,1)S(1)} %add_convert_fusion.3), channel_id=1, source_target_pairs={{8,0},{12,4},{16,8},{20,12},{24,16},{28,20},{9,1},{13,5},{17,9},{2... | collective-permute-start | bytes 786440 | tf_op jit(solution)/shard_map/ppermute | solution.py:25
  64.6 13.1 %collective-permute-start.7 = (bf16[64,5376]{1,0:T(8,128)(2,1)S(1)}, bf16[64,5376]{1,0:T(8,128)(2,1)S(1)}, u32[]{:S(2)}, u32[]{:S(2)}) collective-permute-start(bf16[64,5376]{1,0:T(8,128)(2,1)S(1)} %add_convert_fusion.1), channel_id=1, source_target_pairs={{0,2},{1,3},{2,0},{3,1},{4,6},{5,7},{6,4},{7,5},{8,10},{9,11},{10,... | collective-permute-start | bytes 2064392 | tf_op jit(solution)/shard_map/ppermute | solution.py:30

commit v2 on v1

--- a/solution.py
+++ b/solution.py
@@ -12,6 +12,7 @@
 NEG = -1e30
 F32 = jnp.float32
 BF16 = jnp.bfloat16
+SMALL = pl.CostEstimate(flops=1, bytes_accessed=1, transcendentals=0)
 VMEM = pl.BlockSpec(memory_space=pltpu.VMEM)
 
 
@@ -44,7 +45,8 @@
     return jnp.concatenate([mat[:, low : low + HEAD_SIZE], mat[:, low + HEAD_SIZE : low + 2 * HEAD_SIZE]], 0)
 
 
-def forward_kernel(q_ref, k_ref, v_ref, r1_ref, r2_ref, x1_ref, p0_ref, x2_ref, o_ref, p_ref):
+def forward_kernel(q_ref, k_ref, v_ref, r1_ref, r2_ref, x1_ref, p0k_ref, p0v_ref, x2_ref, w_ref,
+                   o_ref, p_ref, near_own_ref, near_core_ref, far_own_ref, far_core_ref):
     seq, head = lax.axis_index("seq"), lax.axis_index("head")
     odd = lax.rem(seq, 2) == 1
     tok = q_ref.shape[0]
@@ -65,8 +67,8 @@
         kc = slice(g * HEAD_SIZE, (g + 1) * HEAD_SIZE)
         vc = slice(kv_cols + g * HEAD_SIZE, kv_cols + (g + 1) * HEAD_SIZE)
         qg = stacked(q_rel, g)
-        key_blocks = [k_ref[:, kc], r1_ref[:, kc], r2_ref[:, kc], x1_ref[:, kc], jnp.where(odd, p0_ref[:, kc], x2_ref[:, kc])]
-        value_blocks = [v_ref[:, kc], r1_ref[:, vc], r2_ref[:, vc], x1_ref[:, vc], jnp.where(odd, p0_ref[:, vc], x2_ref[:, vc])]
+        key_blocks = [k_ref[:, kc], r1_ref[:, kc], r2_ref[:, kc], x1_ref[:, kc], jnp.where(odd, p0k_ref[:, kc], x2_ref[:, kc])]
+        value_blocks = [v_ref[:, kc], r1_ref[:, vc], r2_ref[:, vc], x1_ref[:, vc], jnp.where(odd, p0v_ref[:, kc], x2_ref[:, vc])]
         scores = [dot(kb, qg, 1, 1) for kb in key_blocks]
         scores[0] = jnp.where(causal, scores[0], NEG)
         scores[2] = jnp.where(causal, NEG, scores[2])
@@ -88,9 +90,25 @@
         low = 2 * g * HEAD_SIZE
         o_ref[:, low : low + HEAD_SIZE] = out[:tok]
         o_ref[:, low + HEAD_SIZE : low + 2 * HEAD_SIZE] = out[tok:]
-
-
-def backward_kernel(q_ref, k_ref, v_ref, r1_ref, r2_ref, x1_ref, p0_ref, x2_ref, p_ref, o_ref, d0_ref, d1_ref,
+    project(o_ref[...], w_ref, (near_own_ref, near_core_ref, far_own_ref, far_core_ref))
+
+
+def project(rows, w_ref, part_refs):
+    size = part_refs[0].shape[0]
+    cols = w_ref.shape[1]
+    step = cols // 7 if cols % (7 * HEAD_SIZE) == 0 else cols
+    for low in range(0, cols, step):
+        part = dot(rows, w_ref[:, low : low + step], 1, 0).astype(BF16)
+        for i, ref in enumerate(part_refs):
+            ref[:, low : low + step] = part[i * size : (i + 1) * size]
+
+
+def back_kernel(own_ref, core_ref, y_ref, yc_ref, w_ref, d_ref):
+    rows = jnp.concatenate([own_ref[...], core_ref[...], y_ref[...], yc_ref[...]], 0)
+    d_ref[...] = dot(rows, w_ref[...], 1, 1).astype(BF16)
+
+
+def backward_kernel(q_ref, k_ref, v_ref, r1_ref, r2_ref, x1_ref, p0k_ref, p0v_ref, x2_ref, p_ref, o_ref, d_ref,
                     dq_ref, town_ref, t1_ref, t2_ref, tx_ref, tz_ref):
     seq, head = lax.axis_index("seq"), lax.axis_index("head")
     odd = lax.rem(seq, 2) == 1
@@ -99,15 +117,15 @@
     kv_heads = kv_cols // HEAD_SIZE
     size = tok // 4
     q_rel = jnp.concatenate([q_ref[group_rows(g, head, size), :] for g in range(4)], 0)
-    do_rel = jnp.concatenate([d0_ref[...], d1_ref[...]], 0)
+    do_rel = d_ref[...]
     o_rel = o_ref[...]
     outs = [town_ref, t1_ref, t2_ref, tx_ref, tz_ref]
     for g in range(kv_heads):
         kc = slice(g * HEAD_SIZE, (g + 1) * HEAD_SIZE)
         vc = slice(kv_cols + g * HEAD_SIZE, kv_cols + (g + 1) * HEAD_SIZE)
         qg, dg, og = stacked(q_rel, g), stacked(do_rel, g), stacked(o_rel, g)
-        key_blocks = [k_ref[:, kc], r1_ref[:, kc], r2_ref[:, kc], x1_ref[:, kc], jnp.where(odd, p0_ref[:, kc], x2_ref[:, kc])]
-        value_blocks = [v_ref[:, kc], r1_ref[:, vc], r2_ref[:, vc], x1_ref[:, vc], jnp.where(odd, p0_ref[:, vc], x2_ref[:, vc])]
+        key_blocks = [k_ref[:, kc], r1_ref[:, kc], r2_ref[:, kc], x1_ref[:, kc], jnp.where(odd, p0k_ref[:, kc], x2_ref[:, kc])]
+        value_blocks = [v_ref[:, kc], r1_ref[:, vc], r2_ref[:, vc], x1_ref[:, vc], jnp.where(odd, p0v_ref[:, kc], x2_ref[:, vc])]
         delta = jnp.sum((dg.astype(F32) * og.astype(F32)).T, axis=0, keepdims=True)
         dq = jnp.zeros((HEAD_SIZE, 2 * tok), F32)
         for b in range(5):
@@ -130,44 +148,53 @@
     kv_cols = keys.shape[1]
     kv_heads = kv_cols // HEAD_SIZE
     odd = lax.rem(lax.axis_index("seq"), 2) == 1
-    params = pltpu.CompilerParams(vmem_limit_bytes=32 << 20)
-
+    params = pltpu.CompilerParams(vmem_limit_bytes=16 << 20)
+
+    def wide(a):
+        return a.astype(F32)
+
+    def gate(value, *others):
+        return lax.optimization_barrier((value, *others))[0]
+
+    r1_parts = [shifted(keys, 2), shifted(values, 2)]
+    p0_parts = [to_parity(keys, 1), to_parity(values, 1)]
     og_y = swapped(out_grad, "head", 2)
-    own_kv = jnp.concatenate([keys, values], 1)
-    r1 = shifted(own_kv, 2)
-    p0 = to_parity(own_kv, 1)
     og_c = swapped(out_grad, "head", 1)
+    r1 = jnp.concatenate(r1_parts, 1)
+    r1 = gate(r1, *p0_parts)
     r2 = shifted(r1, 2)
     x1 = swapped(r1, "seq", 1)
-    x2 = to_parity(r2, 0)
-    og_yc = swapped(og_y, "head", 1)
-
-    attended, probs = pl.pallas_call(
+    x2 = to_parity(gate(r2, x1), 0)
+    og_yc = swapped(gate(og_y, r2, x1), "head", 1)
+    half, size = tok // 2, tok // 4
+    rows = jax.ShapeDtypeStruct((size, out_weight.shape[1]), BF16)
+    attended_grad = pl.pallas_call(
+        back_kernel,
+        out_shape=jax.ShapeDtypeStruct((tok, q_cols), BF16),
+        in_specs=[VMEM] * 5,
+        out_specs=VMEM,
+        compiler_params=params,
+        cost_estimate=SMALL,
+        name="turn_back",
+    )(out_grad, og_c, og_y, og_yc, out_weight)
+
+    attended, probs, near_own, near_core, far_own, far_core = pl.pallas_call(
         forward_kernel,
         out_shape=(
             jax.ShapeDtypeStruct((tok, q_cols), BF16),
             jax.ShapeDtypeStruct((kv_heads, 5, tok, 2 * tok), BF16),
+            rows, rows, rows, rows,
         ),
-        in_specs=[VMEM] * 8,
-        out_specs=(VMEM, VMEM),
+        in_specs=[VMEM] * 10,
+        out_specs=(VMEM,) * 6,
         compiler_params=params,
+        cost_estimate=SMALL,
         name="attend",
-    )(queries, keys, values, r1, r2, x1, p0, x2)
-
-    half, size = tok // 2, tok // 4
-    far_part = jnp.dot(attended[half:], out_weight, preferred_element_type=F32).astype(BF16)
-    sent = swapped(far_part[size:], "head", 1)
-    far_sum = (far_part[:size].astype(F32) + sent.astype(F32)).astype(BF16)
-    near_part = jnp.dot(attended[:half], out_weight, preferred_element_type=F32).astype(BF16)
-    from_y = swapped(far_sum, "head", 2)
-    from_core = swapped(near_part[size:], "head", 1)
-    projected = (near_part[:size].astype(F32) + from_core.astype(F32) + from_y.astype(F32)).astype(BF16)
-
-    def back(rows):
-        return dot(rows, out_weight, 1, 1).astype(BF16)
-
-    near_grad = back(jnp.concatenate([out_grad, og_c], 0))
-    far_grad = back(jnp.concatenate([og_y, og_yc], 0))
+    )(gate(queries, attended_grad), keys, values, r1, r2, x1, *p0_parts, x2, out_weight)
+    sent = swapped(far_core, "head", 1)
+    cuts = (0, size * 3 // 8, size * 3 // 4, size)
+    far_sums = [(wide(far_own[i:j]) + wide(sent[i:j])).astype(BF16) for i, j in zip(cuts, cuts[1:])]
+    from_y = [swapped(part, "head", 2) for part in far_sums]
 
     block = jax.ShapeDtypeStruct((tok, 2 * kv_cols), BF16)
     query_gradient, t_own, t_1, t_2, t_x, t_z = pl.pallas_call(
@@ -180,19 +207,23 @@
         in_specs=[VMEM] * 12,
         out_specs=(VMEM,) * 6,
         compiler_params=params,
+        cost_estimate=SMALL,
         name="attend_grad",
-    )(queries, keys, values, r1, r2, x1, p0, x2, probs, attended, near_grad, far_grad)
-
-    def wide(a):
-        return a.astype(F32)
-
-    g = swapped(t_z, "seq", 1)
+    )(queries, keys, values, r1, r2, x1, *p0_parts, x2, probs, attended, attended_grad)
+
+    g = swapped(gate(t_z, *far_sums), "seq", 1)
+    d1 = swapped(gate(t_x, g), "seq", 1)
     zero = jnp.zeros_like(g)
-    c1 = shifted((wide(t_2) + wide(jnp.where(odd, g, zero))).astype(BF16), -2)
-    d1 = swapped(t_x, "seq", 1)
-    e1 = shifted((wide(t_1) + wide(c1) + wide(d1)).astype(BF16), -2)
-    own = (t_own + wide(e1) + wide(jnp.where(odd, zero, g))).astype(BF16)
-    return (projected, query_gradient, own[:, :kv_cols], own[:, kv_cols:])
+    c1 = shifted(gate((wide(t_2) + wide(jnp.where(odd, g, zero))).astype(BF16), from_y[0]), -2)
+    from_core = swapped(gate(near_core, g), "head", 1)
+    e1 = shifted(gate((wide(t_1) + wide(c1) + wide(d1)).astype(BF16), from_y[1]), -2)
+    kept = jnp.where(odd, zero, g)
+
+    def total(cols):
+        return (t_own[:, cols] + wide(e1[:, cols]) + wide(kept[:, cols])).astype(BF16)
+
+    projected = (wide(near_own) + wide(from_core) + wide(jnp.concatenate(from_y, 0))).astype(BF16)
+    return (projected, query_gradient, total(slice(0, kv_cols)), total(slice(kv_cols, 2 * kv_cols)))
 
 
 def solution(mesh):

time: 79.2 us -> 80.4 us (1.015)
  matrix products: 8.34 us -> 0 us
  starting transfers between devices: 22 us -> 27.9 us
  waiting for transfers between devices: 37.2 us -> 33.7 us
  Pallas kernels: 6.28 us -> 9.3 us
  other arithmetic: 1.58 us -> 4.6 us
  local copies, waits for them, and re-layouts: 2.66 us -> 3.68 us
    dot_general x4 -> x0, matrix products: 8.34 us -> none  [the longest x2 6.53 us: dot(): lax.dot_general(a, b, (((ca,), (cb,)), ((), ())), preferred_element_type=...]
    ppermute x9 -> x11, waiting for transfers between devices: 17.1 us -> 12.5 us  [swapped(): return lax.ppermute(value, axis, [(i, i ^ bit) for i in range(count)])]
    ppermute x2 -> x3, waiting for transfers between devices: 2.36 us -> 6.81 us  [to_parity(): lax.ppermute(value, 'seq', [(i ^ 1, i) for i in range(parity, count, 2)])]
    ppermute x4 -> x5, waiting for transfers between devices: 17.7 us -> 14.3 us  [shifted(): lax.ppermute(value, 'seq', [(i, i + steps) for i in range(first, last)])]
    convert_element_type x5 -> x6, other arithmetic: 1.58 us -> 4.55 us  [the longest x1 2.07 us: per_device(): (wide(near_own) + wide(from_core) + wide(jnp.concatenate(from_y, 0))).ast...]
    unnamed x9 -> x14, local copies, waits for them, and re-layouts: 0.94 us -> 3.68 us
    ppermute x4 -> x5, starting transfers between devices: 10.5 us -> 13 us  [shifted(): lax.ppermute(value, 'seq', [(i, i + steps) for i in range(first, last)])]
    ppermute x9 -> x11, starting transfers between devices: 6.83 us -> 8.95 us  [swapped(): return lax.ppermute(value, axis, [(i, i ^ bit) for i in range(count)])]
  transfers between devices with their start and end apart: 15 -> 19, of which waited for: 9 -> 11; matrix products, arithmetic and copies ran while one was open for 12% -> 1% of each run, Pallas kernels for 4% -> 6%
where the time goes in v2:
time: 80.4 us; the launch traced here: 80 us
  waiting for transfers between devices  33.7 us (42%)
  starting transfers between devices  27.9 us (35%)
  Pallas kernels  9.3 us (12%)
  other arithmetic  4.6 us (6%)
  local copies, waits for them, and re-layouts  3.68 us (5%)
  between operations  0.82 us (1%)
    ppermute x5, waiting for transfers between devices, shifted(): lax.ppermute(value, 'seq', [(i, i + steps) for i in range(first, last)])  14.3 us
    ppermute x5, starting transfers between devices, shifted(): lax.ppermute(value, 'seq', [(i, i + steps) for i in range(first, last)])  13 us
    ppermute x11, waiting for transfers between devices, swapped(): return lax.ppermute(value, axis, [(i, i ^ bit) for i in range(count)])  12.5 us
    ppermute x11, starting transfers between devices, swapped(): return lax.ppermute(value, axis, [(i, i ^ bit) for i in range(count)])  8.95 us
    ppermute x3, waiting for transfers between devices, to_parity(): lax.ppermute(value, 'seq', [(i ^ 1, i) for i in range(parity, count, 2)])  6.81 us
    ppermute x3, starting transfers between devices, to_parity(): lax.ppermute(value, 'seq', [(i ^ 1, i) for i in range(parity, count, 2)])  5.98 us
    pallas_call x1, Pallas kernels, per_device(): pl.pallas_call(forward_kernel, out_shape=(jax.ShapeDtypeStruct((tok, q_co...  4.31 us
    unnamed x14, local copies, waits for them, and re-layouts  3.68 us
  transfers between devices with their start and end apart: 19, of which 11 were waited for; matrix products, arithmetic and copies ran while one was open for 1% of the time, Pallas kernels for 6%

profile of v2, /device:TPU:0, one launch (start us, length us, event | category | flops | bytes accessed | tf_op | source)
XLA Modules:
  0.0 80.0 jit_solution(2606085387991148352)
XLA Ops:
  0.6 3.0 %collective-permute-start.1 = (bf16[64,5376]{1,0:T(8,128)(2,1)}, bf16[64,5376]{1,0:T(8,128)(2,1)S(1)}, u32[]{:S(2)}, u32[]{:S(2)}) collective-permute-start(bf16[64,5376]{1,0:T(8,128)(2,1)} %own_ref.1), channel_id=1, source_target_pairs={{0,2},{1,3},{2,0},{3,1},{4,6},{5,7},{6,4},{7,5},{8,10},{9,11},{10,... | collective-permute-start | bytes 2064392 | tf_op jit(solution)/shard_map/ppermute | solution.py:31
  3.7 3.5 %collective-permute-start.2 = (bf16[256,256]{1,0:T(8,128)(2,1)}, bf16[256,256]{1,0:T(8,128)(2,1)S(1)}, u32[]{:S(2)}, u32[]{:S(2)}) collective-permute-start(bf16[256,256]{1,0:T(8,128)(2,1)} %k_ref.3), channel_id=1, source_target_pairs={{0,8},{4,12},{8,16},{12,20},{16,24},{20,28},{1,9},{5,13},{9,17},{1... | collective-permute-start | bytes 393224 | tf_op jit(solution)/shard_map/ppermute | solution.py:26
  7.1 3.5 %collective-permute-start.3 = (bf16[256,256]{1,0:T(8,128)(2,1)}, bf16[256,256]{1,0:T(8,128)(2,1)S(1)}, u32[]{:S(2)}, u32[]{:S(2)}) collective-permute-start(bf16[256,256]{1,0:T(8,128)(2,1)} %v_ref.3), channel_id=1, source_target_pairs={{0,8},{4,12},{8,16},{12,20},{16,24},{20,28},{1,9},{5,13},{9,17},{1... | collective-permute-start | bytes 393224 | tf_op jit(solution)/shard_map/ppermute | solution.py:26
  10.6 3.4 %collective-permute-start.4 = (bf16[256,256]{1,0:T(8,128)(2,1)}, bf16[256,256]{1,0:T(8,128)(2,1)S(1)}, u32[]{:S(2)}, u32[]{:S(2)}) collective-permute-start(bf16[256,256]{1,0:T(8,128)(2,1)} %k_ref.3), channel_id=1, source_target_pairs={{0,4},{8,12},{16,20},{24,28},{1,5},{9,13},{17,21},{25,29},{2,6},{1... | collective-permute-start | bytes 393224 | tf_op jit(solution)/shard_map/ppermute | solution.py:36
  14.0 1.3 %collective-permute-start.5 = (bf16[256,256]{1,0:T(8,128)(2,1)}, bf16[256,256]{1,0:T(8,128)(2,1)S(1)}, u32[]{:S(2)}, u32[]{:S(2)}) collective-permute-start(bf16[256,256]{1,0:T(8,128)(2,1)} %v_ref.3), channel_id=1, source_target_pairs={{0,4},{8,12},{16,20},{24,28},{1,5},{9,13},{17,21},{25,29},{2,6},{1... | collective-permute-start | bytes 393224 | tf_op jit(solution)/shard_map/ppermute | solution.py:36
  15.4 0.0 collective-permute-done.2
  15.4 0.0 collective-permute-done.3
  15.4 0.0 copy-start.2
  15.4 0.0 copy-start.4
  15.4 0.0 copy-start.5
  15.4 2.2 %collective-permute-done.4.p0k_ref = bf16[256,256]{1,0:T(8,128)(2,1)S(1)} collective-permute-done((bf16[256,256]{1,0:T(8,128)(2,1)}, bf16[256,256]{1,0:T(8,128)(2,1)S(1)}, u32[]{:S(2)}, u32[]{:S(2)}) %collective-permute-start.4) | collective-permute-done | bytes 131104 | tf_op jit(solution)/shard_map/ppermute | solution.py:36
  17.7 1.4 %collective-permute-done.5.p0v_ref = bf16[256,256]{1,0:T(8,128)(2,1)S(1)} collective-permute-done((bf16[256,256]{1,0:T(8,128)(2,1)}, bf16[256,256]{1,0:T(8,128)(2,1)S(1)}, u32[]{:S(2)}, u32[]{:S(2)}) %collective-permute-start.5) | collective-permute-done | bytes 131104 | tf_op jit(solution)/shard_map/ppermute | solution.py:36
  19.1 3.5 %collective-permute-start.6 = (bf16[256,512]{1,0:T(8,128)(2,1)S(1)}, bf16[256,512]{1,0:T(8,128)(2,1)S(1)}, u32[]{:S(2)}, u32[]{:S(2)}) collective-permute-start(bf16[256,512]{1,0:T(8,128)(2,1)S(1)} %pad_maximum_fusion.r1_ref), channel_id=1, source_target_pairs={{0,8},{4,12},{8,16},{12,20},{16,24},{20,28},{1,9},{5,13},{9,17},{1... | collective-permute-start | bytes 786440 | tf_op jit(solution)/shard_map/ppermute | solution.py:26
  22.6 2.4 %collective-permute-start.7 = (bf16[256,512]{1,0:T(8,128)(2,1)S(1)}, bf16[256,512]{1,0:T(8,128)(2,1)S(1)}, u32[]{:S(2)}, u32[]{:S(2)}) collective-permute-start(bf16[256,512]{1,0:T(8,128)(2,1)S(1)} %pad_maximum_fusion.r1_ref), channel_id=1, source_target_pairs={{0,4},{4,0},{8,12},{12,8},{16,20},{20,16},{24,28},{28,24},{1,5},{5... | collective-permute-start | bytes 786440 | tf_op jit(solution)/shard_map/ppermute | solution.py:31
  25.0 0.0 collective-permute-start
  25.0 1.4 %collective-permute-done.6.r2_ref = bf16[256,512]{1,0:T(8,128)(2,1)S(1)} collective-permute-done((bf16[256,512]{1,0:T(8,128)(2,1)S(1)}, bf16[256,512]{1,0:T(8,128)(2,1)S(1)}, u32[]{:S(2)}, u32[]{:S(2)}) %collective-permute-start.6) | collective-permute-done | bytes 262176 | tf_op jit(solution)/shard_map/ppermute | solution.py:26
  26.4 2.9 %collective-permute-done.7.x1_ref = bf16[256,512]{1,0:T(8,128)(2,1)S(1)} collective-permute-done((bf16[256,512]{1,0:T(8,128)(2,1)S(1)}, bf16[256,512]{1,0:T(8,128)(2,1)S(1)}, u32[]{:S(2)}, u32[]{:S(2)}) %collective-permute-start.7) | collective-permute-done | bytes 262176 | tf_op jit(solution)/shard_map/ppermute | solution.py:31
  29.3 0.0 collective-permute-done.1.y_ref
  29.4 0.0 collective-permute-start.8
  29.4 1.3 %collective-permute-start.9 = (bf16[256,512]{1,0:T(8,128)(2,1)S(1)}, bf16[256,512]{1,0:T(8,128)(2,1)S(1)}, u32[]{:S(2)}, u32[]{:S(2)}) collective-permute-start(bf16[256,512]{1,0:T(8,128)(2,1)S(1)} %collective-permute-done.6.r2_ref), channel_id=1, source_target_pairs={{4,0},{12,8},{20,16},{28,24},{5,1},{13,9},{21,17},{29,25},{6,2},{1... | collective-permute-start | bytes 786440 | tf_op jit(solution)/shard_map/ppermute | solution.py:36
  30.6 0.0 collective-permute-done.core_ref
  30.7 0.8 %collective-permute-done.8.yc_ref = bf16[64,5376]{1,0:T(8,128)(2,1)S(1)} collective-permute-done((bf16[64,5376]{1,0:T(8,128)(2,1)S(1)}, bf16[64,5376]{1,0:T(8,128)(2,1)S(1)}, u32[]{:S(2)}, u32[]{:S(2)}) %collective-permute-start.8) | collective-permute-done | bytes 688160 | tf_op jit(solution)/shard_map/ppermute | solution.py:31
  31.5 0.0 copy-start
  31.5 2.6 %copy-done = bf16[512,5376]{1,0:T(8,128)(2,1)S(1)} copy-done((bf16[512,5376]{1,0:T(8,128)(2,1)S(1)}, bf16[512,5376]{1,0:T(8,128)(2,1)}, u32[]{:S(2)}) %copy-start) | copy-done | bytes 5505048
  34.1 0.0 copy-start.3
  34.1 1.1 %copy-done.3 = bf16[64,5376]{1,0:T(8,128)(2,1)S(1)} copy-done((bf16[64,5376]{1,0:T(8,128)(2,1)S(1)}, bf16[64,5376]{1,0:T(8,128)(2,1)}, u32[]{:S(2)}) %copy-start.3) | copy-done | bytes 688152
  35.2 0.0 copy-start.1
  35.2 1.6 %turn_back.1.d_ref = bf16[256,512]{1,0:T(8,128)(2,1)S(1)} custom-call(bf16[64,5376]{1,0:T(8,128)(2,1)S(1)} %copy-done.3, bf16[64,5376]{1,0:T(8,128)(2,1)S(1)} %collective-permute-done.core_ref, bf16[64,5376]{1,0:T(8,128)(2,1)S(1)} %collective-permute-done.1.y_ref, bf16[64,5376]{1,0:T(8,128)(2,1)S(1)} %collective-permute-done.8.yc_ref, ...), custom_call_target="tpu_custom_call" | custom-call | flops 1 | bytes 1 | tf_op jit(solution)/shard_map/turn_back/pallas_call | solution.py:171
  36.8 3.2 %collective-permute-done.9.x2_ref = bf16[256,512]{1,0:T(8,128)(2,1)S(1)} collective-permute-done((bf16[256,512]{1,0:T(8,128)(2,1)S(1)}, bf16[256,512]{1,0:T(8,128)(2,1)S(1)}, u32[]{:S(2)}, u32[]{:S(2)}) %collective-permute-start.9) | collective-permute-done | bytes 262176 | tf_op jit(solution)/shard_map/ppermute | solution.py:36
  40.0 0.0 copy-done.2
  40.0 0.0 copy-done.4
  40.0 0.0 copy-done.5
  40.0 0.0 copy-done.1
  40.0 4.3 %attend.1 = (bf16[256,512]{1,0:T(8,128)(2,1)S(1)}, bf16[2,5,256,512]{3,2,1,0:T(8,128)(2,1)S(1)}, bf16[64,5376]{1,0:T(8,128)(2,1)S(1)}, bf16[64,5376]{1,0:T(8,128...) custom-call(bf16[256,512]{1,0:T(8,128)(2,1)S(1)} %copy-done.2, bf16[256,256]{1,0:T(8,128)(2,1)S(1)} %copy-done.4, ...), custom_call_target="tpu_custom_call" | custom-call | flops 1 | bytes 1 | tf_op jit(solution)/shard_map/attend/pallas_call | solution.py:181
  44.3 0.1 collective-permute-start.10
  44.4 3.4 %attend_grad.1 = (bf16[256,512]{1,0:T(8,128)(2,1)}, f32[256,512]{1,0:T(8,128)S(1)}, bf16[256,512]{1,0:T(8,128)(2,1)S(1)}, bf16[256,512]{1,0:T(8,128)(2,1)S(1)}, ...) custom-call(bf16[256,512]{1,0:T(8,128)(2,1)S(1)} %copy-done.2, bf16[256,256]{1,0:T(8,128)(2,1)S(1)} %copy-done.4, ...), custom_call_target="tpu_custom_call" | custom-call | flops 1 | bytes 1 | tf_op jit(solution)/shard_map/attend_grad/pallas_call | solution.py:200
  47.8 0.0 collective-permute-done.10
  47.8 0.7 add_convert_fusion.5
  48.5 0.8 %add_convert_fusion.3 = (bf16[24,5376]{1,0:T(8,128)(2,1)S(1)}, bf16[24,5376]{1,0:T(8,128)(2,1)}) fusion(bf16[64,5376]{1,0:T(8,128)(2,1)S(1)} %collective-permute-done.10, bf16[64,5376]{1,0:T(8,128)(2,1)S(1)} %get-tuple-element.34), kind=kLoop, calls=%fused_computation.3 | loop fusion | flops 1032192 | bytes 1548288 | tf_op jit(solution)/shard_map/convert_element_type | solution.py:196
  49.3 0.0 collective-permute-start.11
  49.3 0.5 collective-permute-start.13
  49.8 0.0 copy-start.6
  49.8 8.2 %collective-permute-done.11 = bf16[256,512]{1,0:T(8,128)(2,1)S(1)} collective-permute-done((bf16[256,512]{1,0:T(8,128)(2,1)S(1)}, bf16[256,512]{1,0:T(8,128)(2,1)S(1)}, u32[]{:S(2)}, u32[]{:S(2)}) %collective-permute-start.11) | collective-permute-done | bytes 262176 | tf_op jit(solution)/shard_map/ppermute | solution.py:31
  58.0 0.1 add_convert_fusion.2
  58.1 0.1 collective-permute-done.13
  58.2 1.3 %collective-permute-start.16 = (bf16[256,512]{1,0:T(8,128)(2,1)S(1)}, bf16[256,512]{1,0:T(8,128)(2,1)S(1)}, u32[]{:S(2)}, u32[]{:S(2)}) collective-permute-start(bf16[256,512]{1,0:T(8,128)(2,1)S(1)} %add_convert_fusion.2), channel_id=1, source_target_pairs={{8,0},{12,4},{16,8},{20,12},{24,16},{28,20},{9,1},{13,5},{17,9},{2... | collective-permute-start | bytes 786440 | tf_op jit(solution)/shard_map/ppermute | solution.py:26
  59.5 1.8 %collective-permute-start.17 = (bf16[256,512]{1,0:T(8,128)(2,1)S(1)}, bf16[256,512]{1,0:T(8,128)(2,1)S(1)}, u32[]{:S(2)}, u32[]{:S(2)}) collective-permute-start(bf16[256,512]{1,0:T(8,128)(2,1)S(1)} %get-tuple-element.44), channel_id=1, source_target_pairs={{0,4},{4,0},{8,12},{12,8},{16,20},{20,16},{24,28},{28,24},{1,5},{5... | collective-permute-start | bytes 786440 | tf_op jit(solution)/shard_map/ppermute | solution.py:31
  61.3 0.5 collective-permute-start.14
  61.8 0.0 collective-permute-start.12
  61.8 6.2 %collective-permute-done.16 = bf16[256,512]{1,0:T(8,128)(2,1)S(1)} collective-permute-done((bf16[256,512]{1,0:T(8,128)(2,1)S(1)}, bf16[256,512]{1,0:T(8,128)(2,1)S(1)}, u32[]{:S(2)}, u32[]{:S(2)}) %collective-permute-start.16) | collective-permute-done | bytes 262176 | tf_op jit(solution)/shard_map/ppermute | solution.py:26
  68.0 0.0 collective-permute-done.17
  68.0 0.1 add_convert_fusion.1
  68.1 0.4 collective-permute-done.14
  68.5 1.3 %collective-permute-start.18 = (bf16[256,512]{1,0:T(8,128)(2,1)S(1)}, bf16[256,512]{1,0:T(8,128)(2,1)S(1)}, u32[]{:S(2)}, u32[]{:S(2)}) collective-permute-start(bf16[256,512]{1,0:T(8,128)(2,1)S(1)} %add_convert_fusion.1), channel_id=1, source_target_pairs={{8,0},{12,4},{16,8},{20,12},{24,16},{28,20},{9,1},{13,5},{17,9},{2... | collective-permute-start | bytes 786440 | tf_op jit(solution)/shard_map/ppermute | solution.py:26
  69.8 0.0 copy-done.6
  69.8 0.6 collective-permute-start.15
  70.4 6.7 %collective-permute-done.18 = bf16[256,512]{1,0:T(8,128)(2,1)S(1)} collective-permute-done((bf16[256,512]{1,0:T(8,128)(2,1)S(1)}, bf16[256,512]{1,0:T(8,128)(2,1)S(1)}, u32[]{:S(2)}, u32[]{:S(2)}) %collective-permute-start.18) | collective-permute-done | bytes 262176 | tf_op jit(solution)/shard_map/ppermute | solution.py:26
  77.2 0.8 add_convert_fusion.6
  78.0 0.0 collective-permute-done.15
  78.0 0.0 collective-permute-done.12
  78.0 2.1 %add_convert_fusion = bf16[64,5376]{1,0:T(8,128)(2,1)} fusion(bf16[64,5376]{1,0:T(8,128)(2,1)S(1)} %collective-permute-done.12, bf16[64,5376]{1,0:T(8,128)(2,1)S(1)} %get-tuple-element.29, bf16[16,5376]{1,0:T(8,128)(2,1)S(1)} %collective-permute-done.15, bf16[24,5376]{1,0:T(8,128)(2,1)S(1)} %collective-permute-done.14, bf16[24,5376]{1,0:T(8,128)(2,1)} %collective-permute-done.13), kind=kLoop, calls=%fused_computation | loop fusion | flops 3784704 | bytes 2752512 | tf_op jit(solution)/shard_map/convert_element_type | solution.py:225
  (2 shorter events, 0.0 us)
Async XLA Ops:
  0.6 28.7 %collective-permute-start.1 = (bf16[64,5376]{1,0:T(8,128)(2,1)}, bf16[64,5376]{1,0:T(8,128)(2,1)S(1)}, u32[]{:S(2)}, u32[]{:S(2)}) collective-permute-start(bf16[64,5376]{1,0:T(8,128)(2,1)} %own_ref.1), channel_id=1, source_target_pairs={{0,2},{1,3},{2,0},{3,1},{4,6},{5,7},{6,4},{7,5},{8,10},{9,11},{10,... | collective-permute-start | bytes 2064392 | tf_op jit(solution)/shard_map/ppermute | solution.py:31
  3.7 11.7 %collective-permute-start.2 = (bf16[256,256]{1,0:T(8,128)(2,1)}, bf16[256,256]{1,0:T(8,128)(2,1)S(1)}, u32[]{:S(2)}, u32[]{:S(2)}) collective-permute-start(bf16[256,256]{1,0:T(8,128)(2,1)} %k_ref.3), channel_id=1, source_target_pairs={{0,8},{4,12},{8,16},{12,20},{16,24},{20,28},{1,9},{5,13},{9,17},{1... | collective-permute-start | bytes 393224 | tf_op jit(solution)/shard_map/ppermute | solution.py:26
  7.1 8.2 %collective-permute-start.3 = (bf16[256,256]{1,0:T(8,128)(2,1)}, bf16[256,256]{1,0:T(8,128)(2,1)S(1)}, u32[]{:S(2)}, u32[]{:S(2)}) collective-permute-start(bf16[256,256]{1,0:T(8,128)(2,1)} %v_ref.3), channel_id=1, source_target_pairs={{0,8},{4,12},{8,16},{12,20},{16,24},{20,28},{1,9},{5,13},{9,17},{1... | collective-permute-start | bytes 393224 | tf_op jit(solution)/shard_map/ppermute | solution.py:26
  10.6 7.0 %collective-permute-start.4 = (bf16[256,256]{1,0:T(8,128)(2,1)}, bf16[256,256]{1,0:T(8,128)(2,1)S(1)}, u32[]{:S(2)}, u32[]{:S(2)}) collective-permute-start(bf16[256,256]{1,0:T(8,128)(2,1)} %k_ref.3), channel_id=1, source_target_pairs={{0,4},{8,12},{16,20},{24,28},{1,5},{9,13},{17,21},{25,29},{2,6},{1... | collective-permute-start | bytes 393224 | tf_op jit(solution)/shard_map/ppermute | solution.py:36
  14.0 5.0 %collective-permute-start.5 = (bf16[256,256]{1,0:T(8,128)(2,1)}, bf16[256,256]{1,0:T(8,128)(2,1)S(1)}, u32[]{:S(2)}, u32[]{:S(2)}) collective-permute-start(bf16[256,256]{1,0:T(8,128)(2,1)} %v_ref.3), channel_id=1, source_target_pairs={{0,4},{8,12},{16,20},{24,28},{1,5},{9,13},{17,21},{25,29},{2,6},{1... | collective-permute-start | bytes 393224 | tf_op jit(solution)/shard_map/ppermute | solution.py:36
  15.4 24.6 %copy-start.2 = (bf16[256,512]{1,0:T(8,128)(2,1)S(1)}, bf16[256,512]{1,0:T(8,128)(2,1)}, u32[]{:S(2)}) copy-start(bf16[256,512]{1,0:T(8,128)(2,1)} %q_ref.2) | copy-start | bytes 786436
  15.4 24.6 %copy-start.4 = (bf16[256,256]{1,0:T(8,128)(2,1)S(1)}, bf16[256,256]{1,0:T(8,128)(2,1)}, u32[]{:S(2)}) copy-start(bf16[256,256]{1,0:T(8,128)(2,1)} %k_ref.3) | copy-start | bytes 393220
  15.4 24.6 %copy-start.5 = (bf16[256,256]{1,0:T(8,128)(2,1)S(1)}, bf16[256,256]{1,0:T(8,128)(2,1)}, u32[]{:S(2)}) copy-start(bf16[256,256]{1,0:T(8,128)(2,1)} %v_ref.3) | copy-start | bytes 393220
  19.1 7.3 %collective-permute-start.6 = (bf16[256,512]{1,0:T(8,128)(2,1)S(1)}, bf16[256,512]{1,0:T(8,128)(2,1)S(1)}, u32[]{:S(2)}, u32[]{:S(2)}) collective-permute-start(bf16[256,512]{1,0:T(8,128)(2,1)S(1)} %pad_maximum_fusion.r1_ref), channel_id=1, source_target_pairs={{0,8},{4,12},{8,16},{12,20},{16,24},{20,28},{1,9},{5,13},{9,17},{1... | collective-permute-start | bytes 786440 | tf_op jit(solution)/shard_map/ppermute | solution.py:26
  22.6 6.8 %collective-permute-start.7 = (bf16[256,512]{1,0:T(8,128)(2,1)S(1)}, bf16[256,512]{1,0:T(8,128)(2,1)S(1)}, u32[]{:S(2)}, u32[]{:S(2)}) collective-permute-start(bf16[256,512]{1,0:T(8,128)(2,1)S(1)} %pad_maximum_fusion.r1_ref), channel_id=1, source_target_pairs={{0,4},{4,0},{8,12},{12,8},{16,20},{20,16},{24,28},{28,24},{1,5},{5... | collective-permute-start | bytes 786440 | tf_op jit(solution)/shard_map/ppermute | solution.py:31
  25.0 5.7 %collective-permute-start = (bf16[64,5376]{1,0:T(8,128)(2,1)}, bf16[64,5376]{1,0:T(8,128)(2,1)S(1)}, u32[]{:S(2)}, u32[]{:S(2)}) collective-permute-start(bf16[64,5376]{1,0:T(8,128)(2,1)} %own_ref.1), channel_id=1, source_target_pairs={{0,1},{1,0},{2,3},{3,2},{4,5},{5,4},{6,7},{7,6},{8,9},{9,8},{10,11... | collective-permute-start | bytes 2064392 | tf_op jit(solution)/shard_map/ppermute | solution.py:31
  29.4 2.1 %collective-permute-start.8 = (bf16[64,5376]{1,0:T(8,128)(2,1)S(1)}, bf16[64,5376]{1,0:T(8,128)(2,1)S(1)}, u32[]{:S(2)}, u32[]{:S(2)}) collective-permute-start(bf16[64,5376]{1,0:T(8,128)(2,1)S(1)} %collective-permute-done.1.y_ref), channel_id=1, source_target_pairs={{0,1},{1,0},{2,3},{3,2},{4,5},{5,4},{6,7},{7,6},{8,9},{9,8},{10,11... | collective-permute-start | bytes 2064392 | tf_op jit(solution)/shard_map/ppermute | solution.py:31
  29.4 10.6 %collective-permute-start.9 = (bf16[256,512]{1,0:T(8,128)(2,1)S(1)}, bf16[256,512]{1,0:T(8,128)(2,1)S(1)}, u32[]{:S(2)}, u32[]{:S(2)}) collective-permute-start(bf16[256,512]{1,0:T(8,128)(2,1)S(1)} %collective-permute-done.6.r2_ref), channel_id=1, source_target_pairs={{4,0},{12,8},{20,16},{28,24},{5,1},{13,9},{21,17},{29,25},{6,2},{1... | collective-permute-start | bytes 786440 | tf_op jit(solution)/shard_map/ppermute | solution.py:36
  31.5 2.6 %copy-start = (bf16[512,5376]{1,0:T(8,128)(2,1)S(1)}, bf16[512,5376]{1,0:T(8,128)(2,1)}, u32[]{:S(2)}) copy-start(bf16[512,5376]{1,0:T(8,128)(2,1)} %w_ref.3) | copy-start | bytes 16515076
  34.1 1.1 %copy-start.3 = (bf16[64,5376]{1,0:T(8,128)(2,1)S(1)}, bf16[64,5376]{1,0:T(8,128)(2,1)}, u32[]{:S(2)}) copy-start(bf16[64,5376]{1,0:T(8,128)(2,1)} %own_ref.1) | copy-start | bytes 2064388
  35.2 4.8 %copy-start.1 = (bf16[512,5376]{1,0:T(8,128)(2,1)S(1)}, bf16[512,5376]{1,0:T(8,128)(2,1)}, u32[]{:S(2)}) copy-start(bf16[512,5376]{1,0:T(8,128)(2,1)} %w_ref.3) | copy-start | bytes 16515076
  44.3 3.5 %collective-permute-start.10 = (bf16[64,5376]{1,0:T(8,128)(2,1)S(1)}, bf16[64,5376]{1,0:T(8,128)(2,1)S(1)}, u32[]{:S(2)}, u32[]{:S(2)}) collective-permute-start(bf16[64,5376]{1,0:T(8,128)(2,1)S(1)} %get-tuple-element.35), channel_id=1, source_target_pairs={{0,1},{1,0},{2,3},{3,2},{4,5},{5,4},{6,7},{7,6},{8,9},{9,8},{10,11... | collective-permute-start | bytes 2064392 | tf_op jit(solution)/shard_map/ppermute | solution.py:31
  49.3 8.7 %collective-permute-start.11 = (bf16[256,512]{1,0:T(8,128)(2,1)S(1)}, bf16[256,512]{1,0:T(8,128)(2,1)S(1)}, u32[]{:S(2)}, u32[]{:S(2)}) collective-permute-start(bf16[256,512]{1,0:T(8,128)(2,1)S(1)} %get-tuple-element.36), channel_id=1, source_target_pairs={{0,4},{4,0},{8,12},{12,8},{16,20},{20,16},{24,28},{28,24},{1,5},{5... | collective-permute-start | bytes 786440 | tf_op jit(solution)/shard_map/ppermute | solution.py:31
  49.3 8.9 %collective-permute-start.13 = (bf16[24,5376]{1,0:T(8,128)(2,1)}, bf16[24,5376]{1,0:T(8,128)(2,1)}, u32[]{:S(2)}, u32[]{:S(2)}) collective-permute-start(bf16[24,5376]{1,0:T(8,128)(2,1)} %get-tuple-element.47), channel_id=1, source_target_pairs={{0,2},{1,3},{2,0},{3,1},{4,6},{5,7},{6,4},{7,5},{8,10},{9,11},{10,... | collective-permute-start | bytes 774152 | tf_op jit(solution)/shard_map/ppermute | solution.py:31
  49.8 20.0 %copy-start.6 = (bf16[16,5376]{1,0:T(8,128)(2,1)S(1)}, bf16[16,5376]{1,0:T(8,128)(2,1)}, u32[]{:S(2)}) copy-start(bf16[16,5376]{1,0:T(8,128)(2,1)} %add_convert_fusion.5) | copy-start | bytes 516100
  58.2 9.8 %collective-permute-start.16 = (bf16[256,512]{1,0:T(8,128)(2,1)S(1)}, bf16[256,512]{1,0:T(8,128)(2,1)S(1)}, u32[]{:S(2)}, u32[]{:S(2)}) collective-permute-start(bf16[256,512]{1,0:T(8,128)(2,1)S(1)} %add_convert_fusion.2), channel_id=1, source_target_pairs={{8,0},{12,4},{16,8},{20,12},{24,16},{28,20},{9,1},{13,5},{17,9},{2... | collective-permute-start | bytes 786440 | tf_op jit(solution)/shard_map/ppermute | solution.py:26
  59.5 8.5 %collective-permute-start.17 = (bf16[256,512]{1,0:T(8,128)(2,1)S(1)}, bf16[256,512]{1,0:T(8,128)(2,1)S(1)}, u32[]{:S(2)}, u32[]{:S(2)}) collective-permute-start(bf16[256,512]{1,0:T(8,128)(2,1)S(1)} %get-tuple-element.44), channel_id=1, source_target_pairs={{0,4},{4,0},{8,12},{12,8},{16,20},{20,16},{24,28},{28,24},{1,5},{5... | collective-permute-start | bytes 786440 | tf_op jit(solution)/shard_map/ppermute | solution.py:31
  61.3 7.2 %collective-permute-start.14 = (bf16[24,5376]{1,0:T(8,128)(2,1)S(1)}, bf16[24,5376]{1,0:T(8,128)(2,1)S(1)}, u32[]{:S(2)}, u32[]{:S(2)}) collective-permute-start(bf16[24,5376]{1,0:T(8,128)(2,1)S(1)} %get-tuple-element.46), channel_id=1, source_target_pairs={{0,2},{1,3},{2,0},{3,1},{4,6},{5,7},{6,4},{7,5},{8,10},{9,11},{10,... | collective-permute-start | bytes 774152 | tf_op jit(solution)/shard_map/ppermute | solution.py:31
  61.8 16.1 %collective-permute-start.12 = (bf16[64,5376]{1,0:T(8,128)(2,1)S(1)}, bf16[64,5376]{1,0:T(8,128)(2,1)S(1)}, u32[]{:S(2)}, u32[]{:S(2)}) collective-permute-start(bf16[64,5376]{1,0:T(8,128)(2,1)S(1)} %get-tuple-element.37), channel_id=1, source_target_pairs={{0,1},{1,0},{2,3},{3,2},{4,5},{5,4},{6,7},{7,6},{8,9},{9,8},{10,11... | collective-permute-start | bytes 2064392 | tf_op jit(solution)/shard_map/ppermute | solution.py:31
  68.5 8.6 %collective-permute-start.18 = (bf16[256,512]{1,0:T(8,128)(2,1)S(1)}, bf16[256,512]{1,0:T(8,128)(2,1)S(1)}, u32[]{:S(2)}, u32[]{:S(2)}) collective-permute-start(bf16[256,512]{1,0:T(8,128)(2,1)S(1)} %add_convert_fusion.1), channel_id=1, source_target_pairs={{8,0},{12,4},{16,8},{20,12},{24,16},{28,20},{9,1},{13,5},{17,9},{2... | collective-permute-start | bytes 786440 | tf_op jit(solution)/shard_map/ppermute | solution.py:26
  69.8 8.1 %collective-permute-start.15 = (bf16[16,5376]{1,0:T(8,128)(2,1)S(1)}, bf16[16,5376]{1,0:T(8,128)(2,1)S(1)}, u32[]{:S(2)}, u32[]{:S(2)}) collective-permute-start(bf16[16,5376]{1,0:T(8,128)(2,1)S(1)} %copy-done.6), channel_id=1, source_target_pairs={{0,2},{1,3},{2,0},{3,1},{4,6},{5,7},{6,4},{7,5},{8,10},{9,11},{10,... | collective-permute-start | bytes 516104 | tf_op jit(solution)/shard_map/ppermute | solution.py:31

commit v3 on v2

v3 whole, which is shorter than its diff:
```python
import jax
import jax.numpy as jnp
from jax import lax
from jax.experimental import pallas as pl
from jax.experimental.pallas import tpu as pltpu
from jax.sharding import PartitionSpec as P

HEAD_SIZE = 128
WIN = 1024
LOGIT_SCALE = 168.0 ** (-0.5)
LOG2E = 1.4426950408889634
NEG = -1e30
FAR = 4
F32 = jnp.float32
BF16 = jnp.bfloat16
SMALL = pl.CostEstimate(flops=1, bytes_accessed=1, transcendentals=0)
VMEM = pl.BlockSpec(memory_space=pltpu.VMEM)


def dot(a, b, ca, cb):
    return lax.dot_general(a, b, (((ca,), (cb,)), ((), ())), preferred_element_type=F32)


def shifted(value, steps):
    count = lax.axis_size("seq")
    first, last = (max(0, -steps), min(count, count - steps))
    return lax.ppermute(value, "seq", [(i, i + steps) for i in range(first, last)])


def swapped(value, axis, bit):
    count = lax.axis_size(axis)
    return lax.ppermute(value, axis, [(i, i ^ bit) for i in range(count)])


def far_swapped(lower, upper):
    count = lax.axis_size("seq")
    side = lax.rem(lax.div(lax.axis_index("seq"), FAR), 2)
    rounds = []
    for r in range(2):
        pairs = [(i, i + FAR) for i in range(count - FAR) if (i // FAR) % 2 == r]
        if pairs:
            pairs = pairs + [(j, i) for i, j in pairs]
            rounds.append(lax.ppermute(lower() if lower is upper else jnp.where(side == r, lower(), upper()), "seq", pairs))
    if len(rounds) == 1:
        return rounds[0], rounds[0]
    return jnp.where(side == 1, rounds[0], rounds[1]), jnp.where(side == 0, rounds[0], rounds[1])


def group_rows(group, head, size):
    return pl.ds(pl.multiple_of(jnp.bitwise_xor(group, head) * size, size), size)


def own_order(ref, head):
    size = ref.shape[0] // 4
    return jnp.concatenate([ref[group_rows(g, head, size), :] for g in range(4)], 0)


def stacked(mat, kv_head):
    low = 2 * kv_head * HEAD_SIZE
    return jnp.concatenate([mat[:, low : low + HEAD_SIZE], mat[:, low + HEAD_SIZE : low + 2 * HEAD_SIZE]], 0)


def causal_mask(tok, head):
    key_pos = lax.broadcasted_iota(jnp.int32, (tok, 2 * tok), 0)
    lane = lax.broadcasted_iota(jnp.int32, (tok, 2 * tok), 1)
    query_pos = jnp.bitwise_xor(jnp.bitwise_and(lane, tok - 1), head * (tok // 4))
    return query_pos >= key_pos


def columns(kv_cols, kv_head):
    low = kv_head * HEAD_SIZE
    return slice(low, low + HEAD_SIZE), slice(kv_cols + low, kv_cols + low + HEAD_SIZE)


def window(kv_ref, r1_ref, r2_ref, x1_ref, p0_ref, x2_ref, odd, cols):
    return [kv_ref[:, cols], r1_ref[:, cols], r2_ref[:, cols], x1_ref[:, cols], jnp.where(odd, p0_ref[:, cols], x2_ref[:, cols])]


def join_kernel(k_ref, v_ref, q_ref, kv_ref, sent_ref):
    lower = lax.rem(lax.div(lax.axis_index("seq"), FAR), 2) == 0
    kv = jnp.concatenate([k_ref[...], v_ref[...]], 1)
    kv_ref[...] = kv
    sent_ref[...] = jnp.where(lower, kv, q_ref[...])


def forward_kernel(q_ref, kv_ref, r1_ref, r2_ref, x1_ref, p0_ref, x2_ref, d_ref, w_ref,
                   p_ref, stat_ref, near_own_ref, near_core_ref, far_own_ref, far_core_ref, o_ref):
    seq, head = lax.axis_index("seq"), lax.axis_index("head")
    odd = lax.rem(seq, 2) == 1
    tok = q_ref.shape[0]
    kv_cols = kv_ref.shape[1] // 2
    q_rel = own_order(q_ref, head)
    causal = causal_mask(tok, head)
    near = jnp.where(seq >= 2, 0.0, NEG).astype(F32)
    far = jnp.where(seq >= 4, 0.0, NEG).astype(F32)
    mixed = jnp.where(jnp.logical_or(odd, seq >= 4), 0.0, NEG).astype(F32)
    biases = [None, near, far, near, mixed]
    scale = LOGIT_SCALE * LOG2E
    stats = []
    for g in range(kv_cols // HEAD_SIZE):
        kc, vc = columns(kv_cols, g)
        qg = stacked(q_rel, g)
        blocks = (kv_ref, r1_ref, r2_ref, x1_ref, p0_ref, x2_ref)
        key_blocks, value_blocks = window(*blocks, odd, kc), window(*blocks, odd, vc)
        scores = [dot(kb, qg, 1, 1) for kb in key_blocks]
        scores[0] = jnp.where(causal, scores[0], NEG)
        scores[2] = jnp.where(causal, NEG, scores[2])
        tops = [jnp.max(sb, axis=0, keepdims=True) for sb in scores]
        tops = [t if b is None else t + b for t, b in zip(tops, biases)]
        top = tops[0]
        for t in tops[1:]:
            top = jnp.maximum(top, t)
        top = top * scale
        probs = [jnp.exp2(sb * scale - (top if b is None else top - b)) for sb, b in zip(scores, biases)]
        total = sum(jnp.sum(pb, axis=0, keepdims=True) for pb in probs)
        inv = 1.0 / total
        out = jnp.zeros((HEAD_SIZE, 2 * tok), F32)
        for b in range(5):
            pb = (probs[b] * inv).astype(BF16)
            p_ref[g, b] = pb
            out = out + dot(value_blocks[b], pb, 0, 0)
        out = out.astype(BF16)
        grad = stacked(d_ref[...], g)
        delta = jnp.sum(grad.astype(F32).T * out.astype(F32), axis=0, keepdims=True)
        stats += [top + jnp.log2(total), delta]
        out = out.astype(F32).T.astype(BF16)
        low = 2 * g * HEAD_SIZE
        o_ref[:, low : low + HEAD_SIZE] = out[:tok]
        o_ref[:, low + HEAD_SIZE : low + 2 * HEAD_SIZE] = out[tok:]
    spare = stat_ref.shape[0] - len(stats)
    stat_ref[...] = jnp.concatenate(stats + [jnp.zeros((spare, 2 * tok), F32)], 0)
    project(o_ref[...], w_ref, (near_own_ref, near_core_ref, far_own_ref, far_core_ref))


def project(rows, w_ref, part_refs):
    size = part_refs[0].shape[0]
    cols = w_ref.shape[1]
    step = cols // 7 if cols % (7 * HEAD_SIZE) == 0 else cols
    for low in range(0, cols, step):
        part = dot(rows, w_ref[:, low : low + step], 1, 0).astype(BF16)
        for i, ref in enumerate(part_refs):
            ref[:, low : low + step] = part[i * size : (i + 1) * size]


def back_kernel(own_ref, core_ref, y_ref, yc_ref, w_ref, d_ref):
    rows = jnp.concatenate([own_ref[...], core_ref[...], y_ref[...], yc_ref[...]], 0)
    d_ref[...] = dot(rows, w_ref[...], 1, 1).astype(BF16)


def backward_kernel(q_ref, kv_ref, r1_ref, r2_ref, x1_ref, p0_ref, x2_ref, p_ref, stat_ref, d_ref,
                    dq_ref, town_ref, t1_ref, tx_ref, tz_ref):
    seq, head = lax.axis_index("seq"), lax.axis_index("head")
    odd = lax.rem(seq, 2) == 1
    tok = q_ref.shape[0]
    kv_cols = kv_ref.shape[1] // 2
    size = tok // 4
    q_rel = own_order(q_ref, head)
    outs = [town_ref, t1_ref, None, tx_ref, tz_ref]
    for g in range(kv_cols // HEAD_SIZE):
        kc, vc = columns(kv_cols, g)
        qg, dg = stacked(q_rel, g), stacked(d_ref[...], g)
        blocks = (kv_ref, r1_ref, r2_ref, x1_ref, p0_ref, x2_ref)
        key_blocks, value_blocks = window(*blocks, odd, kc), window(*blocks, odd, vc)
        delta = stat_ref[2 * g + 1 : 2 * g + 2, :]
        dq = jnp.zeros((HEAD_SIZE, 2 * tok), F32)
        for b in range(5):
            pb = p_ref[g, b]
            dp = dot(value_blocks[b], dg, 1, 1)
            ds = (pb.astype(F32) * (dp - delta)).astype(BF16)
            if outs[b] is not None:
                outs[b][:, vc] = dot(pb, dg, 1, 0).astype(outs[b].dtype)
                outs[b][:, kc] = (dot(ds, qg, 1, 0) * LOGIT_SCALE).astype(outs[b].dtype)
            dq = dq + dot(key_blocks[b], ds, 0, 0)
        dq = (dq * LOGIT_SCALE).T.astype(BF16)
        low = 2 * g * HEAD_SIZE
        for r in range(4):
            rows = group_rows(r, head, size)
            dq_ref[rows, low : low + HEAD_SIZE] = dq[r * size : (r + 1) * size]
            dq_ref[rows, low + HEAD_SIZE : low + 2 * HEAD_SIZE] = dq[tok + r * size : tok + (r + 1) * size]


def far_kernel(kv_ref, qf_ref, df_ref, sf_ref, qx_ref, dx_ref, sx_ref, t_ref):
    seq, head = lax.axis_index("seq"), lax.axis_index("head")
    count = lax.axis_size("seq")
    tok = kv_ref.shape[0]
    kv_cols = kv_ref.shape[1] // 2
    straight = jnp.logical_and(jnp.logical_not(causal_mask(tok, head)), seq + FAR < count)
    across = jnp.logical_and(lax.rem(seq, 2) == 1, seq + FAR - 1 < count)
    sources = ((qf_ref, df_ref, sf_ref, straight), (qx_ref, dx_ref, sx_ref, across))
    sources = [(own_order(q, head), d[...], st, keep) for q, d, st, keep in sources]
    scale = LOGIT_SCALE * LOG2E
    for g in range(kv_cols // HEAD_SIZE):
        kc, vc = columns(kv_cols, g)
        key, value = kv_ref[:, kc], kv_ref[:, vc]
        dk = jnp.zeros((tok, HEAD_SIZE), F32)
        dv = jnp.zeros((tok, HEAD_SIZE), F32)
        for q_rel, d_rel, st, keep in sources:
            qg, dg = stacked(q_rel, g), stacked(d_rel, g)
            prob = jnp.exp2(dot(key, qg, 1, 1) * scale - st[2 * g : 2 * g + 1, :])
            prob = jnp.where(keep, prob, 0.0).astype(BF16)
            dp = dot(value, dg, 1, 1)
            ds = (prob.astype(F32) * (dp - st[2 * g + 1 : 2 * g + 2, :])).astype(BF16)
            dv = dv + dot(prob, dg, 1, 0)
            dk = dk + dot(ds, qg, 1, 0)
        t_ref[:, kc] = dk * LOGIT_SCALE
        t_ref[:, vc] = dv


def per_device(queries, keys, values, out_weight, out_grad):
    tok, q_cols = queries.shape
    kv_cols = keys.shape[1]
    kv_heads = kv_cols // HEAD_SIZE
    odd = lax.rem(lax.axis_index("seq"), 2) == 1
    half, size = tok // 2, tok // 4
    rows = jax.ShapeDtypeStruct((size, out_weight.shape[1]), BF16)
    block = jax.ShapeDtypeStruct((tok, 2 * kv_cols), BF16)
    wide_block = jax.ShapeDtypeStruct((tok, 2 * kv_cols), F32)

    def call(kernel, name, outs, scratch, *operands):
        return pl.pallas_call(
            kernel,
            out_shape=outs,
            in_specs=[VMEM] * len(operands),
            out_specs=jax.tree.map(lambda _: VMEM, outs),
            scratch_shapes=scratch,
            compiler_params=pltpu.CompilerParams(vmem_limit_bytes=16 << 20),
            cost_estimate=SMALL,
            name=name,
        )(*operands)

    def wide(a):
        return a.astype(F32)

    def gate(value, *others):
        return lax.optimization_barrier((value, *others))[0]

    og_y = swapped(out_grad, "head", 2)
    kv, far_sent = call(join_kernel, "join", (block, block), [], keys, values, queries)
    r1 = shifted(kv, 2)
    r2, q_far = far_swapped(lambda: kv, lambda: queries) if lax.axis_size("seq") > 2 * FAR else (far_swapped(*[lambda: far_sent] * 2))
    p0 = swapped(kv, "seq", 1)
    og_c = swapped(out_grad, "head", 1)
    x1 = swapped(gate(r1, p0), "seq", 1)
    x2 = swapped(r2 if r2 is q_far else jnp.where(odd, r2, q_far), "seq", 1)
    og_yc = swapped(gate(og_y, x1, r2), "head", 1)
    grad = call(back_kernel, "turn_back", jax.ShapeDtypeStruct((tok, q_cols), BF16), [], out_grad, og_c, og_y, og_yc, out_weight)

    def down(value):
        return far_swapped(*[lambda: value] * 2)[1]

    grad_far = down(grad)
    probs, stats, near_own, near_core, far_own, far_core = call(
        forward_kernel,
        "attend",
        (
            jax.ShapeDtypeStruct((kv_heads, 5, tok, 2 * tok), BF16),
            jax.ShapeDtypeStruct((8 * pl.cdiv(2 * kv_heads, 8), 2 * tok), F32),
            rows, rows, rows, rows,
        ),
        [pltpu.VMEM((tok, q_cols), BF16)],
        queries, kv, r1, r2, x1, p0, x2, grad, out_weight,
    )
    sent = swapped(far_core, "head", 1)
    stats_far = down(stats)
    far_sum = (wide(far_own) + wide(sent)).astype(BF16)
    from_y = swapped(far_sum, "head", 2)
    stats_x = swapped(stats_far, "seq", 1)
    grad_x = swapped(gate(grad_far, stats_x), "seq", 1)

    query_gradient, t_own, t_1, t_x, t_z = call(
        backward_kernel,
        "attend_grad",
        (jax.ShapeDtypeStruct((tok, q_cols), BF16), wide_block, block, block, block),
        [],
        queries, kv, r1, r2, x1, p0, x2, probs, stats, grad,
    )
    d1 = swapped(gate(t_x, far_sum), "seq", 1)
    e1 = shifted((wide(t_1) + wide(d1)).astype(BF16), -2)
    g = swapped(gate(t_z, d1), "seq", 1)
    from_core = swapped(gate(near_core, d1), "head", 1)
    t_far = call(far_kernel, "far_grad", wide_block, [], gate(kv, from_y), q_far, grad_far, stats_far, x2, grad_x, stats_x)

    def total(cols):
        kept = jnp.where(odd, 0.0, wide(g[:, cols]))
        return (t_own[:, cols] + t_far[:, cols] + wide(e1[:, cols]) + kept).astype(BF16)

    projected = (wide(near_own) + wide(from_core) + wide(from_y)).astype(BF16)
    return (projected, query_gradient, total(slice(0, kv_cols)), total(slice(kv_cols, 2 * kv_cols)))


def solution(mesh):
    return jax.shard_map(
        per_device,
        mesh=mesh,
        in_specs=(
            P("seq", "head"),
            P("seq", "head"),
            P("seq", "head"),
            P("head", None),
            P(("seq", "head"), None),
        ),
        out_specs=(P(("seq", "head"), None), P("seq", "head"), P("seq", "head"), P("seq", "head")),
        check_vma=False,
    )
```

time: 80.4 us -> 80.3 us (level)
  waiting for transfers between devices: 33.7 us -> 29.1 us
  local copies, waits for them, and re-layouts: 3.68 us -> 6.42 us
  other arithmetic: 4.6 us -> 6.12 us
  Pallas kernels: 9.3 us -> 10.7 us
  starting transfers between devices: 27.9 us -> 26.8 us
    ppermute x5 -> x2, starting transfers between devices: 13 us -> 4.91 us  [shifted(): lax.ppermute(value, 'seq', [(i, i + steps) for i in range(first, last)])]
    ppermute x5 -> x2, waiting for transfers between devices: 14.3 us -> 6.48 us  [shifted(): lax.ppermute(value, 'seq', [(i, i + steps) for i in range(first, last)])]
    ppermute x3, waiting for transfers between devices: 6.81 us -> 13.1 us  [far_swapped(): lax.ppermute(lower() if lower is upper else jnp.where(side == r, lower(),...]
    ppermute x3, starting transfers between devices: 5.98 us -> 9.58 us  [far_swapped(): lax.ppermute(lower() if lower is upper else jnp.where(side == r, lower(),...]
    ppermute x11 -> x13, starting transfers between devices: 8.95 us -> 12.3 us  [swapped(): return lax.ppermute(value, axis, [(i, i ^ bit) for i in range(count)])]
    ppermute x11 -> x13, waiting for transfers between devices: 12.5 us -> 9.57 us  [swapped(): return lax.ppermute(value, axis, [(i, i ^ bit) for i in range(count)])]
    unnamed x14, local copies, waits for them, and re-layouts: 3.68 us -> 6.42 us
    convert_element_type x6 -> x4, other arithmetic: 4.55 us -> 6.12 us  [the longest x1 2.4 us: per_device(): projected = (wide(near_own) + wide(from_core) + wide(from_y)).astype(BF16)]
  transfers between devices with their start and end apart: 19 -> 18, of which waited for: 11 -> 10; matrix products, arithmetic and copies ran while one was open for 1% -> 5% of each run, Pallas kernels for 6% -> 8%
where the time goes in v3:
time: 80.3 us; the launch traced here: 79.9 us
  waiting for transfers between devices  29.1 us (36%)
  starting transfers between devices  26.8 us (33%)
  Pallas kernels  10.7 us (13%)
  local copies, waits for them, and re-layouts  6.42 us (8%)
  other arithmetic  6.12 us (8%)
    ppermute x3, waiting for transfers between devices, far_swapped(): lax.ppermute(lower() if lower is upper else jnp.where(side == r, lower(),...  13.1 us
    ppermute x13, starting transfers between devices, swapped(): return lax.ppermute(value, axis, [(i, i ^ bit) for i in range(count)])  12.3 us
    pallas_call x5, Pallas kernels, call(): pl.pallas_call(kernel, out_shape=outs, in_specs=[VMEM] * len(operands), o...  10.7 us
    ppermute x3, starting transfers between devices, far_swapped(): lax.ppermute(lower() if lower is upper else jnp.where(side == r, lower(),...  9.58 us
    ppermute x13, waiting for transfers between devices, swapped(): return lax.ppermute(value, axis, [(i, i ^ bit) for i in range(count)])  9.57 us
    ppermute x2, waiting for transfers between devices, shifted(): lax.ppermute(value, 'seq', [(i, i + steps) for i in range(first, last)])  6.48 us
    unnamed x14, local copies, waits for them, and re-layouts  6.42 us
    ppermute x2, starting transfers between devices, shifted(): lax.ppermute(value, 'seq', [(i, i + steps) for i in range(first, last)])  4.91 us
  transfers between devices with their start and end apart: 18, of which 10 were waited for; matrix products, arithmetic and copies ran while one was open for 5% of the time, Pallas kernels for 8%

profile of v3, /device:TPU:0, one launch (start us, length us, event | category | flops | bytes accessed | tf_op | source)
XLA Modules:
  0.0 79.9 jit_solution(6487252011938250135)
XLA Ops:
  0.6 3.0 %collective-permute-start.6 = (bf16[64,5376]{1,0:T(8,128)(2,1)}, bf16[64,5376]{1,0:T(8,128)(2,1)S(1)}, u32[]{:S(2)}, u32[]{:S(2)}) collective-permute-start(bf16[64,5376]{1,0:T(8,128)(2,1)} %own_ref.1), channel_id=1, source_target_pairs={{0,2},{1,3},{2,0},{3,1},{4,6},{5,7},{6,4},{7,5},{8,10},{9,11},{10,... | collective-permute-start | bytes 2064392 | tf_op jit(solution)/shard_map/ppermute | solution.py:32
  3.7 0.0 copy-start.2
  3.7 0.9 %copy-done.2 = bf16[256,512]{1,0:T(8,128)(2,1)S(1)} copy-done((bf16[256,512]{1,0:T(8,128)(2,1)S(1)}, bf16[256,512]{1,0:T(8,128)(2,1)}, u32[]{:S(2)}) %copy-start.2) | copy-done | bytes 262168
  4.6 0.0 copy-start.5
  4.6 0.9 %copy-done.5 = bf16[256,256]{1,0:T(8,128)(2,1)S(1)} copy-done((bf16[256,256]{1,0:T(8,128)(2,1)S(1)}, bf16[256,256]{1,0:T(8,128)(2,1)}, u32[]{:S(2)}) %copy-start.5) | copy-done | bytes 131096
  5.5 0.0 copy-start.6
  5.5 0.9 %copy-done.6 = bf16[256,256]{1,0:T(8,128)(2,1)S(1)} copy-done((bf16[256,256]{1,0:T(8,128)(2,1)S(1)}, bf16[256,256]{1,0:T(8,128)(2,1)}, u32[]{:S(2)}) %copy-start.6) | copy-done | bytes 131096
  6.4 0.0 copy-start.3
  6.4 0.1 join.1
  6.5 3.6 %collective-permute-start = (bf16[256,512]{1,0:T(8,128)(2,1)S(1)}, bf16[256,512]{1,0:T(8,128)(2,1)S(1)}, u32[]{:S(2)}, u32[]{:S(2)}) collective-permute-start(bf16[256,512]{1,0:T(8,128)(2,1)S(1)} %get-tuple-element.39.kv_ref), channel_id=1, source_target_pairs={{0,8},{4,12},{8,16},{12,20},{16,24},{20,28},{1,9},{5,13},{9,17},{1... | collective-permute-start | bytes 786440 | tf_op jit(solution)/shard_map/ppermute | solution.py:27
  10.1 1.6 %collective-permute-start.2 = (bf16[256,512]{1,0:T(8,128)(2,1)S(1)}, bf16[256,512]{1,0:T(8,128)(2,1)S(1)}, u32[]{:S(2)}, u32[]{:S(2)}) collective-permute-start(bf16[256,512]{1,0:T(8,128)(2,1)S(1)} %get-tuple-element.39.kv_ref), channel_id=1, source_target_pairs={{0,4},{4,0},{8,12},{12,8},{16,20},{20,16},{24,28},{28,24},{1,5},{5... | collective-permute-start | bytes 786440 | tf_op jit(solution)/shard_map/ppermute | solution.py:32
  11.7 2.6 %collective-permute-start.1 = (bf16[256,512]{1,0:T(8,128)(2,1)S(1)}, bf16[256,512]{1,0:T(8,128)(2,1)S(1)}, u32[]{:S(2)}, u32[]{:S(2)}) collective-permute-start(bf16[256,512]{1,0:T(8,128)(2,1)S(1)} %get-tuple-element.25), channel_id=1, source_target_pairs={{0,16},{4,20},{8,24},{12,28},{16,0},{20,4},{24,8},{28,12},{1,17},{... | collective-permute-start | bytes 786440 | tf_op jit(solution)/shard_map/ppermute | solution.py:43
  14.3 2.6 %collective-permute-done.r1_ref = bf16[256,512]{1,0:T(8,128)(2,1)S(1)} collective-permute-done((bf16[256,512]{1,0:T(8,128)(2,1)S(1)}, bf16[256,512]{1,0:T(8,128)(2,1)S(1)}, u32[]{:S(2)}, u32[]{:S(2)}) %collective-permute-start) | collective-permute-done | bytes 262176 | tf_op jit(solution)/shard_map/ppermute | solution.py:27
  16.8 0.8 %collective-permute-done.2.p0_ref = bf16[256,512]{1,0:T(8,128)(2,1)S(1)} collective-permute-done((bf16[256,512]{1,0:T(8,128)(2,1)S(1)}, bf16[256,512]{1,0:T(8,128)(2,1)S(1)}, u32[]{:S(2)}, u32[]{:S(2)}) %collective-permute-start.2) | collective-permute-done | bytes 262176 | tf_op jit(solution)/shard_map/ppermute | solution.py:32
  17.7 1.5 %collective-permute-start.3 = (bf16[256,512]{1,0:T(8,128)(2,1)S(1)}, bf16[256,512]{1,0:T(8,128)(2,1)S(1)}, u32[]{:S(2)}, u32[]{:S(2)}) collective-permute-start(bf16[256,512]{1,0:T(8,128)(2,1)S(1)} %collective-permute-done.r1_ref), channel_id=1, source_target_pairs={{0,4},{4,0},{8,12},{12,8},{16,20},{20,16},{24,28},{28,24},{1,5},{5... | collective-permute-start | bytes 786440 | tf_op jit(solution)/shard_map/ppermute | solution.py:32
  19.2 0.0 collective-permute-start.5
  19.2 6.2 %collective-permute-done.1.r2_ref.qf_ref = bf16[256,512]{1,0:T(8,128)(2,1)S(1)} collective-permute-done((bf16[256,512]{1,0:T(8,128)(2,1)S(1)}, bf16[256,512]{1,0:T(8,128)(2,1)S(1)}, u32[]{:S(2)}, u32[]{:S(2)}) %collective-permute-start.1) | collective-permute-done | bytes 262176 | tf_op jit(solution)/shard_map/ppermute | solution.py:43
  25.4 0.0 collective-permute-done.3.x1_ref
  25.4 0.0 collective-permute-done.6.y_ref
  25.4 0.0 collective-permute-start.7
  25.4 0.6 collective-permute-start.4
  26.0 0.0 collective-permute-done.5.core_ref
  26.0 1.5 %collective-permute-done.7.yc_ref = bf16[64,5376]{1,0:T(8,128)(2,1)S(1)} collective-permute-done((bf16[64,5376]{1,0:T(8,128)(2,1)S(1)}, bf16[64,5376]{1,0:T(8,128)(2,1)S(1)}, u32[]{:S(2)}, u32[]{:S(2)}) %collective-permute-start.7) | collective-permute-done | bytes 688160 | tf_op jit(solution)/shard_map/ppermute | solution.py:32
  27.6 0.0 copy-start
  27.6 2.6 %copy-done = bf16[512,5376]{1,0:T(8,128)(2,1)S(1)} copy-done((bf16[512,5376]{1,0:T(8,128)(2,1)S(1)}, bf16[512,5376]{1,0:T(8,128)(2,1)}, u32[]{:S(2)}) %copy-start) | copy-done | bytes 5505048
  30.1 0.0 copy-start.4
  30.1 1.1 %copy-done.4 = bf16[64,5376]{1,0:T(8,128)(2,1)S(1)} copy-done((bf16[64,5376]{1,0:T(8,128)(2,1)S(1)}, bf16[64,5376]{1,0:T(8,128)(2,1)}, u32[]{:S(2)}) %copy-start.4) | copy-done | bytes 688152
  31.2 0.0 copy-start.1
  31.2 1.6 %turn_back.1.d_ref = bf16[256,512]{1,0:T(8,128)(2,1)S(1)} custom-call(bf16[64,5376]{1,0:T(8,128)(2,1)S(1)} %copy-done.4, bf16[64,5376]{1,0:T(8,128)(2,1)S(1)} %collective-permute-done.5.core_ref, bf16[64,5376]{1,0:T(8,128)(2,1)S(1)} %collective-permute-done.6.y_ref, bf16[64,5376]{1,0:T(8,128)(2,1)S(1)} %collective-permute-done.7.yc_ref, ...), custom_call_target="tpu_custom_call" | custom-call | flops 1 | bytes 1 | tf_op jit(solution)/shard_map/turn_back/pallas_call | solution.py:220
  32.8 1.3 %collective-permute-done.4.x2_ref.qx_ref = bf16[256,512]{1,0:T(8,128)(2,1)S(1)} collective-permute-done((bf16[256,512]{1,0:T(8,128)(2,1)S(1)}, bf16[256,512]{1,0:T(8,128)(2,1)S(1)}, u32[]{:S(2)}, u32[]{:S(2)}) %collective-permute-start.4) | collective-permute-done | bytes 262176 | tf_op jit(solution)/shard_map/ppermute | solution.py:32
  34.1 0.0 copy-done.3
  34.1 0.0 copy-done.1
  34.1 4.2 %attend.1 = (bf16[2,5,256,512]{3,2,1,0:T(8,128)(2,1)S(1)}, f32[8,512]{1,0:T(8,128)S(1)}, bf16[64,5376]{1,0:T(8,128)(2,1)S(1)}, bf16[64,5376]{1,0:T(8,128)(2,1)S(...) custom-call(bf16[256,512]{1,0:T(8,128)(2,1)S(1)} %copy-done.3, ...), custom_call_target="tpu_custom_call" | custom-call | flops 1 | bytes 1 | tf_op jit(solution)/shard_map/attend/pallas_call | solution.py:220
  38.4 0.1 collective-permute-start.8
  38.4 7.0 %collective-permute-start.12 = (bf16[256,512]{1,0:T(8,128)(2,1)S(1)}, bf16[256,512]{1,0:T(8,128)(2,1)S(1)}, u32[]{:S(2)}, u32[]{:S(2)}) collective-permute-start(bf16[256,512]{1,0:T(8,128)(2,1)S(1)} %turn_back.1.d_ref), channel_id=1, source_target_pairs={{0,16},{4,20},{8,24},{12,28},{16,0},{20,4},{24,8},{28,12},{1,17},{... | collective-permute-start | bytes 786440 | tf_op jit(solution)/shard_map/ppermute | solution.py:43
  45.4 3.3 %attend_grad.1 = (bf16[256,512]{1,0:T(8,128)(2,1)}, f32[256,512]{1,0:T(8,128)S(1)}, bf16[256,512]{1,0:T(8,128)(2,1)S(1)}, bf16[256,512]{1,0:T(8,128)(2,1)S(1)}, bf16[256,512]{1,0:T(8,128)(2,1)S(1)}) custom-call(bf16[256,512]{1,0:T(8,128)(2,1)S(1)} %copy-done.3, bf16[256,512]{1,0:T(8,128)(2,1)S(1)} %get-tuple-element.39.kv_ref, ...), custom_call_target="tpu_custom_call" | custom-call | flops 1 | bytes 1 | tf_op jit(solution)/shard_map/attend_grad/pallas_call | solution.py:220
  48.8 0.0 collective-permute-done.8
  48.8 1.0 %add_convert_fusion.1 = bf16[64,5376]{1,0:T(8,128)(2,1)} fusion(bf16[64,5376]{1,0:T(8,128)(2,1)S(1)} %collective-permute-done.8, bf16[64,5376]{1,0:T(8,128)(2,1)S(1)} %get-tuple-element.33), kind=kLoop, calls=%fused_computation.1 | loop fusion | flops 1376256 | bytes 2064384 | tf_op jit(solution)/shard_map/convert_element_type | solution.py:265
  49.8 1.5 %collective-permute-start.9 = (bf16[256,512]{1,0:T(8,128)(2,1)S(1)}, bf16[256,512]{1,0:T(8,128)(2,1)S(1)}, u32[]{:S(2)}, u32[]{:S(2)}) collective-permute-start(bf16[256,512]{1,0:T(8,128)(2,1)S(1)} %get-tuple-element.35), channel_id=1, source_target_pairs={{0,4},{4,0},{8,12},{12,8},{16,20},{20,16},{24,28},{28,24},{1,5},{5... | collective-permute-start | bytes 786440 | tf_op jit(solution)/shard_map/ppermute | solution.py:32
  51.3 0.5 collective-permute-start.11
  51.8 0.0 collective-permute-start.13
  51.8 6.9 %collective-permute-done.13.sf_ref = f32[8,512]{1,0:T(8,128)S(1)} collective-permute-done((f32[8,512]{1,0:T(8,128)S(1)}, f32[8,512]{1,0:T(8,128)S(1)}, u32[]{:S(2)}, u32[]{:S(2)}) %collective-permute-start.13) | collective-permute-done | bytes 16416 | tf_op jit(solution)/shard_map/ppermute | solution.py:43
  58.6 1.5 %collective-permute-start.14 = (f32[8,512]{1,0:T(8,128)S(1)}, f32[8,512]{1,0:T(8,128)S(1)}, u32[]{:S(2)}, u32[]{:S(2)}) collective-permute-start(f32[8,512]{1,0:T(8,128)S(1)} %collective-permute-done.13.sf_ref), channel_id=1, source_target_pairs={{0,4},{4,0},{8,12},{12,8},{16,20},{20,16},{24,28},{28,24},{1,5},{5... | collective-permute-start | bytes 49160 | tf_op jit(solution)/shard_map/ppermute | solution.py:32
  60.1 2.3 %collective-permute-done.14.sx_ref = f32[8,512]{1,0:T(8,128)S(1)} collective-permute-done((f32[8,512]{1,0:T(8,128)S(1)}, f32[8,512]{1,0:T(8,128)S(1)}, u32[]{:S(2)}, u32[]{:S(2)}) %collective-permute-start.14) | collective-permute-done | bytes 16416 | tf_op jit(solution)/shard_map/ppermute | solution.py:32
  62.4 0.0 collective-permute-done.12.df_ref
  62.4 1.5 %collective-permute-start.15 = (bf16[256,512]{1,0:T(8,128)(2,1)S(1)}, bf16[256,512]{1,0:T(8,128)(2,1)S(1)}, u32[]{:S(2)}, u32[]{:S(2)}) collective-permute-start(bf16[256,512]{1,0:T(8,128)(2,1)S(1)} %collective-permute-done.12.df_ref), channel_id=1, source_target_pairs={{0,4},{4,0},{8,12},{12,8},{16,20},{20,16},{24,28},{28,24},{1,5},{5... | collective-permute-start | bytes 786440 | tf_op jit(solution)/shard_map/ppermute | solution.py:32
  63.9 0.0 collective-permute-done.9
  63.9 0.0 collective-permute-start.10
  63.9 0.8 %add_convert_fusion.2 = bf16[256,512]{1,0:T(8,128)(2,1)} fusion(bf16[256,512]{1,0:T(8,128)(2,1)S(1)} %collective-permute-done.9, bf16[256,512]{1,0:T(8,128)(2,1)S(1)} %get-tuple-element.41), kind=kLoop, calls=%fused_computation.2 | loop fusion | flops 524288 | bytes 786432 | tf_op jit(solution)/shard_map/convert_element_type | solution.py:278
  64.7 1.3 %collective-permute-start.16 = (bf16[256,512]{1,0:T(8,128)(2,1)}, bf16[256,512]{1,0:T(8,128)(2,1)}, u32[]{:S(2)}, u32[]{:S(2)}) collective-permute-start(bf16[256,512]{1,0:T(8,128)(2,1)} %add_convert_fusion.2), channel_id=1, source_target_pairs={{8,0},{12,4},{16,8},{20,12},{24,16},{28,20},{9,1},{13,5},{17,9},{2... | collective-permute-start | bytes 786440 | tf_op jit(solution)/shard_map/ppermute | solution.py:27
  66.0 0.6 collective-permute-start.17
  66.6 2.2 %collective-permute-done.11 = bf16[64,5376]{1,0:T(8,128)(2,1)} collective-permute-done((bf16[64,5376]{1,0:T(8,128)(2,1)}, bf16[64,5376]{1,0:T(8,128)(2,1)}, u32[]{:S(2)}, u32[]{:S(2)}) %collective-permute-start.11) | collective-permute-done | bytes 688160 | tf_op jit(solution)/shard_map/ppermute | solution.py:32
  68.8 1.4 %collective-permute-done.15.dx_ref = bf16[256,512]{1,0:T(8,128)(2,1)S(1)} collective-permute-done((bf16[256,512]{1,0:T(8,128)(2,1)S(1)}, bf16[256,512]{1,0:T(8,128)(2,1)S(1)}, u32[]{:S(2)}, u32[]{:S(2)}) %collective-permute-start.15) | collective-permute-done | bytes 262176 | tf_op jit(solution)/shard_map/ppermute | solution.py:32
  70.2 1.5 %far_grad.1 = f32[256,512]{1,0:T(8,128)S(1)} custom-call(bf16[256,512]{1,0:T(8,128)(2,1)S(1)} %get-tuple-element.39.kv_ref, bf16[256,512]{1,0:T(8,128)(2,1)S(1)} %collective-permute-done.1.r2_ref.qf_ref, bf16[256,512]{1,0:T(8,128)(2,1)S(1)} %collective-permute-done.12.df_ref, f32[8,512]{1,0:T(8,128)S(1)} %collective-permute-done.13.sf_ref, ...), custom_call_target="tpu_custom_call" | custom-call | flops 1 | bytes 1 | tf_op jit(solution)/shard_map/far_grad/pallas_call | solution.py:220
  71.7 3.9 %collective-permute-done.16 = bf16[256,512]{1,0:T(8,128)(2,1)} collective-permute-done((bf16[256,512]{1,0:T(8,128)(2,1)}, bf16[256,512]{1,0:T(8,128)(2,1)}, u32[]{:S(2)}, u32[]{:S(2)}) %collective-permute-start.16) | collective-permute-done | bytes 262176 | tf_op jit(solution)/shard_map/ppermute | solution.py:27
  75.6 0.0 collective-permute-done.17
  75.6 1.9 %fusion.2 = (bf16[256,256]{1,0:T(8,128)(2,1)}, bf16[256,256]{1,0:T(8,128)(2,1)}) fusion(f32[256,512]{1,0:T(8,128)S(1)} %far_grad.1, f32[256,512]{1,0:T(8,128)S(1)} %get-tuple-element.38, bf16[256,512]{1,0:T(8,128)(2,1)} %collective-permute-done.17, bf16[256,512]{1,0:T(8,128)(2,1)} %collective-permute-done.16, pred[]{:T(512)S(6)} %eq.3), kind=kLoop, calls=%fused_computation.6 | loop fusion | flops 917504 | bytes 1835009 | tf_op jit(solution)/shard_map/convert_element_type | solution.py:285
  77.5 0.0 collective-permute-done.10
  77.5 2.4 %add_convert_fusion = bf16[64,5376]{1,0:T(8,128)(2,1)} fusion(bf16[64,5376]{1,0:T(8,128)(2,1)} %collective-permute-done.11, bf16[64,5376]{1,0:T(8,128)(2,1)} %collective-permute-done.10, bf16[64,5376]{1,0:T(8,128)(2,1)S(1)} %get-tuple-element.28), kind=kLoop, calls=%fused_computation | loop fusion | flops 2064384 | bytes 2752512 | tf_op jit(solution)/shard_map/convert_element_type | solution.py:287
Async XLA Ops:
  0.6 24.8 %collective-permute-start.6 = (bf16[64,5376]{1,0:T(8,128)(2,1)}, bf16[64,5376]{1,0:T(8,128)(2,1)S(1)}, u32[]{:S(2)}, u32[]{:S(2)}) collective-permute-start(bf16[64,5376]{1,0:T(8,128)(2,1)} %own_ref.1), channel_id=1, source_target_pairs={{0,2},{1,3},{2,0},{3,1},{4,6},{5,7},{6,4},{7,5},{8,10},{9,11},{10,... | collective-permute-start | bytes 2064392 | tf_op jit(solution)/shard_map/ppermute | solution.py:32
  3.7 0.9 %copy-start.2 = (bf16[256,512]{1,0:T(8,128)(2,1)S(1)}, bf16[256,512]{1,0:T(8,128)(2,1)}, u32[]{:S(2)}) copy-start(bf16[256,512]{1,0:T(8,128)(2,1)} %q_ref.5) | copy-start | bytes 786436
  4.6 0.9 %copy-start.5 = (bf16[256,256]{1,0:T(8,128)(2,1)S(1)}, bf16[256,256]{1,0:T(8,128)(2,1)}, u32[]{:S(2)}) copy-start(bf16[256,256]{1,0:T(8,128)(2,1)} %k_ref.1) | copy-start | bytes 393220
  5.5 0.9 %copy-start.6 = (bf16[256,256]{1,0:T(8,128)(2,1)S(1)}, bf16[256,256]{1,0:T(8,128)(2,1)}, u32[]{:S(2)}) copy-start(bf16[256,256]{1,0:T(8,128)(2,1)} %v_ref.1) | copy-start | bytes 393220
  6.4 27.7 %copy-start.3 = (bf16[256,512]{1,0:T(8,128)(2,1)S(1)}, bf16[256,512]{1,0:T(8,128)(2,1)}, u32[]{:S(2)}) copy-start(bf16[256,512]{1,0:T(8,128)(2,1)} %q_ref.5) | copy-start | bytes 786436
  6.5 10.4 %collective-permute-start = (bf16[256,512]{1,0:T(8,128)(2,1)S(1)}, bf16[256,512]{1,0:T(8,128)(2,1)S(1)}, u32[]{:S(2)}, u32[]{:S(2)}) collective-permute-start(bf16[256,512]{1,0:T(8,128)(2,1)S(1)} %get-tuple-element.39.kv_ref), channel_id=1, source_target_pairs={{0,8},{4,12},{8,16},{12,20},{16,24},{20,28},{1,9},{5,13},{9,17},{1... | collective-permute-start | bytes 786440 | tf_op jit(solution)/shard_map/ppermute | solution.py:27
  10.1 7.6 %collective-permute-start.2 = (bf16[256,512]{1,0:T(8,128)(2,1)S(1)}, bf16[256,512]{1,0:T(8,128)(2,1)S(1)}, u32[]{:S(2)}, u32[]{:S(2)}) collective-permute-start(bf16[256,512]{1,0:T(8,128)(2,1)S(1)} %get-tuple-element.39.kv_ref), channel_id=1, source_target_pairs={{0,4},{4,0},{8,12},{12,8},{16,20},{20,16},{24,28},{28,24},{1,5},{5... | collective-permute-start | bytes 786440 | tf_op jit(solution)/shard_map/ppermute | solution.py:32
  11.7 13.7 %collective-permute-start.1 = (bf16[256,512]{1,0:T(8,128)(2,1)S(1)}, bf16[256,512]{1,0:T(8,128)(2,1)S(1)}, u32[]{:S(2)}, u32[]{:S(2)}) collective-permute-start(bf16[256,512]{1,0:T(8,128)(2,1)S(1)} %get-tuple-element.25), channel_id=1, source_target_pairs={{0,16},{4,20},{8,24},{12,28},{16,0},{20,4},{24,8},{28,12},{1,17},{... | collective-permute-start | bytes 786440 | tf_op jit(solution)/shard_map/ppermute | solution.py:43
  17.7 7.7 %collective-permute-start.3 = (bf16[256,512]{1,0:T(8,128)(2,1)S(1)}, bf16[256,512]{1,0:T(8,128)(2,1)S(1)}, u32[]{:S(2)}, u32[]{:S(2)}) collective-permute-start(bf16[256,512]{1,0:T(8,128)(2,1)S(1)} %collective-permute-done.r1_ref), channel_id=1, source_target_pairs={{0,4},{4,0},{8,12},{12,8},{16,20},{20,16},{24,28},{28,24},{1,5},{5... | collective-permute-start | bytes 786440 | tf_op jit(solution)/shard_map/ppermute | solution.py:32
  19.2 6.9 %collective-permute-start.5 = (bf16[64,5376]{1,0:T(8,128)(2,1)}, bf16[64,5376]{1,0:T(8,128)(2,1)S(1)}, u32[]{:S(2)}, u32[]{:S(2)}) collective-permute-start(bf16[64,5376]{1,0:T(8,128)(2,1)} %own_ref.1), channel_id=1, source_target_pairs={{0,1},{1,0},{2,3},{3,2},{4,5},{5,4},{6,7},{7,6},{8,9},{9,8},{10,11... | collective-permute-start | bytes 2064392 | tf_op jit(solution)/shard_map/ppermute | solution.py:32
  25.4 2.1 %collective-permute-start.7 = (bf16[64,5376]{1,0:T(8,128)(2,1)S(1)}, bf16[64,5376]{1,0:T(8,128)(2,1)S(1)}, u32[]{:S(2)}, u32[]{:S(2)}) collective-permute-start(bf16[64,5376]{1,0:T(8,128)(2,1)S(1)} %collective-permute-done.6.y_ref), channel_id=1, source_target_pairs={{0,1},{1,0},{2,3},{3,2},{4,5},{5,4},{6,7},{7,6},{8,9},{9,8},{10,11... | collective-permute-start | bytes 2064392 | tf_op jit(solution)/shard_map/ppermute | solution.py:32
  25.4 8.7 %collective-permute-start.4 = (bf16[256,512]{1,0:T(8,128)(2,1)S(1)}, bf16[256,512]{1,0:T(8,128)(2,1)S(1)}, u32[]{:S(2)}, u32[]{:S(2)}) collective-permute-start(bf16[256,512]{1,0:T(8,128)(2,1)S(1)} %collective-permute-done.1.r2_ref.qf_ref), channel_id=1, source_target_pairs={{0,4},{4,0},{8,12},{12,8},{16,20},{20,16},{24,28},{28,24},{1,5},{5... | collective-permute-start | bytes 786440 | tf_op jit(solution)/shard_map/ppermute | solution.py:32
  27.6 2.6 %copy-start = (bf16[512,5376]{1,0:T(8,128)(2,1)S(1)}, bf16[512,5376]{1,0:T(8,128)(2,1)}, u32[]{:S(2)}) copy-start(bf16[512,5376]{1,0:T(8,128)(2,1)} %w_ref.3) | copy-start | bytes 16515076
  30.1 1.1 %copy-start.4 = (bf16[64,5376]{1,0:T(8,128)(2,1)S(1)}, bf16[64,5376]{1,0:T(8,128)(2,1)}, u32[]{:S(2)}) copy-start(bf16[64,5376]{1,0:T(8,128)(2,1)} %own_ref.1) | copy-start | bytes 2064388
  31.2 2.9 %copy-start.1 = (bf16[512,5376]{1,0:T(8,128)(2,1)S(1)}, bf16[512,5376]{1,0:T(8,128)(2,1)}, u32[]{:S(2)}) copy-start(bf16[512,5376]{1,0:T(8,128)(2,1)} %w_ref.3) | copy-start | bytes 16515076
  38.4 10.4 %collective-permute-start.8 = (bf16[64,5376]{1,0:T(8,128)(2,1)S(1)}, bf16[64,5376]{1,0:T(8,128)(2,1)S(1)}, u32[]{:S(2)}, u32[]{:S(2)}) collective-permute-start(bf16[64,5376]{1,0:T(8,128)(2,1)S(1)} %get-tuple-element.34), channel_id=1, source_target_pairs={{0,1},{1,0},{2,3},{3,2},{4,5},{5,4},{6,7},{7,6},{8,9},{9,8},{10,11... | collective-permute-start | bytes 2064392 | tf_op jit(solution)/shard_map/ppermute | solution.py:32
  38.4 23.9 %collective-permute-start.12 = (bf16[256,512]{1,0:T(8,128)(2,1)S(1)}, bf16[256,512]{1,0:T(8,128)(2,1)S(1)}, u32[]{:S(2)}, u32[]{:S(2)}) collective-permute-start(bf16[256,512]{1,0:T(8,128)(2,1)S(1)} %turn_back.1.d_ref), channel_id=1, source_target_pairs={{0,16},{4,20},{8,24},{12,28},{16,0},{20,4},{24,8},{28,12},{1,17},{... | collective-permute-start | bytes 786440 | tf_op jit(solution)/shard_map/ppermute | solution.py:43
  49.8 14.1 %collective-permute-start.9 = (bf16[256,512]{1,0:T(8,128)(2,1)S(1)}, bf16[256,512]{1,0:T(8,128)(2,1)S(1)}, u32[]{:S(2)}, u32[]{:S(2)}) collective-permute-start(bf16[256,512]{1,0:T(8,128)(2,1)S(1)} %get-tuple-element.35), channel_id=1, source_target_pairs={{0,4},{4,0},{8,12},{12,8},{16,20},{20,16},{24,28},{28,24},{1,5},{5... | collective-permute-start | bytes 786440 | tf_op jit(solution)/shard_map/ppermute | solution.py:32
  51.3 17.5 %collective-permute-start.11 = (bf16[64,5376]{1,0:T(8,128)(2,1)}, bf16[64,5376]{1,0:T(8,128)(2,1)}, u32[]{:S(2)}, u32[]{:S(2)}) collective-permute-start(bf16[64,5376]{1,0:T(8,128)(2,1)} %add_convert_fusion.1), channel_id=1, source_target_pairs={{0,2},{1,3},{2,0},{3,1},{4,6},{5,7},{6,4},{7,5},{8,10},{9,11},{10,... | collective-permute-start | bytes 2064392 | tf_op jit(solution)/shard_map/ppermute | solution.py:32
  51.8 6.9 %collective-permute-start.13 = (f32[8,512]{1,0:T(8,128)S(1)}, f32[8,512]{1,0:T(8,128)S(1)}, u32[]{:S(2)}, u32[]{:S(2)}) collective-permute-start(f32[8,512]{1,0:T(8,128)S(1)} %get-tuple-element.31.stat_ref), channel_id=1, source_target_pairs={{0,16},{4,20},{8,24},{12,28},{16,0},{20,4},{24,8},{28,12},{1,17},{... | collective-permute-start | bytes 49160 | tf_op jit(solution)/shard_map/ppermute | solution.py:43
  58.6 3.7 %collective-permute-start.14 = (f32[8,512]{1,0:T(8,128)S(1)}, f32[8,512]{1,0:T(8,128)S(1)}, u32[]{:S(2)}, u32[]{:S(2)}) collective-permute-start(f32[8,512]{1,0:T(8,128)S(1)} %collective-permute-done.13.sf_ref), channel_id=1, source_target_pairs={{0,4},{4,0},{8,12},{12,8},{16,20},{20,16},{24,28},{28,24},{1,5},{5... | collective-permute-start | bytes 49160 | tf_op jit(solution)/shard_map/ppermute | solution.py:32
  62.4 7.8 %collective-permute-start.15 = (bf16[256,512]{1,0:T(8,128)(2,1)S(1)}, bf16[256,512]{1,0:T(8,128)(2,1)S(1)}, u32[]{:S(2)}, u32[]{:S(2)}) collective-permute-start(bf16[256,512]{1,0:T(8,128)(2,1)S(1)} %collective-permute-done.12.df_ref), channel_id=1, source_target_pairs={{0,4},{4,0},{8,12},{12,8},{16,20},{20,16},{24,28},{28,24},{1,5},{5... | collective-permute-start | bytes 786440 | tf_op jit(solution)/shard_map/ppermute | solution.py:32
  63.9 13.6 %collective-permute-start.10 = (bf16[64,5376]{1,0:T(8,128)(2,1)S(1)}, bf16[64,5376]{1,0:T(8,128)(2,1)}, u32[]{:S(2)}, u32[]{:S(2)}) collective-permute-start(bf16[64,5376]{1,0:T(8,128)(2,1)S(1)} %get-tuple-element.36), channel_id=1, source_target_pairs={{0,1},{1,0},{2,3},{3,2},{4,5},{5,4},{6,7},{7,6},{8,9},{9,8},{10,11... | collective-permute-start | bytes 2064392 | tf_op jit(solution)/shard_map/ppermute | solution.py:32
  64.7 10.9 %collective-permute-start.16 = (bf16[256,512]{1,0:T(8,128)(2,1)}, bf16[256,512]{1,0:T(8,128)(2,1)}, u32[]{:S(2)}, u32[]{:S(2)}) collective-permute-start(bf16[256,512]{1,0:T(8,128)(2,1)} %add_convert_fusion.2), channel_id=1, source_target_pairs={{8,0},{12,4},{16,8},{20,12},{24,16},{28,20},{9,1},{13,5},{17,9},{2... | collective-permute-start | bytes 786440 | tf_op jit(solution)/shard_map/ppermute | solution.py:27
  66.0 9.6 %collective-permute-start.17 = (bf16[256,512]{1,0:T(8,128)(2,1)S(1)}, bf16[256,512]{1,0:T(8,128)(2,1)}, u32[]{:S(2)}, u32[]{:S(2)}) collective-permute-start(bf16[256,512]{1,0:T(8,128)(2,1)S(1)} %get-tuple-element.43), channel_id=1, source_target_pairs={{0,4},{4,0},{8,12},{12,8},{16,20},{20,16},{24,28},{28,24},{1,5},{5... | collective-permute-start | bytes 786440 | tf_op jit(solution)/shard_map/ppermute | solution.py:32

commit v4 on v3

--- a/solution.py
+++ b/solution.py
@@ -14,6 +14,8 @@
 F32 = jnp.float32
 BF16 = jnp.bfloat16
 SMALL = pl.CostEstimate(flops=1, bytes_accessed=1, transcendentals=0)
+MEDIUM = pl.CostEstimate(flops=50 * 10**8, bytes_accessed=1, transcendentals=0)
+LARGE = pl.CostEstimate(flops=10**10, bytes_accessed=1, transcendentals=0)
 VMEM = pl.BlockSpec(memory_space=pltpu.VMEM)
 
 
@@ -206,17 +208,32 @@
         t_ref[:, vc] = dv
 
 
+def sum_kernel(*refs):
+    total = refs[0][...].astype(F32)
+    for ref in refs[1:-1]:
+        total = total + ref[...].astype(F32)
+    refs[-1][...] = total.astype(refs[-1].dtype)
+
+
+def finish_kernel(own_ref, far_ref, hop_ref, pair_ref, dk_ref, dv_ref):
+    odd = lax.rem(lax.axis_index("seq"), 2) == 1
+    total = own_ref[...] + far_ref[...] + hop_ref[...].astype(F32) + jnp.where(odd, 0.0, pair_ref[...].astype(F32))
+    kv_cols = dk_ref.shape[1]
+    dk_ref[...] = total[:, :kv_cols].astype(BF16)
+    dv_ref[...] = total[:, kv_cols:].astype(BF16)
+
+
 def per_device(queries, keys, values, out_weight, out_grad):
     tok, q_cols = queries.shape
     kv_cols = keys.shape[1]
     kv_heads = kv_cols // HEAD_SIZE
     odd = lax.rem(lax.axis_index("seq"), 2) == 1
-    half, size = tok // 2, tok // 4
+    size = tok // 4
     rows = jax.ShapeDtypeStruct((size, out_weight.shape[1]), BF16)
     block = jax.ShapeDtypeStruct((tok, 2 * kv_cols), BF16)
     wide_block = jax.ShapeDtypeStruct((tok, 2 * kv_cols), F32)
 
-    def call(kernel, name, outs, scratch, *operands):
+    def call(kernel, name, outs, scratch, *operands, cost=SMALL):
         return pl.pallas_call(
             kernel,
             out_shape=outs,
@@ -224,12 +241,9 @@
             out_specs=jax.tree.map(lambda _: VMEM, outs),
             scratch_shapes=scratch,
             compiler_params=pltpu.CompilerParams(vmem_limit_bytes=16 << 20),
-            cost_estimate=SMALL,
+            cost_estimate=cost,
             name=name,
         )(*operands)
-
-    def wide(a):
-        return a.astype(F32)
 
     def gate(value, *others):
         return lax.optimization_barrier((value, *others))[0]
@@ -248,7 +262,7 @@
     def down(value):
         return far_swapped(*[lambda: value] * 2)[1]
 
-    grad_far = down(grad)
+    grad_far = [down(grad[:, : q_cols // 2]), down(grad[:, q_cols // 2 :])]
     probs, stats, near_own, near_core, far_own, far_core = call(
         forward_kernel,
         "attend",
@@ -262,30 +276,30 @@
     )
     sent = swapped(far_core, "head", 1)
     stats_far = down(stats)
-    far_sum = (wide(far_own) + wide(sent)).astype(BF16)
+    far_sum = call(sum_kernel, "far_sum", rows, [], far_own, sent)
     from_y = swapped(far_sum, "head", 2)
-    stats_x = swapped(stats_far, "seq", 1)
-    grad_x = swapped(gate(grad_far, stats_x), "seq", 1)
+    stats_x = swapped(gate(stats_far, grad_far[1]), "seq", 1)
+    first_far, grad_far = grad_far[0], jnp.concatenate(grad_far, 1)
+    grad_x = swapped(grad_far, "seq", 1)
 
     query_gradient, t_own, t_1, t_x, t_z = call(
         backward_kernel,
         "attend_grad",
         (jax.ShapeDtypeStruct((tok, q_cols), BF16), wide_block, block, block, block),
         [],
-        queries, kv, r1, r2, x1, p0, x2, probs, stats, grad,
+        queries, kv, r1, r2, x1, p0, x2, probs, stats, gate(grad, first_far),
+        cost=LARGE,
     )
-    d1 = swapped(gate(t_x, far_sum), "seq", 1)
-    e1 = shifted((wide(t_1) + wide(d1)).astype(BF16), -2)
+    d1 = gate(swapped(gate(t_x, far_sum, stats_far), "seq", 1), stats_x)
+    e1 = shifted(call(sum_kernel, "hop_sum", block, [], t_1, d1), -2)
     g = swapped(gate(t_z, d1), "seq", 1)
     from_core = swapped(gate(near_core, d1), "head", 1)
-    t_far = call(far_kernel, "far_grad", wide_block, [], gate(kv, from_y), q_far, grad_far, stats_far, x2, grad_x, stats_x)
-
-    def total(cols):
-        kept = jnp.where(odd, 0.0, wide(g[:, cols]))
-        return (t_own[:, cols] + t_far[:, cols] + wide(e1[:, cols]) + kept).astype(BF16)
-
-    projected = (wide(near_own) + wide(from_core) + wide(from_y)).astype(BF16)
-    return (projected, query_gradient, total(slice(0, kv_cols)), total(slice(kv_cols, 2 * kv_cols)))
+    t_far = call(far_kernel, "far_grad", wide_block, [], kv, q_far, grad_far, stats_far, x2, grad_x, stats_x, cost=MEDIUM)
+
+    narrow = jax.ShapeDtypeStruct(keys.shape, BF16)
+    key_gradient, value_gradient = call(finish_kernel, "finish", (narrow, narrow), [], t_own, t_far, e1, g)
+    projected = call(sum_kernel, "projected", rows, [], near_own, from_core, from_y, cost=LARGE)
+    return (projected, query_gradient, key_gradient, value_gradient)
 
 
 def solution(mesh):

time: 80.3 us -> 79.5 us (0.990)
  other arithmetic: 6.12 us -> 0 us
  starting transfers between devices: 26.8 us -> 29.8 us
  Pallas kernels: 10.7 us -> 12.8 us
    ppermute x13, waiting for transfers between devices: 9.57 us -> 16 us  [swapped(): return lax.ppermute(value, axis, [(i, i ^ bit) for i in range(count)])]
    convert_element_type x4 -> x0, other arithmetic: 6.12 us -> none  [the longest x1 2.4 us: per_device(): projected = (wide(near_own) + wide(from_core) + wide(from_y)).astype(BF16)]
    ppermute x3 -> x4, waiting for transfers between devices: 13.1 us -> 7.61 us  [far_swapped(): lax.ppermute(lower() if lower is upper else jnp.where(side == r, lower(),...]
    ppermute x3 -> x4, starting transfers between devices: 9.58 us -> 12.6 us  [far_swapped(): lax.ppermute(lower() if lower is upper else jnp.where(side == r, lower(),...]
    pallas_call x5 -> x9, Pallas kernels: 10.7 us -> 12.8 us  [call(): pl.pallas_call(kernel, out_shape=outs, in_specs=[VMEM] * len(operands), o...]
    unnamed x14 -> x15, local copies, waits for them, and re-layouts: 6.42 us -> 6.43 us
  transfers between devices with their start and end apart: 18 -> 19, of which waited for: 10 -> 9; matrix products, arithmetic and copies ran while one was open for 5% -> 0% of each run, Pallas kernels for 8% -> 15%
where the time goes in v4:
time: 79.5 us; the launch traced here: 79.1 us
  starting transfers between devices  29.8 us (37%)
  waiting for transfers between devices  29.4 us (37%)
  Pallas kernels  12.8 us (16%)
  local copies, waits for them, and re-layouts  6.46 us (8%)
    ppermute x13, waiting for transfers between devices, swapped(): return lax.ppermute(value, axis, [(i, i ^ bit) for i in range(count)])  16 us
    pallas_call x9, Pallas kernels, call(): pl.pallas_call(kernel, out_shape=outs, in_specs=[VMEM] * len(operands), o...  12.8 us
    ppermute x4, starting transfers between devices, far_swapped(): lax.ppermute(lower() if lower is upper else jnp.where(side == r, lower(),...  12.6 us
    ppermute x13, starting transfers between devices, swapped(): return lax.ppermute(value, axis, [(i, i ^ bit) for i in range(count)])  12.3 us
    ppermute x4, waiting for transfers between devices, far_swapped(): lax.ppermute(lower() if lower is upper else jnp.where(side == r, lower(),...  7.61 us
    unnamed x15, local copies, waits for them, and re-layouts  6.43 us
    ppermute x2, waiting for transfers between devices, shifted(): lax.ppermute(value, 'seq', [(i, i + steps) for i in range(first, last)])  5.76 us
    ppermute x2, starting transfers between devices, shifted(): lax.ppermute(value, 'seq', [(i, i + steps) for i in range(first, last)])  4.92 us
  transfers between devices with their start and end apart: 19, of which 9 were waited for; matrix products, arithmetic and copies ran while one was open for 0% of the time, Pallas kernels for 15%

profile of v4, /device:TPU:0, one launch (start us, length us, event | category | flops | bytes accessed | tf_op | source)
XLA Modules:
  0.0 79.1 jit_solution(10101824692325753492)
XLA Ops:
  0.6 3.0 %collective-permute-start.6 = (bf16[64,5376]{1,0:T(8,128)(2,1)}, bf16[64,5376]{1,0:T(8,128)(2,1)S(1)}, u32[]{:S(2)}, u32[]{:S(2)}) collective-permute-start(bf16[64,5376]{1,0:T(8,128)(2,1)} %own_ref.1), channel_id=1, source_target_pairs={{0,2},{1,3},{2,0},{3,1},{4,6},{5,7},{6,4},{7,5},{8,10},{9,11},{10,... | collective-permute-start | bytes 2064392 | tf_op jit(solution)/shard_map/ppermute | solution.py:34
  3.7 0.0 copy-start.2
  3.7 0.9 %copy-done.2 = bf16[256,512]{1,0:T(8,128)(2,1)S(1)} copy-done((bf16[256,512]{1,0:T(8,128)(2,1)S(1)}, bf16[256,512]{1,0:T(8,128)(2,1)}, u32[]{:S(2)}) %copy-start.2) | copy-done | bytes 262168
  4.6 0.0 copy-start.5
  4.6 0.9 %copy-done.5 = bf16[256,256]{1,0:T(8,128)(2,1)S(1)} copy-done((bf16[256,256]{1,0:T(8,128)(2,1)S(1)}, bf16[256,256]{1,0:T(8,128)(2,1)}, u32[]{:S(2)}) %copy-start.5) | copy-done | bytes 131096
  5.5 0.0 copy-start.6
  5.5 0.9 %copy-done.6 = bf16[256,256]{1,0:T(8,128)(2,1)S(1)} copy-done((bf16[256,256]{1,0:T(8,128)(2,1)S(1)}, bf16[256,256]{1,0:T(8,128)(2,1)}, u32[]{:S(2)}) %copy-start.6) | copy-done | bytes 131096
  6.4 0.0 copy-start.3
  6.4 0.1 join.1
  6.5 3.6 %collective-permute-start = (bf16[256,512]{1,0:T(8,128)(2,1)S(1)}, bf16[256,512]{1,0:T(8,128)(2,1)S(1)}, u32[]{:S(2)}, u32[]{:S(2)}) collective-permute-start(bf16[256,512]{1,0:T(8,128)(2,1)S(1)} %get-tuple-element.27.kv_ref), channel_id=1, source_target_pairs={{0,8},{4,12},{8,16},{12,20},{16,24},{20,28},{1,9},{5,13},{9,17},{1... | collective-permute-start | bytes 786440 | tf_op jit(solution)/shard_map/ppermute | solution.py:29
  10.1 1.6 %collective-permute-start.2 = (bf16[256,512]{1,0:T(8,128)(2,1)S(1)}, bf16[256,512]{1,0:T(8,128)(2,1)S(1)}, u32[]{:S(2)}, u32[]{:S(2)}) collective-permute-start(bf16[256,512]{1,0:T(8,128)(2,1)S(1)} %get-tuple-element.27.kv_ref), channel_id=1, source_target_pairs={{0,4},{4,0},{8,12},{12,8},{16,20},{20,16},{24,28},{28,24},{1,5},{5... | collective-permute-start | bytes 786440 | tf_op jit(solution)/shard_map/ppermute | solution.py:34
  11.7 2.6 %collective-permute-start.1 = (bf16[256,512]{1,0:T(8,128)(2,1)S(1)}, bf16[256,512]{1,0:T(8,128)(2,1)S(1)}, u32[]{:S(2)}, u32[]{:S(2)}) collective-permute-start(bf16[256,512]{1,0:T(8,128)(2,1)S(1)} %get-tuple-element.28), channel_id=1, source_target_pairs={{0,16},{4,20},{8,24},{12,28},{16,0},{20,4},{24,8},{28,12},{1,17},{... | collective-permute-start | bytes 786440 | tf_op jit(solution)/shard_map/ppermute | solution.py:45
  14.3 2.6 %collective-permute-done.r1_ref = bf16[256,512]{1,0:T(8,128)(2,1)S(1)} collective-permute-done((bf16[256,512]{1,0:T(8,128)(2,1)S(1)}, bf16[256,512]{1,0:T(8,128)(2,1)S(1)}, u32[]{:S(2)}, u32[]{:S(2)}) %collective-permute-start) | collective-permute-done | bytes 262176 | tf_op jit(solution)/shard_map/ppermute | solution.py:29
  16.8 0.8 %collective-permute-done.2.p0_ref = bf16[256,512]{1,0:T(8,128)(2,1)S(1)} collective-permute-done((bf16[256,512]{1,0:T(8,128)(2,1)S(1)}, bf16[256,512]{1,0:T(8,128)(2,1)S(1)}, u32[]{:S(2)}, u32[]{:S(2)}) %collective-permute-start.2) | collective-permute-done | bytes 262176 | tf_op jit(solution)/shard_map/ppermute | solution.py:34
  17.7 1.5 %collective-permute-start.3 = (bf16[256,512]{1,0:T(8,128)(2,1)S(1)}, bf16[256,512]{1,0:T(8,128)(2,1)S(1)}, u32[]{:S(2)}, u32[]{:S(2)}) collective-permute-start(bf16[256,512]{1,0:T(8,128)(2,1)S(1)} %collective-permute-done.r1_ref), channel_id=1, source_target_pairs={{0,4},{4,0},{8,12},{12,8},{16,20},{20,16},{24,28},{28,24},{1,5},{5... | collective-permute-start | bytes 786440 | tf_op jit(solution)/shard_map/ppermute | solution.py:34
  19.2 0.0 collective-permute-start.5
  19.2 6.2 %collective-permute-done.1.r2_ref.qf_ref = bf16[256,512]{1,0:T(8,128)(2,1)S(1)} collective-permute-done((bf16[256,512]{1,0:T(8,128)(2,1)S(1)}, bf16[256,512]{1,0:T(8,128)(2,1)S(1)}, u32[]{:S(2)}, u32[]{:S(2)}) %collective-permute-start.1) | collective-permute-done | bytes 262176 | tf_op jit(solution)/shard_map/ppermute | solution.py:45
  25.4 0.0 collective-permute-done.3.x1_ref
  25.4 0.0 collective-permute-done.6.y_ref
  25.4 0.0 collective-permute-start.7
  25.4 0.6 collective-permute-start.4
  26.0 0.0 collective-permute-done.5.core_ref
  26.0 1.5 %collective-permute-done.7.yc_ref = bf16[64,5376]{1,0:T(8,128)(2,1)S(1)} collective-permute-done((bf16[64,5376]{1,0:T(8,128)(2,1)S(1)}, bf16[64,5376]{1,0:T(8,128)(2,1)S(1)}, u32[]{:S(2)}, u32[]{:S(2)}) %collective-permute-start.7) | collective-permute-done | bytes 688160 | tf_op jit(solution)/shard_map/ppermute | solution.py:34
  27.6 0.0 copy-start
  27.6 2.6 %copy-done = bf16[512,5376]{1,0:T(8,128)(2,1)S(1)} copy-done((bf16[512,5376]{1,0:T(8,128)(2,1)S(1)}, bf16[512,5376]{1,0:T(8,128)(2,1)}, u32[]{:S(2)}) %copy-start) | copy-done | bytes 5505048
  30.1 0.0 copy-start.4
  30.1 1.1 %copy-done.4 = bf16[64,5376]{1,0:T(8,128)(2,1)S(1)} copy-done((bf16[64,5376]{1,0:T(8,128)(2,1)S(1)}, bf16[64,5376]{1,0:T(8,128)(2,1)}, u32[]{:S(2)}) %copy-start.4) | copy-done | bytes 688152
  31.2 0.0 copy-start.1
  31.2 1.6 %turn_back.1.d_ref = bf16[256,512]{1,0:T(8,128)(2,1)S(1)} custom-call(bf16[64,5376]{1,0:T(8,128)(2,1)S(1)} %copy-done.4, bf16[64,5376]{1,0:T(8,128)(2,1)S(1)} %collective-permute-done.5.core_ref, bf16[64,5376]{1,0:T(8,128)(2,1)S(1)} %collective-permute-done.6.y_ref, bf16[64,5376]{1,0:T(8,128)(2,1)S(1)} %collective-permute-done.7.yc_ref, ...), custom_call_target="tpu_custom_call" | custom-call | flops 1 | bytes 1 | tf_op jit(solution)/shard_map/turn_back/pallas_call | solution.py:237
  32.9 7.0 %collective-permute-start.8 = (bf16[256,256]{1,0:T(8,128)(2,1)S(1)}, bf16[256,256]{1,0:T(8,128)(2,1)S(1)}, u32[]{:S(2)}, u32[]{:S(2)}) collective-permute-start(bf16[256,256]{1,0:T(8,128)(2,1)S(1)} %get-tuple-element.51), channel_id=1, source_target_pairs={{0,16},{4,20},{8,24},{12,28},{16,0},{20,4},{24,8},{28,12},{1,17},{... | collective-permute-start | bytes 393224 | tf_op jit(solution)/shard_map/ppermute | solution.py:45
  39.9 0.0 collective-permute-done.4.x2_ref.qx_ref
  39.9 0.0 copy-done.3
  39.9 0.0 copy-done.1
  39.9 4.2 %attend.1 = (bf16[2,5,256,512]{3,2,1,0:T(8,128)(2,1)S(1)}, f32[8,512]{1,0:T(8,128)S(1)}, bf16[64,5376]{1,0:T(8,128)(2,1)S(1)}, bf16[64,5376]{1,0:T(8,128)(2,1)S(...) custom-call(bf16[256,512]{1,0:T(8,128)(2,1)S(1)} %copy-done.3, ...), custom_call_target="tpu_custom_call" | custom-call | flops 1 | bytes 1 | tf_op jit(solution)/shard_map/attend/pallas_call | solution.py:237
  44.1 1.3 %collective-permute-start.10 = (f32[8,512]{1,0:T(8,128)S(1)}, f32[8,512]{1,0:T(8,128)S(1)}, u32[]{:S(2)}, u32[]{:S(2)}) collective-permute-start(f32[8,512]{1,0:T(8,128)S(1)} %get-tuple-element.34.stat_ref), channel_id=1, source_target_pairs={{0,16},{4,20},{8,24},{12,28},{16,0},{20,4},{24,8},{28,12},{1,17},{... | collective-permute-start | bytes 49160 | tf_op jit(solution)/shard_map/ppermute | solution.py:45
  45.4 1.7 %collective-permute-start.12 = (bf16[256,256]{1,0:T(8,128)(2,1)S(1)}, bf16[256,256]{1,0:T(8,128)(2,1)S(1)}, u32[]{:S(2)}, u32[]{:S(2)}) collective-permute-start(bf16[256,256]{1,0:T(8,128)(2,1)S(1)} %get-tuple-element.50), channel_id=1, source_target_pairs={{0,16},{4,20},{8,24},{12,28},{16,0},{20,4},{24,8},{28,12},{1,17},{... | collective-permute-start | bytes 393224 | tf_op jit(solution)/shard_map/ppermute | solution.py:45
  47.1 0.0 collective-permute-start.9
  47.1 0.0 collective-permute-done.8
  47.1 3.3 %attend_grad.1 = (bf16[256,512]{1,0:T(8,128)(2,1)}, f32[256,512]{1,0:T(8,128)S(1)}, bf16[256,512]{1,0:T(8,128)(2,1)S(1)}, bf16[256,512]{1,0:T(8,128)(2,1)S(1)}, bf16[256,512]{1,0:T(8,128)(2,1)S(1)}) custom-call(bf16[256,512]{1,0:T(8,128)(2,1)S(1)} %copy-done.3, bf16[256,512]{1,0:T(8,128)(2,1)S(1)} %get-tuple-element.27.kv_ref, ...), custom_call_target="tpu_custom_call" | custom-call | flops 10000000000 | bytes 1 | tf_op jit(solution)/shard_map/attend_grad/pallas_call | solution.py:237
  50.4 0.0 collective-permute-done.9.refs_1_
  50.4 0.2 far_sum.1
  50.6 0.3 collective-permute-done.10.sf_ref
  50.9 1.5 %collective-permute-start.11 = (bf16[256,512]{1,0:T(8,128)(2,1)S(1)}, bf16[256,512]{1,0:T(8,128)(2,1)S(1)}, u32[]{:S(2)}, u32[]{:S(2)}) collective-permute-start(bf16[256,512]{1,0:T(8,128)(2,1)S(1)} %get-tuple-element.39), channel_id=1, source_target_pairs={{0,4},{4,0},{8,12},{12,8},{16,20},{20,16},{24,28},{28,24},{1,5},{5... | collective-permute-start | bytes 786440 | tf_op jit(solution)/shard_map/ppermute | solution.py:34
  52.4 1.1 %collective-permute-done.12 = bf16[256,256]{1,0:T(8,128)(2,1)S(1)} collective-permute-done((bf16[256,256]{1,0:T(8,128)(2,1)S(1)}, bf16[256,256]{1,0:T(8,128)(2,1)S(1)}, u32[]{:S(2)}, u32[]{:S(2)}) %collective-permute-start.12) | collective-permute-done | bytes 131104 | tf_op jit(solution)/shard_map/ppermute | solution.py:45
  53.5 1.6 %collective-permute-start.16 = (bf16[256,512]{1,0:T(8,128)(2,1)S(1)}, bf16[256,512]{1,0:T(8,128)(2,1)S(1)}, u32[]{:S(2)}, u32[]{:S(2)}) collective-permute-start(bf16[256,512]{1,0:T(8,128)(2,1)S(1)} %constant_dynamic-update-slice_fusion.df_ref), channel_id=1, source_target_pairs={{0,4},{4,0},{8,12},{12,8},{16,20},{20,16},{24,28},{28,24},{1,5},{5... | collective-permute-start | bytes 786440 | tf_op jit(solution)/shard_map/ppermute | solution.py:34
  55.0 0.5 collective-permute-start.13
  55.6 0.5 collective-permute-start.15
  56.1 9.3 %collective-permute-done.13.sx_ref = f32[8,512]{1,0:T(8,128)S(1)} collective-permute-done((f32[8,512]{1,0:T(8,128)S(1)}, f32[8,512]{1,0:T(8,128)S(1)}, u32[]{:S(2)}, u32[]{:S(2)}) %collective-permute-start.13) | collective-permute-done | bytes 16416 | tf_op jit(solution)/shard_map/ppermute | solution.py:34
  65.4 0.0 collective-permute-done.11.refs_1_
  65.4 0.0 collective-permute-start.14
  65.4 1.5 %collective-permute-start.18 = (bf16[256,512]{1,0:T(8,128)(2,1)S(1)}, bf16[256,512]{1,0:T(8,128)(2,1)S(1)}, u32[]{:S(2)}, u32[]{:S(2)}) collective-permute-start(bf16[256,512]{1,0:T(8,128)(2,1)S(1)} %get-tuple-element.47), channel_id=1, source_target_pairs={{0,4},{4,0},{8,12},{12,8},{16,20},{20,16},{24,28},{28,24},{1,5},{5... | collective-permute-start | bytes 786440 | tf_op jit(solution)/shard_map/ppermute | solution.py:34
  66.9 0.1 hop_sum.1
  66.9 1.3 %collective-permute-start.17 = (bf16[256,512]{1,0:T(8,128)(2,1)S(1)}, bf16[256,512]{1,0:T(8,128)(2,1)S(1)}, u32[]{:S(2)}, u32[]{:S(2)}) collective-permute-start(bf16[256,512]{1,0:T(8,128)(2,1)S(1)} %hop_sum.1), channel_id=1, source_target_pairs={{8,0},{12,4},{16,8},{20,12},{24,16},{28,20},{9,1},{13,5},{17,9},{2... | collective-permute-start | bytes 786440 | tf_op jit(solution)/shard_map/ppermute | solution.py:29
  68.2 0.0 collective-permute-done.16.dx_ref
  68.2 1.5 %far_grad.1.far_ref = f32[256,512]{1,0:T(8,128)S(1)} custom-call(bf16[256,512]{1,0:T(8,128)(2,1)S(1)} %get-tuple-element.27.kv_ref, bf16[256,512]{1,0:T(8,128)(2,1)S(1)} %collective-permute-done.1.r2_ref.qf_ref, bf16[256,512]{1,0:T(8,128)(2,1)S(1)} %constant_dynamic-update-slice_fusion.df_ref, f32[8,512]{1,0:T(8,128)S(1)} %collective-permute-done.10.sf_ref, ...), custom_call_target="tpu_custom_call" | custom-call | flops 5000000000 | bytes 1 | tf_op jit(solution)/shard_map/far_grad/pallas_call | solution.py:237
  69.7 4.4 %collective-permute-done.18.pair_ref = bf16[256,512]{1,0:T(8,128)(2,1)S(1)} collective-permute-done((bf16[256,512]{1,0:T(8,128)(2,1)S(1)}, bf16[256,512]{1,0:T(8,128)(2,1)S(1)}, u32[]{:S(2)}, u32[]{:S(2)}) %collective-permute-start.18) | collective-permute-done | bytes 262176 | tf_op jit(solution)/shard_map/ppermute | solution.py:34
  74.1 3.2 %collective-permute-done.17.hop_ref = bf16[256,512]{1,0:T(8,128)(2,1)S(1)} collective-permute-done((bf16[256,512]{1,0:T(8,128)(2,1)S(1)}, bf16[256,512]{1,0:T(8,128)(2,1)S(1)}, u32[]{:S(2)}, u32[]{:S(2)}) %collective-permute-start.17) | collective-permute-done | bytes 262176 | tf_op jit(solution)/shard_map/ppermute | solution.py:29
  77.3 0.8 finish.1
  78.0 0.0 collective-permute-done.15.refs_2_
  78.0 0.0 collective-permute-done.14.refs_1_
  78.0 1.1 %projected.1 = bf16[64,5376]{1,0:T(8,128)(2,1)} custom-call(bf16[64,5376]{1,0:T(8,128)(2,1)S(1)} %get-tuple-element.31.refs_0_, bf16[64,5376]{1,0:T(8,128)(2,1)S(1)} %collective-permute-done.14.refs_1_, bf16[64,5376]{1,0:T(8,128)(2,1)S(1)} %collective-permute-done.15.refs_2_), custom_call_target="tpu_custom_call" | custom-call | flops 10000000000 | bytes 1 | tf_op jit(solution)/shard_map/projected/pallas_call | solution.py:237
  (3 shorter events, 0.0 us)
Async XLA Ops:
  0.6 24.8 %collective-permute-start.6 = (bf16[64,5376]{1,0:T(8,128)(2,1)}, bf16[64,5376]{1,0:T(8,128)(2,1)S(1)}, u32[]{:S(2)}, u32[]{:S(2)}) collective-permute-start(bf16[64,5376]{1,0:T(8,128)(2,1)} %own_ref.1), channel_id=1, source_target_pairs={{0,2},{1,3},{2,0},{3,1},{4,6},{5,7},{6,4},{7,5},{8,10},{9,11},{10,... | collective-permute-start | bytes 2064392 | tf_op jit(solution)/shard_map/ppermute | solution.py:34
  3.7 0.9 %copy-start.2 = (bf16[256,512]{1,0:T(8,128)(2,1)S(1)}, bf16[256,512]{1,0:T(8,128)(2,1)}, u32[]{:S(2)}) copy-start(bf16[256,512]{1,0:T(8,128)(2,1)} %q_ref.5) | copy-start | bytes 786436
  4.6 0.9 %copy-start.5 = (bf16[256,256]{1,0:T(8,128)(2,1)S(1)}, bf16[256,256]{1,0:T(8,128)(2,1)}, u32[]{:S(2)}) copy-start(bf16[256,256]{1,0:T(8,128)(2,1)} %k_ref.1) | copy-start | bytes 393220
  5.5 0.9 %copy-start.6 = (bf16[256,256]{1,0:T(8,128)(2,1)S(1)}, bf16[256,256]{1,0:T(8,128)(2,1)}, u32[]{:S(2)}) copy-start(bf16[256,256]{1,0:T(8,128)(2,1)} %v_ref.1) | copy-start | bytes 393220
  6.4 33.4 %copy-start.3 = (bf16[256,512]{1,0:T(8,128)(2,1)S(1)}, bf16[256,512]{1,0:T(8,128)(2,1)}, u32[]{:S(2)}) copy-start(bf16[256,512]{1,0:T(8,128)(2,1)} %q_ref.5) | copy-start | bytes 786436
  6.5 10.4 %collective-permute-start = (bf16[256,512]{1,0:T(8,128)(2,1)S(1)}, bf16[256,512]{1,0:T(8,128)(2,1)S(1)}, u32[]{:S(2)}, u32[]{:S(2)}) collective-permute-start(bf16[256,512]{1,0:T(8,128)(2,1)S(1)} %get-tuple-element.27.kv_ref), channel_id=1, source_target_pairs={{0,8},{4,12},{8,16},{12,20},{16,24},{20,28},{1,9},{5,13},{9,17},{1... | collective-permute-start | bytes 786440 | tf_op jit(solution)/shard_map/ppermute | solution.py:29
  10.1 7.6 %collective-permute-start.2 = (bf16[256,512]{1,0:T(8,128)(2,1)S(1)}, bf16[256,512]{1,0:T(8,128)(2,1)S(1)}, u32[]{:S(2)}, u32[]{:S(2)}) collective-permute-start(bf16[256,512]{1,0:T(8,128)(2,1)S(1)} %get-tuple-element.27.kv_ref), channel_id=1, source_target_pairs={{0,4},{4,0},{8,12},{12,8},{16,20},{20,16},{24,28},{28,24},{1,5},{5... | collective-permute-start | bytes 786440 | tf_op jit(solution)/shard_map/ppermute | solution.py:34
  11.7 13.7 %collective-permute-start.1 = (bf16[256,512]{1,0:T(8,128)(2,1)S(1)}, bf16[256,512]{1,0:T(8,128)(2,1)S(1)}, u32[]{:S(2)}, u32[]{:S(2)}) collective-permute-start(bf16[256,512]{1,0:T(8,128)(2,1)S(1)} %get-tuple-element.28), channel_id=1, source_target_pairs={{0,16},{4,20},{8,24},{12,28},{16,0},{20,4},{24,8},{28,12},{1,17},{... | collective-permute-start | bytes 786440 | tf_op jit(solution)/shard_map/ppermute | solution.py:45
  17.7 7.7 %collective-permute-start.3 = (bf16[256,512]{1,0:T(8,128)(2,1)S(1)}, bf16[256,512]{1,0:T(8,128)(2,1)S(1)}, u32[]{:S(2)}, u32[]{:S(2)}) collective-permute-start(bf16[256,512]{1,0:T(8,128)(2,1)S(1)} %collective-permute-done.r1_ref), channel_id=1, source_target_pairs={{0,4},{4,0},{8,12},{12,8},{16,20},{20,16},{24,28},{28,24},{1,5},{5... | collective-permute-start | bytes 786440 | tf_op jit(solution)/shard_map/ppermute | solution.py:34
  19.2 6.9 %collective-permute-start.5 = (bf16[64,5376]{1,0:T(8,128)(2,1)}, bf16[64,5376]{1,0:T(8,128)(2,1)S(1)}, u32[]{:S(2)}, u32[]{:S(2)}) collective-permute-start(bf16[64,5376]{1,0:T(8,128)(2,1)} %own_ref.1), channel_id=1, source_target_pairs={{0,1},{1,0},{2,3},{3,2},{4,5},{5,4},{6,7},{7,6},{8,9},{9,8},{10,11... | collective-permute-start | bytes 2064392 | tf_op jit(solution)/shard_map/ppermute | solution.py:34
  25.4 2.1 %collective-permute-start.7 = (bf16[64,5376]{1,0:T(8,128)(2,1)S(1)}, bf16[64,5376]{1,0:T(8,128)(2,1)S(1)}, u32[]{:S(2)}, u32[]{:S(2)}) collective-permute-start(bf16[64,5376]{1,0:T(8,128)(2,1)S(1)} %collective-permute-done.6.y_ref), channel_id=1, source_target_pairs={{0,1},{1,0},{2,3},{3,2},{4,5},{5,4},{6,7},{7,6},{8,9},{9,8},{10,11... | collective-permute-start | bytes 2064392 | tf_op jit(solution)/shard_map/ppermute | solution.py:34
  25.4 14.4 %collective-permute-start.4 = (bf16[256,512]{1,0:T(8,128)(2,1)S(1)}, bf16[256,512]{1,0:T(8,128)(2,1)S(1)}, u32[]{:S(2)}, u32[]{:S(2)}) collective-permute-start(bf16[256,512]{1,0:T(8,128)(2,1)S(1)} %collective-permute-done.1.r2_ref.qf_ref), channel_id=1, source_target_pairs={{0,4},{4,0},{8,12},{12,8},{16,20},{20,16},{24,28},{28,24},{1,5},{5... | collective-permute-start | bytes 786440 | tf_op jit(solution)/shard_map/ppermute | solution.py:34
  27.6 2.6 %copy-start = (bf16[512,5376]{1,0:T(8,128)(2,1)S(1)}, bf16[512,5376]{1,0:T(8,128)(2,1)}, u32[]{:S(2)}) copy-start(bf16[512,5376]{1,0:T(8,128)(2,1)} %w_ref.3) | copy-start | bytes 16515076
  30.1 1.1 %copy-start.4 = (bf16[64,5376]{1,0:T(8,128)(2,1)S(1)}, bf16[64,5376]{1,0:T(8,128)(2,1)}, u32[]{:S(2)}) copy-start(bf16[64,5376]{1,0:T(8,128)(2,1)} %own_ref.1) | copy-start | bytes 2064388
  31.2 8.6 %copy-start.1 = (bf16[512,5376]{1,0:T(8,128)(2,1)S(1)}, bf16[512,5376]{1,0:T(8,128)(2,1)}, u32[]{:S(2)}) copy-start(bf16[512,5376]{1,0:T(8,128)(2,1)} %w_ref.3) | copy-start | bytes 16515076
  32.9 14.2 %collective-permute-start.8 = (bf16[256,256]{1,0:T(8,128)(2,1)S(1)}, bf16[256,256]{1,0:T(8,128)(2,1)S(1)}, u32[]{:S(2)}, u32[]{:S(2)}) collective-permute-start(bf16[256,256]{1,0:T(8,128)(2,1)S(1)} %get-tuple-element.51), channel_id=1, source_target_pairs={{0,16},{4,20},{8,24},{12,28},{16,0},{20,4},{24,8},{28,12},{1,17},{... | collective-permute-start | bytes 393224 | tf_op jit(solution)/shard_map/ppermute | solution.py:45
  44.1 6.8 %collective-permute-start.10 = (f32[8,512]{1,0:T(8,128)S(1)}, f32[8,512]{1,0:T(8,128)S(1)}, u32[]{:S(2)}, u32[]{:S(2)}) collective-permute-start(f32[8,512]{1,0:T(8,128)S(1)} %get-tuple-element.34.stat_ref), channel_id=1, source_target_pairs={{0,16},{4,20},{8,24},{12,28},{16,0},{20,4},{24,8},{28,12},{1,17},{... | collective-permute-start | bytes 49160 | tf_op jit(solution)/shard_map/ppermute | solution.py:45
  45.4 8.1 %collective-permute-start.12 = (bf16[256,256]{1,0:T(8,128)(2,1)S(1)}, bf16[256,256]{1,0:T(8,128)(2,1)S(1)}, u32[]{:S(2)}, u32[]{:S(2)}) collective-permute-start(bf16[256,256]{1,0:T(8,128)(2,1)S(1)} %get-tuple-element.50), channel_id=1, source_target_pairs={{0,16},{4,20},{8,24},{12,28},{16,0},{20,4},{24,8},{28,12},{1,17},{... | collective-permute-start | bytes 393224 | tf_op jit(solution)/shard_map/ppermute | solution.py:45
  47.1 3.4 %collective-permute-start.9 = (bf16[64,5376]{1,0:T(8,128)(2,1)S(1)}, bf16[64,5376]{1,0:T(8,128)(2,1)S(1)}, u32[]{:S(2)}, u32[]{:S(2)}) collective-permute-start(bf16[64,5376]{1,0:T(8,128)(2,1)S(1)} %get-tuple-element.38), channel_id=1, source_target_pairs={{0,1},{1,0},{2,3},{3,2},{4,5},{5,4},{6,7},{7,6},{8,9},{9,8},{10,11... | collective-permute-start | bytes 2064392 | tf_op jit(solution)/shard_map/ppermute | solution.py:34
  50.9 14.5 %collective-permute-start.11 = (bf16[256,512]{1,0:T(8,128)(2,1)S(1)}, bf16[256,512]{1,0:T(8,128)(2,1)S(1)}, u32[]{:S(2)}, u32[]{:S(2)}) collective-permute-start(bf16[256,512]{1,0:T(8,128)(2,1)S(1)} %get-tuple-element.39), channel_id=1, source_target_pairs={{0,4},{4,0},{8,12},{12,8},{16,20},{20,16},{24,28},{28,24},{1,5},{5... | collective-permute-start | bytes 786440 | tf_op jit(solution)/shard_map/ppermute | solution.py:34
  53.5 14.7 %collective-permute-start.16 = (bf16[256,512]{1,0:T(8,128)(2,1)S(1)}, bf16[256,512]{1,0:T(8,128)(2,1)S(1)}, u32[]{:S(2)}, u32[]{:S(2)}) collective-permute-start(bf16[256,512]{1,0:T(8,128)(2,1)S(1)} %constant_dynamic-update-slice_fusion.df_ref), channel_id=1, source_target_pairs={{0,4},{4,0},{8,12},{12,8},{16,20},{20,16},{24,28},{28,24},{1,5},{5... | collective-permute-start | bytes 786440 | tf_op jit(solution)/shard_map/ppermute | solution.py:34
  55.0 10.3 %collective-permute-start.13 = (f32[8,512]{1,0:T(8,128)S(1)}, f32[8,512]{1,0:T(8,128)S(1)}, u32[]{:S(2)}, u32[]{:S(2)}) collective-permute-start(f32[8,512]{1,0:T(8,128)S(1)} %collective-permute-done.10.sf_ref), channel_id=1, source_target_pairs={{0,4},{4,0},{8,12},{12,8},{16,20},{20,16},{24,28},{28,24},{1,5},{5... | collective-permute-start | bytes 49160 | tf_op jit(solution)/shard_map/ppermute | solution.py:34
  55.6 22.5 %collective-permute-start.15 = (bf16[64,5376]{1,0:T(8,128)(2,1)S(1)}, bf16[64,5376]{1,0:T(8,128)(2,1)S(1)}, u32[]{:S(2)}, u32[]{:S(2)}) collective-permute-start(bf16[64,5376]{1,0:T(8,128)(2,1)S(1)} %far_sum.1), channel_id=1, source_target_pairs={{0,2},{1,3},{2,0},{3,1},{4,6},{5,7},{6,4},{7,5},{8,10},{9,11},{10,... | collective-permute-start | bytes 2064392 | tf_op jit(solution)/shard_map/ppermute | solution.py:34
  65.4 12.7 %collective-permute-start.14 = (bf16[64,5376]{1,0:T(8,128)(2,1)S(1)}, bf16[64,5376]{1,0:T(8,128)(2,1)S(1)}, u32[]{:S(2)}, u32[]{:S(2)}) collective-permute-start(bf16[64,5376]{1,0:T(8,128)(2,1)S(1)} %get-tuple-element.42), channel_id=1, source_target_pairs={{0,1},{1,0},{2,3},{3,2},{4,5},{5,4},{6,7},{7,6},{8,9},{9,8},{10,11... | collective-permute-start | bytes 2064392 | tf_op jit(solution)/shard_map/ppermute | solution.py:34
  65.4 8.7 %collective-permute-start.18 = (bf16[256,512]{1,0:T(8,128)(2,1)S(1)}, bf16[256,512]{1,0:T(8,128)(2,1)S(1)}, u32[]{:S(2)}, u32[]{:S(2)}) collective-permute-start(bf16[256,512]{1,0:T(8,128)(2,1)S(1)} %get-tuple-element.47), channel_id=1, source_target_pairs={{0,4},{4,0},{8,12},{12,8},{16,20},{20,16},{24,28},{28,24},{1,5},{5... | collective-permute-start | bytes 786440 | tf_op jit(solution)/shard_map/ppermute | solution.py:34
  66.9 10.3 %collective-permute-start.17 = (bf16[256,512]{1,0:T(8,128)(2,1)S(1)}, bf16[256,512]{1,0:T(8,128)(2,1)S(1)}, u32[]{:S(2)}, u32[]{:S(2)}) collective-permute-start(bf16[256,512]{1,0:T(8,128)(2,1)S(1)} %hop_sum.1), channel_id=1, source_target_pairs={{8,0},{12,4},{16,8},{20,12},{24,16},{28,20},{9,1},{13,5},{17,9},{2... | collective-permute-start | bytes 786440 | tf_op jit(solution)/shard_map/ppermute | solution.py:29

commit v5 on v4

--- a/solution.py
+++ b/solution.py
@@ -10,11 +10,12 @@
 LOGIT_SCALE = 168.0 ** (-0.5)
 LOG2E = 1.4426950408889634
 NEG = -1e30
+PACK = 16
 FAR = 4
 F32 = jnp.float32
 BF16 = jnp.bfloat16
 SMALL = pl.CostEstimate(flops=1, bytes_accessed=1, transcendentals=0)
-MEDIUM = pl.CostEstimate(flops=50 * 10**8, bytes_accessed=1, transcendentals=0)
+MEDIUM = pl.CostEstimate(flops=35 * 10**8, bytes_accessed=1, transcendentals=0)
 LARGE = pl.CostEstimate(flops=10**10, bytes_accessed=1, transcendentals=0)
 VMEM = pl.BlockSpec(memory_space=pltpu.VMEM)
 
@@ -85,13 +86,14 @@
     sent_ref[...] = jnp.where(lower, kv, q_ref[...])
 
 
-def forward_kernel(q_ref, kv_ref, r1_ref, r2_ref, x1_ref, p0_ref, x2_ref, d_ref, w_ref,
-                   p_ref, stat_ref, near_own_ref, near_core_ref, far_own_ref, far_core_ref, o_ref):
+def forward_kernel(q_ref, kv_ref, r1_ref, r2_ref, x1_ref, p0_ref, x2_ref, dn_ref, df_ref, w_ref,
+                   p_ref, stat_ref, second_ref, near_own_ref, near_core_ref, far_own_ref, far_core_ref, o_ref):
     seq, head = lax.axis_index("seq"), lax.axis_index("head")
     odd = lax.rem(seq, 2) == 1
     tok = q_ref.shape[0]
     kv_cols = kv_ref.shape[1] // 2
     q_rel = own_order(q_ref, head)
+    d_rel = jnp.concatenate([dn_ref[...], df_ref[...]], 0)
     causal = causal_mask(tok, head)
     near = jnp.where(seq >= 2, 0.0, NEG).astype(F32)
     far = jnp.where(seq >= 4, 0.0, NEG).astype(F32)
@@ -122,15 +124,23 @@
             p_ref[g, b] = pb
             out = out + dot(value_blocks[b], pb, 0, 0)
         out = out.astype(BF16)
-        grad = stacked(d_ref[...], g)
+        grad = stacked(d_rel, g)
         delta = jnp.sum(grad.astype(F32).T * out.astype(F32), axis=0, keepdims=True)
         stats += [top + jnp.log2(total), delta]
         out = out.astype(F32).T.astype(BF16)
         low = 2 * g * HEAD_SIZE
         o_ref[:, low : low + HEAD_SIZE] = out[:tok]
         o_ref[:, low + HEAD_SIZE : low + 2 * HEAD_SIZE] = out[tok:]
-    spare = stat_ref.shape[0] - len(stats)
-    stat_ref[...] = jnp.concatenate(stats + [jnp.zeros((spare, 2 * tok), F32)], 0)
+    spare = jnp.zeros((stat_ref.shape[0] - len(stats), 2 * tok), F32)
+    stat_ref[...] = jnp.concatenate(stats + [spare], 0)
+    half = d_rel.shape[1] // 2
+    packed = jnp.concatenate([st[:, :tok] for st in stats] + [st[:, tok:] for st in stats], 0)
+    packed = jnp.concatenate([packed, jnp.zeros((PACK - packed.shape[0], tok), F32)], 0)
+    second_ref[:tok, :] = d_rel[:, half:]
+    for part in range(3):
+        rounded = packed.astype(BF16)
+        second_ref[tok + part * PACK : tok + (part + 1) * PACK, :] = rounded
+        packed = packed - rounded.astype(F32)
     project(o_ref[...], w_ref, (near_own_ref, near_core_ref, far_own_ref, far_core_ref))
 
 
@@ -144,12 +154,20 @@
             ref[:, low : low + step] = part[i * size : (i + 1) * size]
 
 
-def back_kernel(own_ref, core_ref, y_ref, yc_ref, w_ref, d_ref):
-    rows = jnp.concatenate([own_ref[...], core_ref[...], y_ref[...], yc_ref[...]], 0)
+def near_back_kernel(own_ref, core_ref, w_ref, d_ref):
+    rows = jnp.concatenate([own_ref[...], core_ref[...]], 0)
     d_ref[...] = dot(rows, w_ref[...], 1, 1).astype(BF16)
 
 
-def backward_kernel(q_ref, kv_ref, r1_ref, r2_ref, x1_ref, p0_ref, x2_ref, p_ref, stat_ref, d_ref,
+def far_back_kernel(y_ref, yc_ref, w_ref, near_ref, d_ref, first_ref):
+    rows = jnp.concatenate([y_ref[...], yc_ref[...]], 0)
+    grad = dot(rows, w_ref[...], 1, 1).astype(BF16)
+    d_ref[...] = grad
+    cols = first_ref.shape[1]
+    first_ref[...] = jnp.concatenate([near_ref[:, :cols], grad[:, :cols]], 0)
+
+
+def backward_kernel(q_ref, kv_ref, r1_ref, r2_ref, x1_ref, p0_ref, x2_ref, p_ref, stat_ref, dn_ref, df_ref,
                     dq_ref, town_ref, t1_ref, tx_ref, tz_ref):
     seq, head = lax.axis_index("seq"), lax.axis_index("head")
     odd = lax.rem(seq, 2) == 1
@@ -157,10 +175,11 @@
     kv_cols = kv_ref.shape[1] // 2
     size = tok // 4
     q_rel = own_order(q_ref, head)
+    d_rel = jnp.concatenate([dn_ref[...], df_ref[...]], 0)
     outs = [town_ref, t1_ref, None, tx_ref, tz_ref]
     for g in range(kv_cols // HEAD_SIZE):
         kc, vc = columns(kv_cols, g)
-        qg, dg = stacked(q_rel, g), stacked(d_ref[...], g)
+        qg, dg = stacked(q_rel, g), stacked(d_rel, g)
         blocks = (kv_ref, r1_ref, r2_ref, x1_ref, p0_ref, x2_ref)
         key_blocks, value_blocks = window(*blocks, odd, kc), window(*blocks, odd, vc)
         delta = stat_ref[2 * g + 1 : 2 * g + 2, :]
@@ -181,27 +200,45 @@
             dq_ref[rows, low + HEAD_SIZE : low + 2 * HEAD_SIZE] = dq[tok + r * size : tok + (r + 1) * size]
 
 
-def far_kernel(kv_ref, qf_ref, df_ref, sf_ref, qx_ref, dx_ref, sx_ref, t_ref):
+def unpacked(second_ref, tok, kv_heads):
+    parts = [second_ref[tok + i * PACK : tok + (i + 1) * PACK, :tok].astype(F32) for i in range(3)]
+    packed = parts[0] + (parts[1] + parts[2])
+    count = 2 * kv_heads
+    return [jnp.concatenate([packed[i : i + 1], packed[count + i : count + i + 1]], 1) for i in range(count)]
+
+
+def pair_kernel(t_ref, a_ref, b_ref, out_ref):
+    tok, half = a_ref.shape
+    odd = lax.rem(lax.axis_index("seq"), 2) == 1
+    out_ref[:tok, :] = jnp.where(odd, t_ref[...], jnp.concatenate([a_ref[...], b_ref[:tok, :]], 1))
+    out_ref[tok:, :half] = b_ref[tok:, :]
+    out_ref[tok:, half:] = jnp.zeros((b_ref.shape[0] - tok, half), BF16)
+
+
+def far_kernel(kv_ref, qf_ref, af_ref, bf_ref, qx_ref, px_ref, t_ref):
     seq, head = lax.axis_index("seq"), lax.axis_index("head")
     count = lax.axis_size("seq")
     tok = kv_ref.shape[0]
     kv_cols = kv_ref.shape[1] // 2
+    kv_heads = kv_cols // HEAD_SIZE
     straight = jnp.logical_and(jnp.logical_not(causal_mask(tok, head)), seq + FAR < count)
     across = jnp.logical_and(lax.rem(seq, 2) == 1, seq + FAR - 1 < count)
-    sources = ((qf_ref, df_ref, sf_ref, straight), (qx_ref, dx_ref, sx_ref, across))
-    sources = [(own_order(q, head), d[...], st, keep) for q, d, st, keep in sources]
+    sources = [
+        (own_order(qf_ref, head), jnp.concatenate([af_ref[...], bf_ref[:tok, :]], 1), unpacked(bf_ref, tok, kv_heads), straight),
+        (own_order(qx_ref, head), px_ref[:tok, :], unpacked(px_ref, tok, kv_heads), across),
+    ]
     scale = LOGIT_SCALE * LOG2E
-    for g in range(kv_cols // HEAD_SIZE):
+    for g in range(kv_heads):
         kc, vc = columns(kv_cols, g)
         key, value = kv_ref[:, kc], kv_ref[:, vc]
         dk = jnp.zeros((tok, HEAD_SIZE), F32)
         dv = jnp.zeros((tok, HEAD_SIZE), F32)
-        for q_rel, d_rel, st, keep in sources:
+        for q_rel, d_rel, stats, keep in sources:
             qg, dg = stacked(q_rel, g), stacked(d_rel, g)
-            prob = jnp.exp2(dot(key, qg, 1, 1) * scale - st[2 * g : 2 * g + 1, :])
+            prob = jnp.exp2(dot(key, qg, 1, 1) * scale - stats[2 * g])
             prob = jnp.where(keep, prob, 0.0).astype(BF16)
             dp = dot(value, dg, 1, 1)
-            ds = (prob.astype(F32) * (dp - st[2 * g + 1 : 2 * g + 2, :])).astype(BF16)
+            ds = jnp.where(keep, prob.astype(F32) * (dp - stats[2 * g + 1]), 0.0).astype(BF16)
             dv = dv + dot(prob, dg, 1, 0)
             dk = dk + dot(ds, qg, 1, 0)
         t_ref[:, kc] = dk * LOGIT_SCALE
@@ -217,7 +254,7 @@
 
 def finish_kernel(own_ref, far_ref, hop_ref, pair_ref, dk_ref, dv_ref):
     odd = lax.rem(lax.axis_index("seq"), 2) == 1
-    total = own_ref[...] + far_ref[...] + hop_ref[...].astype(F32) + jnp.where(odd, 0.0, pair_ref[...].astype(F32))
+    total = own_ref[...] + far_ref[...] + hop_ref[...].astype(F32) + jnp.where(odd, 0.0, pair_ref[: own_ref.shape[0], :].astype(F32))
     kv_cols = dk_ref.shape[1]
     dk_ref[...] = total[:, :kv_cols].astype(BF16)
     dv_ref[...] = total[:, kv_cols:].astype(BF16)
@@ -254,50 +291,54 @@
     r2, q_far = far_swapped(lambda: kv, lambda: queries) if lax.axis_size("seq") > 2 * FAR else (far_swapped(*[lambda: far_sent] * 2))
     p0 = swapped(kv, "seq", 1)
     og_c = swapped(out_grad, "head", 1)
+    half_grad = jax.ShapeDtypeStruct((tok // 2, q_cols), BF16)
+    grad_near = call(near_back_kernel, "near_back", half_grad, [], out_grad, og_c, out_weight, cost=SMALL)
     x1 = swapped(gate(r1, p0), "seq", 1)
     x2 = swapped(r2 if r2 is q_far else jnp.where(odd, r2, q_far), "seq", 1)
-    og_yc = swapped(gate(og_y, x1, r2), "head", 1)
-    grad = call(back_kernel, "turn_back", jax.ShapeDtypeStruct((tok, q_cols), BF16), [], out_grad, og_c, og_y, og_yc, out_weight)
+    og_yc = swapped(gate(og_y, r1, r2, p0, grad_near), "head", 1)
+    first = jax.ShapeDtypeStruct((tok, q_cols // 2), BF16)
+    second = jax.ShapeDtypeStruct((tok + 3 * PACK, q_cols // 2), BF16)
+    grad_far, sent_first = call(far_back_kernel, "far_back", (half_grad, first), [], gate(og_y, x1), og_yc, out_weight, grad_near,
+                                cost=LARGE)
 
     def down(value):
         return far_swapped(*[lambda: value] * 2)[1]
 
-    grad_far = [down(grad[:, : q_cols // 2]), down(grad[:, q_cols // 2 :])]
-    probs, stats, near_own, near_core, far_own, far_core = call(
+    far_first = down(sent_first)
+    probs, stats, sent_second, near_own, near_core, far_own, far_core = call(
         forward_kernel,
         "attend",
         (
             jax.ShapeDtypeStruct((kv_heads, 5, tok, 2 * tok), BF16),
             jax.ShapeDtypeStruct((8 * pl.cdiv(2 * kv_heads, 8), 2 * tok), F32),
-            rows, rows, rows, rows,
+            second, rows, rows, rows, rows,
         ),
         [pltpu.VMEM((tok, q_cols), BF16)],
-        queries, kv, r1, r2, x1, p0, x2, grad, out_weight,
+        queries, kv, r1, r2, x1, p0, x2, grad_near, grad_far, out_weight,
     )
     sent = swapped(far_core, "head", 1)
-    stats_far = down(stats)
+    far_second = down(sent_second)
     far_sum = call(sum_kernel, "far_sum", rows, [], far_own, sent)
     from_y = swapped(far_sum, "head", 2)
-    stats_x = swapped(gate(stats_far, grad_far[1]), "seq", 1)
-    first_far, grad_far = grad_far[0], jnp.concatenate(grad_far, 1)
-    grad_x = swapped(grad_far, "seq", 1)
 
     query_gradient, t_own, t_1, t_x, t_z = call(
         backward_kernel,
         "attend_grad",
         (jax.ShapeDtypeStruct((tok, q_cols), BF16), wide_block, block, block, block),
         [],
-        queries, kv, r1, r2, x1, p0, x2, probs, stats, gate(grad, first_far),
+        queries, kv, r1, r2, x1, p0, x2, probs, stats, grad_near, gate(grad_far, far_first),
         cost=LARGE,
     )
-    d1 = gate(swapped(gate(t_x, far_sum, stats_far), "seq", 1), stats_x)
+    d1 = swapped(gate(t_x, far_sum), "seq", 1)
     e1 = shifted(call(sum_kernel, "hop_sum", block, [], t_1, d1), -2)
-    g = swapped(gate(t_z, d1), "seq", 1)
+    pair = jax.ShapeDtypeStruct((second.shape[0], q_cols), BF16)
+    pair = swapped(call(pair_kernel, "pair", pair, [], t_z, far_first, far_second), "seq", 1)
     from_core = swapped(gate(near_core, d1), "head", 1)
-    t_far = call(far_kernel, "far_grad", wide_block, [], kv, q_far, grad_far, stats_far, x2, grad_x, stats_x, cost=MEDIUM)
+    t_far = call(far_kernel, "far_grad", wide_block, [],
+                 kv, q_far, far_first, far_second, x2, pair, cost=MEDIUM)
 
     narrow = jax.ShapeDtypeStruct(keys.shape, BF16)
-    key_gradient, value_gradient = call(finish_kernel, "finish", (narrow, narrow), [], t_own, t_far, e1, g)
+    key_gradient, value_gradient = call(finish_kernel, "finish", (narrow, narrow), [], t_own, t_far, e1, pair)
     projected = call(sum_kernel, "projected", rows, [], near_own, from_core, from_y, cost=LARGE)
     return (projected, query_gradient, key_gradient, value_gradient)
 

time: 79.5 us -> 72.3 us (0.909)
  starting transfers between devices: 29.8 us -> 20 us
  Pallas kernels: 12.8 us -> 15.1 us
    ppermute x4 -> x3, starting transfers between devices: 12.6 us -> 3.56 us  [far_swapped(): lax.ppermute(lower() if lower is upper else jnp.where(side == r, lower(),...]
    ppermute x13 -> x11, waiting for transfers between devices: 16 us -> 21.8 us  [swapped(): return lax.ppermute(value, axis, [(i, i ^ bit) for i in range(count)])]
    ppermute x2, waiting for transfers between devices: 5.76 us -> 1.8 us  [shifted(): lax.ppermute(value, 'seq', [(i, i + steps) for i in range(first, last)])]
    pallas_call x9 -> x11, Pallas kernels: 12.8 us -> 15.1 us  [call(): pl.pallas_call(kernel, out_shape=outs, in_specs=[VMEM] * len(operands), o...]
    ppermute x4 -> x3, waiting for transfers between devices: 7.61 us -> 6.18 us  [far_swapped(): lax.ppermute(lower() if lower is upper else jnp.where(side == r, lower(),...]
    ppermute x13 -> x11, starting transfers between devices: 12.3 us -> 11.6 us  [swapped(): return lax.ppermute(value, axis, [(i, i ^ bit) for i in range(count)])]
    unnamed x15 -> x14, local copies, waits for them, and re-layouts: 6.43 us -> 6.43 us
  transfers between devices with their start and end apart: 19 -> 16, of which waited for: 9 -> 6; matrix products, arithmetic and copies ran while one was open for 0% -> 0% of each run, Pallas kernels for 15% -> 19%
where the time goes in v5:
time: 72.3 us; the launch traced here: 72 us
  waiting for transfers between devices  29.8 us (41%)
  starting transfers between devices  20 us (28%)
  Pallas kernels  15.1 us (21%)
  local copies, waits for them, and re-layouts  6.43 us (9%)
  between operations  0.75 us (1%)
    ppermute x11, waiting for transfers between devices, swapped(): return lax.ppermute(value, axis, [(i, i ^ bit) for i in range(count)])  21.8 us
    pallas_call x11, Pallas kernels, call(): pl.pallas_call(kernel, out_shape=outs, in_specs=[VMEM] * len(operands), o...  15.1 us
    ppermute x11, starting transfers between devices, swapped(): return lax.ppermute(value, axis, [(i, i ^ bit) for i in range(count)])  11.6 us
    unnamed x14, local copies, waits for them, and re-layouts  6.43 us
    ppermute x3, waiting for transfers between devices, far_swapped(): lax.ppermute(lower() if lower is upper else jnp.where(side == r, lower(),...  6.18 us
    ppermute x2, starting transfers between devices, shifted(): lax.ppermute(value, 'seq', [(i, i + steps) for i in range(first, last)])  4.79 us
    ppermute x3, starting transfers between devices, far_swapped(): lax.ppermute(lower() if lower is upper else jnp.where(side == r, lower(),...  3.56 us
    ppermute x2, waiting for transfers between devices, shifted(): lax.ppermute(value, 'seq', [(i, i + steps) for i in range(first, last)])  1.8 us
  transfers between devices with their start and end apart: 16, of which 6 were waited for; matrix products, arithmetic and copies ran while one was open for 0% of the time, Pallas kernels for 19%

profile of v5, /device:TPU:0, one launch (start us, length us, event | category | flops | bytes accessed | tf_op | source)
XLA Modules:
  0.0 72.0 jit_solution(867066177159113022)
XLA Ops:
  0.6 0.5 collective-permute-start.5
  1.1 2.6 %collective-permute-start.6 = (bf16[64,5376]{1,0:T(8,128)(2,1)}, bf16[64,5376]{1,0:T(8,128)(2,1)S(1)}, u32[]{:S(2)}, u32[]{:S(2)}) collective-permute-start(bf16[64,5376]{1,0:T(8,128)(2,1)} %own_ref.1), channel_id=1, source_target_pairs={{0,2},{1,3},{2,0},{3,1},{4,6},{5,7},{6,4},{7,5},{8,10},{9,11},{10,... | collective-permute-start | bytes 2064392 | tf_op jit(solution)/shard_map/ppermute | solution.py:35
  3.7 0.0 copy-start.2
  3.7 0.9 %copy-done.2 = bf16[256,512]{1,0:T(8,128)(2,1)S(1)} copy-done((bf16[256,512]{1,0:T(8,128)(2,1)S(1)}, bf16[256,512]{1,0:T(8,128)(2,1)}, u32[]{:S(2)}) %copy-start.2) | copy-done | bytes 262168
  4.7 0.0 copy-start.5
  4.7 0.9 %copy-done.5 = bf16[256,256]{1,0:T(8,128)(2,1)S(1)} copy-done((bf16[256,256]{1,0:T(8,128)(2,1)S(1)}, bf16[256,256]{1,0:T(8,128)(2,1)}, u32[]{:S(2)}) %copy-start.5) | copy-done | bytes 131096
  5.6 0.0 copy-start.6
  5.6 0.9 %copy-done.6 = bf16[256,256]{1,0:T(8,128)(2,1)S(1)} copy-done((bf16[256,256]{1,0:T(8,128)(2,1)S(1)}, bf16[256,256]{1,0:T(8,128)(2,1)}, u32[]{:S(2)}) %copy-start.6) | copy-done | bytes 131096
  6.5 0.1 join.1
  6.6 3.5 %collective-permute-start = (bf16[256,512]{1,0:T(8,128)(2,1)S(1)}, bf16[256,512]{1,0:T(8,128)(2,1)S(1)}, u32[]{:S(2)}, u32[]{:S(2)}) collective-permute-start(bf16[256,512]{1,0:T(8,128)(2,1)S(1)} %get-tuple-element.28.kv_ref), channel_id=1, source_target_pairs={{0,8},{4,12},{8,16},{12,20},{16,24},{20,28},{1,9},{5,13},{9,17},{1... | collective-permute-start | bytes 786440 | tf_op jit(solution)/shard_map/ppermute | solution.py:30
  10.1 1.6 %collective-permute-start.2 = (bf16[256,512]{1,0:T(8,128)(2,1)S(1)}, bf16[256,512]{1,0:T(8,128)(2,1)S(1)}, u32[]{:S(2)}, u32[]{:S(2)}) collective-permute-start(bf16[256,512]{1,0:T(8,128)(2,1)S(1)} %get-tuple-element.28.kv_ref), channel_id=1, source_target_pairs={{0,4},{4,0},{8,12},{12,8},{16,20},{20,16},{24,28},{28,24},{1,5},{5... | collective-permute-start | bytes 786440 | tf_op jit(solution)/shard_map/ppermute | solution.py:35
  11.6 2.6 %collective-permute-start.1 = (bf16[256,512]{1,0:T(8,128)(2,1)S(1)}, bf16[256,512]{1,0:T(8,128)(2,1)S(1)}, u32[]{:S(2)}, u32[]{:S(2)}) collective-permute-start(bf16[256,512]{1,0:T(8,128)(2,1)S(1)} %get-tuple-element.29), channel_id=1, source_target_pairs={{0,16},{4,20},{8,24},{12,28},{16,0},{20,4},{24,8},{28,12},{1,17},{... | collective-permute-start | bytes 786440 | tf_op jit(solution)/shard_map/ppermute | solution.py:46
  14.2 0.0 collective-permute-done.5.core_ref
  14.2 0.0 copy-start
  14.2 2.6 %copy-done = bf16[512,5376]{1,0:T(8,128)(2,1)S(1)} copy-done((bf16[512,5376]{1,0:T(8,128)(2,1)S(1)}, bf16[512,5376]{1,0:T(8,128)(2,1)}, u32[]{:S(2)}) %copy-start) | copy-done | bytes 5505048
  16.8 0.0 copy-start.4
  16.8 1.1 %copy-done.4 = bf16[64,5376]{1,0:T(8,128)(2,1)S(1)} copy-done((bf16[64,5376]{1,0:T(8,128)(2,1)S(1)}, bf16[64,5376]{1,0:T(8,128)(2,1)}, u32[]{:S(2)}) %copy-start.4) | copy-done | bytes 688152
  17.9 0.0 copy-start.1
  17.9 1.9 %near_back.1.near_ref.dn_ref = bf16[128,512]{1,0:T(8,128)(2,1)S(1)} custom-call(bf16[64,5376]{1,0:T(8,128)(2,1)S(1)} %copy-done.4, bf16[64,5376]{1,0:T(8,128)(2,1)S(1)} %collective-permute-done.5.core_ref, bf16[512,5376]{1,0:T(8,128)(2,1)S(1)} %copy-done), custom_call_target="tpu_custom_call" | custom-call | flops 1 | bytes 1 | tf_op jit(solution)/shard_map/near_back/pallas_call | solution.py:274
  19.8 0.0 copy-start.3
  19.8 0.0 collective-permute-done.r1_ref
  19.8 0.0 collective-permute-done.2.p0_ref
  19.8 6.2 %collective-permute-done.1.r2_ref.qf_ref = bf16[256,512]{1,0:T(8,128)(2,1)S(1)} collective-permute-done((bf16[256,512]{1,0:T(8,128)(2,1)S(1)}, bf16[256,512]{1,0:T(8,128)(2,1)S(1)}, u32[]{:S(2)}, u32[]{:S(2)}) %collective-permute-start.1) | collective-permute-done | bytes 262176 | tf_op jit(solution)/shard_map/ppermute | solution.py:46
  26.0 0.0 collective-permute-done.6.y_ref
  26.0 0.0 collective-permute-start.7
  26.0 0.5 collective-permute-start.3
  26.5 1.5 %collective-permute-start.4 = (bf16[256,512]{1,0:T(8,128)(2,1)S(1)}, bf16[256,512]{1,0:T(8,128)(2,1)S(1)}, u32[]{:S(2)}, u32[]{:S(2)}) collective-permute-start(bf16[256,512]{1,0:T(8,128)(2,1)S(1)} %collective-permute-done.1.r2_ref.qf_ref), channel_id=1, source_target_pairs={{0,4},{4,0},{8,12},{12,8},{16,20},{20,16},{24,28},{28,24},{1,5},{5... | collective-permute-start | bytes 786440 | tf_op jit(solution)/shard_map/ppermute | solution.py:35
  28.0 7.1 %collective-permute-done.3.x1_ref = bf16[256,512]{1,0:T(8,128)(2,1)S(1)} collective-permute-done((bf16[256,512]{1,0:T(8,128)(2,1)S(1)}, bf16[256,512]{1,0:T(8,128)(2,1)S(1)}, u32[]{:S(2)}, u32[]{:S(2)}) %collective-permute-start.3) | collective-permute-done | bytes 262176 | tf_op jit(solution)/shard_map/ppermute | solution.py:35
  35.1 0.0 collective-permute-done.7.yc_ref
  35.1 0.0 copy-done.1
  35.1 1.9 %far_back.1 = (bf16[128,512]{1,0:T(8,128)(2,1)S(1)}, bf16[256,256]{1,0:T(8,128)(2,1)S(1)}) custom-call(bf16[64,5376]{1,0:T(8,128)(2,1)S(1)} %collective-permute-done.6.y_ref, bf16[64,5376]{1,0:T(8,128)(2,1)S(1)} %collective-permute-done.7.yc_ref, bf16[512,5376]{1,0:T(8,128)(2,1)S(1)} %copy-done.1, bf16[128,512]{1,0:T(8,128)(2,1)S(1)} %near_back.1.near_ref.dn_ref), custom_call_target="tpu_custom_call" | custom-call | flops 10000000000 | bytes 1 | tf_op jit(solution)/shard_map/far_back/pallas_call | solution.py:274
  37.0 0.1 collective-permute-start.8
  37.0 3.3 %collective-permute-done.4.x2_ref.qx_ref = bf16[256,512]{1,0:T(8,128)(2,1)S(1)} collective-permute-done((bf16[256,512]{1,0:T(8,128)(2,1)S(1)}, bf16[256,512]{1,0:T(8,128)(2,1)S(1)}, u32[]{:S(2)}, u32[]{:S(2)}) %collective-permute-start.4) | collective-permute-done | bytes 262176 | tf_op jit(solution)/shard_map/ppermute | solution.py:35
  40.3 0.0 copy-done.3
  40.3 4.2 %attend.1 = (bf16[2,5,256,512]{3,2,1,0:T(8,128)(2,1)S(1)}, f32[8,512]{1,0:T(8,128)S(1)}, bf16[304,256]{1,0:T(8,128)(2,1)S(1)}, bf16[64,5376]{1,0:T(8,128)(2,1)S(...) custom-call(bf16[256,512]{1,0:T(8,128)(2,1)S(1)} %copy-done.3, ...), custom_call_target="tpu_custom_call" | custom-call | flops 1 | bytes 1 | tf_op jit(solution)/shard_map/attend/pallas_call | solution.py:274
  44.6 0.1 collective-permute-start.9
  44.6 0.0 collective-permute-done.8.a_ref.af_ref
  44.6 3.4 %attend_grad.1 = (bf16[256,512]{1,0:T(8,128)(2,1)}, f32[256,512]{1,0:T(8,128)S(1)}, bf16[256,512]{1,0:T(8,128)(2,1)S(1)}, bf16[256,512]{1,0:T(8,128)(2,1)S(1)}, bf16[256,512]{1,0:T(8,128)(2,1)S(1)}) custom-call(bf16[256,512]{1,0:T(8,128)(2,1)S(1)} %copy-done.3, bf16[256,512]{1,0:T(8,128)(2,1)S(1)} %get-tuple-element.28.kv_ref, ...), custom_call_target="tpu_custom_call" | custom-call | flops 10000000000 | bytes 1 | tf_op jit(solution)/shard_map/attend_grad/pallas_call | solution.py:274
  48.0 0.0 collective-permute-done.9.refs_1_
  48.0 0.2 far_sum.1
  48.2 0.6 collective-permute-start.10
  48.8 0.9 %collective-permute-start.13 = (bf16[304,256]{1,0:T(8,128)(2,1)S(1)}, bf16[304,256]{1,0:T(8,128)(2,1)S(1)}, u32[]{:S(2)}, u32[]{:S(2)}) collective-permute-start(bf16[304,256]{1,0:T(8,128)(2,1)S(1)} %get-tuple-element.47), channel_id=1, source_target_pairs={{0,16},{4,20},{8,24},{12,28},{16,0},{20,4},{24,8},{28,12},{1,17},{... | collective-permute-start | bytes 466952 | tf_op jit(solution)/shard_map/ppermute | solution.py:46
  49.7 0.5 collective-permute-start.12
  50.2 6.8 %collective-permute-done.10.refs_1_ = bf16[256,512]{1,0:T(8,128)(2,1)S(1)} collective-permute-done((bf16[256,512]{1,0:T(8,128)(2,1)S(1)}, bf16[256,512]{1,0:T(8,128)(2,1)S(1)}, u32[]{:S(2)}, u32[]{:S(2)}) %collective-permute-start.10) | collective-permute-done | bytes 262176 | tf_op jit(solution)/shard_map/ppermute | solution.py:35
  57.0 0.0 collective-permute-start.11
  57.0 0.0 collective-permute-done.13.b_ref.bf_ref
  57.0 3.8 %collective-permute-start.14 = (bf16[304,512]{1,0:T(8,128)(2,1)S(1)}, bf16[304,512]{1,0:T(8,128)(2,1)S(1)}, u32[]{:S(2)}, u32[]{:S(2)}) collective-permute-start(bf16[304,512]{1,0:T(8,128)(2,1)S(1)} %pair.1), channel_id=1, source_target_pairs={{0,4},{4,0},{8,12},{12,8},{16,20},{20,16},{24,28},{28,24},{1,5},{5... | collective-permute-start | bytes 933896 | tf_op jit(solution)/shard_map/ppermute | solution.py:35
  60.8 0.1 hop_sum.1
  60.8 1.3 %collective-permute-start.15 = (bf16[256,512]{1,0:T(8,128)(2,1)S(1)}, bf16[256,512]{1,0:T(8,128)(2,1)S(1)}, u32[]{:S(2)}, u32[]{:S(2)}) collective-permute-start(bf16[256,512]{1,0:T(8,128)(2,1)S(1)} %hop_sum.1), channel_id=1, source_target_pairs={{8,0},{12,4},{16,8},{20,12},{24,16},{28,20},{9,1},{13,5},{17,9},{2... | collective-permute-start | bytes 786440 | tf_op jit(solution)/shard_map/ppermute | solution.py:30
  62.1 4.7 %collective-permute-done.14.px_ref.pair_ref = bf16[304,512]{1,0:T(8,128)(2,1)S(1)} collective-permute-done((bf16[304,512]{1,0:T(8,128)(2,1)S(1)}, bf16[304,512]{1,0:T(8,128)(2,1)S(1)}, u32[]{:S(2)}, u32[]{:S(2)}) %collective-permute-start.14) | collective-permute-done | bytes 311328 | tf_op jit(solution)/shard_map/ppermute | solution.py:35
  66.8 1.5 %far_grad.1.far_ref = f32[256,512]{1,0:T(8,128)S(1)} custom-call(bf16[256,512]{1,0:T(8,128)(2,1)S(1)} %get-tuple-element.28.kv_ref, bf16[256,512]{1,0:T(8,128)(2,1)S(1)} %collective-permute-done.1.r2_ref.qf_ref, bf16[256,256]{1,0:T(8,128)(2,1)S(1)} %collective-permute-done.8.a_ref.af_ref, bf16[304,256]{1,0:T(8,128)(2,1)S(1)} %collective-permute-done.13.b_ref.bf_ref, ...), custom_call_target="tpu_custom_call" | custom-call | flops 3500000000 | bytes 1 | tf_op jit(solution)/shard_map/far_grad/pallas_call | solution.py:274
  68.3 1.8 %collective-permute-done.15.hop_ref = bf16[256,512]{1,0:T(8,128)(2,1)S(1)} collective-permute-done((bf16[256,512]{1,0:T(8,128)(2,1)S(1)}, bf16[256,512]{1,0:T(8,128)(2,1)S(1)}, u32[]{:S(2)}, u32[]{:S(2)}) %collective-permute-start.15) | collective-permute-done | bytes 262176 | tf_op jit(solution)/shard_map/ppermute | solution.py:30
  70.1 0.8 %finish.1 = (bf16[256,256]{1,0:T(8,128)(2,1)}, bf16[256,256]{1,0:T(8,128)(2,1)}) custom-call(f32[256,512]{1,0:T(8,128)S(1)} %get-tuple-element.46.own_ref, f32[256,512]{1,0:T(8,128)S(1)} %far_grad.1.far_ref, bf16[256,512]{1,0:T(8,128)(2,1)S(1)} %collective-permute-done.15.hop_ref, bf16[304,512]{1,0:T(8,128)(2,1)S(1)} %collective-permute-done.14.px_ref.pair_ref), custom_call_target="tpu_custom_call" | custom-call | flops 1 | bytes 1 | tf_op jit(solution)/shard_map/finish/pallas_call | solution.py:274
  70.9 0.0 collective-permute-done.12.refs_2_
  70.9 0.0 collective-permute-done.11.refs_1_
  70.9 1.1 %projected.1 = bf16[64,5376]{1,0:T(8,128)(2,1)} custom-call(bf16[64,5376]{1,0:T(8,128)(2,1)S(1)} %get-tuple-element.34.refs_0_, bf16[64,5376]{1,0:T(8,128)(2,1)S(1)} %collective-permute-done.11.refs_1_, bf16[64,5376]{1,0:T(8,128)(2,1)S(1)} %collective-permute-done.12.refs_2_), custom_call_target="tpu_custom_call" | custom-call | flops 10000000000 | bytes 1 | tf_op jit(solution)/shard_map/projected/pallas_call | solution.py:274
  (1 shorter events, 0.0 us)
Async XLA Ops:
  0.6 13.6 %collective-permute-start.5 = (bf16[64,5376]{1,0:T(8,128)(2,1)}, bf16[64,5376]{1,0:T(8,128)(2,1)S(1)}, u32[]{:S(2)}, u32[]{:S(2)}) collective-permute-start(bf16[64,5376]{1,0:T(8,128)(2,1)} %own_ref.1), channel_id=1, source_target_pairs={{0,1},{1,0},{2,3},{3,2},{4,5},{5,4},{6,7},{7,6},{8,9},{9,8},{10,11... | collective-permute-start | bytes 2064392 | tf_op jit(solution)/shard_map/ppermute | solution.py:35
  1.1 24.8 %collective-permute-start.6 = (bf16[64,5376]{1,0:T(8,128)(2,1)}, bf16[64,5376]{1,0:T(8,128)(2,1)S(1)}, u32[]{:S(2)}, u32[]{:S(2)}) collective-permute-start(bf16[64,5376]{1,0:T(8,128)(2,1)} %own_ref.1), channel_id=1, source_target_pairs={{0,2},{1,3},{2,0},{3,1},{4,6},{5,7},{6,4},{7,5},{8,10},{9,11},{10,... | collective-permute-start | bytes 2064392 | tf_op jit(solution)/shard_map/ppermute | solution.py:35
  3.7 0.9 %copy-start.2 = (bf16[256,512]{1,0:T(8,128)(2,1)S(1)}, bf16[256,512]{1,0:T(8,128)(2,1)}, u32[]{:S(2)}) copy-start(bf16[256,512]{1,0:T(8,128)(2,1)} %q_ref.5) | copy-start | bytes 786436
  4.7 0.9 %copy-start.5 = (bf16[256,256]{1,0:T(8,128)(2,1)S(1)}, bf16[256,256]{1,0:T(8,128)(2,1)}, u32[]{:S(2)}) copy-start(bf16[256,256]{1,0:T(8,128)(2,1)} %k_ref.1) | copy-start | bytes 393220
  5.6 0.9 %copy-start.6 = (bf16[256,256]{1,0:T(8,128)(2,1)S(1)}, bf16[256,256]{1,0:T(8,128)(2,1)}, u32[]{:S(2)}) copy-start(bf16[256,256]{1,0:T(8,128)(2,1)} %v_ref.1) | copy-start | bytes 393220
  6.6 13.2 %collective-permute-start = (bf16[256,512]{1,0:T(8,128)(2,1)S(1)}, bf16[256,512]{1,0:T(8,128)(2,1)S(1)}, u32[]{:S(2)}, u32[]{:S(2)}) collective-permute-start(bf16[256,512]{1,0:T(8,128)(2,1)S(1)} %get-tuple-element.28.kv_ref), channel_id=1, source_target_pairs={{0,8},{4,12},{8,16},{12,20},{16,24},{20,28},{1,9},{5,13},{9,17},{1... | collective-permute-start | bytes 786440 | tf_op jit(solution)/shard_map/ppermute | solution.py:30
  10.1 9.7 %collective-permute-start.2 = (bf16[256,512]{1,0:T(8,128)(2,1)S(1)}, bf16[256,512]{1,0:T(8,128)(2,1)S(1)}, u32[]{:S(2)}, u32[]{:S(2)}) collective-permute-start(bf16[256,512]{1,0:T(8,128)(2,1)S(1)} %get-tuple-element.28.kv_ref), channel_id=1, source_target_pairs={{0,4},{4,0},{8,12},{12,8},{16,20},{20,16},{24,28},{28,24},{1,5},{5... | collective-permute-start | bytes 786440 | tf_op jit(solution)/shard_map/ppermute | solution.py:35
  11.6 14.3 %collective-permute-start.1 = (bf16[256,512]{1,0:T(8,128)(2,1)S(1)}, bf16[256,512]{1,0:T(8,128)(2,1)S(1)}, u32[]{:S(2)}, u32[]{:S(2)}) collective-permute-start(bf16[256,512]{1,0:T(8,128)(2,1)S(1)} %get-tuple-element.29), channel_id=1, source_target_pairs={{0,16},{4,20},{8,24},{12,28},{16,0},{20,4},{24,8},{28,12},{1,17},{... | collective-permute-start | bytes 786440 | tf_op jit(solution)/shard_map/ppermute | solution.py:46
  14.2 2.6 %copy-start = (bf16[512,5376]{1,0:T(8,128)(2,1)S(1)}, bf16[512,5376]{1,0:T(8,128)(2,1)}, u32[]{:S(2)}) copy-start(bf16[512,5376]{1,0:T(8,128)(2,1)} %w_ref.5) | copy-start | bytes 16515076
  16.8 1.1 %copy-start.4 = (bf16[64,5376]{1,0:T(8,128)(2,1)S(1)}, bf16[64,5376]{1,0:T(8,128)(2,1)}, u32[]{:S(2)}) copy-start(bf16[64,5376]{1,0:T(8,128)(2,1)} %own_ref.1) | copy-start | bytes 2064388
  17.9 17.2 %copy-start.1 = (bf16[512,5376]{1,0:T(8,128)(2,1)S(1)}, bf16[512,5376]{1,0:T(8,128)(2,1)}, u32[]{:S(2)}) copy-start(bf16[512,5376]{1,0:T(8,128)(2,1)} %w_ref.5) | copy-start | bytes 16515076
  19.8 20.6 %copy-start.3 = (bf16[256,512]{1,0:T(8,128)(2,1)S(1)}, bf16[256,512]{1,0:T(8,128)(2,1)}, u32[]{:S(2)}) copy-start(bf16[256,512]{1,0:T(8,128)(2,1)} %q_ref.5) | copy-start | bytes 786436
  26.0 9.1 %collective-permute-start.7 = (bf16[64,5376]{1,0:T(8,128)(2,1)S(1)}, bf16[64,5376]{1,0:T(8,128)(2,1)S(1)}, u32[]{:S(2)}, u32[]{:S(2)}) collective-permute-start(bf16[64,5376]{1,0:T(8,128)(2,1)S(1)} %collective-permute-done.6.y_ref), channel_id=1, source_target_pairs={{0,1},{1,0},{2,3},{3,2},{4,5},{5,4},{6,7},{7,6},{8,9},{9,8},{10,11... | collective-permute-start | bytes 2064392 | tf_op jit(solution)/shard_map/ppermute | solution.py:35
  26.0 9.1 %collective-permute-start.3 = (bf16[256,512]{1,0:T(8,128)(2,1)S(1)}, bf16[256,512]{1,0:T(8,128)(2,1)S(1)}, u32[]{:S(2)}, u32[]{:S(2)}) collective-permute-start(bf16[256,512]{1,0:T(8,128)(2,1)S(1)} %collective-permute-done.r1_ref), channel_id=1, source_target_pairs={{0,4},{4,0},{8,12},{12,8},{16,20},{20,16},{24,28},{28,24},{1,5},{5... | collective-permute-start | bytes 786440 | tf_op jit(solution)/shard_map/ppermute | solution.py:35
  26.5 13.8 %collective-permute-start.4 = (bf16[256,512]{1,0:T(8,128)(2,1)S(1)}, bf16[256,512]{1,0:T(8,128)(2,1)S(1)}, u32[]{:S(2)}, u32[]{:S(2)}) collective-permute-start(bf16[256,512]{1,0:T(8,128)(2,1)S(1)} %collective-permute-done.1.r2_ref.qf_ref), channel_id=1, source_target_pairs={{0,4},{4,0},{8,12},{12,8},{16,20},{20,16},{24,28},{28,24},{1,5},{5... | collective-permute-start | bytes 786440 | tf_op jit(solution)/shard_map/ppermute | solution.py:35
  37.0 7.7 %collective-permute-start.8 = (bf16[256,256]{1,0:T(8,128)(2,1)S(1)}, bf16[256,256]{1,0:T(8,128)(2,1)S(1)}, u32[]{:S(2)}, u32[]{:S(2)}) collective-permute-start(bf16[256,256]{1,0:T(8,128)(2,1)S(1)} %get-tuple-element.38), channel_id=1, source_target_pairs={{0,16},{4,20},{8,24},{12,28},{16,0},{20,4},{24,8},{28,12},{1,17},{... | collective-permute-start | bytes 393224 | tf_op jit(solution)/shard_map/ppermute | solution.py:46
  44.6 3.5 %collective-permute-start.9 = (bf16[64,5376]{1,0:T(8,128)(2,1)S(1)}, bf16[64,5376]{1,0:T(8,128)(2,1)S(1)}, u32[]{:S(2)}, u32[]{:S(2)}) collective-permute-start(bf16[64,5376]{1,0:T(8,128)(2,1)S(1)} %get-tuple-element.42), channel_id=1, source_target_pairs={{0,1},{1,0},{2,3},{3,2},{4,5},{5,4},{6,7},{7,6},{8,9},{9,8},{10,11... | collective-permute-start | bytes 2064392 | tf_op jit(solution)/shard_map/ppermute | solution.py:35
  48.2 8.8 %collective-permute-start.10 = (bf16[256,512]{1,0:T(8,128)(2,1)S(1)}, bf16[256,512]{1,0:T(8,128)(2,1)S(1)}, u32[]{:S(2)}, u32[]{:S(2)}) collective-permute-start(bf16[256,512]{1,0:T(8,128)(2,1)S(1)} %get-tuple-element.43), channel_id=1, source_target_pairs={{0,4},{4,0},{8,12},{12,8},{16,20},{20,16},{24,28},{28,24},{1,5},{5... | collective-permute-start | bytes 786440 | tf_op jit(solution)/shard_map/ppermute | solution.py:35
  48.8 8.2 %collective-permute-start.13 = (bf16[304,256]{1,0:T(8,128)(2,1)S(1)}, bf16[304,256]{1,0:T(8,128)(2,1)S(1)}, u32[]{:S(2)}, u32[]{:S(2)}) collective-permute-start(bf16[304,256]{1,0:T(8,128)(2,1)S(1)} %get-tuple-element.47), channel_id=1, source_target_pairs={{0,16},{4,20},{8,24},{12,28},{16,0},{20,4},{24,8},{28,12},{1,17},{... | collective-permute-start | bytes 466952 | tf_op jit(solution)/shard_map/ppermute | solution.py:46
  49.7 21.2 %collective-permute-start.12 = (bf16[64,5376]{1,0:T(8,128)(2,1)S(1)}, bf16[64,5376]{1,0:T(8,128)(2,1)S(1)}, u32[]{:S(2)}, u32[]{:S(2)}) collective-permute-start(bf16[64,5376]{1,0:T(8,128)(2,1)S(1)} %far_sum.1), channel_id=1, source_target_pairs={{0,2},{1,3},{2,0},{3,1},{4,6},{5,7},{6,4},{7,5},{8,10},{9,11},{10,... | collective-permute-start | bytes 2064392 | tf_op jit(solution)/shard_map/ppermute | solution.py:35
  57.0 14.0 %collective-permute-start.11 = (bf16[64,5376]{1,0:T(8,128)(2,1)S(1)}, bf16[64,5376]{1,0:T(8,128)(2,1)S(1)}, u32[]{:S(2)}, u32[]{:S(2)}) collective-permute-start(bf16[64,5376]{1,0:T(8,128)(2,1)S(1)} %get-tuple-element.44), channel_id=1, source_target_pairs={{0,1},{1,0},{2,3},{3,2},{4,5},{5,4},{6,7},{7,6},{8,9},{9,8},{10,11... | collective-permute-start | bytes 2064392 | tf_op jit(solution)/shard_map/ppermute | solution.py:35
  57.0 9.8 %collective-permute-start.14 = (bf16[304,512]{1,0:T(8,128)(2,1)S(1)}, bf16[304,512]{1,0:T(8,128)(2,1)S(1)}, u32[]{:S(2)}, u32[]{:S(2)}) collective-permute-start(bf16[304,512]{1,0:T(8,128)(2,1)S(1)} %pair.1), channel_id=1, source_target_pairs={{0,4},{4,0},{8,12},{12,8},{16,20},{20,16},{24,28},{28,24},{1,5},{5... | collective-permute-start | bytes 933896 | tf_op jit(solution)/shard_map/ppermute | solution.py:35
  60.8 9.3 %collective-permute-start.15 = (bf16[256,512]{1,0:T(8,128)(2,1)S(1)}, bf16[256,512]{1,0:T(8,128)(2,1)S(1)}, u32[]{:S(2)}, u32[]{:S(2)}) collective-permute-start(bf16[256,512]{1,0:T(8,128)(2,1)S(1)} %hop_sum.1), channel_id=1, source_target_pairs={{8,0},{12,4},{16,8},{20,12},{24,16},{28,20},{9,1},{13,5},{17,9},{2... | collective-permute-start | bytes 786440 | tf_op jit(solution)/shard_map/ppermute | solution.py:30

commit v6 on v5

--- a/solution.py
+++ b/solution.py
@@ -1,3 +1,5 @@
+import functools
+
 import jax
 import jax.numpy as jnp
 from jax import lax
@@ -15,7 +17,7 @@
 F32 = jnp.float32
 BF16 = jnp.bfloat16
 SMALL = pl.CostEstimate(flops=1, bytes_accessed=1, transcendentals=0)
-MEDIUM = pl.CostEstimate(flops=35 * 10**8, bytes_accessed=1, transcendentals=0)
+MEDIUM = pl.CostEstimate(flops=1 * 10**8, bytes_accessed=1, transcendentals=0)
 LARGE = pl.CostEstimate(flops=10**10, bytes_accessed=1, transcendentals=0)
 VMEM = pl.BlockSpec(memory_space=pltpu.VMEM)
 
@@ -79,15 +81,26 @@
     return [kv_ref[:, cols], r1_ref[:, cols], r2_ref[:, cols], x1_ref[:, cols], jnp.where(odd, p0_ref[:, cols], x2_ref[:, cols])]
 
 
-def join_kernel(k_ref, v_ref, q_ref, kv_ref, sent_ref):
-    lower = lax.rem(lax.div(lax.axis_index("seq"), FAR), 2) == 0
-    kv = jnp.concatenate([k_ref[...], v_ref[...]], 1)
-    kv_ref[...] = kv
-    sent_ref[...] = jnp.where(lower, kv, q_ref[...])
-
-
-def forward_kernel(q_ref, kv_ref, r1_ref, r2_ref, x1_ref, p0_ref, x2_ref, dn_ref, df_ref, w_ref,
-                   p_ref, stat_ref, second_ref, near_own_ref, near_core_ref, far_own_ref, far_core_ref, o_ref):
+def join_kernel(k_ref, v_ref, kv_ref):
+    cols = k_ref.shape[1]
+    kv_ref[:, :cols] = k_ref[...]
+    kv_ref[:, cols:] = v_ref[...]
+
+
+def either_kernel(first, a_ref, b_ref, out_ref):
+    out_ref[...] = jnp.where(first(lax.axis_index("seq")), a_ref[...], b_ref[...])
+
+
+def is_odd(seq):
+    return lax.rem(seq, 2) == 1
+
+
+def is_lower(seq):
+    return lax.rem(lax.div(seq, FAR), 2) == 0
+
+
+def forward_kernel(q_ref, kv_ref, r1_ref, r2_ref, x1_ref, p0_ref, x2_ref, dn_ref, df_ref,
+                   o_ref, p_ref, stat_ref, second_ref):
     seq, head = lax.axis_index("seq"), lax.axis_index("head")
     odd = lax.rem(seq, 2) == 1
     tok = q_ref.shape[0]
@@ -141,15 +154,14 @@
         rounded = packed.astype(BF16)
         second_ref[tok + part * PACK : tok + (part + 1) * PACK, :] = rounded
         packed = packed - rounded.astype(F32)
-    project(o_ref[...], w_ref, (near_own_ref, near_core_ref, far_own_ref, far_core_ref))
-
-
-def project(rows, w_ref, part_refs):
+
+
+def project_kernel(o_ref, w_ref, *part_refs):
     size = part_refs[0].shape[0]
     cols = w_ref.shape[1]
     step = cols // 7 if cols % (7 * HEAD_SIZE) == 0 else cols
     for low in range(0, cols, step):
-        part = dot(rows, w_ref[:, low : low + step], 1, 0).astype(BF16)
+        part = dot(o_ref[...], w_ref[:, low : low + step], 1, 0).astype(BF16)
         for i, ref in enumerate(part_refs):
             ref[:, low : low + step] = part[i * size : (i + 1) * size]
 
@@ -167,8 +179,23 @@
     first_ref[...] = jnp.concatenate([near_ref[:, :cols], grad[:, :cols]], 0)
 
 
+def across_kernel(q_ref, x1_ref, p_ref, stat_ref, dn_ref, df_ref, tx_ref):
+    tok = q_ref.shape[0]
+    kv_cols = x1_ref.shape[1] // 2
+    q_rel = own_order(q_ref, lax.axis_index("head"))
+    d_rel = jnp.concatenate([dn_ref[...], df_ref[...]], 0)
+    for g in range(kv_cols // HEAD_SIZE):
+        kc, vc = columns(kv_cols, g)
+        qg, dg = stacked(q_rel, g), stacked(d_rel, g)
+        pb = p_ref[g, 3]
+        dp = dot(x1_ref[:, vc], dg, 1, 1)
+        ds = (pb.astype(F32) * (dp - stat_ref[2 * g + 1 : 2 * g + 2, :])).astype(BF16)
+        tx_ref[:, vc] = dot(pb, dg, 1, 0).astype(BF16)
+        tx_ref[:, kc] = (dot(ds, qg, 1, 0) * LOGIT_SCALE).astype(BF16)
+
+
 def backward_kernel(q_ref, kv_ref, r1_ref, r2_ref, x1_ref, p0_ref, x2_ref, p_ref, stat_ref, dn_ref, df_ref,
-                    dq_ref, town_ref, t1_ref, tx_ref, tz_ref):
+                    dq_ref, town_ref, t1_ref, tz_ref):
     seq, head = lax.axis_index("seq"), lax.axis_index("head")
     odd = lax.rem(seq, 2) == 1
     tok = q_ref.shape[0]
@@ -176,7 +203,7 @@
     size = tok // 4
     q_rel = own_order(q_ref, head)
     d_rel = jnp.concatenate([dn_ref[...], df_ref[...]], 0)
-    outs = [town_ref, t1_ref, None, tx_ref, tz_ref]
+    outs = [town_ref, t1_ref, None, None, tz_ref]
     for g in range(kv_cols // HEAD_SIZE):
         kc, vc = columns(kv_cols, g)
         qg, dg = stacked(q_rel, g), stacked(d_rel, g)
@@ -264,7 +291,6 @@
     tok, q_cols = queries.shape
     kv_cols = keys.shape[1]
     kv_heads = kv_cols // HEAD_SIZE
-    odd = lax.rem(lax.axis_index("seq"), 2) == 1
     size = tok // 4
     rows = jax.ShapeDtypeStruct((size, out_weight.shape[1]), BF16)
     block = jax.ShapeDtypeStruct((tok, 2 * kv_cols), BF16)
@@ -286,7 +312,8 @@
         return lax.optimization_barrier((value, *others))[0]
 
     og_y = swapped(out_grad, "head", 2)
-    kv, far_sent = call(join_kernel, "join", (block, block), [], keys, values, queries)
+    kv = call(join_kernel, "join", block, [], keys, values)
+    far_sent = call(functools.partial(either_kernel, is_lower), "far_sent", block, [], kv, queries)
     r1 = shifted(kv, 2)
     r2, q_far = far_swapped(lambda: kv, lambda: queries) if lax.axis_size("seq") > 2 * FAR else (far_swapped(*[lambda: far_sent] * 2))
     p0 = swapped(kv, "seq", 1)
@@ -294,7 +321,7 @@
     half_grad = jax.ShapeDtypeStruct((tok // 2, q_cols), BF16)
     grad_near = call(near_back_kernel, "near_back", half_grad, [], out_grad, og_c, out_weight, cost=SMALL)
     x1 = swapped(gate(r1, p0), "seq", 1)
-    x2 = swapped(r2 if r2 is q_far else jnp.where(odd, r2, q_far), "seq", 1)
+    x2 = swapped(call(functools.partial(either_kernel, is_odd), "pick", block, [], r2, q_far, cost=LARGE), "seq", 1)
     og_yc = swapped(gate(og_y, r1, r2, p0, grad_near), "head", 1)
     first = jax.ShapeDtypeStruct((tok, q_cols // 2), BF16)
     second = jax.ShapeDtypeStruct((tok + 3 * PACK, q_cols // 2), BF16)
@@ -305,35 +332,40 @@
         return far_swapped(*[lambda: value] * 2)[1]
 
     far_first = down(sent_first)
-    probs, stats, sent_second, near_own, near_core, far_own, far_core = call(
+    attended, probs, stats, sent_second = call(
         forward_kernel,
         "attend",
         (
+            jax.ShapeDtypeStruct((tok, q_cols), BF16),
             jax.ShapeDtypeStruct((kv_heads, 5, tok, 2 * tok), BF16),
             jax.ShapeDtypeStruct((8 * pl.cdiv(2 * kv_heads, 8), 2 * tok), F32),
-            second, rows, rows, rows, rows,
+            second,
         ),
-        [pltpu.VMEM((tok, q_cols), BF16)],
-        queries, kv, r1, r2, x1, p0, x2, grad_near, grad_far, out_weight,
+        [],
+        queries, kv, r1, r2, x1, p0, x2, grad_near, grad_far,
     )
-    sent = swapped(far_core, "head", 1)
+    t_x = call(across_kernel, "across_grad", block, [], queries, x1, probs, stats, grad_near, grad_far)
+    d1 = swapped(t_x, "seq", 1)
     far_second = down(sent_second)
+    near_own, near_core, far_own, far_core = call(
+        project_kernel, "project", (rows,) * 4, [], gate(attended, t_x), out_weight
+    )
+    sent = swapped(gate(far_core, far_first), "head", 1)
     far_sum = call(sum_kernel, "far_sum", rows, [], far_own, sent)
     from_y = swapped(far_sum, "head", 2)
 
-    query_gradient, t_own, t_1, t_x, t_z = call(
+    query_gradient, t_own, t_1, t_z = call(
         backward_kernel,
         "attend_grad",
-        (jax.ShapeDtypeStruct((tok, q_cols), BF16), wide_block, block, block, block),
+        (jax.ShapeDtypeStruct((tok, q_cols), BF16), wide_block, block, block),
         [],
         queries, kv, r1, r2, x1, p0, x2, probs, stats, grad_near, gate(grad_far, far_first),
         cost=LARGE,
     )
-    d1 = swapped(gate(t_x, far_sum), "seq", 1)
     e1 = shifted(call(sum_kernel, "hop_sum", block, [], t_1, d1), -2)
     pair = jax.ShapeDtypeStruct((second.shape[0], q_cols), BF16)
     pair = swapped(call(pair_kernel, "pair", pair, [], t_z, far_first, far_second), "seq", 1)
-    from_core = swapped(gate(near_core, d1), "head", 1)
+    from_core = swapped(gate(near_core, far_sum), "head", 1)
     t_far = call(far_kernel, "far_grad", wide_block, [],
                  kv, q_far, far_first, far_second, x2, pair, cost=MEDIUM)
 

time: 72.3 us -> 67.7 us (0.936)
  waiting for transfers between devices: 29.8 us -> 18.6 us
  starting transfers between devices: 20 us -> 26 us
    ppermute x11, waiting for transfers between devices: 21.8 us -> 9.44 us  [swapped(): return lax.ppermute(value, axis, [(i, i ^ bit) for i in range(count)])]
    ppermute x3, starting transfers between devices: 3.56 us -> 11.8 us  [far_swapped(): lax.ppermute(lower() if lower is upper else jnp.where(side == r, lower(),...]
    ppermute x11, starting transfers between devices: 11.6 us -> 9.43 us  [swapped(): return lax.ppermute(value, axis, [(i, i ^ bit) for i in range(count)])]
    ppermute x3, waiting for transfers between devices: 6.18 us -> 7.1 us  [far_swapped(): lax.ppermute(lower() if lower is upper else jnp.where(side == r, lower(),...]
    pallas_call x11 -> x15, Pallas kernels: 15.1 us -> 15.6 us  [call(): pl.pallas_call(kernel, out_shape=outs, in_specs=[VMEM] * len(operands), o...]
    unnamed x14 -> x16, local copies, waits for them, and re-layouts: 6.43 us -> 6.43 us
  transfers between devices with their start and end apart: 16 -> 16, of which waited for: 6 -> 8; matrix products, arithmetic and copies ran while one was open for 0% -> 0% of each run, Pallas kernels for 19% -> 21%
where the time goes in v6:
time: 67.7 us; the launch traced here: 67.4 us
  starting transfers between devices  26 us (38%)
  waiting for transfers between devices  18.6 us (27%)
  Pallas kernels  15.6 us (23%)
  local copies, waits for them, and re-layouts  6.43 us (9%)
  between operations  0.76 us (1%)
    pallas_call x15, Pallas kernels, call(): pl.pallas_call(kernel, out_shape=outs, in_specs=[VMEM] * len(operands), o...  15.6 us
    ppermute x3, starting transfers between devices, far_swapped(): lax.ppermute(lower() if lower is upper else jnp.where(side == r, lower(),...  11.8 us
    ppermute x11, waiting for transfers between devices, swapped(): return lax.ppermute(value, axis, [(i, i ^ bit) for i in range(count)])  9.44 us
    ppermute x11, starting transfers between devices, swapped(): return lax.ppermute(value, axis, [(i, i ^ bit) for i in range(count)])  9.43 us
    ppermute x3, waiting for transfers between devices, far_swapped(): lax.ppermute(lower() if lower is upper else jnp.where(side == r, lower(),...  7.1 us
    unnamed x16, local copies, waits for them, and re-layouts  6.43 us
    ppermute x2, starting transfers between devices, shifted(): lax.ppermute(value, 'seq', [(i, i + steps) for i in range(first, last)])  4.79 us
    ppermute x2, waiting for transfers between devices, shifted(): lax.ppermute(value, 'seq', [(i, i + steps) for i in range(first, last)])  2.08 us
  transfers between devices with their start and end apart: 16, of which 8 were waited for; matrix products, arithmetic and copies ran while one was open for 0% of the time, Pallas kernels for 21%

profile of v6, /device:TPU:0, one launch (start us, length us, event | category | flops | bytes accessed | tf_op | source)
XLA Modules:
  0.0 67.4 jit_solution(13283260655780253987)
XLA Ops:
  0.6 0.5 collective-permute-start.5
  1.1 2.6 %collective-permute-start.6 = (bf16[64,5376]{1,0:T(8,128)(2,1)}, bf16[64,5376]{1,0:T(8,128)(2,1)S(1)}, u32[]{:S(2)}, u32[]{:S(2)}) collective-permute-start(bf16[64,5376]{1,0:T(8,128)(2,1)} %own_ref.1), channel_id=1, source_target_pairs={{0,2},{1,3},{2,0},{3,1},{4,6},{5,7},{6,4},{7,5},{8,10},{9,11},{10,... | collective-permute-start | bytes 2064392 | tf_op jit(solution)/shard_map/ppermute | solution.py:37
  3.7 0.0 copy-start.4
  3.7 0.9 %copy-done.4 = bf16[256,256]{1,0:T(8,128)(2,1)S(1)} copy-done((bf16[256,256]{1,0:T(8,128)(2,1)S(1)}, bf16[256,256]{1,0:T(8,128)(2,1)}, u32[]{:S(2)}) %copy-start.4) | copy-done | bytes 131096
  4.6 0.0 copy-start.5
  4.7 0.9 %copy-done.5 = bf16[256,256]{1,0:T(8,128)(2,1)S(1)} copy-done((bf16[256,256]{1,0:T(8,128)(2,1)S(1)}, bf16[256,256]{1,0:T(8,128)(2,1)}, u32[]{:S(2)}) %copy-start.5) | copy-done | bytes 131096
  5.6 3.5 %collective-permute-start = (bf16[256,512]{1,0:T(8,128)(2,1)S(1)}, bf16[256,512]{1,0:T(8,128)(2,1)S(1)}, u32[]{:S(2)}, u32[]{:S(2)}) collective-permute-start(bf16[256,512]{1,0:T(8,128)(2,1)S(1)} %join.1.a_ref.kv_ref), channel_id=1, source_target_pairs={{0,8},{4,12},{8,16},{12,20},{16,24},{20,28},{1,9},{5,13},{9,17},{1... | collective-permute-start | bytes 786440 | tf_op jit(solution)/shard_map/ppermute | solution.py:32
  9.1 1.6 %collective-permute-start.2 = (bf16[256,512]{1,0:T(8,128)(2,1)S(1)}, bf16[256,512]{1,0:T(8,128)(2,1)S(1)}, u32[]{:S(2)}, u32[]{:S(2)}) collective-permute-start(bf16[256,512]{1,0:T(8,128)(2,1)S(1)} %join.1.a_ref.kv_ref), channel_id=1, source_target_pairs={{0,4},{4,0},{8,12},{12,8},{16,20},{20,16},{24,28},{28,24},{1,5},{5... | collective-permute-start | bytes 786440 | tf_op jit(solution)/shard_map/ppermute | solution.py:37
  10.6 0.0 copy-start.1
  10.6 0.9 %copy-done.1 = bf16[256,512]{1,0:T(8,128)(2,1)S(1)} copy-done((bf16[256,512]{1,0:T(8,128)(2,1)S(1)}, bf16[256,512]{1,0:T(8,128)(2,1)}, u32[]{:S(2)}) %copy-start.1) | copy-done | bytes 262168
  11.6 2.6 %collective-permute-start.1 = (bf16[256,512]{1,0:T(8,128)(2,1)S(1)}, bf16[256,512]{1,0:T(8,128)(2,1)S(1)}, u32[]{:S(2)}, u32[]{:S(2)}) collective-permute-start(bf16[256,512]{1,0:T(8,128)(2,1)S(1)} %far_sent.1), channel_id=1, source_target_pairs={{0,16},{4,20},{8,24},{12,28},{16,0},{20,4},{24,8},{28,12},{1,17},{... | collective-permute-start | bytes 786440 | tf_op jit(solution)/shard_map/ppermute | solution.py:48
  14.3 1.4 %collective-permute-done.r1_ref = bf16[256,512]{1,0:T(8,128)(2,1)S(1)} collective-permute-done((bf16[256,512]{1,0:T(8,128)(2,1)S(1)}, bf16[256,512]{1,0:T(8,128)(2,1)S(1)}, u32[]{:S(2)}, u32[]{:S(2)}) %collective-permute-start) | collective-permute-done | bytes 262176 | tf_op jit(solution)/shard_map/ppermute | solution.py:32
  15.7 1.5 %collective-permute-done.2.p0_ref = bf16[256,512]{1,0:T(8,128)(2,1)S(1)} collective-permute-done((bf16[256,512]{1,0:T(8,128)(2,1)S(1)}, bf16[256,512]{1,0:T(8,128)(2,1)S(1)}, u32[]{:S(2)}, u32[]{:S(2)}) %collective-permute-start.2) | collective-permute-done | bytes 262176 | tf_op jit(solution)/shard_map/ppermute | solution.py:37
  17.2 1.5 %collective-permute-start.3 = (bf16[256,512]{1,0:T(8,128)(2,1)S(1)}, bf16[256,512]{1,0:T(8,128)(2,1)S(1)}, u32[]{:S(2)}, u32[]{:S(2)}) collective-permute-start(bf16[256,512]{1,0:T(8,128)(2,1)S(1)} %collective-permute-done.r1_ref), channel_id=1, source_target_pairs={{0,4},{4,0},{8,12},{12,8},{16,20},{20,16},{24,28},{28,24},{1,5},{5... | collective-permute-start | bytes 786440 | tf_op jit(solution)/shard_map/ppermute | solution.py:37
  18.7 0.0 collective-permute-done.5.core_ref
  18.7 0.0 copy-start
  18.7 2.6 %copy-done = bf16[512,5376]{1,0:T(8,128)(2,1)S(1)} copy-done((bf16[512,5376]{1,0:T(8,128)(2,1)S(1)}, bf16[512,5376]{1,0:T(8,128)(2,1)}, u32[]{:S(2)}) %copy-start) | copy-done | bytes 5505048
  21.3 0.0 copy-start.3
  21.3 1.1 %copy-done.3 = bf16[64,5376]{1,0:T(8,128)(2,1)S(1)} copy-done((bf16[64,5376]{1,0:T(8,128)(2,1)S(1)}, bf16[64,5376]{1,0:T(8,128)(2,1)}, u32[]{:S(2)}) %copy-start.3) | copy-done | bytes 688152
  22.4 0.0 slice-start
  22.4 1.9 %near_back.1.near_ref.dn_ref = bf16[128,512]{1,0:T(8,128)(2,1)S(1)} custom-call(bf16[64,5376]{1,0:T(8,128)(2,1)S(1)} %copy-done.3, bf16[64,5376]{1,0:T(8,128)(2,1)S(1)} %collective-permute-done.5.core_ref, bf16[512,5376]{1,0:T(8,128)(2,1)S(1)} %copy-done), custom_call_target="tpu_custom_call" | custom-call | flops 1 | bytes 1 | tf_op jit(solution)/shard_map/near_back/pallas_call | solution.py:300
  24.3 0.0 slice-start.1
  24.3 1.7 %collective-permute-done.1.a_ref.b_ref.r2_ref.qf_ref = bf16[256,512]{1,0:T(8,128)(2,1)S(1)} collective-permute-done((bf16[256,512]{1,0:T(8,128)(2,1)S(1)}, bf16[256,512]{1,0:T(8,128)(2,1)S(1)}, u32[]{:S(2)}, u32[]{:S(2)}) %collective-permute-start.1) | collective-permute-done | bytes 262176 | tf_op jit(solution)/shard_map/ppermute | solution.py:48
  26.0 0.0 collective-permute-done.6.y_ref
  26.0 0.0 collective-permute-start.7
  26.1 0.0 copy-start.2
  26.1 0.6 collective-permute-start.4
  26.7 0.0 collective-permute-done.3.x1_ref
  26.7 1.5 %collective-permute-done.7.yc_ref = bf16[64,5376]{1,0:T(8,128)(2,1)S(1)} collective-permute-done((bf16[64,5376]{1,0:T(8,128)(2,1)S(1)}, bf16[64,5376]{1,0:T(8,128)(2,1)S(1)}, u32[]{:S(2)}, u32[]{:S(2)}) %collective-permute-start.7) | collective-permute-done | bytes 688160 | tf_op jit(solution)/shard_map/ppermute | solution.py:37
  28.2 0.0 slice-done
  28.2 0.0 slice-done.1
  28.2 1.9 %far_back.1 = (bf16[128,512]{1,0:T(8,128)(2,1)S(1)}, bf16[256,256]{1,0:T(8,128)(2,1)S(1)}) custom-call(bf16[64,5376]{1,0:T(8,128)(2,1)S(1)} %collective-permute-done.6.y_ref, bf16[64,5376]{1,0:T(8,128)(2,1)S(1)} %collective-permute-done.7.yc_ref, bf16[512,5376]{1,0:T(8,128)(2,1)S(1)} %bitcast.1, bf16[128,512]{1,0:T(8,128)(2,1)S(1)} %near_back.1.near_ref.dn_ref), custom_call_target="tpu_custom_call" | custom-call | flops 10000000000 | bytes 1 | tf_op jit(solution)/shard_map/far_back/pallas_call | solution.py:300
  30.1 6.0 %collective-permute-start.8 = (bf16[256,256]{1,0:T(8,128)(2,1)S(1)}, bf16[256,256]{1,0:T(8,128)(2,1)S(1)}, u32[]{:S(2)}, u32[]{:S(2)}) collective-permute-start(bf16[256,256]{1,0:T(8,128)(2,1)S(1)} %get-tuple-element.39), channel_id=1, source_target_pairs={{0,16},{4,20},{8,24},{12,28},{16,0},{20,4},{24,8},{28,12},{1,17},{... | collective-permute-start | bytes 393224 | tf_op jit(solution)/shard_map/ppermute | solution.py:48
  36.1 0.0 collective-permute-done.4.x2_ref.qx_ref
  36.1 0.0 copy-done.2
  36.1 2.6 %attend.1 = (bf16[256,512]{1,0:T(8,128)(2,1)S(1)}, bf16[2,5,256,512]{3,2,1,0:T(8,128)(2,1)S(1)}, f32[8,512]{1,0:T(8,128)S(1)}, bf16[304,256]{1,0:T(8,128)(2,1)S(1)}) custom-call(bf16[256,512]{1,0:T(8,128)(2,1)S(1)} %copy-done.2, bf16[256,512]{1,0:T(8,128)(2,1)S(1)} %join.1.a_ref.kv_ref, bf16[256,512]{1,0:T(8,128)(2,1)S(1)} %collective-permute-done.r1_ref, ...), custom_call_target="tpu_custom_call" | custom-call | flops 1 | bytes 1 | tf_op jit(solution)/shard_map/attend/pallas_call | solution.py:300
  38.7 0.6 across_grad.1
  39.3 1.6 %project.1 = (bf16[64,5376]{1,0:T(8,128)(2,1)S(1)}, bf16[64,5376]{1,0:T(8,128)(2,1)S(1)}, bf16[64,5376]{1,0:T(8,128)(2,1)S(1)}, bf16[64,5376]{1,0:T(8,128)(2,1)S(1)}) custom-call(bf16[256,512]{1,0:T(8,128)(2,1)S(1)} %get-tuple-element.34.o_ref, bf16[512,5376]{1,0:T(8,128)(2,1)S(1)} %bitcast.1), custom_call_target="tpu_custom_call" | custom-call | flops 1 | bytes 1 | tf_op jit(solution)/shard_map/project/pallas_call | solution.py:300
  40.9 1.8 %collective-permute-done.8.a_ref.af_ref = bf16[256,256]{1,0:T(8,128)(2,1)S(1)} collective-permute-done((bf16[256,256]{1,0:T(8,128)(2,1)S(1)}, bf16[256,256]{1,0:T(8,128)(2,1)S(1)}, u32[]{:S(2)}, u32[]{:S(2)}) %collective-permute-start.8) | collective-permute-done | bytes 131104 | tf_op jit(solution)/shard_map/ppermute | solution.py:48
  42.7 0.0 collective-permute-start.9
  42.7 0.5 collective-permute-start.14
  43.2 3.1 %collective-permute-start.12 = (bf16[304,256]{1,0:T(8,128)(2,1)S(1)}, bf16[304,256]{1,0:T(8,128)(2,1)S(1)}, u32[]{:S(2)}, u32[]{:S(2)}) collective-permute-start(bf16[304,256]{1,0:T(8,128)(2,1)S(1)} %get-tuple-element.45), channel_id=1, source_target_pairs={{0,16},{4,20},{8,24},{12,28},{16,0},{20,4},{24,8},{28,12},{1,17},{... | collective-permute-start | bytes 466952 | tf_op jit(solution)/shard_map/ppermute | solution.py:48
  46.3 0.0 collective-permute-done.9.refs_1_
  46.3 0.2 far_sum.1
  46.5 0.6 collective-permute-start.11
  47.1 0.0 collective-permute-start.10
  47.1 3.4 %attend_grad.1 = (bf16[256,512]{1,0:T(8,128)(2,1)}, f32[256,512]{1,0:T(8,128)S(1)}, bf16[256,512]{1,0:T(8,128)(2,1)S(1)}, bf16[256,512]{1,0:T(8,128)(2,1)S(1)}) custom-call(bf16[256,512]{1,0:T(8,128)(2,1)S(1)} %copy-done.2, bf16[256,512]{1,0:T(8,128)(2,1)S(1)} %join.1.a_ref.kv_ref, bf16[256,512]{1,0:T(8,128)(2,1)S(1)} %collective-permute-done.r1_ref, ...), custom_call_target="tpu_custom_call" | custom-call | flops 10000000000 | bytes 1 | tf_op jit(solution)/shard_map/attend_grad/pallas_call | solution.py:300
  50.4 3.6 %collective-permute-done.12.b_ref.bf_ref = bf16[304,256]{1,0:T(8,128)(2,1)S(1)} collective-permute-done((bf16[304,256]{1,0:T(8,128)(2,1)S(1)}, bf16[304,256]{1,0:T(8,128)(2,1)S(1)}, u32[]{:S(2)}, u32[]{:S(2)}) %collective-permute-start.12) | collective-permute-done | bytes 155680 | tf_op jit(solution)/shard_map/ppermute | solution.py:48
  54.0 1.6 %collective-permute-start.13 = (bf16[304,512]{1,0:T(8,128)(2,1)S(1)}, bf16[304,512]{1,0:T(8,128)(2,1)S(1)}, u32[]{:S(2)}, u32[]{:S(2)}) collective-permute-start(bf16[304,512]{1,0:T(8,128)(2,1)S(1)} %pair.1), channel_id=1, source_target_pairs={{0,4},{4,0},{8,12},{12,8},{16,20},{20,16},{24,28},{28,24},{1,5},{5... | collective-permute-start | bytes 933896 | tf_op jit(solution)/shard_map/ppermute | solution.py:37
  55.6 0.0 collective-permute-done.14.refs_1_
  55.6 0.1 hop_sum.1
  55.7 1.3 %collective-permute-start.15 = (bf16[256,512]{1,0:T(8,128)(2,1)S(1)}, bf16[256,512]{1,0:T(8,128)(2,1)S(1)}, u32[]{:S(2)}, u32[]{:S(2)}) collective-permute-start(bf16[256,512]{1,0:T(8,128)(2,1)S(1)} %hop_sum.1), channel_id=1, source_target_pairs={{8,0},{12,4},{16,8},{20,12},{24,16},{28,20},{9,1},{13,5},{17,9},{2... | collective-permute-start | bytes 786440 | tf_op jit(solution)/shard_map/ppermute | solution.py:32
  57.0 6.4 %collective-permute-done.13.px_ref.pair_ref = bf16[304,512]{1,0:T(8,128)(2,1)S(1)} collective-permute-done((bf16[304,512]{1,0:T(8,128)(2,1)S(1)}, bf16[304,512]{1,0:T(8,128)(2,1)S(1)}, u32[]{:S(2)}, u32[]{:S(2)}) %collective-permute-start.13) | collective-permute-done | bytes 311328 | tf_op jit(solution)/shard_map/ppermute | solution.py:37
  63.4 1.5 %far_grad.1.far_ref = f32[256,512]{1,0:T(8,128)S(1)} custom-call(bf16[256,512]{1,0:T(8,128)(2,1)S(1)} %join.1.a_ref.kv_ref, bf16[256,512]{1,0:T(8,128)(2,1)S(1)} %collective-permute-done.1.a_ref.b_ref.r2_ref.qf_ref, bf16[256,256]{1,0:T(8,128)(2,1)S(1)} %collective-permute-done.8.a_ref.af_ref, bf16[304,256]{1,0:T(8,128)(2,1)S(1)} %collective-permute-done.12.b_ref.bf_ref, ...), custom_call_target="tpu_custom_call" | custom-call | flops 100000000 | bytes 1 | tf_op jit(solution)/shard_map/far_grad/pallas_call | solution.py:300
  64.9 0.6 collective-permute-done.15.hop_ref
  65.5 0.8 %finish.1 = (bf16[256,256]{1,0:T(8,128)(2,1)}, bf16[256,256]{1,0:T(8,128)(2,1)}) custom-call(f32[256,512]{1,0:T(8,128)S(1)} %get-tuple-element.44.own_ref, f32[256,512]{1,0:T(8,128)S(1)} %far_grad.1.far_ref, bf16[256,512]{1,0:T(8,128)(2,1)S(1)} %collective-permute-done.15.hop_ref, bf16[304,512]{1,0:T(8,128)(2,1)S(1)} %collective-permute-done.13.px_ref.pair_ref), custom_call_target="tpu_custom_call" | custom-call | flops 1 | bytes 1 | tf_op jit(solution)/shard_map/finish/pallas_call | solution.py:300
  66.3 0.0 collective-permute-done.10.refs_1_
  66.3 0.0 collective-permute-done.11.refs_2_
  66.3 1.1 %projected.1 = bf16[64,5376]{1,0:T(8,128)(2,1)} custom-call(bf16[64,5376]{1,0:T(8,128)(2,1)S(1)} %get-tuple-element.35.refs_0_, bf16[64,5376]{1,0:T(8,128)(2,1)S(1)} %collective-permute-done.10.refs_1_, bf16[64,5376]{1,0:T(8,128)(2,1)S(1)} %collective-permute-done.11.refs_2_), custom_call_target="tpu_custom_call" | custom-call | flops 10000000000 | bytes 1 | tf_op jit(solution)/shard_map/projected/pallas_call | solution.py:300
  (5 shorter events, 0.1 us)
Async XLA Ops:
  0.6 18.1 %collective-permute-start.5 = (bf16[64,5376]{1,0:T(8,128)(2,1)}, bf16[64,5376]{1,0:T(8,128)(2,1)S(1)}, u32[]{:S(2)}, u32[]{:S(2)}) collective-permute-start(bf16[64,5376]{1,0:T(8,128)(2,1)} %own_ref.1), channel_id=1, source_target_pairs={{0,1},{1,0},{2,3},{3,2},{4,5},{5,4},{6,7},{7,6},{8,9},{9,8},{10,11... | collective-permute-start | bytes 2064392 | tf_op jit(solution)/shard_map/ppermute | solution.py:37
  1.1 24.9 %collective-permute-start.6 = (bf16[64,5376]{1,0:T(8,128)(2,1)}, bf16[64,5376]{1,0:T(8,128)(2,1)S(1)}, u32[]{:S(2)}, u32[]{:S(2)}) collective-permute-start(bf16[64,5376]{1,0:T(8,128)(2,1)} %own_ref.1), channel_id=1, source_target_pairs={{0,2},{1,3},{2,0},{3,1},{4,6},{5,7},{6,4},{7,5},{8,10},{9,11},{10,... | collective-permute-start | bytes 2064392 | tf_op jit(solution)/shard_map/ppermute | solution.py:37
  3.7 0.9 %copy-start.4 = (bf16[256,256]{1,0:T(8,128)(2,1)S(1)}, bf16[256,256]{1,0:T(8,128)(2,1)}, u32[]{:S(2)}) copy-start(bf16[256,256]{1,0:T(8,128)(2,1)} %k_ref.1) | copy-start | bytes 393220
  4.6 0.9 %copy-start.5 = (bf16[256,256]{1,0:T(8,128)(2,1)S(1)}, bf16[256,256]{1,0:T(8,128)(2,1)}, u32[]{:S(2)}) copy-start(bf16[256,256]{1,0:T(8,128)(2,1)} %v_ref.1) | copy-start | bytes 393220
  5.6 10.1 %collective-permute-start = (bf16[256,512]{1,0:T(8,128)(2,1)S(1)}, bf16[256,512]{1,0:T(8,128)(2,1)S(1)}, u32[]{:S(2)}, u32[]{:S(2)}) collective-permute-start(bf16[256,512]{1,0:T(8,128)(2,1)S(1)} %join.1.a_ref.kv_ref), channel_id=1, source_target_pairs={{0,8},{4,12},{8,16},{12,20},{16,24},{20,28},{1,9},{5,13},{9,17},{1... | collective-permute-start | bytes 786440 | tf_op jit(solution)/shard_map/ppermute | solution.py:32
  9.1 8.2 %collective-permute-start.2 = (bf16[256,512]{1,0:T(8,128)(2,1)S(1)}, bf16[256,512]{1,0:T(8,128)(2,1)S(1)}, u32[]{:S(2)}, u32[]{:S(2)}) collective-permute-start(bf16[256,512]{1,0:T(8,128)(2,1)S(1)} %join.1.a_ref.kv_ref), channel_id=1, source_target_pairs={{0,4},{4,0},{8,12},{12,8},{16,20},{20,16},{24,28},{28,24},{1,5},{5... | collective-permute-start | bytes 786440 | tf_op jit(solution)/shard_map/ppermute | solution.py:37
  10.6 0.9 %copy-start.1 = (bf16[256,512]{1,0:T(8,128)(2,1)S(1)}, bf16[256,512]{1,0:T(8,128)(2,1)}, u32[]{:S(2)}) copy-start(bf16[256,512]{1,0:T(8,128)(2,1)} %q_ref.5) | copy-start | bytes 786436
  11.6 14.4 %collective-permute-start.1 = (bf16[256,512]{1,0:T(8,128)(2,1)S(1)}, bf16[256,512]{1,0:T(8,128)(2,1)S(1)}, u32[]{:S(2)}, u32[]{:S(2)}) collective-permute-start(bf16[256,512]{1,0:T(8,128)(2,1)S(1)} %far_sent.1), channel_id=1, source_target_pairs={{0,16},{4,20},{8,24},{12,28},{16,0},{20,4},{24,8},{28,12},{1,17},{... | collective-permute-start | bytes 786440 | tf_op jit(solution)/shard_map/ppermute | solution.py:48
  17.2 9.4 %collective-permute-start.3 = (bf16[256,512]{1,0:T(8,128)(2,1)S(1)}, bf16[256,512]{1,0:T(8,128)(2,1)S(1)}, u32[]{:S(2)}, u32[]{:S(2)}) collective-permute-start(bf16[256,512]{1,0:T(8,128)(2,1)S(1)} %collective-permute-done.r1_ref), channel_id=1, source_target_pairs={{0,4},{4,0},{8,12},{12,8},{16,20},{20,16},{24,28},{28,24},{1,5},{5... | collective-permute-start | bytes 786440 | tf_op jit(solution)/shard_map/ppermute | solution.py:37
  18.7 2.6 %copy-start = (bf16[512,5376]{1,0:T(8,128)(2,1)S(1)}, bf16[512,5376]{1,0:T(8,128)(2,1)}, u32[]{:S(2)}) copy-start(bf16[512,5376]{1,0:T(8,128)(2,1)} %w_ref.5) | copy-start | bytes 16515076
  21.3 1.1 %copy-start.3 = (bf16[64,5376]{1,0:T(8,128)(2,1)S(1)}, bf16[64,5376]{1,0:T(8,128)(2,1)}, u32[]{:S(2)}) copy-start(bf16[64,5376]{1,0:T(8,128)(2,1)} %own_ref.1) | copy-start | bytes 2064388
  22.4 5.8 %slice-start = ((s8[5505024]{0:T(1024)(128)(4,1)}), s8[4194304]{0:T(1024)(128)(4,1)S(1)}, s32[]{:S(2)}) async-start(s8[5505024]{0:T(1024)(128)(4,1)} %bitcast), calls=%async_computation | async-start | bytes 8388608
  24.3 3.9 %slice-start.1 = ((s8[5505024]{0:T(1024)(128)(4,1)}), s8[1310720]{0:T(1024)(128)(4,1)S(1)}, s32[]{:S(2)}) async-start(s8[5505024]{0:T(1024)(128)(4,1)} %bitcast), calls=%async_computation.1 | async-start | bytes 2621440
  26.0 2.1 %collective-permute-start.7 = (bf16[64,5376]{1,0:T(8,128)(2,1)S(1)}, bf16[64,5376]{1,0:T(8,128)(2,1)S(1)}, u32[]{:S(2)}, u32[]{:S(2)}) collective-permute-start(bf16[64,5376]{1,0:T(8,128)(2,1)S(1)} %collective-permute-done.6.y_ref), channel_id=1, source_target_pairs={{0,1},{1,0},{2,3},{3,2},{4,5},{5,4},{6,7},{7,6},{8,9},{9,8},{10,11... | collective-permute-start | bytes 2064392 | tf_op jit(solution)/shard_map/ppermute | solution.py:37
  26.1 10.0 %copy-start.2 = (bf16[256,512]{1,0:T(8,128)(2,1)S(1)}, bf16[256,512]{1,0:T(8,128)(2,1)}, u32[]{:S(2)}) copy-start(bf16[256,512]{1,0:T(8,128)(2,1)} %q_ref.5) | copy-start | bytes 786436
  26.1 10.0 %collective-permute-start.4 = (bf16[256,512]{1,0:T(8,128)(2,1)S(1)}, bf16[256,512]{1,0:T(8,128)(2,1)S(1)}, u32[]{:S(2)}, u32[]{:S(2)}) collective-permute-start(bf16[256,512]{1,0:T(8,128)(2,1)S(1)} %pick.1), channel_id=1, source_target_pairs={{0,4},{4,0},{8,12},{12,8},{16,20},{20,16},{24,28},{28,24},{1,5},{5... | collective-permute-start | bytes 786440 | tf_op jit(solution)/shard_map/ppermute | solution.py:37
  30.1 12.6 %collective-permute-start.8 = (bf16[256,256]{1,0:T(8,128)(2,1)S(1)}, bf16[256,256]{1,0:T(8,128)(2,1)S(1)}, u32[]{:S(2)}, u32[]{:S(2)}) collective-permute-start(bf16[256,256]{1,0:T(8,128)(2,1)S(1)} %get-tuple-element.39), channel_id=1, source_target_pairs={{0,16},{4,20},{8,24},{12,28},{16,0},{20,4},{24,8},{28,12},{1,17},{... | collective-permute-start | bytes 393224 | tf_op jit(solution)/shard_map/ppermute | solution.py:48
  42.7 3.7 %collective-permute-start.9 = (bf16[64,5376]{1,0:T(8,128)(2,1)S(1)}, bf16[64,5376]{1,0:T(8,128)(2,1)S(1)}, u32[]{:S(2)}, u32[]{:S(2)}) collective-permute-start(bf16[64,5376]{1,0:T(8,128)(2,1)S(1)} %get-tuple-element.40), channel_id=1, source_target_pairs={{0,1},{1,0},{2,3},{3,2},{4,5},{5,4},{6,7},{7,6},{8,9},{9,8},{10,11... | collective-permute-start | bytes 2064392 | tf_op jit(solution)/shard_map/ppermute | solution.py:37
  42.7 12.9 %collective-permute-start.14 = (bf16[256,512]{1,0:T(8,128)(2,1)S(1)}, bf16[256,512]{1,0:T(8,128)(2,1)S(1)}, u32[]{:S(2)}, u32[]{:S(2)}) collective-permute-start(bf16[256,512]{1,0:T(8,128)(2,1)S(1)} %across_grad.1), channel_id=1, source_target_pairs={{0,4},{4,0},{8,12},{12,8},{16,20},{20,16},{24,28},{28,24},{1,5},{5... | collective-permute-start | bytes 786440 | tf_op jit(solution)/shard_map/ppermute | solution.py:37
  43.2 10.8 %collective-permute-start.12 = (bf16[304,256]{1,0:T(8,128)(2,1)S(1)}, bf16[304,256]{1,0:T(8,128)(2,1)S(1)}, u32[]{:S(2)}, u32[]{:S(2)}) collective-permute-start(bf16[304,256]{1,0:T(8,128)(2,1)S(1)} %get-tuple-element.45), channel_id=1, source_target_pairs={{0,16},{4,20},{8,24},{12,28},{16,0},{20,4},{24,8},{28,12},{1,17},{... | collective-permute-start | bytes 466952 | tf_op jit(solution)/shard_map/ppermute | solution.py:48
  46.5 19.8 %collective-permute-start.11 = (bf16[64,5376]{1,0:T(8,128)(2,1)S(1)}, bf16[64,5376]{1,0:T(8,128)(2,1)S(1)}, u32[]{:S(2)}, u32[]{:S(2)}) collective-permute-start(bf16[64,5376]{1,0:T(8,128)(2,1)S(1)} %far_sum.1), channel_id=1, source_target_pairs={{0,2},{1,3},{2,0},{3,1},{4,6},{5,7},{6,4},{7,5},{8,10},{9,11},{10,... | collective-permute-start | bytes 2064392 | tf_op jit(solution)/shard_map/ppermute | solution.py:37
  47.1 19.2 %collective-permute-start.10 = (bf16[64,5376]{1,0:T(8,128)(2,1)S(1)}, bf16[64,5376]{1,0:T(8,128)(2,1)S(1)}, u32[]{:S(2)}, u32[]{:S(2)}) collective-permute-start(bf16[64,5376]{1,0:T(8,128)(2,1)S(1)} %get-tuple-element.41), channel_id=1, source_target_pairs={{0,1},{1,0},{2,3},{3,2},{4,5},{5,4},{6,7},{7,6},{8,9},{9,8},{10,11... | collective-permute-start | bytes 2064392 | tf_op jit(solution)/shard_map/ppermute | solution.py:37
  54.0 9.3 %collective-permute-start.13 = (bf16[304,512]{1,0:T(8,128)(2,1)S(1)}, bf16[304,512]{1,0:T(8,128)(2,1)S(1)}, u32[]{:S(2)}, u32[]{:S(2)}) collective-permute-start(bf16[304,512]{1,0:T(8,128)(2,1)S(1)} %pair.1), channel_id=1, source_target_pairs={{0,4},{4,0},{8,12},{12,8},{16,20},{20,16},{24,28},{28,24},{1,5},{5... | collective-permute-start | bytes 933896 | tf_op jit(solution)/shard_map/ppermute | solution.py:37
  55.7 9.8 %collective-permute-start.15 = (bf16[256,512]{1,0:T(8,128)(2,1)S(1)}, bf16[256,512]{1,0:T(8,128)(2,1)S(1)}, u32[]{:S(2)}, u32[]{:S(2)}) collective-permute-start(bf16[256,512]{1,0:T(8,128)(2,1)S(1)} %hop_sum.1), channel_id=1, source_target_pairs={{8,0},{12,4},{16,8},{20,12},{24,16},{28,20},{9,1},{13,5},{17,9},{2... | collective-permute-start | bytes 786440 | tf_op jit(solution)/shard_map/ppermute | solution.py:32

commit v7 on v6

--- a/solution.py
+++ b/solution.py
@@ -319,10 +319,10 @@
     p0 = swapped(kv, "seq", 1)
     og_c = swapped(out_grad, "head", 1)
     half_grad = jax.ShapeDtypeStruct((tok // 2, q_cols), BF16)
-    grad_near = call(near_back_kernel, "near_back", half_grad, [], out_grad, og_c, out_weight, cost=SMALL)
-    x1 = swapped(gate(r1, p0), "seq", 1)
+    grad_near = call(near_back_kernel, "near_back", half_grad, [], out_grad, og_c, out_weight, cost=LARGE)
+    x1 = swapped(gate(r1, p0, grad_near), "seq", 1)
     x2 = swapped(call(functools.partial(either_kernel, is_odd), "pick", block, [], r2, q_far, cost=LARGE), "seq", 1)
-    og_yc = swapped(gate(og_y, r1, r2, p0, grad_near), "head", 1)
+    og_yc = swapped(gate(og_y, r2, grad_near), "head", 1)
     first = jax.ShapeDtypeStruct((tok, q_cols // 2), BF16)
     second = jax.ShapeDtypeStruct((tok + 3 * PACK, q_cols // 2), BF16)
     grad_far, sent_first = call(far_back_kernel, "far_back", (half_grad, first), [], gate(og_y, x1), og_yc, out_weight, grad_near,

time: 67.7 us -> 64.2 us (0.948)
  starting transfers between devices: 26 us -> 22.3 us
    ppermute x3, starting transfers between devices: 11.8 us -> 7.87 us  [far_swapped(): lax.ppermute(lower() if lower is upper else jnp.where(side == r, lower(),...]
    ppermute x2, waiting for transfers between devices: 2.08 us -> 0.66 us  [shifted(): lax.ppermute(value, 'seq', [(i, i + steps) for i in range(first, last)])]
    ppermute x3, waiting for transfers between devices: 7.1 us -> 8.26 us  [far_swapped(): lax.ppermute(lower() if lower is upper else jnp.where(side == r, lower(),...]
    ppermute x2, starting transfers between devices: 4.79 us -> 5.8 us  [shifted(): lax.ppermute(value, 'seq', [(i, i + steps) for i in range(first, last)])]
    ppermute x11, starting transfers between devices: 9.43 us -> 8.61 us  [swapped(): return lax.ppermute(value, axis, [(i, i ^ bit) for i in range(count)])]
  transfers between devices with their start and end apart: 16 -> 16, of which waited for: 8 -> 8; matrix products, arithmetic and copies ran while one was open for 0% -> 0% of each run, Pallas kernels for 21% -> 23%
where the time goes in v7:
time: 64.2 us; the launch traced here: 63.9 us
  starting transfers between devices  22.3 us (35%)
  waiting for transfers between devices  18.8 us (29%)
  Pallas kernels  15.6 us (24%)
  local copies, waits for them, and re-layouts  6.43 us (10%)
  between operations  0.79 us (1%)
    pallas_call x15, Pallas kernels, call(): pl.pallas_call(kernel, out_shape=outs, in_specs=[VMEM] * len(operands), o...  15.6 us
    ppermute x11, waiting for transfers between devices, swapped(): return lax.ppermute(value, axis, [(i, i ^ bit) for i in range(count)])  9.92 us
    ppermute x11, starting transfers between devices, swapped(): return lax.ppermute(value, axis, [(i, i ^ bit) for i in range(count)])  8.61 us
    ppermute x3, waiting for transfers between devices, far_swapped(): lax.ppermute(lower() if lower is upper else jnp.where(side == r, lower(),...  8.26 us
    ppermute x3, starting transfers between devices, far_swapped(): lax.ppermute(lower() if lower is upper else jnp.where(side == r, lower(),...  7.87 us
    unnamed x16, local copies, waits for them, and re-layouts  6.43 us
    ppermute x2, starting transfers between devices, shifted(): lax.ppermute(value, 'seq', [(i, i + steps) for i in range(first, last)])  5.8 us
  transfers between devices with their start and end apart: 16, of which 8 were waited for; matrix products, arithmetic and copies ran while one was open for 0% of the time, Pallas kernels for 23%

profile of v7, /device:TPU:0, one launch (start us, length us, event | category | flops | bytes accessed | tf_op | source)
XLA Modules:
  0.0 63.9 jit_solution(18397646894942857458)
XLA Ops:
  0.6 0.5 collective-permute-start.3
  1.1 0.0 copy-start.3
  1.2 0.9 %copy-done.3 = bf16[256,256]{1,0:T(8,128)(2,1)S(1)} copy-done((bf16[256,256]{1,0:T(8,128)(2,1)S(1)}, bf16[256,256]{1,0:T(8,128)(2,1)}, u32[]{:S(2)}) %copy-start.3) | copy-done | bytes 131096
  2.1 0.0 copy-start.4
  2.1 0.9 %copy-done.4 = bf16[256,256]{1,0:T(8,128)(2,1)S(1)} copy-done((bf16[256,256]{1,0:T(8,128)(2,1)S(1)}, bf16[256,256]{1,0:T(8,128)(2,1)}, u32[]{:S(2)}) %copy-start.4) | copy-done | bytes 131096
  3.0 4.5 %collective-permute-start = (bf16[256,512]{1,0:T(8,128)(2,1)S(1)}, bf16[256,512]{1,0:T(8,128)(2,1)S(1)}, u32[]{:S(2)}, u32[]{:S(2)}) collective-permute-start(bf16[256,512]{1,0:T(8,128)(2,1)S(1)} %join.1.a_ref.kv_ref), channel_id=1, source_target_pairs={{0,8},{4,12},{8,16},{12,20},{16,24},{20,28},{1,9},{5,13},{9,17},{1... | collective-permute-start | bytes 786440 | tf_op jit(solution)/shard_map/ppermute | solution.py:32
  7.5 1.6 %collective-permute-start.2 = (bf16[256,512]{1,0:T(8,128)(2,1)S(1)}, bf16[256,512]{1,0:T(8,128)(2,1)S(1)}, u32[]{:S(2)}, u32[]{:S(2)}) collective-permute-start(bf16[256,512]{1,0:T(8,128)(2,1)S(1)} %join.1.a_ref.kv_ref), channel_id=1, source_target_pairs={{0,4},{4,0},{8,12},{12,8},{16,20},{20,16},{24,28},{28,24},{1,5},{5... | collective-permute-start | bytes 786440 | tf_op jit(solution)/shard_map/ppermute | solution.py:37
  9.1 1.5 %collective-permute-start.6 = (bf16[64,5376]{1,0:T(8,128)(2,1)}, bf16[64,5376]{1,0:T(8,128)(2,1)S(1)}, u32[]{:S(2)}, u32[]{:S(2)}) collective-permute-start(bf16[64,5376]{1,0:T(8,128)(2,1)} %own_ref.1), channel_id=1, source_target_pairs={{0,2},{1,3},{2,0},{3,1},{4,6},{5,7},{6,4},{7,5},{8,10},{9,11},{10,... | collective-permute-start | bytes 2064392 | tf_op jit(solution)/shard_map/ppermute | solution.py:37
  10.6 0.0 copy-start.1
  10.6 0.9 %copy-done.1 = bf16[256,512]{1,0:T(8,128)(2,1)S(1)} copy-done((bf16[256,512]{1,0:T(8,128)(2,1)S(1)}, bf16[256,512]{1,0:T(8,128)(2,1)}, u32[]{:S(2)}) %copy-start.1) | copy-done | bytes 262168
  11.6 2.6 %collective-permute-start.1 = (bf16[256,512]{1,0:T(8,128)(2,1)S(1)}, bf16[256,512]{1,0:T(8,128)(2,1)S(1)}, u32[]{:S(2)}, u32[]{:S(2)}) collective-permute-start(bf16[256,512]{1,0:T(8,128)(2,1)S(1)} %far_sent.1), channel_id=1, source_target_pairs={{0,16},{4,20},{8,24},{12,28},{16,0},{20,4},{24,8},{28,12},{1,17},{... | collective-permute-start | bytes 786440 | tf_op jit(solution)/shard_map/ppermute | solution.py:48
  14.2 0.0 collective-permute-done.3.core_ref
  14.2 0.0 copy-start
  14.2 2.6 %copy-done = bf16[512,5376]{1,0:T(8,128)(2,1)S(1)} copy-done((bf16[512,5376]{1,0:T(8,128)(2,1)S(1)}, bf16[512,5376]{1,0:T(8,128)(2,1)}, u32[]{:S(2)}) %copy-start) | copy-done | bytes 5505048
  16.8 0.0 copy-start.5
  16.8 1.1 %copy-done.5 = bf16[64,5376]{1,0:T(8,128)(2,1)S(1)} copy-done((bf16[64,5376]{1,0:T(8,128)(2,1)S(1)}, bf16[64,5376]{1,0:T(8,128)(2,1)}, u32[]{:S(2)}) %copy-start.5) | copy-done | bytes 688152
  17.9 0.0 slice-start
  17.9 1.9 %near_back.1.near_ref.dn_ref = bf16[128,512]{1,0:T(8,128)(2,1)S(1)} custom-call(bf16[64,5376]{1,0:T(8,128)(2,1)S(1)} %copy-done.5, bf16[64,5376]{1,0:T(8,128)(2,1)S(1)} %collective-permute-done.3.core_ref, bf16[512,5376]{1,0:T(8,128)(2,1)S(1)} %copy-done), custom_call_target="tpu_custom_call" | custom-call | flops 10000000000 | bytes 1 | tf_op jit(solution)/shard_map/near_back/pallas_call | solution.py:300
  19.8 0.0 slice-start.1
  19.8 0.0 collective-permute-done.r1_ref
  19.8 0.0 collective-permute-done.2.p0_ref
  19.8 0.6 collective-permute-start.4
  20.4 5.6 %collective-permute-done.1.a_ref.b_ref.r2_ref.qf_ref = bf16[256,512]{1,0:T(8,128)(2,1)S(1)} collective-permute-done((bf16[256,512]{1,0:T(8,128)(2,1)S(1)}, bf16[256,512]{1,0:T(8,128)(2,1)S(1)}, u32[]{:S(2)}, u32[]{:S(2)}) %collective-permute-start.1) | collective-permute-done | bytes 262176 | tf_op jit(solution)/shard_map/ppermute | solution.py:48
  26.0 0.5 collective-permute-done.6.y_ref
  26.5 0.0 collective-permute-start.7
  26.6 0.0 copy-start.2
  26.6 0.6 collective-permute-start.5
  27.2 0.2 collective-permute-done.4.x1_ref
  27.4 1.2 %collective-permute-done.7.yc_ref = bf16[64,5376]{1,0:T(8,128)(2,1)S(1)} collective-permute-done((bf16[64,5376]{1,0:T(8,128)(2,1)S(1)}, bf16[64,5376]{1,0:T(8,128)(2,1)S(1)}, u32[]{:S(2)}, u32[]{:S(2)}) %collective-permute-start.7) | collective-permute-done | bytes 688160 | tf_op jit(solution)/shard_map/ppermute | solution.py:37
  28.7 0.0 slice-done
  28.7 0.0 slice-done.1
  28.7 1.9 %far_back.1 = (bf16[128,512]{1,0:T(8,128)(2,1)S(1)}, bf16[256,256]{1,0:T(8,128)(2,1)S(1)}) custom-call(bf16[64,5376]{1,0:T(8,128)(2,1)S(1)} %collective-permute-done.6.y_ref, bf16[64,5376]{1,0:T(8,128)(2,1)S(1)} %collective-permute-done.7.yc_ref, bf16[512,5376]{1,0:T(8,128)(2,1)S(1)} %bitcast.1, bf16[128,512]{1,0:T(8,128)(2,1)S(1)} %near_back.1.near_ref.dn_ref), custom_call_target="tpu_custom_call" | custom-call | flops 10000000000 | bytes 1 | tf_op jit(solution)/shard_map/far_back/pallas_call | solution.py:300
  30.6 2.6 %collective-permute-start.8 = (bf16[256,256]{1,0:T(8,128)(2,1)S(1)}, bf16[256,256]{1,0:T(8,128)(2,1)S(1)}, u32[]{:S(2)}, u32[]{:S(2)}) collective-permute-start(bf16[256,256]{1,0:T(8,128)(2,1)S(1)} %get-tuple-element.39), channel_id=1, source_target_pairs={{0,16},{4,20},{8,24},{12,28},{16,0},{20,4},{24,8},{28,12},{1,17},{... | collective-permute-start | bytes 393224 | tf_op jit(solution)/shard_map/ppermute | solution.py:48
  33.2 2.2 %collective-permute-done.5.x2_ref.qx_ref = bf16[256,512]{1,0:T(8,128)(2,1)S(1)} collective-permute-done((bf16[256,512]{1,0:T(8,128)(2,1)S(1)}, bf16[256,512]{1,0:T(8,128)(2,1)S(1)}, u32[]{:S(2)}, u32[]{:S(2)}) %collective-permute-start.5) | collective-permute-done | bytes 262176 | tf_op jit(solution)/shard_map/ppermute | solution.py:37
  35.4 0.0 copy-done.2
  35.4 2.6 %attend.1 = (bf16[256,512]{1,0:T(8,128)(2,1)S(1)}, bf16[2,5,256,512]{3,2,1,0:T(8,128)(2,1)S(1)}, f32[8,512]{1,0:T(8,128)S(1)}, bf16[304,256]{1,0:T(8,128)(2,1)S(1)}) custom-call(bf16[256,512]{1,0:T(8,128)(2,1)S(1)} %copy-done.2, bf16[256,512]{1,0:T(8,128)(2,1)S(1)} %join.1.a_ref.kv_ref, bf16[256,512]{1,0:T(8,128)(2,1)S(1)} %collective-permute-done.r1_ref, ...), custom_call_target="tpu_custom_call" | custom-call | flops 1 | bytes 1 | tf_op jit(solution)/shard_map/attend/pallas_call | solution.py:300
  38.0 0.6 across_grad.1
  38.6 1.6 %project.1 = (bf16[64,5376]{1,0:T(8,128)(2,1)S(1)}, bf16[64,5376]{1,0:T(8,128)(2,1)S(1)}, bf16[64,5376]{1,0:T(8,128)(2,1)S(1)}, bf16[64,5376]{1,0:T(8,128)(2,1)S(1)}) custom-call(bf16[256,512]{1,0:T(8,128)(2,1)S(1)} %get-tuple-element.34.o_ref, bf16[512,5376]{1,0:T(8,128)(2,1)S(1)} %bitcast.1), custom_call_target="tpu_custom_call" | custom-call | flops 1 | bytes 1 | tf_op jit(solution)/shard_map/project/pallas_call | solution.py:300
  40.2 0.0 collective-permute-done.8.a_ref.af_ref
  40.2 0.1 collective-permute-start.9
  40.3 0.6 collective-permute-start.14
  40.9 2.6 %collective-permute-start.12 = (bf16[304,256]{1,0:T(8,128)(2,1)S(1)}, bf16[304,256]{1,0:T(8,128)(2,1)S(1)}, u32[]{:S(2)}, u32[]{:S(2)}) collective-permute-start(bf16[304,256]{1,0:T(8,128)(2,1)S(1)} %get-tuple-element.45), channel_id=1, source_target_pairs={{0,16},{4,20},{8,24},{12,28},{16,0},{20,4},{24,8},{28,12},{1,17},{... | collective-permute-start | bytes 466952 | tf_op jit(solution)/shard_map/ppermute | solution.py:48
  43.5 0.0 collective-permute-done.9.refs_1_
  43.5 0.2 far_sum.1
  43.6 1.6 %collective-permute-start.11 = (bf16[64,5376]{1,0:T(8,128)(2,1)S(1)}, bf16[64,5376]{1,0:T(8,128)(2,1)S(1)}, u32[]{:S(2)}, u32[]{:S(2)}) collective-permute-start(bf16[64,5376]{1,0:T(8,128)(2,1)S(1)} %far_sum.1), channel_id=1, source_target_pairs={{0,2},{1,3},{2,0},{3,1},{4,6},{5,7},{6,4},{7,5},{8,10},{9,11},{10,... | collective-permute-start | bytes 2064392 | tf_op jit(solution)/shard_map/ppermute | solution.py:37
  45.2 0.0 collective-permute-start.10
  45.2 3.4 %attend_grad.1 = (bf16[256,512]{1,0:T(8,128)(2,1)}, f32[256,512]{1,0:T(8,128)S(1)}, bf16[256,512]{1,0:T(8,128)(2,1)S(1)}, bf16[256,512]{1,0:T(8,128)(2,1)S(1)}) custom-call(bf16[256,512]{1,0:T(8,128)(2,1)S(1)} %copy-done.2, bf16[256,512]{1,0:T(8,128)(2,1)S(1)} %join.1.a_ref.kv_ref, bf16[256,512]{1,0:T(8,128)(2,1)S(1)} %collective-permute-done.r1_ref, ...), custom_call_target="tpu_custom_call" | custom-call | flops 10000000000 | bytes 1 | tf_op jit(solution)/shard_map/attend_grad/pallas_call | solution.py:300
  48.6 2.6 %collective-permute-done.12.b_ref.bf_ref = bf16[304,256]{1,0:T(8,128)(2,1)S(1)} collective-permute-done((bf16[304,256]{1,0:T(8,128)(2,1)S(1)}, bf16[304,256]{1,0:T(8,128)(2,1)S(1)}, u32[]{:S(2)}, u32[]{:S(2)}) %collective-permute-start.12) | collective-permute-done | bytes 155680 | tf_op jit(solution)/shard_map/ppermute | solution.py:48
  51.2 1.6 %collective-permute-start.13 = (bf16[304,512]{1,0:T(8,128)(2,1)S(1)}, bf16[304,512]{1,0:T(8,128)(2,1)S(1)}, u32[]{:S(2)}, u32[]{:S(2)}) collective-permute-start(bf16[304,512]{1,0:T(8,128)(2,1)S(1)} %pair.1), channel_id=1, source_target_pairs={{0,4},{4,0},{8,12},{12,8},{16,20},{20,16},{24,28},{28,24},{1,5},{5... | collective-permute-start | bytes 933896 | tf_op jit(solution)/shard_map/ppermute | solution.py:37
  52.8 0.0 collective-permute-done.14.refs_1_
  52.8 0.1 hop_sum.1
  52.9 1.3 %collective-permute-start.15 = (bf16[256,512]{1,0:T(8,128)(2,1)S(1)}, bf16[256,512]{1,0:T(8,128)(2,1)S(1)}, u32[]{:S(2)}, u32[]{:S(2)}) collective-permute-start(bf16[256,512]{1,0:T(8,128)(2,1)S(1)} %hop_sum.1), channel_id=1, source_target_pairs={{8,0},{12,4},{16,8},{20,12},{24,16},{28,20},{9,1},{13,5},{17,9},{2... | collective-permute-start | bytes 786440 | tf_op jit(solution)/shard_map/ppermute | solution.py:32
  54.2 5.7 %collective-permute-done.13.px_ref.pair_ref = bf16[304,512]{1,0:T(8,128)(2,1)S(1)} collective-permute-done((bf16[304,512]{1,0:T(8,128)(2,1)S(1)}, bf16[304,512]{1,0:T(8,128)(2,1)S(1)}, u32[]{:S(2)}, u32[]{:S(2)}) %collective-permute-start.13) | collective-permute-done | bytes 311328 | tf_op jit(solution)/shard_map/ppermute | solution.py:37
  59.9 1.5 %far_grad.1.far_ref = f32[256,512]{1,0:T(8,128)S(1)} custom-call(bf16[256,512]{1,0:T(8,128)(2,1)S(1)} %join.1.a_ref.kv_ref, bf16[256,512]{1,0:T(8,128)(2,1)S(1)} %collective-permute-done.1.a_ref.b_ref.r2_ref.qf_ref, bf16[256,256]{1,0:T(8,128)(2,1)S(1)} %collective-permute-done.8.a_ref.af_ref, bf16[304,256]{1,0:T(8,128)(2,1)S(1)} %collective-permute-done.12.b_ref.bf_ref, ...), custom_call_target="tpu_custom_call" | custom-call | flops 100000000 | bytes 1 | tf_op jit(solution)/shard_map/far_grad/pallas_call | solution.py:300
  61.4 0.7 %collective-permute-done.15.hop_ref = bf16[256,512]{1,0:T(8,128)(2,1)S(1)} collective-permute-done((bf16[256,512]{1,0:T(8,128)(2,1)S(1)}, bf16[256,512]{1,0:T(8,128)(2,1)S(1)}, u32[]{:S(2)}, u32[]{:S(2)}) %collective-permute-start.15) | collective-permute-done | bytes 262176 | tf_op jit(solution)/shard_map/ppermute | solution.py:32
  62.0 0.8 %finish.1 = (bf16[256,256]{1,0:T(8,128)(2,1)}, bf16[256,256]{1,0:T(8,128)(2,1)}) custom-call(f32[256,512]{1,0:T(8,128)S(1)} %get-tuple-element.44.own_ref, f32[256,512]{1,0:T(8,128)S(1)} %far_grad.1.far_ref, bf16[256,512]{1,0:T(8,128)(2,1)S(1)} %collective-permute-done.15.hop_ref, bf16[304,512]{1,0:T(8,128)(2,1)S(1)} %collective-permute-done.13.px_ref.pair_ref), custom_call_target="tpu_custom_call" | custom-call | flops 1 | bytes 1 | tf_op jit(solution)/shard_map/finish/pallas_call | solution.py:300
  62.8 0.0 collective-permute-done.10.refs_1_
  62.8 0.0 collective-permute-done.11.refs_2_
  62.8 1.1 %projected.1 = bf16[64,5376]{1,0:T(8,128)(2,1)} custom-call(bf16[64,5376]{1,0:T(8,128)(2,1)S(1)} %get-tuple-element.35.refs_0_, bf16[64,5376]{1,0:T(8,128)(2,1)S(1)} %collective-permute-done.10.refs_1_, bf16[64,5376]{1,0:T(8,128)(2,1)S(1)} %collective-permute-done.11.refs_2_), custom_call_target="tpu_custom_call" | custom-call | flops 10000000000 | bytes 1 | tf_op jit(solution)/shard_map/projected/pallas_call | solution.py:300
  (5 shorter events, 0.1 us)
Async XLA Ops:
  0.6 13.6 %collective-permute-start.3 = (bf16[64,5376]{1,0:T(8,128)(2,1)}, bf16[64,5376]{1,0:T(8,128)(2,1)S(1)}, u32[]{:S(2)}, u32[]{:S(2)}) collective-permute-start(bf16[64,5376]{1,0:T(8,128)(2,1)} %own_ref.1), channel_id=1, source_target_pairs={{0,1},{1,0},{2,3},{3,2},{4,5},{5,4},{6,7},{7,6},{8,9},{9,8},{10,11... | collective-permute-start | bytes 2064392 | tf_op jit(solution)/shard_map/ppermute | solution.py:37
  1.1 0.9 %copy-start.3 = (bf16[256,256]{1,0:T(8,128)(2,1)S(1)}, bf16[256,256]{1,0:T(8,128)(2,1)}, u32[]{:S(2)}) copy-start(bf16[256,256]{1,0:T(8,128)(2,1)} %k_ref.1) | copy-start | bytes 393220
  2.1 0.9 %copy-start.4 = (bf16[256,256]{1,0:T(8,128)(2,1)S(1)}, bf16[256,256]{1,0:T(8,128)(2,1)}, u32[]{:S(2)}) copy-start(bf16[256,256]{1,0:T(8,128)(2,1)} %v_ref.1) | copy-start | bytes 393220
  3.0 16.8 %collective-permute-start = (bf16[256,512]{1,0:T(8,128)(2,1)S(1)}, bf16[256,512]{1,0:T(8,128)(2,1)S(1)}, u32[]{:S(2)}, u32[]{:S(2)}) collective-permute-start(bf16[256,512]{1,0:T(8,128)(2,1)S(1)} %join.1.a_ref.kv_ref), channel_id=1, source_target_pairs={{0,8},{4,12},{8,16},{12,20},{16,24},{20,28},{1,9},{5,13},{9,17},{1... | collective-permute-start | bytes 786440 | tf_op jit(solution)/shard_map/ppermute | solution.py:32
  7.5 12.3 %collective-permute-start.2 = (bf16[256,512]{1,0:T(8,128)(2,1)S(1)}, bf16[256,512]{1,0:T(8,128)(2,1)S(1)}, u32[]{:S(2)}, u32[]{:S(2)}) collective-permute-start(bf16[256,512]{1,0:T(8,128)(2,1)S(1)} %join.1.a_ref.kv_ref), channel_id=1, source_target_pairs={{0,4},{4,0},{8,12},{12,8},{16,20},{20,16},{24,28},{28,24},{1,5},{5... | collective-permute-start | bytes 786440 | tf_op jit(solution)/shard_map/ppermute | solution.py:37
  9.1 17.5 %collective-permute-start.6 = (bf16[64,5376]{1,0:T(8,128)(2,1)}, bf16[64,5376]{1,0:T(8,128)(2,1)S(1)}, u32[]{:S(2)}, u32[]{:S(2)}) collective-permute-start(bf16[64,5376]{1,0:T(8,128)(2,1)} %own_ref.1), channel_id=1, source_target_pairs={{0,2},{1,3},{2,0},{3,1},{4,6},{5,7},{6,4},{7,5},{8,10},{9,11},{10,... | collective-permute-start | bytes 2064392 | tf_op jit(solution)/shard_map/ppermute | solution.py:37
  10.6 0.9 %copy-start.1 = (bf16[256,512]{1,0:T(8,128)(2,1)S(1)}, bf16[256,512]{1,0:T(8,128)(2,1)}, u32[]{:S(2)}) copy-start(bf16[256,512]{1,0:T(8,128)(2,1)} %q_ref.5) | copy-start | bytes 786436
  11.6 14.4 %collective-permute-start.1 = (bf16[256,512]{1,0:T(8,128)(2,1)S(1)}, bf16[256,512]{1,0:T(8,128)(2,1)S(1)}, u32[]{:S(2)}, u32[]{:S(2)}) collective-permute-start(bf16[256,512]{1,0:T(8,128)(2,1)S(1)} %far_sent.1), channel_id=1, source_target_pairs={{0,16},{4,20},{8,24},{12,28},{16,0},{20,4},{24,8},{28,12},{1,17},{... | collective-permute-start | bytes 786440 | tf_op jit(solution)/shard_map/ppermute | solution.py:48
  14.2 2.6 %copy-start = (bf16[512,5376]{1,0:T(8,128)(2,1)S(1)}, bf16[512,5376]{1,0:T(8,128)(2,1)}, u32[]{:S(2)}) copy-start(bf16[512,5376]{1,0:T(8,128)(2,1)} %w_ref.5) | copy-start | bytes 16515076
  16.8 1.1 %copy-start.5 = (bf16[64,5376]{1,0:T(8,128)(2,1)S(1)}, bf16[64,5376]{1,0:T(8,128)(2,1)}, u32[]{:S(2)}) copy-start(bf16[64,5376]{1,0:T(8,128)(2,1)} %own_ref.1) | copy-start | bytes 2064388
  17.9 10.8 %slice-start = ((s8[5505024]{0:T(1024)(128)(4,1)}), s8[4194304]{0:T(1024)(128)(4,1)S(1)}, s32[]{:S(2)}) async-start(s8[5505024]{0:T(1024)(128)(4,1)} %bitcast), calls=%async_computation | async-start | bytes 8388608
  19.8 8.9 %slice-start.1 = ((s8[5505024]{0:T(1024)(128)(4,1)}), s8[1310720]{0:T(1024)(128)(4,1)S(1)}, s32[]{:S(2)}) async-start(s8[5505024]{0:T(1024)(128)(4,1)} %bitcast), calls=%async_computation.1 | async-start | bytes 2621440
  19.8 7.6 %collective-permute-start.4 = (bf16[256,512]{1,0:T(8,128)(2,1)S(1)}, bf16[256,512]{1,0:T(8,128)(2,1)S(1)}, u32[]{:S(2)}, u32[]{:S(2)}) collective-permute-start(bf16[256,512]{1,0:T(8,128)(2,1)S(1)} %collective-permute-done.r1_ref), channel_id=1, source_target_pairs={{0,4},{4,0},{8,12},{12,8},{16,20},{20,16},{24,28},{28,24},{1,5},{5... | collective-permute-start | bytes 786440 | tf_op jit(solution)/shard_map/ppermute | solution.py:37
  26.5 2.1 %collective-permute-start.7 = (bf16[64,5376]{1,0:T(8,128)(2,1)S(1)}, bf16[64,5376]{1,0:T(8,128)(2,1)S(1)}, u32[]{:S(2)}, u32[]{:S(2)}) collective-permute-start(bf16[64,5376]{1,0:T(8,128)(2,1)S(1)} %collective-permute-done.6.y_ref), channel_id=1, source_target_pairs={{0,1},{1,0},{2,3},{3,2},{4,5},{5,4},{6,7},{7,6},{8,9},{9,8},{10,11... | collective-permute-start | bytes 2064392 | tf_op jit(solution)/shard_map/ppermute | solution.py:37
  26.6 8.8 %copy-start.2 = (bf16[256,512]{1,0:T(8,128)(2,1)S(1)}, bf16[256,512]{1,0:T(8,128)(2,1)}, u32[]{:S(2)}) copy-start(bf16[256,512]{1,0:T(8,128)(2,1)} %q_ref.5) | copy-start | bytes 786436
  26.6 8.8 %collective-permute-start.5 = (bf16[256,512]{1,0:T(8,128)(2,1)S(1)}, bf16[256,512]{1,0:T(8,128)(2,1)S(1)}, u32[]{:S(2)}, u32[]{:S(2)}) collective-permute-start(bf16[256,512]{1,0:T(8,128)(2,1)S(1)} %pick.1), channel_id=1, source_target_pairs={{0,4},{4,0},{8,12},{12,8},{16,20},{20,16},{24,28},{28,24},{1,5},{5... | collective-permute-start | bytes 786440 | tf_op jit(solution)/shard_map/ppermute | solution.py:37
  30.6 9.6 %collective-permute-start.8 = (bf16[256,256]{1,0:T(8,128)(2,1)S(1)}, bf16[256,256]{1,0:T(8,128)(2,1)S(1)}, u32[]{:S(2)}, u32[]{:S(2)}) collective-permute-start(bf16[256,256]{1,0:T(8,128)(2,1)S(1)} %get-tuple-element.39), channel_id=1, source_target_pairs={{0,16},{4,20},{8,24},{12,28},{16,0},{20,4},{24,8},{28,12},{1,17},{... | collective-permute-start | bytes 393224 | tf_op jit(solution)/shard_map/ppermute | solution.py:48
  40.2 3.3 %collective-permute-start.9 = (bf16[64,5376]{1,0:T(8,128)(2,1)S(1)}, bf16[64,5376]{1,0:T(8,128)(2,1)S(1)}, u32[]{:S(2)}, u32[]{:S(2)}) collective-permute-start(bf16[64,5376]{1,0:T(8,128)(2,1)S(1)} %get-tuple-element.40), channel_id=1, source_target_pairs={{0,1},{1,0},{2,3},{3,2},{4,5},{5,4},{6,7},{7,6},{8,9},{9,8},{10,11... | collective-permute-start | bytes 2064392 | tf_op jit(solution)/shard_map/ppermute | solution.py:37
  40.3 12.5 %collective-permute-start.14 = (bf16[256,512]{1,0:T(8,128)(2,1)S(1)}, bf16[256,512]{1,0:T(8,128)(2,1)S(1)}, u32[]{:S(2)}, u32[]{:S(2)}) collective-permute-start(bf16[256,512]{1,0:T(8,128)(2,1)S(1)} %across_grad.1), channel_id=1, source_target_pairs={{0,4},{4,0},{8,12},{12,8},{16,20},{20,16},{24,28},{28,24},{1,5},{5... | collective-permute-start | bytes 786440 | tf_op jit(solution)/shard_map/ppermute | solution.py:37
  40.9 10.3 %collective-permute-start.12 = (bf16[304,256]{1,0:T(8,128)(2,1)S(1)}, bf16[304,256]{1,0:T(8,128)(2,1)S(1)}, u32[]{:S(2)}, u32[]{:S(2)}) collective-permute-start(bf16[304,256]{1,0:T(8,128)(2,1)S(1)} %get-tuple-element.45), channel_id=1, source_target_pairs={{0,16},{4,20},{8,24},{12,28},{16,0},{20,4},{24,8},{28,12},{1,17},{... | collective-permute-start | bytes 466952 | tf_op jit(solution)/shard_map/ppermute | solution.py:48
  43.6 19.2 %collective-permute-start.11 = (bf16[64,5376]{1,0:T(8,128)(2,1)S(1)}, bf16[64,5376]{1,0:T(8,128)(2,1)S(1)}, u32[]{:S(2)}, u32[]{:S(2)}) collective-permute-start(bf16[64,5376]{1,0:T(8,128)(2,1)S(1)} %far_sum.1), channel_id=1, source_target_pairs={{0,2},{1,3},{2,0},{3,1},{4,6},{5,7},{6,4},{7,5},{8,10},{9,11},{10,... | collective-permute-start | bytes 2064392 | tf_op jit(solution)/shard_map/ppermute | solution.py:37
  45.2 17.6 %collective-permute-start.10 = (bf16[64,5376]{1,0:T(8,128)(2,1)S(1)}, bf16[64,5376]{1,0:T(8,128)(2,1)S(1)}, u32[]{:S(2)}, u32[]{:S(2)}) collective-permute-start(bf16[64,5376]{1,0:T(8,128)(2,1)S(1)} %get-tuple-element.41), channel_id=1, source_target_pairs={{0,1},{1,0},{2,3},{3,2},{4,5},{5,4},{6,7},{7,6},{8,9},{9,8},{10,11... | collective-permute-start | bytes 2064392 | tf_op jit(solution)/shard_map/ppermute | solution.py:37
  51.2 8.7 %collective-permute-start.13 = (bf16[304,512]{1,0:T(8,128)(2,1)S(1)}, bf16[304,512]{1,0:T(8,128)(2,1)S(1)}, u32[]{:S(2)}, u32[]{:S(2)}) collective-permute-start(bf16[304,512]{1,0:T(8,128)(2,1)S(1)} %pair.1), channel_id=1, source_target_pairs={{0,4},{4,0},{8,12},{12,8},{16,20},{20,16},{24,28},{28,24},{1,5},{5... | collective-permute-start | bytes 933896 | tf_op jit(solution)/shard_map/ppermute | solution.py:37
  52.9 9.2 %collective-permute-start.15 = (bf16[256,512]{1,0:T(8,128)(2,1)S(1)}, bf16[256,512]{1,0:T(8,128)(2,1)S(1)}, u32[]{:S(2)}, u32[]{:S(2)}) collective-permute-start(bf16[256,512]{1,0:T(8,128)(2,1)S(1)} %hop_sum.1), channel_id=1, source_target_pairs={{8,0},{12,4},{16,8},{20,12},{24,16},{28,20},{9,1},{13,5},{17,9},{2... | collective-permute-start | bytes 786440 | tf_op jit(solution)/shard_map/ppermute | solution.py:32

commit v8 on v7

--- a/solution.py
+++ b/solution.py
@@ -99,43 +99,66 @@
     return lax.rem(lax.div(seq, FAR), 2) == 0
 
 
-def forward_kernel(q_ref, kv_ref, r1_ref, r2_ref, x1_ref, p0_ref, x2_ref, dn_ref, df_ref,
+def early_kernel(q_ref, kv_ref, r1_ref, r2_ref, x1_ref, e_ref, m_ref, part_ref):
+    seq, head = lax.axis_index("seq"), lax.axis_index("head")
+    tok = q_ref.shape[0]
+    kv_cols = kv_ref.shape[1] // 2
+    q_rel = own_order(q_ref, head)
+    causal = causal_mask(tok, head)
+    near = jnp.where(seq >= 2, 0.0, NEG).astype(F32)
+    far = jnp.where(seq >= FAR, 0.0, NEG).astype(F32)
+    biases = [None, near, far, near]
+    scale = LOGIT_SCALE * LOG2E
+    marks = []
+    for g in range(kv_cols // HEAD_SIZE):
+        kc, vc = columns(kv_cols, g)
+        qg = stacked(q_rel, g)
+        blocks = (kv_ref, r1_ref, r2_ref, x1_ref)
+        scores = [dot(ref[:, kc], qg, 1, 1) for ref in blocks]
+        scores[0] = jnp.where(causal, scores[0], NEG)
+        scores[2] = jnp.where(causal, NEG, scores[2])
+        tops = [jnp.max(sb, axis=0, keepdims=True) for sb in scores]
+        tops = [t if b is None else t + b for t, b in zip(tops, biases)]
+        top = jnp.maximum(jnp.maximum(tops[0], tops[1]), jnp.maximum(tops[2], tops[3])) * scale
+        total = jnp.zeros_like(top)
+        part = jnp.zeros((HEAD_SIZE, 2 * tok), F32)
+        for b, bias in enumerate(biases):
+            eb = jnp.exp2(scores[b] * scale - (top if bias is None else top - bias))
+            e_ref[g, b] = eb
+            total = total + jnp.sum(eb, axis=0, keepdims=True)
+            part = part + dot(blocks[b][:, vc], eb.astype(BF16), 0, 0)
+        part_ref[g] = part
+        marks += [top, total]
+    spare = jnp.zeros((m_ref.shape[0] - len(marks), 2 * tok), F32)
+    m_ref[...] = jnp.concatenate(marks + [spare], 0)
+
+
+def forward_kernel(q_ref, p0_ref, x2_ref, e_ref, m_ref, part_ref, dn_ref, df_ref,
                    o_ref, p_ref, stat_ref, second_ref):
     seq, head = lax.axis_index("seq"), lax.axis_index("head")
     odd = lax.rem(seq, 2) == 1
     tok = q_ref.shape[0]
-    kv_cols = kv_ref.shape[1] // 2
+    kv_cols = p0_ref.shape[1] // 2
     q_rel = own_order(q_ref, head)
     d_rel = jnp.concatenate([dn_ref[...], df_ref[...]], 0)
-    causal = causal_mask(tok, head)
-    near = jnp.where(seq >= 2, 0.0, NEG).astype(F32)
-    far = jnp.where(seq >= 4, 0.0, NEG).astype(F32)
-    mixed = jnp.where(jnp.logical_or(odd, seq >= 4), 0.0, NEG).astype(F32)
-    biases = [None, near, far, near, mixed]
+    bias = jnp.where(jnp.logical_or(odd, seq >= FAR), 0.0, NEG).astype(F32)
     scale = LOGIT_SCALE * LOG2E
     stats = []
     for g in range(kv_cols // HEAD_SIZE):
         kc, vc = columns(kv_cols, g)
-        qg = stacked(q_rel, g)
-        blocks = (kv_ref, r1_ref, r2_ref, x1_ref, p0_ref, x2_ref)
-        key_blocks, value_blocks = window(*blocks, odd, kc), window(*blocks, odd, vc)
-        scores = [dot(kb, qg, 1, 1) for kb in key_blocks]
-        scores[0] = jnp.where(causal, scores[0], NEG)
-        scores[2] = jnp.where(causal, NEG, scores[2])
-        tops = [jnp.max(sb, axis=0, keepdims=True) for sb in scores]
-        tops = [t if b is None else t + b for t, b in zip(tops, biases)]
-        top = tops[0]
-        for t in tops[1:]:
-            top = jnp.maximum(top, t)
-        top = top * scale
-        probs = [jnp.exp2(sb * scale - (top if b is None else top - b)) for sb, b in zip(scores, biases)]
-        total = sum(jnp.sum(pb, axis=0, keepdims=True) for pb in probs)
+        score = dot(jnp.where(odd, p0_ref[:, kc], x2_ref[:, kc]), stacked(q_rel, g), 1, 1)
+        top_early = m_ref[2 * g : 2 * g + 1, :]
+        top = jnp.maximum(top_early, (jnp.max(score, axis=0, keepdims=True) + bias) * scale)
+        last = jnp.exp2(score * scale - (top - bias))
+        shrink = jnp.exp2(top_early - top)
+        total = m_ref[2 * g + 1 : 2 * g + 2, :] * shrink + jnp.sum(last, axis=0, keepdims=True)
         inv = 1.0 / total
-        out = jnp.zeros((HEAD_SIZE, 2 * tok), F32)
-        for b in range(5):
-            pb = (probs[b] * inv).astype(BF16)
-            p_ref[g, b] = pb
-            out = out + dot(value_blocks[b], pb, 0, 0)
+        shrink = shrink * inv
+        last = (last * inv).astype(BF16)
+        p_ref[g, 4] = last
+        out = part_ref[g] * shrink + dot(jnp.where(odd, p0_ref[:, vc], x2_ref[:, vc]), last, 0, 0)
+        for b in range(4):
+            p_ref[g, b] = (e_ref[g, b] * shrink).astype(BF16)
         out = out.astype(BF16)
         grad = stacked(d_rel, g)
         delta = jnp.sum(grad.astype(F32).T * out.astype(F32), axis=0, keepdims=True)
@@ -279,9 +302,11 @@
     refs[-1][...] = total.astype(refs[-1].dtype)
 
 
-def finish_kernel(own_ref, far_ref, hop_ref, pair_ref, dk_ref, dv_ref):
+def closing_kernel(own_ref, far_ref, hop_ref, pair_ref, near_ref, core_ref, y_ref, dk_ref, dv_ref, proj_ref):
     odd = lax.rem(lax.axis_index("seq"), 2) == 1
-    total = own_ref[...] + far_ref[...] + hop_ref[...].astype(F32) + jnp.where(odd, 0.0, pair_ref[: own_ref.shape[0], :].astype(F32))
+    proj_ref[...] = (near_ref[...].astype(F32) + core_ref[...].astype(F32) + y_ref[...].astype(F32)).astype(BF16)
+    kept = jnp.where(odd, 0.0, pair_ref[: own_ref.shape[0], :].astype(F32))
+    total = own_ref[...] + far_ref[...] + hop_ref[...].astype(F32) + kept
     kv_cols = dk_ref.shape[1]
     dk_ref[...] = total[:, :kv_cols].astype(BF16)
     dv_ref[...] = total[:, kv_cols:].astype(BF16)
@@ -332,17 +357,29 @@
         return far_swapped(*[lambda: value] * 2)[1]
 
     far_first = down(sent_first)
+    table = jax.ShapeDtypeStruct((8 * pl.cdiv(2 * kv_heads, 8), 2 * tok), F32)
+    early = call(
+        early_kernel,
+        "attend_early",
+        (
+            jax.ShapeDtypeStruct((kv_heads, 4, tok, 2 * tok), F32),
+            table,
+            jax.ShapeDtypeStruct((kv_heads, HEAD_SIZE, 2 * tok), F32),
+        ),
+        [],
+        queries, kv, r1, r2, x1,
+    )
     attended, probs, stats, sent_second = call(
         forward_kernel,
         "attend",
         (
             jax.ShapeDtypeStruct((tok, q_cols), BF16),
             jax.ShapeDtypeStruct((kv_heads, 5, tok, 2 * tok), BF16),
-            jax.ShapeDtypeStruct((8 * pl.cdiv(2 * kv_heads, 8), 2 * tok), F32),
+            table,
             second,
         ),
         [],
-        queries, kv, r1, r2, x1, p0, x2, grad_near, grad_far,
+        queries, p0, x2, *early, grad_near, grad_far,
     )
     t_x = call(across_kernel, "across_grad", block, [], queries, x1, probs, stats, grad_near, grad_far)
     d1 = swapped(t_x, "seq", 1)
@@ -370,8 +407,9 @@
                  kv, q_far, far_first, far_second, x2, pair, cost=MEDIUM)
 
     narrow = jax.ShapeDtypeStruct(keys.shape, BF16)
-    key_gradient, value_gradient = call(finish_kernel, "finish", (narrow, narrow), [], t_own, t_far, e1, pair)
-    projected = call(sum_kernel, "projected", rows, [], near_own, from_core, from_y, cost=LARGE)
+    key_gradient, value_gradient, projected = call(
+        closing_kernel, "closing", (narrow, narrow, rows), [], t_own, t_far, e1, pair, near_own, from_core, from_y
+    )
     return (projected, query_gradient, key_gradient, value_gradient)
 
 

time: 64.2 us -> 63.3 us (0.986)
  starting transfers between devices: 22.3 us -> 21.5 us
    ppermute x11, waiting for transfers between devices: 9.92 us -> 7.95 us  [swapped(): return lax.ppermute(value, axis, [(i, i ^ bit) for i in range(count)])]
    ppermute x3, waiting for transfers between devices: 8.26 us -> 9.95 us  [far_swapped(): lax.ppermute(lower() if lower is upper else jnp.where(side == r, lower(),...]
    ppermute x2, starting transfers between devices: 5.8 us -> 4.78 us  [shifted(): lax.ppermute(value, 'seq', [(i, i + steps) for i in range(first, last)])]
    ppermute x11, starting transfers between devices: 8.61 us -> 9.55 us  [swapped(): return lax.ppermute(value, axis, [(i, i ^ bit) for i in range(count)])]
    ppermute x3, starting transfers between devices: 7.87 us -> 7.13 us  [far_swapped(): lax.ppermute(lower() if lower is upper else jnp.where(side == r, lower(),...]
  transfers between devices with their start and end apart: 16 -> 16, of which waited for: 8 -> 9; matrix products, arithmetic and copies ran while one was open for 0% -> 0% of each run, Pallas kernels for 23% -> 23%
where the time goes in v8:
time: 63.3 us; the launch traced here: 63 us
  starting transfers between devices  21.5 us (34%)
  waiting for transfers between devices  18.5 us (29%)
  Pallas kernels  15.8 us (25%)
  local copies, waits for them, and re-layouts  6.43 us (10%)
  between operations  0.77 us (1%)
    pallas_call x15, Pallas kernels, call(): pl.pallas_call(kernel, out_shape=outs, in_specs=[VMEM] * len(operands), o...  15.8 us
    ppermute x3, waiting for transfers between devices, far_swapped(): lax.ppermute(lower() if lower is upper else jnp.where(side == r, lower(),...  9.95 us
    ppermute x11, starting transfers between devices, swapped(): return lax.ppermute(value, axis, [(i, i ^ bit) for i in range(count)])  9.55 us
    ppermute x11, waiting for transfers between devices, swapped(): return lax.ppermute(value, axis, [(i, i ^ bit) for i in range(count)])  7.95 us
    ppermute x3, starting transfers between devices, far_swapped(): lax.ppermute(lower() if lower is upper else jnp.where(side == r, lower(),...  7.13 us
    unnamed x16, local copies, waits for them, and re-layouts  6.43 us
    ppermute x2, starting transfers between devices, shifted(): lax.ppermute(value, 'seq', [(i, i + steps) for i in range(first, last)])  4.78 us
  transfers between devices with their start and end apart: 16, of which 9 were waited for; matrix products, arithmetic and copies ran while one was open for 0% of the time, Pallas kernels for 23%

profile of v8, /device:TPU:0, one launch (start us, length us, event | category | flops | bytes accessed | tf_op | source)
XLA Modules:
  0.0 63.0 jit_solution(14184241439771368747)
XLA Ops:
  0.6 0.5 collective-permute-start.3
  1.1 0.0 copy-start.3
  1.2 0.9 %copy-done.3 = bf16[256,256]{1,0:T(8,128)(2,1)S(1)} copy-done((bf16[256,256]{1,0:T(8,128)(2,1)S(1)}, bf16[256,256]{1,0:T(8,128)(2,1)}, u32[]{:S(2)}) %copy-start.3) | copy-done | bytes 131096
  2.1 0.0 copy-start.4
  2.1 0.9 %copy-done.4 = bf16[256,256]{1,0:T(8,128)(2,1)S(1)} copy-done((bf16[256,256]{1,0:T(8,128)(2,1)S(1)}, bf16[256,256]{1,0:T(8,128)(2,1)}, u32[]{:S(2)}) %copy-start.4) | copy-done | bytes 131096
  3.0 2.6 %collective-permute-start.2 = (bf16[256,512]{1,0:T(8,128)(2,1)S(1)}, bf16[256,512]{1,0:T(8,128)(2,1)S(1)}, u32[]{:S(2)}, u32[]{:S(2)}) collective-permute-start(bf16[256,512]{1,0:T(8,128)(2,1)S(1)} %join.1.a_ref.kv_ref), channel_id=1, source_target_pairs={{0,4},{4,0},{8,12},{12,8},{16,20},{20,16},{24,28},{28,24},{1,5},{5... | collective-permute-start | bytes 786440 | tf_op jit(solution)/shard_map/ppermute | solution.py:37
  5.5 3.5 %collective-permute-start = (bf16[256,512]{1,0:T(8,128)(2,1)S(1)}, bf16[256,512]{1,0:T(8,128)(2,1)S(1)}, u32[]{:S(2)}, u32[]{:S(2)}) collective-permute-start(bf16[256,512]{1,0:T(8,128)(2,1)S(1)} %join.1.a_ref.kv_ref), channel_id=1, source_target_pairs={{0,8},{4,12},{8,16},{12,20},{16,24},{20,28},{1,9},{5,13},{9,17},{1... | collective-permute-start | bytes 786440 | tf_op jit(solution)/shard_map/ppermute | solution.py:32
  9.0 1.6 %collective-permute-start.6 = (bf16[64,5376]{1,0:T(8,128)(2,1)}, bf16[64,5376]{1,0:T(8,128)(2,1)S(1)}, u32[]{:S(2)}, u32[]{:S(2)}) collective-permute-start(bf16[64,5376]{1,0:T(8,128)(2,1)} %own_ref.1), channel_id=1, source_target_pairs={{0,2},{1,3},{2,0},{3,1},{4,6},{5,7},{6,4},{7,5},{8,10},{9,11},{10,... | collective-permute-start | bytes 2064392 | tf_op jit(solution)/shard_map/ppermute | solution.py:37
  10.6 0.0 copy-start.1
  10.6 0.9 %copy-done.1 = bf16[256,512]{1,0:T(8,128)(2,1)S(1)} copy-done((bf16[256,512]{1,0:T(8,128)(2,1)S(1)}, bf16[256,512]{1,0:T(8,128)(2,1)}, u32[]{:S(2)}) %copy-start.1) | copy-done | bytes 262168
  11.6 2.6 %collective-permute-start.1 = (bf16[256,512]{1,0:T(8,128)(2,1)S(1)}, bf16[256,512]{1,0:T(8,128)(2,1)S(1)}, u32[]{:S(2)}, u32[]{:S(2)}) collective-permute-start(bf16[256,512]{1,0:T(8,128)(2,1)S(1)} %far_sent.1), channel_id=1, source_target_pairs={{0,16},{4,20},{8,24},{12,28},{16,0},{20,4},{24,8},{28,12},{1,17},{... | collective-permute-start | bytes 786440 | tf_op jit(solution)/shard_map/ppermute | solution.py:48
  14.3 0.0 collective-permute-done.3.core_ref
  14.3 0.0 copy-start
  14.3 2.6 %copy-done = bf16[512,5376]{1,0:T(8,128)(2,1)S(1)} copy-done((bf16[512,5376]{1,0:T(8,128)(2,1)S(1)}, bf16[512,5376]{1,0:T(8,128)(2,1)}, u32[]{:S(2)}) %copy-start) | copy-done | bytes 5505048
  16.8 0.0 copy-start.5
  16.8 1.1 %copy-done.5 = bf16[64,5376]{1,0:T(8,128)(2,1)S(1)} copy-done((bf16[64,5376]{1,0:T(8,128)(2,1)S(1)}, bf16[64,5376]{1,0:T(8,128)(2,1)}, u32[]{:S(2)}) %copy-start.5) | copy-done | bytes 688152
  17.9 0.0 slice-start
  17.9 1.9 %near_back.1.near_ref.dn_ref = bf16[128,512]{1,0:T(8,128)(2,1)S(1)} custom-call(bf16[64,5376]{1,0:T(8,128)(2,1)S(1)} %copy-done.5, bf16[64,5376]{1,0:T(8,128)(2,1)S(1)} %collective-permute-done.3.core_ref, bf16[512,5376]{1,0:T(8,128)(2,1)S(1)} %copy-done), custom_call_target="tpu_custom_call" | custom-call | flops 10000000000 | bytes 1 | tf_op jit(solution)/shard_map/near_back/pallas_call | solution.py:325
  19.8 0.0 slice-start.1
  19.8 0.0 collective-permute-done.2.p0_ref
  19.8 0.0 collective-permute-done.r1_ref
  19.8 0.6 collective-permute-start.4
  20.4 5.6 %collective-permute-done.1.a_ref.b_ref.r2_ref.qf_ref = bf16[256,512]{1,0:T(8,128)(2,1)S(1)} collective-permute-done((bf16[256,512]{1,0:T(8,128)(2,1)S(1)}, bf16[256,512]{1,0:T(8,128)(2,1)S(1)}, u32[]{:S(2)}, u32[]{:S(2)}) %collective-permute-start.1) | collective-permute-done | bytes 262176 | tf_op jit(solution)/shard_map/ppermute | solution.py:48
  26.1 0.5 collective-permute-done.6.y_ref
  26.6 0.0 collective-permute-start.7
  26.6 0.0 copy-start.2
  26.6 0.6 collective-permute-start.5
  27.2 0.2 collective-permute-done.4.x1_ref
  27.5 1.2 %collective-permute-done.7.yc_ref = bf16[64,5376]{1,0:T(8,128)(2,1)S(1)} collective-permute-done((bf16[64,5376]{1,0:T(8,128)(2,1)S(1)}, bf16[64,5376]{1,0:T(8,128)(2,1)S(1)}, u32[]{:S(2)}, u32[]{:S(2)}) %collective-permute-start.7) | collective-permute-done | bytes 688160 | tf_op jit(solution)/shard_map/ppermute | solution.py:37
  28.7 0.0 slice-done
  28.7 0.0 slice-done.1
  28.7 1.9 %far_back.1 = (bf16[128,512]{1,0:T(8,128)(2,1)S(1)}, bf16[256,256]{1,0:T(8,128)(2,1)S(1)}) custom-call(bf16[64,5376]{1,0:T(8,128)(2,1)S(1)} %collective-permute-done.6.y_ref, bf16[64,5376]{1,0:T(8,128)(2,1)S(1)} %collective-permute-done.7.yc_ref, bf16[512,5376]{1,0:T(8,128)(2,1)S(1)} %bitcast.1, bf16[128,512]{1,0:T(8,128)(2,1)S(1)} %near_back.1.near_ref.dn_ref), custom_call_target="tpu_custom_call" | custom-call | flops 10000000000 | bytes 1 | tf_op jit(solution)/shard_map/far_back/pallas_call | solution.py:325
  30.6 2.6 %collective-permute-start.8 = (bf16[256,256]{1,0:T(8,128)(2,1)S(1)}, bf16[256,256]{1,0:T(8,128)(2,1)S(1)}, u32[]{:S(2)}, u32[]{:S(2)}) collective-permute-start(bf16[256,256]{1,0:T(8,128)(2,1)S(1)} %get-tuple-element.40), channel_id=1, source_target_pairs={{0,16},{4,20},{8,24},{12,28},{16,0},{20,4},{24,8},{28,12},{1,17},{... | collective-permute-start | bytes 393224 | tf_op jit(solution)/shard_map/ppermute | solution.py:48
  33.3 0.0 copy-done.2
  33.3 2.0 %attend_early.1 = (f32[2,4,256,512]{3,2,1,0:T(8,128)S(1)}, f32[8,512]{1,0:T(8,128)S(1)}, f32[2,128,512]{2,1,0:T(8,128)S(1)}) custom-call(bf16[256,512]{1,0:T(8,128)(2,1)S(1)} %copy-done.2, bf16[256,512]{1,0:T(8,128)(2,1)S(1)} %join.1.a_ref.kv_ref, bf16[256,512]{1,0:T(8,128)(2,1)S(1)} %collective-permute-done.r1_ref, ...), custom_call_target="tpu_custom_call" | custom-call | flops 1 | bytes 1 | tf_op jit(solution)/shard_map/attend_early/pallas_call | solution.py:325
  35.3 0.1 collective-permute-done.5.x2_ref.qx_ref
  35.4 1.4 %attend.1 = (bf16[256,512]{1,0:T(8,128)(2,1)S(1)}, bf16[2,5,256,512]{3,2,1,0:T(8,128)(2,1)S(1)}, f32[8,512]{1,0:T(8,128)S(1)}, bf16[304,256]{1,0:T(8,128)(2,1)S(1)}) custom-call(bf16[256,512]{1,0:T(8,128)(2,1)S(1)} %copy-done.2, bf16[256,512]{1,0:T(8,128)(2,1)S(1)} %collective-permute-done.2.p0_ref, ...), custom_call_target="tpu_custom_call" | custom-call | flops 1 | bytes 1 | tf_op jit(solution)/shard_map/attend/pallas_call | solution.py:325
  36.9 0.6 across_grad.1
  37.4 1.6 %project.1 = (bf16[64,5376]{1,0:T(8,128)(2,1)S(1)}, bf16[64,5376]{1,0:T(8,128)(2,1)S(1)}, bf16[64,5376]{1,0:T(8,128)(2,1)S(1)}, bf16[64,5376]{1,0:T(8,128)(2,1)S(1)}) custom-call(bf16[256,512]{1,0:T(8,128)(2,1)S(1)} %get-tuple-element.47.o_ref, bf16[512,5376]{1,0:T(8,128)(2,1)S(1)} %bitcast.1), custom_call_target="tpu_custom_call" | custom-call | flops 1 | bytes 1 | tf_op jit(solution)/shard_map/project/pallas_call | solution.py:325
  39.0 0.9 %collective-permute-done.8.a_ref.af_ref = bf16[256,256]{1,0:T(8,128)(2,1)S(1)} collective-permute-done((bf16[256,256]{1,0:T(8,128)(2,1)S(1)}, bf16[256,256]{1,0:T(8,128)(2,1)S(1)}, u32[]{:S(2)}, u32[]{:S(2)}) %collective-permute-start.8) | collective-permute-done | bytes 131104 | tf_op jit(solution)/shard_map/ppermute | solution.py:48
  39.9 0.0 collective-permute-start.13
  39.9 0.5 collective-permute-start.11
  40.5 1.8 %collective-permute-start.9 = (bf16[304,256]{1,0:T(8,128)(2,1)S(1)}, bf16[304,256]{1,0:T(8,128)(2,1)S(1)}, u32[]{:S(2)}, u32[]{:S(2)}) collective-permute-start(bf16[304,256]{1,0:T(8,128)(2,1)S(1)} %get-tuple-element.43), channel_id=1, source_target_pairs={{0,16},{4,20},{8,24},{12,28},{16,0},{20,4},{24,8},{28,12},{1,17},{... | collective-permute-start | bytes 466952 | tf_op jit(solution)/shard_map/ppermute | solution.py:48
  42.3 0.0 collective-permute-done.13.refs_1_
  42.3 0.2 far_sum.1
  42.5 1.6 %collective-permute-start.15 = (bf16[64,5376]{1,0:T(8,128)(2,1)S(1)}, bf16[64,5376]{1,0:T(8,128)(2,1)S(1)}, u32[]{:S(2)}, u32[]{:S(2)}) collective-permute-start(bf16[64,5376]{1,0:T(8,128)(2,1)S(1)} %far_sum.1), channel_id=1, source_target_pairs={{0,2},{1,3},{2,0},{3,1},{4,6},{5,7},{6,4},{7,5},{8,10},{9,11},{10,... | collective-permute-start | bytes 2064392 | tf_op jit(solution)/shard_map/ppermute | solution.py:37
  44.1 0.0 collective-permute-start.14
  44.1 3.4 %attend_grad.1 = (bf16[256,512]{1,0:T(8,128)(2,1)}, f32[256,512]{1,0:T(8,128)S(1)}, bf16[256,512]{1,0:T(8,128)(2,1)S(1)}, bf16[256,512]{1,0:T(8,128)(2,1)S(1)}) custom-call(bf16[256,512]{1,0:T(8,128)(2,1)S(1)} %copy-done.2, bf16[256,512]{1,0:T(8,128)(2,1)S(1)} %join.1.a_ref.kv_ref, bf16[256,512]{1,0:T(8,128)(2,1)S(1)} %collective-permute-done.r1_ref, ...), custom_call_target="tpu_custom_call" | custom-call | flops 10000000000 | bytes 1 | tf_op jit(solution)/shard_map/attend_grad/pallas_call | solution.py:325
  47.4 3.4 %collective-permute-done.9.b_ref.bf_ref = bf16[304,256]{1,0:T(8,128)(2,1)S(1)} collective-permute-done((bf16[304,256]{1,0:T(8,128)(2,1)S(1)}, bf16[304,256]{1,0:T(8,128)(2,1)S(1)}, u32[]{:S(2)}, u32[]{:S(2)}) %collective-permute-start.9) | collective-permute-done | bytes 155680 | tf_op jit(solution)/shard_map/ppermute | solution.py:48
  50.9 1.6 %collective-permute-start.10 = (bf16[304,512]{1,0:T(8,128)(2,1)S(1)}, bf16[304,512]{1,0:T(8,128)(2,1)S(1)}, u32[]{:S(2)}, u32[]{:S(2)}) collective-permute-start(bf16[304,512]{1,0:T(8,128)(2,1)S(1)} %pair.1), channel_id=1, source_target_pairs={{0,4},{4,0},{8,12},{12,8},{16,20},{20,16},{24,28},{28,24},{1,5},{5... | collective-permute-start | bytes 933896 | tf_op jit(solution)/shard_map/ppermute | solution.py:37
  52.5 0.0 collective-permute-done.11.refs_1_
  52.5 0.1 hop_sum.1
  52.5 1.3 %collective-permute-start.12 = (bf16[256,512]{1,0:T(8,128)(2,1)S(1)}, bf16[256,512]{1,0:T(8,128)(2,1)S(1)}, u32[]{:S(2)}, u32[]{:S(2)}) collective-permute-start(bf16[256,512]{1,0:T(8,128)(2,1)S(1)} %hop_sum.1), channel_id=1, source_target_pairs={{8,0},{12,4},{16,8},{20,12},{24,16},{28,20},{9,1},{13,5},{17,9},{2... | collective-permute-start | bytes 786440 | tf_op jit(solution)/shard_map/ppermute | solution.py:32
  53.8 5.8 %collective-permute-done.10.px_ref.pair_ref = bf16[304,512]{1,0:T(8,128)(2,1)S(1)} collective-permute-done((bf16[304,512]{1,0:T(8,128)(2,1)S(1)}, bf16[304,512]{1,0:T(8,128)(2,1)S(1)}, u32[]{:S(2)}, u32[]{:S(2)}) %collective-permute-start.10) | collective-permute-done | bytes 311328 | tf_op jit(solution)/shard_map/ppermute | solution.py:37
  59.6 1.5 %far_grad.1.far_ref = f32[256,512]{1,0:T(8,128)S(1)} custom-call(bf16[256,512]{1,0:T(8,128)(2,1)S(1)} %join.1.a_ref.kv_ref, bf16[256,512]{1,0:T(8,128)(2,1)S(1)} %collective-permute-done.1.a_ref.b_ref.r2_ref.qf_ref, bf16[256,256]{1,0:T(8,128)(2,1)S(1)} %collective-permute-done.8.a_ref.af_ref, bf16[304,256]{1,0:T(8,128)(2,1)S(1)} %collective-permute-done.9.b_ref.bf_ref, ...), custom_call_target="tpu_custom_call" | custom-call | flops 100000000 | bytes 1 | tf_op jit(solution)/shard_map/far_grad/pallas_call | solution.py:325
  61.1 0.7 %collective-permute-done.12.hop_ref = bf16[256,512]{1,0:T(8,128)(2,1)S(1)} collective-permute-done((bf16[256,512]{1,0:T(8,128)(2,1)S(1)}, bf16[256,512]{1,0:T(8,128)(2,1)S(1)}, u32[]{:S(2)}, u32[]{:S(2)}) %collective-permute-start.12) | collective-permute-done | bytes 262176 | tf_op jit(solution)/shard_map/ppermute | solution.py:32
  61.8 0.0 collective-permute-done.14.core_ref
  61.8 0.0 collective-permute-done.15.y_ref
  61.8 1.2 %closing.1 = (bf16[256,256]{1,0:T(8,128)(2,1)}, bf16[256,256]{1,0:T(8,128)(2,1)}, bf16[64,5376]{1,0:T(8,128)(2,1)}) custom-call(f32[256,512]{1,0:T(8,128)S(1)} %get-tuple-element.42.own_ref, f32[256,512]{1,0:T(8,128)S(1)} %far_grad.1.far_ref, bf16[256,512]{1,0:T(8,128)(2,1)S(1)} %collective-permute-done.12.hop_ref, ...), custom_call_target="tpu_custom_call" | custom-call | flops 1 | bytes 1 | tf_op jit(solution)/shard_map/closing/pallas_call | solution.py:325
  (5 shorter events, 0.1 us)
Async XLA Ops:
  0.6 13.6 %collective-permute-start.3 = (bf16[64,5376]{1,0:T(8,128)(2,1)}, bf16[64,5376]{1,0:T(8,128)(2,1)S(1)}, u32[]{:S(2)}, u32[]{:S(2)}) collective-permute-start(bf16[64,5376]{1,0:T(8,128)(2,1)} %own_ref.1), channel_id=1, source_target_pairs={{0,1},{1,0},{2,3},{3,2},{4,5},{5,4},{6,7},{7,6},{8,9},{9,8},{10,11... | collective-permute-start | bytes 2064392 | tf_op jit(solution)/shard_map/ppermute | solution.py:37
  1.1 0.9 %copy-start.3 = (bf16[256,256]{1,0:T(8,128)(2,1)S(1)}, bf16[256,256]{1,0:T(8,128)(2,1)}, u32[]{:S(2)}) copy-start(bf16[256,256]{1,0:T(8,128)(2,1)} %k_ref.1) | copy-start | bytes 393220
  2.1 0.9 %copy-start.4 = (bf16[256,256]{1,0:T(8,128)(2,1)S(1)}, bf16[256,256]{1,0:T(8,128)(2,1)}, u32[]{:S(2)}) copy-start(bf16[256,256]{1,0:T(8,128)(2,1)} %v_ref.1) | copy-start | bytes 393220
  3.0 16.8 %collective-permute-start.2 = (bf16[256,512]{1,0:T(8,128)(2,1)S(1)}, bf16[256,512]{1,0:T(8,128)(2,1)S(1)}, u32[]{:S(2)}, u32[]{:S(2)}) collective-permute-start(bf16[256,512]{1,0:T(8,128)(2,1)S(1)} %join.1.a_ref.kv_ref), channel_id=1, source_target_pairs={{0,4},{4,0},{8,12},{12,8},{16,20},{20,16},{24,28},{28,24},{1,5},{5... | collective-permute-start | bytes 786440 | tf_op jit(solution)/shard_map/ppermute | solution.py:37
  5.5 14.3 %collective-permute-start = (bf16[256,512]{1,0:T(8,128)(2,1)S(1)}, bf16[256,512]{1,0:T(8,128)(2,1)S(1)}, u32[]{:S(2)}, u32[]{:S(2)}) collective-permute-start(bf16[256,512]{1,0:T(8,128)(2,1)S(1)} %join.1.a_ref.kv_ref), channel_id=1, source_target_pairs={{0,8},{4,12},{8,16},{12,20},{16,24},{20,28},{1,9},{5,13},{9,17},{1... | collective-permute-start | bytes 786440 | tf_op jit(solution)/shard_map/ppermute | solution.py:32
  9.0 17.5 %collective-permute-start.6 = (bf16[64,5376]{1,0:T(8,128)(2,1)}, bf16[64,5376]{1,0:T(8,128)(2,1)S(1)}, u32[]{:S(2)}, u32[]{:S(2)}) collective-permute-start(bf16[64,5376]{1,0:T(8,128)(2,1)} %own_ref.1), channel_id=1, source_target_pairs={{0,2},{1,3},{2,0},{3,1},{4,6},{5,7},{6,4},{7,5},{8,10},{9,11},{10,... | collective-permute-start | bytes 2064392 | tf_op jit(solution)/shard_map/ppermute | solution.py:37
  10.6 0.9 %copy-start.1 = (bf16[256,512]{1,0:T(8,128)(2,1)S(1)}, bf16[256,512]{1,0:T(8,128)(2,1)}, u32[]{:S(2)}) copy-start(bf16[256,512]{1,0:T(8,128)(2,1)} %q_ref.7) | copy-start | bytes 786436
  11.6 14.4 %collective-permute-start.1 = (bf16[256,512]{1,0:T(8,128)(2,1)S(1)}, bf16[256,512]{1,0:T(8,128)(2,1)S(1)}, u32[]{:S(2)}, u32[]{:S(2)}) collective-permute-start(bf16[256,512]{1,0:T(8,128)(2,1)S(1)} %far_sent.1), channel_id=1, source_target_pairs={{0,16},{4,20},{8,24},{12,28},{16,0},{20,4},{24,8},{28,12},{1,17},{... | collective-permute-start | bytes 786440 | tf_op jit(solution)/shard_map/ppermute | solution.py:48
  14.3 2.6 %copy-start = (bf16[512,5376]{1,0:T(8,128)(2,1)S(1)}, bf16[512,5376]{1,0:T(8,128)(2,1)}, u32[]{:S(2)}) copy-start(bf16[512,5376]{1,0:T(8,128)(2,1)} %w_ref.5) | copy-start | bytes 16515076
  16.8 1.1 %copy-start.5 = (bf16[64,5376]{1,0:T(8,128)(2,1)S(1)}, bf16[64,5376]{1,0:T(8,128)(2,1)}, u32[]{:S(2)}) copy-start(bf16[64,5376]{1,0:T(8,128)(2,1)} %own_ref.1) | copy-start | bytes 2064388
  17.9 10.8 %slice-start = ((s8[5505024]{0:T(1024)(128)(4,1)}), s8[4194304]{0:T(1024)(128)(4,1)S(1)}, s32[]{:S(2)}) async-start(s8[5505024]{0:T(1024)(128)(4,1)} %bitcast), calls=%async_computation | async-start | bytes 8388608
  19.8 8.9 %slice-start.1 = ((s8[5505024]{0:T(1024)(128)(4,1)}), s8[1310720]{0:T(1024)(128)(4,1)S(1)}, s32[]{:S(2)}) async-start(s8[5505024]{0:T(1024)(128)(4,1)} %bitcast), calls=%async_computation.1 | async-start | bytes 2621440
  19.8 7.6 %collective-permute-start.4 = (bf16[256,512]{1,0:T(8,128)(2,1)S(1)}, bf16[256,512]{1,0:T(8,128)(2,1)S(1)}, u32[]{:S(2)}, u32[]{:S(2)}) collective-permute-start(bf16[256,512]{1,0:T(8,128)(2,1)S(1)} %collective-permute-done.r1_ref), channel_id=1, source_target_pairs={{0,4},{4,0},{8,12},{12,8},{16,20},{20,16},{24,28},{28,24},{1,5},{5... | collective-permute-start | bytes 786440 | tf_op jit(solution)/shard_map/ppermute | solution.py:37
  26.6 2.1 %collective-permute-start.7 = (bf16[64,5376]{1,0:T(8,128)(2,1)S(1)}, bf16[64,5376]{1,0:T(8,128)(2,1)S(1)}, u32[]{:S(2)}, u32[]{:S(2)}) collective-permute-start(bf16[64,5376]{1,0:T(8,128)(2,1)S(1)} %collective-permute-done.6.y_ref), channel_id=1, source_target_pairs={{0,1},{1,0},{2,3},{3,2},{4,5},{5,4},{6,7},{7,6},{8,9},{9,8},{10,11... | collective-permute-start | bytes 2064392 | tf_op jit(solution)/shard_map/ppermute | solution.py:37
  26.6 6.6 %copy-start.2 = (bf16[256,512]{1,0:T(8,128)(2,1)S(1)}, bf16[256,512]{1,0:T(8,128)(2,1)}, u32[]{:S(2)}) copy-start(bf16[256,512]{1,0:T(8,128)(2,1)} %q_ref.7) | copy-start | bytes 786436
  26.6 8.8 %collective-permute-start.5 = (bf16[256,512]{1,0:T(8,128)(2,1)S(1)}, bf16[256,512]{1,0:T(8,128)(2,1)S(1)}, u32[]{:S(2)}, u32[]{:S(2)}) collective-permute-start(bf16[256,512]{1,0:T(8,128)(2,1)S(1)} %pick.1), channel_id=1, source_target_pairs={{0,4},{4,0},{8,12},{12,8},{16,20},{20,16},{24,28},{28,24},{1,5},{5... | collective-permute-start | bytes 786440 | tf_op jit(solution)/shard_map/ppermute | solution.py:37
  30.6 9.3 %collective-permute-start.8 = (bf16[256,256]{1,0:T(8,128)(2,1)S(1)}, bf16[256,256]{1,0:T(8,128)(2,1)S(1)}, u32[]{:S(2)}, u32[]{:S(2)}) collective-permute-start(bf16[256,256]{1,0:T(8,128)(2,1)S(1)} %get-tuple-element.40), channel_id=1, source_target_pairs={{0,16},{4,20},{8,24},{12,28},{16,0},{20,4},{24,8},{28,12},{1,17},{... | collective-permute-start | bytes 393224 | tf_op jit(solution)/shard_map/ppermute | solution.py:48
  39.9 2.4 %collective-permute-start.13 = (bf16[64,5376]{1,0:T(8,128)(2,1)S(1)}, bf16[64,5376]{1,0:T(8,128)(2,1)S(1)}, u32[]{:S(2)}, u32[]{:S(2)}) collective-permute-start(bf16[64,5376]{1,0:T(8,128)(2,1)S(1)} %get-tuple-element.52), channel_id=1, source_target_pairs={{0,1},{1,0},{2,3},{3,2},{4,5},{5,4},{6,7},{7,6},{8,9},{9,8},{10,11... | collective-permute-start | bytes 2064392 | tf_op jit(solution)/shard_map/ppermute | solution.py:37
  39.9 12.5 %collective-permute-start.11 = (bf16[256,512]{1,0:T(8,128)(2,1)S(1)}, bf16[256,512]{1,0:T(8,128)(2,1)S(1)}, u32[]{:S(2)}, u32[]{:S(2)}) collective-permute-start(bf16[256,512]{1,0:T(8,128)(2,1)S(1)} %across_grad.1), channel_id=1, source_target_pairs={{0,4},{4,0},{8,12},{12,8},{16,20},{20,16},{24,28},{28,24},{1,5},{5... | collective-permute-start | bytes 786440 | tf_op jit(solution)/shard_map/ppermute | solution.py:37
  40.5 10.4 %collective-permute-start.9 = (bf16[304,256]{1,0:T(8,128)(2,1)S(1)}, bf16[304,256]{1,0:T(8,128)(2,1)S(1)}, u32[]{:S(2)}, u32[]{:S(2)}) collective-permute-start(bf16[304,256]{1,0:T(8,128)(2,1)S(1)} %get-tuple-element.43), channel_id=1, source_target_pairs={{0,16},{4,20},{8,24},{12,28},{16,0},{20,4},{24,8},{28,12},{1,17},{... | collective-permute-start | bytes 466952 | tf_op jit(solution)/shard_map/ppermute | solution.py:48
  42.5 19.3 %collective-permute-start.15 = (bf16[64,5376]{1,0:T(8,128)(2,1)S(1)}, bf16[64,5376]{1,0:T(8,128)(2,1)S(1)}, u32[]{:S(2)}, u32[]{:S(2)}) collective-permute-start(bf16[64,5376]{1,0:T(8,128)(2,1)S(1)} %far_sum.1), channel_id=1, source_target_pairs={{0,2},{1,3},{2,0},{3,1},{4,6},{5,7},{6,4},{7,5},{8,10},{9,11},{10,... | collective-permute-start | bytes 2064392 | tf_op jit(solution)/shard_map/ppermute | solution.py:37
  44.1 17.7 %collective-permute-start.14 = (bf16[64,5376]{1,0:T(8,128)(2,1)S(1)}, bf16[64,5376]{1,0:T(8,128)(2,1)S(1)}, u32[]{:S(2)}, u32[]{:S(2)}) collective-permute-start(bf16[64,5376]{1,0:T(8,128)(2,1)S(1)} %get-tuple-element.53), channel_id=1, source_target_pairs={{0,1},{1,0},{2,3},{3,2},{4,5},{5,4},{6,7},{7,6},{8,9},{9,8},{10,11... | collective-permute-start | bytes 2064392 | tf_op jit(solution)/shard_map/ppermute | solution.py:37
  50.9 8.7 %collective-permute-start.10 = (bf16[304,512]{1,0:T(8,128)(2,1)S(1)}, bf16[304,512]{1,0:T(8,128)(2,1)S(1)}, u32[]{:S(2)}, u32[]{:S(2)}) collective-permute-start(bf16[304,512]{1,0:T(8,128)(2,1)S(1)} %pair.1), channel_id=1, source_target_pairs={{0,4},{4,0},{8,12},{12,8},{16,20},{20,16},{24,28},{28,24},{1,5},{5... | collective-permute-start | bytes 933896 | tf_op jit(solution)/shard_map/ppermute | solution.py:37
  52.5 9.2 %collective-permute-start.12 = (bf16[256,512]{1,0:T(8,128)(2,1)S(1)}, bf16[256,512]{1,0:T(8,128)(2,1)S(1)}, u32[]{:S(2)}, u32[]{:S(2)}) collective-permute-start(bf16[256,512]{1,0:T(8,128)(2,1)S(1)} %hop_sum.1), channel_id=1, source_target_pairs={{8,0},{12,4},{16,8},{20,12},{24,16},{28,20},{9,1},{13,5},{17,9},{2... | collective-permute-start | bytes 786440 | tf_op jit(solution)/shard_map/ppermute | solution.py:32

commit v9 on v8

--- a/solution.py
+++ b/solution.py
@@ -81,14 +81,26 @@
     return [kv_ref[:, cols], r1_ref[:, cols], r2_ref[:, cols], x1_ref[:, cols], jnp.where(odd, p0_ref[:, cols], x2_ref[:, cols])]
 
 
-def join_kernel(k_ref, v_ref, kv_ref):
+def join_kernel(k_ref, v_ref, kv_ref, sems):
     cols = k_ref.shape[1]
-    kv_ref[:, :cols] = k_ref[...]
-    kv_ref[:, cols:] = v_ref[...]
+    copies = [
+        pltpu.make_async_copy(k_ref, kv_ref.at[:, pl.ds(0, cols)], sems.at[0]),
+        pltpu.make_async_copy(v_ref, kv_ref.at[:, pl.ds(cols, cols)], sems.at[1]),
+    ]
+    for copy in copies:
+        copy.start()
+    for copy in copies:
+        copy.wait()
 
 
 def either_kernel(first, a_ref, b_ref, out_ref):
     out_ref[...] = jnp.where(first(lax.axis_index("seq")), a_ref[...], b_ref[...])
+
+
+def far_sent_kernel(kv_ref, q_ref, sent_ref, kept_ref):
+    kv = kv_ref[...]
+    kept_ref[...] = kv
+    sent_ref[...] = jnp.where(is_lower(lax.axis_index("seq")), kv, q_ref[...])
 
 
 def is_odd(seq):
@@ -336,16 +348,25 @@
     def gate(value, *others):
         return lax.optimization_barrier((value, *others))[0]
 
+    kv_sent = pl.pallas_call(
+        join_kernel,
+        out_shape=block,
+        in_specs=[pl.BlockSpec(memory_space=pl.ANY)] * 2,
+        out_specs=pl.BlockSpec(memory_space=pl.ANY),
+        scratch_shapes=[pltpu.SemaphoreType.DMA((2,))],
+        compiler_params=pltpu.CompilerParams(vmem_limit_bytes=60 << 20),
+        cost_estimate=SMALL,
+        name="join",
+    )(keys, values)
+    far_sent, kv = call(far_sent_kernel, "far_sent", (block, block), [], kv_sent, queries)
+    r1 = shifted(kv_sent, 2)
+    r2, q_far = far_swapped(lambda: kv, lambda: queries) if lax.axis_size("seq") > 2 * FAR else (far_swapped(*[lambda: far_sent] * 2))
+    og_c = swapped(out_grad, "head", 1)
     og_y = swapped(out_grad, "head", 2)
-    kv = call(join_kernel, "join", block, [], keys, values)
-    far_sent = call(functools.partial(either_kernel, is_lower), "far_sent", block, [], kv, queries)
-    r1 = shifted(kv, 2)
-    r2, q_far = far_swapped(lambda: kv, lambda: queries) if lax.axis_size("seq") > 2 * FAR else (far_swapped(*[lambda: far_sent] * 2))
     p0 = swapped(kv, "seq", 1)
-    og_c = swapped(out_grad, "head", 1)
     half_grad = jax.ShapeDtypeStruct((tok // 2, q_cols), BF16)
     grad_near = call(near_back_kernel, "near_back", half_grad, [], out_grad, og_c, out_weight, cost=LARGE)
-    x1 = swapped(gate(r1, p0, grad_near), "seq", 1)
+    x1 = swapped(gate(r1, grad_near), "seq", 1)
     x2 = swapped(call(functools.partial(either_kernel, is_odd), "pick", block, [], r2, q_far, cost=LARGE), "seq", 1)
     og_yc = swapped(gate(og_y, r2, grad_near), "head", 1)
     first = jax.ShapeDtypeStruct((tok, q_cols // 2), BF16)
@@ -367,7 +388,7 @@
             jax.ShapeDtypeStruct((kv_heads, HEAD_SIZE, 2 * tok), F32),
         ),
         [],
-        queries, kv, r1, r2, x1,
+        queries, kv, gate(r1, p0), r2, x1,
     )
     attended, probs, stats, sent_second = call(
         forward_kernel,

time: 63.3 us -> 72.2 us (1.14)
  Pallas kernels: 15.8 us -> 24.8 us
  starting transfers between devices: 21.5 us -> 22.8 us
  local copies, waits for them, and re-layouts: 6.43 us -> 5.57 us
    pallas_call x0 -> x1, Pallas kernels: none -> 9.06 us  [per_device(): pl.pallas_call(join_kernel, out_shape=block, in_specs=[pl.BlockSpec(memor...]
    ppermute x11, starting transfers between devices: 9.55 us -> 10.5 us  [swapped(): return lax.ppermute(value, axis, [(i, i ^ bit) for i in range(count)])]
    unnamed x16 -> x14, local copies, waits for them, and re-layouts: 6.43 us -> 5.57 us
    pallas_call x15 -> x14, Pallas kernels: 15.8 us -> 15.7 us  [call(): pl.pallas_call(kernel, out_shape=outs, in_specs=[VMEM] * len(operands), o...]
  transfers between devices with their start and end apart: 16 -> 16, of which waited for: 9 -> 4; matrix products, arithmetic and copies ran while one was open for 0% -> 0% of each run, Pallas kernels for 23% -> 33%
where the time goes in v9:
time: 72.2 us; the launch traced here: 71.9 us
  Pallas kernels  24.8 us (34%)
  starting transfers between devices  22.8 us (32%)
  waiting for transfers between devices  17.9 us (25%)
  local copies, waits for them, and re-layouts  5.57 us (8%)
  between operations  0.83 us (1%)
    pallas_call x14, Pallas kernels, call(): pl.pallas_call(kernel, out_shape=outs, in_specs=[VMEM] * len(operands), o...  15.7 us
    ppermute x11, starting transfers between devices, swapped(): return lax.ppermute(value, axis, [(i, i ^ bit) for i in range(count)])  10.5 us
    ppermute x3, waiting for transfers between devices, far_swapped(): lax.ppermute(lower() if lower is upper else jnp.where(side == r, lower(),...  9.5 us
    pallas_call x1, Pallas kernels, per_device(): pl.pallas_call(join_kernel, out_shape=block, in_specs=[pl.BlockSpec(memor...  9.06 us
    ppermute x11, waiting for transfers between devices, swapped(): return lax.ppermute(value, axis, [(i, i ^ bit) for i in range(count)])  8.43 us
    ppermute x3, starting transfers between devices, far_swapped(): lax.ppermute(lower() if lower is upper else jnp.where(side == r, lower(),...  7.5 us
    unnamed x14, local copies, waits for them, and re-layouts  5.57 us
    ppermute x2, starting transfers between devices, shifted(): lax.ppermute(value, 'seq', [(i, i + steps) for i in range(first, last)])  4.79 us
  transfers between devices with their start and end apart: 16, of which 4 were waited for; matrix products, arithmetic and copies ran while one was open for 0% of the time, Pallas kernels for 33%

profile of v9, /device:TPU:0, one launch (start us, length us, event | category | flops | bytes accessed | tf_op | source)
XLA Modules:
  0.0 71.9 jit_solution(9119423874180513976)
XLA Ops:
  0.6 0.5 collective-permute-start.2
  1.1 2.6 %collective-permute-start.6 = (bf16[64,5376]{1,0:T(8,128)(2,1)}, bf16[64,5376]{1,0:T(8,128)(2,1)S(1)}, u32[]{:S(2)}, u32[]{:S(2)}) collective-permute-start(bf16[64,5376]{1,0:T(8,128)(2,1)} %own_ref.1), channel_id=1, source_target_pairs={{0,2},{1,3},{2,0},{3,1},{4,6},{5,7},{6,4},{7,5},{8,10},{9,11},{10,... | collective-permute-start | bytes 2064392 | tf_op jit(solution)/shard_map/ppermute | solution.py:37
  3.7 9.1 %join.1.kv_ref = bf16[256,512]{1,0:T(8,128)(2,1)} custom-call(bf16[256,256]{1,0:T(8,128)(2,1)} %k_ref.1, bf16[256,256]{1,0:T(8,128)(2,1)} %v_ref.1), custom_call_target="tpu_custom_call" | custom-call | flops 1 | bytes 1 | tf_op jit(solution)/shard_map/join/pallas_call | solution.py:351
  12.8 3.5 %collective-permute-start = (bf16[256,512]{1,0:T(8,128)(2,1)}, bf16[256,512]{1,0:T(8,128)(2,1)S(1)}, u32[]{:S(2)}, u32[]{:S(2)}) collective-permute-start(bf16[256,512]{1,0:T(8,128)(2,1)} %join.1.kv_ref), channel_id=1, source_target_pairs={{0,8},{4,12},{8,16},{12,20},{16,24},{20,28},{1,9},{5,13},{9,17},{1... | collective-permute-start | bytes 786440 | tf_op jit(solution)/shard_map/ppermute | solution.py:32
  16.3 0.0 copy-start.1
  16.3 0.9 %copy-done.1 = bf16[256,512]{1,0:T(8,128)(2,1)S(1)} copy-done((bf16[256,512]{1,0:T(8,128)(2,1)S(1)}, bf16[256,512]{1,0:T(8,128)(2,1)}, u32[]{:S(2)}) %copy-start.1) | copy-done | bytes 262168
  17.3 0.0 copy-start.3
  17.3 0.9 %copy-done.3 = bf16[256,512]{1,0:T(8,128)(2,1)S(1)} copy-done((bf16[256,512]{1,0:T(8,128)(2,1)S(1)}, bf16[256,512]{1,0:T(8,128)(2,1)}, u32[]{:S(2)}) %copy-start.3) | copy-done | bytes 262168
  18.3 2.6 %collective-permute-start.1 = (bf16[256,512]{1,0:T(8,128)(2,1)S(1)}, bf16[256,512]{1,0:T(8,128)(2,1)S(1)}, u32[]{:S(2)}, u32[]{:S(2)}) collective-permute-start(bf16[256,512]{1,0:T(8,128)(2,1)S(1)} %get-tuple-element.35), channel_id=1, source_target_pairs={{0,16},{4,20},{8,24},{12,28},{16,0},{20,4},{24,8},{28,12},{1,17},{... | collective-permute-start | bytes 786440 | tf_op jit(solution)/shard_map/ppermute | solution.py:48
  20.9 1.5 %collective-permute-start.4 = (bf16[256,512]{1,0:T(8,128)(2,1)S(1)}, bf16[256,512]{1,0:T(8,128)(2,1)S(1)}, u32[]{:S(2)}, u32[]{:S(2)}) collective-permute-start(bf16[256,512]{1,0:T(8,128)(2,1)S(1)} %get-tuple-element.34.kv_ref), channel_id=1, source_target_pairs={{0,4},{4,0},{8,12},{12,8},{16,20},{20,16},{24,28},{28,24},{1,5},{5... | collective-permute-start | bytes 786440 | tf_op jit(solution)/shard_map/ppermute | solution.py:37
  22.4 0.0 collective-permute-done.2.core_ref
  22.4 0.0 copy-start
  22.4 2.6 %copy-done = bf16[512,5376]{1,0:T(8,128)(2,1)S(1)} copy-done((bf16[512,5376]{1,0:T(8,128)(2,1)S(1)}, bf16[512,5376]{1,0:T(8,128)(2,1)}, u32[]{:S(2)}) %copy-start) | copy-done | bytes 5505048
  25.0 0.0 copy-start.4
  25.0 1.1 %copy-done.4 = bf16[64,5376]{1,0:T(8,128)(2,1)S(1)} copy-done((bf16[64,5376]{1,0:T(8,128)(2,1)S(1)}, bf16[64,5376]{1,0:T(8,128)(2,1)}, u32[]{:S(2)}) %copy-start.4) | copy-done | bytes 688152
  26.1 0.0 slice-start
  26.1 1.9 %near_back.1.near_ref.dn_ref = bf16[128,512]{1,0:T(8,128)(2,1)S(1)} custom-call(bf16[64,5376]{1,0:T(8,128)(2,1)S(1)} %copy-done.4, bf16[64,5376]{1,0:T(8,128)(2,1)S(1)} %collective-permute-done.2.core_ref, bf16[512,5376]{1,0:T(8,128)(2,1)S(1)} %copy-done), custom_call_target="tpu_custom_call" | custom-call | flops 10000000000 | bytes 1 | tf_op jit(solution)/shard_map/near_back/pallas_call | solution.py:337
  27.9 0.0 slice-start.1
  28.0 0.0 collective-permute-done.r1_ref
  28.0 0.6 collective-permute-start.3
  28.6 4.4 %collective-permute-done.1.a_ref.b_ref.r2_ref.qf_ref = bf16[256,512]{1,0:T(8,128)(2,1)S(1)} collective-permute-done((bf16[256,512]{1,0:T(8,128)(2,1)S(1)}, bf16[256,512]{1,0:T(8,128)(2,1)S(1)}, u32[]{:S(2)}, u32[]{:S(2)}) %collective-permute-start.1) | collective-permute-done | bytes 262176 | tf_op jit(solution)/shard_map/ppermute | solution.py:48
  32.9 0.0 collective-permute-done.6.y_ref
  32.9 0.0 collective-permute-start.7
  33.0 0.0 copy-start.2
  33.0 1.6 %collective-permute-start.5 = (bf16[256,512]{1,0:T(8,128)(2,1)S(1)}, bf16[256,512]{1,0:T(8,128)(2,1)S(1)}, u32[]{:S(2)}, u32[]{:S(2)}) collective-permute-start(bf16[256,512]{1,0:T(8,128)(2,1)S(1)} %pick.1), channel_id=1, source_target_pairs={{0,4},{4,0},{8,12},{12,8},{16,20},{20,16},{24,28},{28,24},{1,5},{5... | collective-permute-start | bytes 786440 | tf_op jit(solution)/shard_map/ppermute | solution.py:37
  34.6 1.0 %collective-permute-done.3.x1_ref = bf16[256,512]{1,0:T(8,128)(2,1)S(1)} collective-permute-done((bf16[256,512]{1,0:T(8,128)(2,1)S(1)}, bf16[256,512]{1,0:T(8,128)(2,1)S(1)}, u32[]{:S(2)}, u32[]{:S(2)}) %collective-permute-start.3) | collective-permute-done | bytes 262176 | tf_op jit(solution)/shard_map/ppermute | solution.py:37
  35.6 0.0 collective-permute-done.7.yc_ref
  35.6 0.0 slice-done
  35.6 0.0 slice-done.1
  35.6 1.9 %far_back.1 = (bf16[128,512]{1,0:T(8,128)(2,1)S(1)}, bf16[256,256]{1,0:T(8,128)(2,1)S(1)}) custom-call(bf16[64,5376]{1,0:T(8,128)(2,1)S(1)} %collective-permute-done.6.y_ref, bf16[64,5376]{1,0:T(8,128)(2,1)S(1)} %collective-permute-done.7.yc_ref, bf16[512,5376]{1,0:T(8,128)(2,1)S(1)} %bitcast.1, bf16[128,512]{1,0:T(8,128)(2,1)S(1)} %near_back.1.near_ref.dn_ref), custom_call_target="tpu_custom_call" | custom-call | flops 10000000000 | bytes 1 | tf_op jit(solution)/shard_map/far_back/pallas_call | solution.py:337
  37.5 4.8 %collective-permute-start.8 = (bf16[256,256]{1,0:T(8,128)(2,1)S(1)}, bf16[256,256]{1,0:T(8,128)(2,1)S(1)}, u32[]{:S(2)}, u32[]{:S(2)}) collective-permute-start(bf16[256,256]{1,0:T(8,128)(2,1)S(1)} %get-tuple-element.46), channel_id=1, source_target_pairs={{0,16},{4,20},{8,24},{12,28},{16,0},{20,4},{24,8},{28,12},{1,17},{... | collective-permute-start | bytes 393224 | tf_op jit(solution)/shard_map/ppermute | solution.py:48
  42.2 0.0 collective-permute-done.4.p0_ref
  42.2 0.0 copy-done.2
  42.2 2.0 %attend_early.1 = (f32[2,4,256,512]{3,2,1,0:T(8,128)S(1)}, f32[8,512]{1,0:T(8,128)S(1)}, f32[2,128,512]{2,1,0:T(8,128)S(1)}) custom-call(bf16[256,512]{1,0:T(8,128)(2,1)S(1)} %copy-done.2, bf16[256,512]{1,0:T(8,128)(2,1)S(1)} %get-tuple-element.34.kv_ref, bf16[256,512]{1,0:T(8,128)(2,1)S(1)} %collective-permute-done.r1_ref, ...), custom_call_target="tpu_custom_call" | custom-call | flops 1 | bytes 1 | tf_op jit(solution)/shard_map/attend_early/pallas_call | solution.py:337
  44.2 0.0 collective-permute-done.5.x2_ref.qx_ref
  44.2 1.4 %attend.1 = (bf16[256,512]{1,0:T(8,128)(2,1)S(1)}, bf16[2,5,256,512]{3,2,1,0:T(8,128)(2,1)S(1)}, f32[8,512]{1,0:T(8,128)S(1)}, bf16[304,256]{1,0:T(8,128)(2,1)S(1)}) custom-call(bf16[256,512]{1,0:T(8,128)(2,1)S(1)} %copy-done.2, bf16[256,512]{1,0:T(8,128)(2,1)S(1)} %collective-permute-done.4.p0_ref, ...), custom_call_target="tpu_custom_call" | custom-call | flops 1 | bytes 1 | tf_op jit(solution)/shard_map/attend/pallas_call | solution.py:337
  45.7 0.6 across_grad.1
  46.3 1.6 %project.1 = (bf16[64,5376]{1,0:T(8,128)(2,1)S(1)}, bf16[64,5376]{1,0:T(8,128)(2,1)S(1)}, bf16[64,5376]{1,0:T(8,128)(2,1)S(1)}, bf16[64,5376]{1,0:T(8,128)(2,1)S(1)}) custom-call(bf16[256,512]{1,0:T(8,128)(2,1)S(1)} %get-tuple-element.53.o_ref, bf16[512,5376]{1,0:T(8,128)(2,1)S(1)} %bitcast.1), custom_call_target="tpu_custom_call" | custom-call | flops 1 | bytes 1 | tf_op jit(solution)/shard_map/project/pallas_call | solution.py:337
  47.9 0.0 collective-permute-done.8.a_ref.af_ref
  47.9 0.1 collective-permute-start.13
  48.0 2.5 %collective-permute-start.11 = (bf16[256,512]{1,0:T(8,128)(2,1)S(1)}, bf16[256,512]{1,0:T(8,128)(2,1)S(1)}, u32[]{:S(2)}, u32[]{:S(2)}) collective-permute-start(bf16[256,512]{1,0:T(8,128)(2,1)S(1)} %across_grad.1), channel_id=1, source_target_pairs={{0,4},{4,0},{8,12},{12,8},{16,20},{20,16},{24,28},{28,24},{1,5},{5... | collective-permute-start | bytes 786440 | tf_op jit(solution)/shard_map/ppermute | solution.py:37
  50.5 0.1 collective-permute-start.9
  50.6 0.0 collective-permute-done.13.refs_1_
  50.6 0.2 far_sum.1
  50.7 0.6 collective-permute-start.15
  51.3 0.0 collective-permute-start.14
  51.3 3.4 %attend_grad.1 = (bf16[256,512]{1,0:T(8,128)(2,1)}, f32[256,512]{1,0:T(8,128)S(1)}, bf16[256,512]{1,0:T(8,128)(2,1)S(1)}, bf16[256,512]{1,0:T(8,128)(2,1)S(1)}) custom-call(bf16[256,512]{1,0:T(8,128)(2,1)S(1)} %copy-done.2, bf16[256,512]{1,0:T(8,128)(2,1)S(1)} %get-tuple-element.34.kv_ref, bf16[256,512]{1,0:T(8,128)(2,1)S(1)} %collective-permute-done.r1_ref, ...), custom_call_target="tpu_custom_call" | custom-call | flops 10000000000 | bytes 1 | tf_op jit(solution)/shard_map/attend_grad/pallas_call | solution.py:337
  54.7 5.1 %collective-permute-done.9.b_ref.bf_ref = bf16[304,256]{1,0:T(8,128)(2,1)S(1)} collective-permute-done((bf16[304,256]{1,0:T(8,128)(2,1)S(1)}, bf16[304,256]{1,0:T(8,128)(2,1)S(1)}, u32[]{:S(2)}, u32[]{:S(2)}) %collective-permute-start.9) | collective-permute-done | bytes 155680 | tf_op jit(solution)/shard_map/ppermute | solution.py:48
  59.9 0.6 collective-permute-start.10
  60.5 0.0 collective-permute-done.11.refs_1_
  60.5 0.1 hop_sum.1
  60.5 1.3 %collective-permute-start.12 = (bf16[256,512]{1,0:T(8,128)(2,1)S(1)}, bf16[256,512]{1,0:T(8,128)(2,1)S(1)}, u32[]{:S(2)}, u32[]{:S(2)}) collective-permute-start(bf16[256,512]{1,0:T(8,128)(2,1)S(1)} %hop_sum.1), channel_id=1, source_target_pairs={{8,0},{12,4},{16,8},{20,12},{24,16},{28,20},{9,1},{13,5},{17,9},{2... | collective-permute-start | bytes 786440 | tf_op jit(solution)/shard_map/ppermute | solution.py:32
  61.8 7.4 %collective-permute-done.10.px_ref.pair_ref = bf16[304,512]{1,0:T(8,128)(2,1)S(1)} collective-permute-done((bf16[304,512]{1,0:T(8,128)(2,1)S(1)}, bf16[304,512]{1,0:T(8,128)(2,1)S(1)}, u32[]{:S(2)}, u32[]{:S(2)}) %collective-permute-start.10) | collective-permute-done | bytes 311328 | tf_op jit(solution)/shard_map/ppermute | solution.py:37
  69.2 1.5 %far_grad.1.far_ref = f32[256,512]{1,0:T(8,128)S(1)} custom-call(bf16[256,512]{1,0:T(8,128)(2,1)S(1)} %get-tuple-element.34.kv_ref, bf16[256,512]{1,0:T(8,128)(2,1)S(1)} %collective-permute-done.1.a_ref.b_ref.r2_ref.qf_ref, bf16[256,256]{1,0:T(8,128)(2,1)S(1)} %collective-permute-done.8.a_ref.af_ref, ...), custom_call_target="tpu_custom_call" | custom-call | flops 100000000 | bytes 1 | tf_op jit(solution)/shard_map/far_grad/pallas_call | solution.py:337
  70.7 0.0 collective-permute-done.12.hop_ref
  70.7 0.0 collective-permute-done.14.core_ref
  70.7 0.0 collective-permute-done.15.y_ref
  70.7 1.2 %closing.1 = (bf16[256,256]{1,0:T(8,128)(2,1)}, bf16[256,256]{1,0:T(8,128)(2,1)}, bf16[64,5376]{1,0:T(8,128)(2,1)}) custom-call(f32[256,512]{1,0:T(8,128)S(1)} %get-tuple-element.48.own_ref, f32[256,512]{1,0:T(8,128)S(1)} %far_grad.1.far_ref, bf16[256,512]{1,0:T(8,128)(2,1)S(1)} %collective-permute-done.12.hop_ref, ...), custom_call_target="tpu_custom_call" | custom-call | flops 1 | bytes 1 | tf_op jit(solution)/shard_map/closing/pallas_call | solution.py:337
  (4 shorter events, 0.1 us)
Async XLA Ops:
  0.6 21.8 %collective-permute-start.2 = (bf16[64,5376]{1,0:T(8,128)(2,1)}, bf16[64,5376]{1,0:T(8,128)(2,1)S(1)}, u32[]{:S(2)}, u32[]{:S(2)}) collective-permute-start(bf16[64,5376]{1,0:T(8,128)(2,1)} %own_ref.1), channel_id=1, source_target_pairs={{0,1},{1,0},{2,3},{3,2},{4,5},{5,4},{6,7},{7,6},{8,9},{9,8},{10,11... | collective-permute-start | bytes 2064392 | tf_op jit(solution)/shard_map/ppermute | solution.py:37
  1.1 31.8 %collective-permute-start.6 = (bf16[64,5376]{1,0:T(8,128)(2,1)}, bf16[64,5376]{1,0:T(8,128)(2,1)S(1)}, u32[]{:S(2)}, u32[]{:S(2)}) collective-permute-start(bf16[64,5376]{1,0:T(8,128)(2,1)} %own_ref.1), channel_id=1, source_target_pairs={{0,2},{1,3},{2,0},{3,1},{4,6},{5,7},{6,4},{7,5},{8,10},{9,11},{10,... | collective-permute-start | bytes 2064392 | tf_op jit(solution)/shard_map/ppermute | solution.py:37
  12.8 15.2 %collective-permute-start = (bf16[256,512]{1,0:T(8,128)(2,1)}, bf16[256,512]{1,0:T(8,128)(2,1)S(1)}, u32[]{:S(2)}, u32[]{:S(2)}) collective-permute-start(bf16[256,512]{1,0:T(8,128)(2,1)} %join.1.kv_ref), channel_id=1, source_target_pairs={{0,8},{4,12},{8,16},{12,20},{16,24},{20,28},{1,9},{5,13},{9,17},{1... | collective-permute-start | bytes 786440 | tf_op jit(solution)/shard_map/ppermute | solution.py:32
  16.3 1.0 %copy-start.1 = (bf16[256,512]{1,0:T(8,128)(2,1)S(1)}, bf16[256,512]{1,0:T(8,128)(2,1)}, u32[]{:S(2)}) copy-start(bf16[256,512]{1,0:T(8,128)(2,1)} %q_ref.9) | copy-start | bytes 786436
  17.3 0.9 %copy-start.3 = (bf16[256,512]{1,0:T(8,128)(2,1)S(1)}, bf16[256,512]{1,0:T(8,128)(2,1)}, u32[]{:S(2)}) copy-start(bf16[256,512]{1,0:T(8,128)(2,1)} %join.1.kv_ref) | copy-start | bytes 786436
  18.3 14.7 %collective-permute-start.1 = (bf16[256,512]{1,0:T(8,128)(2,1)S(1)}, bf16[256,512]{1,0:T(8,128)(2,1)S(1)}, u32[]{:S(2)}, u32[]{:S(2)}) collective-permute-start(bf16[256,512]{1,0:T(8,128)(2,1)S(1)} %get-tuple-element.35), channel_id=1, source_target_pairs={{0,16},{4,20},{8,24},{12,28},{16,0},{20,4},{24,8},{28,12},{1,17},{... | collective-permute-start | bytes 786440 | tf_op jit(solution)/shard_map/ppermute | solution.py:48
  20.9 21.3 %collective-permute-start.4 = (bf16[256,512]{1,0:T(8,128)(2,1)S(1)}, bf16[256,512]{1,0:T(8,128)(2,1)S(1)}, u32[]{:S(2)}, u32[]{:S(2)}) collective-permute-start(bf16[256,512]{1,0:T(8,128)(2,1)S(1)} %get-tuple-element.34.kv_ref), channel_id=1, source_target_pairs={{0,4},{4,0},{8,12},{12,8},{16,20},{20,16},{24,28},{28,24},{1,5},{5... | collective-permute-start | bytes 786440 | tf_op jit(solution)/shard_map/ppermute | solution.py:37
  22.4 2.6 %copy-start = (bf16[512,5376]{1,0:T(8,128)(2,1)S(1)}, bf16[512,5376]{1,0:T(8,128)(2,1)}, u32[]{:S(2)}) copy-start(bf16[512,5376]{1,0:T(8,128)(2,1)} %w_ref.5) | copy-start | bytes 16515076
  25.0 1.1 %copy-start.4 = (bf16[64,5376]{1,0:T(8,128)(2,1)S(1)}, bf16[64,5376]{1,0:T(8,128)(2,1)}, u32[]{:S(2)}) copy-start(bf16[64,5376]{1,0:T(8,128)(2,1)} %own_ref.1) | copy-start | bytes 2064388
  26.1 9.5 %slice-start = ((s8[5505024]{0:T(1024)(128)(4,1)}), s8[4194304]{0:T(1024)(128)(4,1)S(1)}, s32[]{:S(2)}) async-start(s8[5505024]{0:T(1024)(128)(4,1)} %bitcast), calls=%async_computation | async-start | bytes 8388608
  27.9 7.6 %slice-start.1 = ((s8[5505024]{0:T(1024)(128)(4,1)}), s8[1310720]{0:T(1024)(128)(4,1)S(1)}, s32[]{:S(2)}) async-start(s8[5505024]{0:T(1024)(128)(4,1)} %bitcast), calls=%async_computation.1 | async-start | bytes 2621440
  28.0 7.6 %collective-permute-start.3 = (bf16[256,512]{1,0:T(8,128)(2,1)S(1)}, bf16[256,512]{1,0:T(8,128)(2,1)S(1)}, u32[]{:S(2)}, u32[]{:S(2)}) collective-permute-start(bf16[256,512]{1,0:T(8,128)(2,1)S(1)} %collective-permute-done.r1_ref), channel_id=1, source_target_pairs={{0,4},{4,0},{8,12},{12,8},{16,20},{20,16},{24,28},{28,24},{1,5},{5... | collective-permute-start | bytes 786440 | tf_op jit(solution)/shard_map/ppermute | solution.py:37
  32.9 2.6 %collective-permute-start.7 = (bf16[64,5376]{1,0:T(8,128)(2,1)S(1)}, bf16[64,5376]{1,0:T(8,128)(2,1)S(1)}, u32[]{:S(2)}, u32[]{:S(2)}) collective-permute-start(bf16[64,5376]{1,0:T(8,128)(2,1)S(1)} %collective-permute-done.6.y_ref), channel_id=1, source_target_pairs={{0,1},{1,0},{2,3},{3,2},{4,5},{5,4},{6,7},{7,6},{8,9},{9,8},{10,11... | collective-permute-start | bytes 2064392 | tf_op jit(solution)/shard_map/ppermute | solution.py:37
  33.0 9.3 %copy-start.2 = (bf16[256,512]{1,0:T(8,128)(2,1)S(1)}, bf16[256,512]{1,0:T(8,128)(2,1)}, u32[]{:S(2)}) copy-start(bf16[256,512]{1,0:T(8,128)(2,1)} %q_ref.9) | copy-start | bytes 786436
  33.0 11.2 %collective-permute-start.5 = (bf16[256,512]{1,0:T(8,128)(2,1)S(1)}, bf16[256,512]{1,0:T(8,128)(2,1)S(1)}, u32[]{:S(2)}, u32[]{:S(2)}) collective-permute-start(bf16[256,512]{1,0:T(8,128)(2,1)S(1)} %pick.1), channel_id=1, source_target_pairs={{0,4},{4,0},{8,12},{12,8},{16,20},{20,16},{24,28},{28,24},{1,5},{5... | collective-permute-start | bytes 786440 | tf_op jit(solution)/shard_map/ppermute | solution.py:37
  37.5 10.4 %collective-permute-start.8 = (bf16[256,256]{1,0:T(8,128)(2,1)S(1)}, bf16[256,256]{1,0:T(8,128)(2,1)S(1)}, u32[]{:S(2)}, u32[]{:S(2)}) collective-permute-start(bf16[256,256]{1,0:T(8,128)(2,1)S(1)} %get-tuple-element.46), channel_id=1, source_target_pairs={{0,16},{4,20},{8,24},{12,28},{16,0},{20,4},{24,8},{28,12},{1,17},{... | collective-permute-start | bytes 393224 | tf_op jit(solution)/shard_map/ppermute | solution.py:48
  47.9 2.7 %collective-permute-start.13 = (bf16[64,5376]{1,0:T(8,128)(2,1)S(1)}, bf16[64,5376]{1,0:T(8,128)(2,1)S(1)}, u32[]{:S(2)}, u32[]{:S(2)}) collective-permute-start(bf16[64,5376]{1,0:T(8,128)(2,1)S(1)} %get-tuple-element.58), channel_id=1, source_target_pairs={{0,1},{1,0},{2,3},{3,2},{4,5},{5,4},{6,7},{7,6},{8,9},{9,8},{10,11... | collective-permute-start | bytes 2064392 | tf_op jit(solution)/shard_map/ppermute | solution.py:37
  48.0 12.5 %collective-permute-start.11 = (bf16[256,512]{1,0:T(8,128)(2,1)S(1)}, bf16[256,512]{1,0:T(8,128)(2,1)S(1)}, u32[]{:S(2)}, u32[]{:S(2)}) collective-permute-start(bf16[256,512]{1,0:T(8,128)(2,1)S(1)} %across_grad.1), channel_id=1, source_target_pairs={{0,4},{4,0},{8,12},{12,8},{16,20},{20,16},{24,28},{28,24},{1,5},{5... | collective-permute-start | bytes 786440 | tf_op jit(solution)/shard_map/ppermute | solution.py:37
  50.5 9.3 %collective-permute-start.9 = (bf16[304,256]{1,0:T(8,128)(2,1)S(1)}, bf16[304,256]{1,0:T(8,128)(2,1)S(1)}, u32[]{:S(2)}, u32[]{:S(2)}) collective-permute-start(bf16[304,256]{1,0:T(8,128)(2,1)S(1)} %get-tuple-element.49), channel_id=1, source_target_pairs={{0,16},{4,20},{8,24},{12,28},{16,0},{20,4},{24,8},{28,12},{1,17},{... | collective-permute-start | bytes 466952 | tf_op jit(solution)/shard_map/ppermute | solution.py:48
  50.7 20.0 %collective-permute-start.15 = (bf16[64,5376]{1,0:T(8,128)(2,1)S(1)}, bf16[64,5376]{1,0:T(8,128)(2,1)S(1)}, u32[]{:S(2)}, u32[]{:S(2)}) collective-permute-start(bf16[64,5376]{1,0:T(8,128)(2,1)S(1)} %far_sum.1), channel_id=1, source_target_pairs={{0,2},{1,3},{2,0},{3,1},{4,6},{5,7},{6,4},{7,5},{8,10},{9,11},{10,... | collective-permute-start | bytes 2064392 | tf_op jit(solution)/shard_map/ppermute | solution.py:37
  51.3 19.4 %collective-permute-start.14 = (bf16[64,5376]{1,0:T(8,128)(2,1)S(1)}, bf16[64,5376]{1,0:T(8,128)(2,1)S(1)}, u32[]{:S(2)}, u32[]{:S(2)}) collective-permute-start(bf16[64,5376]{1,0:T(8,128)(2,1)S(1)} %get-tuple-element.59), channel_id=1, source_target_pairs={{0,1},{1,0},{2,3},{3,2},{4,5},{5,4},{6,7},{7,6},{8,9},{9,8},{10,11... | collective-permute-start | bytes 2064392 | tf_op jit(solution)/shard_map/ppermute | solution.py:37
  59.9 9.4 %collective-permute-start.10 = (bf16[304,512]{1,0:T(8,128)(2,1)S(1)}, bf16[304,512]{1,0:T(8,128)(2,1)S(1)}, u32[]{:S(2)}, u32[]{:S(2)}) collective-permute-start(bf16[304,512]{1,0:T(8,128)(2,1)S(1)} %pair.1), channel_id=1, source_target_pairs={{0,4},{4,0},{8,12},{12,8},{16,20},{20,16},{24,28},{28,24},{1,5},{5... | collective-permute-start | bytes 933896 | tf_op jit(solution)/shard_map/ppermute | solution.py:37
  60.5 10.2 %collective-permute-start.12 = (bf16[256,512]{1,0:T(8,128)(2,1)S(1)}, bf16[256,512]{1,0:T(8,128)(2,1)S(1)}, u32[]{:S(2)}, u32[]{:S(2)}) collective-permute-start(bf16[256,512]{1,0:T(8,128)(2,1)S(1)} %hop_sum.1), channel_id=1, source_target_pairs={{8,0},{12,4},{16,8},{20,12},{24,16},{28,20},{9,1},{13,5},{17,9},{2... | collective-permute-start | bytes 786440 | tf_op jit(solution)/shard_map/ppermute | solution.py:32

commit v10 on v8

--- a/solution.py
+++ b/solution.py
@@ -336,16 +336,16 @@
     def gate(value, *others):
         return lax.optimization_barrier((value, *others))[0]
 
-    og_y = swapped(out_grad, "head", 2)
     kv = call(join_kernel, "join", block, [], keys, values)
     far_sent = call(functools.partial(either_kernel, is_lower), "far_sent", block, [], kv, queries)
     r1 = shifted(kv, 2)
     r2, q_far = far_swapped(lambda: kv, lambda: queries) if lax.axis_size("seq") > 2 * FAR else (far_swapped(*[lambda: far_sent] * 2))
-    p0 = swapped(kv, "seq", 1)
     og_c = swapped(out_grad, "head", 1)
+    og_y = swapped(out_grad, "head", 2)
+    p0 = swapped(gate(kv, far_sent), "seq", 1)
     half_grad = jax.ShapeDtypeStruct((tok // 2, q_cols), BF16)
     grad_near = call(near_back_kernel, "near_back", half_grad, [], out_grad, og_c, out_weight, cost=LARGE)
-    x1 = swapped(gate(r1, p0, grad_near), "seq", 1)
+    x1 = swapped(gate(r1, grad_near), "seq", 1)
     x2 = swapped(call(functools.partial(either_kernel, is_odd), "pick", block, [], r2, q_far, cost=LARGE), "seq", 1)
     og_yc = swapped(gate(og_y, r2, grad_near), "head", 1)
     first = jax.ShapeDtypeStruct((tok, q_cols // 2), BF16)
@@ -367,7 +367,7 @@
             jax.ShapeDtypeStruct((kv_heads, HEAD_SIZE, 2 * tok), F32),
         ),
         [],
-        queries, kv, r1, r2, x1,
+        queries, kv, gate(r1, p0), r2, x1,
     )
     attended, probs, stats, sent_second = call(
         forward_kernel,
@@ -381,13 +381,13 @@
         [],
         queries, p0, x2, *early, grad_near, grad_far,
     )
-    t_x = call(across_kernel, "across_grad", block, [], queries, x1, probs, stats, grad_near, grad_far)
-    d1 = swapped(t_x, "seq", 1)
     far_second = down(sent_second)
     near_own, near_core, far_own, far_core = call(
-        project_kernel, "project", (rows,) * 4, [], gate(attended, t_x), out_weight
+        project_kernel, "project", (rows,) * 4, [], attended, out_weight
     )
     sent = swapped(gate(far_core, far_first), "head", 1)
+    t_x = call(across_kernel, "across_grad", block, [], queries, x1, probs, stats, grad_near, gate(grad_far, far_core))
+    d1 = swapped(t_x, "seq", 1)
     far_sum = call(sum_kernel, "far_sum", rows, [], far_own, sent)
     from_y = swapped(far_sum, "head", 2)
 

time: 63.3 us -> 63.6 us (level)
  starting transfers between devices: 21.5 us -> 25.1 us
  waiting for transfers between devices: 18.5 us -> 15.2 us
    ppermute x3, waiting for transfers between devices: 9.95 us -> 7.07 us  [far_swapped(): lax.ppermute(lower() if lower is upper else jnp.where(side == r, lower(),...]
    ppermute x11, starting transfers between devices: 9.55 us -> 11.4 us  [swapped(): return lax.ppermute(value, axis, [(i, i ^ bit) for i in range(count)])]
    ppermute x3, starting transfers between devices: 7.13 us -> 8.91 us  [far_swapped(): lax.ppermute(lower() if lower is upper else jnp.where(side == r, lower(),...]
  transfers between devices with their start and end apart: 16 -> 16, of which waited for: 9 -> 5; matrix products, arithmetic and copies ran while one was open for 0% -> 0% of each run, Pallas kernels for 23% -> 23%
where the time goes in v10:
time: 63.6 us; the launch traced here: 63.3 us
  starting transfers between devices  25.1 us (39%)
  Pallas kernels  15.8 us (25%)
  waiting for transfers between devices  15.2 us (24%)
  local copies, waits for them, and re-layouts  6.43 us (10%)
  between operations  0.8 us (1%)
    pallas_call x15, Pallas kernels, call(): pl.pallas_call(kernel, out_shape=outs, in_specs=[VMEM] * len(operands), o...  15.8 us
    ppermute x11, starting transfers between devices, swapped(): return lax.ppermute(value, axis, [(i, i ^ bit) for i in range(count)])  11.4 us
    ppermute x3, starting transfers between devices, far_swapped(): lax.ppermute(lower() if lower is upper else jnp.where(side == r, lower(),...  8.91 us
    ppermute x11, waiting for transfers between devices, swapped(): return lax.ppermute(value, axis, [(i, i ^ bit) for i in range(count)])  7.52 us
    ppermute x3, waiting for transfers between devices, far_swapped(): lax.ppermute(lower() if lower is upper else jnp.where(side == r, lower(),...  7.07 us
    unnamed x16, local copies, waits for them, and re-layouts  6.43 us
    ppermute x2, starting transfers between devices, shifted(): lax.ppermute(value, 'seq', [(i, i + steps) for i in range(first, last)])  4.79 us
  transfers between devices with their start and end apart: 16, of which 5 were waited for; matrix products, arithmetic and copies ran while one was open for 0% of the time, Pallas kernels for 23%

profile of v10, /device:TPU:0, one launch (start us, length us, event | category | flops | bytes accessed | tf_op | source)
XLA Modules:
  0.0 63.3 jit_solution(3769842087053661144)
XLA Ops:
  0.6 0.5 collective-permute-start.2
  1.1 2.6 %collective-permute-start.6 = (bf16[64,5376]{1,0:T(8,128)(2,1)}, bf16[64,5376]{1,0:T(8,128)(2,1)S(1)}, u32[]{:S(2)}, u32[]{:S(2)}) collective-permute-start(bf16[64,5376]{1,0:T(8,128)(2,1)} %own_ref.1), channel_id=1, source_target_pairs={{0,2},{1,3},{2,0},{3,1},{4,6},{5,7},{6,4},{7,5},{8,10},{9,11},{10,... | collective-permute-start | bytes 2064392 | tf_op jit(solution)/shard_map/ppermute | solution.py:37
  3.7 0.0 copy-start.3
  3.7 0.9 %copy-done.3 = bf16[256,256]{1,0:T(8,128)(2,1)S(1)} copy-done((bf16[256,256]{1,0:T(8,128)(2,1)S(1)}, bf16[256,256]{1,0:T(8,128)(2,1)}, u32[]{:S(2)}) %copy-start.3) | copy-done | bytes 131096
  4.6 0.0 copy-start.4
  4.7 0.9 %copy-done.4 = bf16[256,256]{1,0:T(8,128)(2,1)S(1)} copy-done((bf16[256,256]{1,0:T(8,128)(2,1)S(1)}, bf16[256,256]{1,0:T(8,128)(2,1)}, u32[]{:S(2)}) %copy-start.4) | copy-done | bytes 131096
  5.6 3.5 %collective-permute-start = (bf16[256,512]{1,0:T(8,128)(2,1)S(1)}, bf16[256,512]{1,0:T(8,128)(2,1)S(1)}, u32[]{:S(2)}, u32[]{:S(2)}) collective-permute-start(bf16[256,512]{1,0:T(8,128)(2,1)S(1)} %join.1.a_ref.kv_ref), channel_id=1, source_target_pairs={{0,8},{4,12},{8,16},{12,20},{16,24},{20,28},{1,9},{5,13},{9,17},{1... | collective-permute-start | bytes 786440 | tf_op jit(solution)/shard_map/ppermute | solution.py:32
  9.1 0.0 copy-start.1
  9.1 0.9 %copy-done.1 = bf16[256,512]{1,0:T(8,128)(2,1)S(1)} copy-done((bf16[256,512]{1,0:T(8,128)(2,1)S(1)}, bf16[256,512]{1,0:T(8,128)(2,1)}, u32[]{:S(2)}) %copy-start.1) | copy-done | bytes 262168
  10.1 2.6 %collective-permute-start.1 = (bf16[256,512]{1,0:T(8,128)(2,1)S(1)}, bf16[256,512]{1,0:T(8,128)(2,1)S(1)}, u32[]{:S(2)}, u32[]{:S(2)}) collective-permute-start(bf16[256,512]{1,0:T(8,128)(2,1)S(1)} %far_sent.1), channel_id=1, source_target_pairs={{0,16},{4,20},{8,24},{12,28},{16,0},{20,4},{24,8},{28,12},{1,17},{... | collective-permute-start | bytes 786440 | tf_op jit(solution)/shard_map/ppermute | solution.py:48
  12.7 1.5 %collective-permute-start.4 = (bf16[256,512]{1,0:T(8,128)(2,1)S(1)}, bf16[256,512]{1,0:T(8,128)(2,1)S(1)}, u32[]{:S(2)}, u32[]{:S(2)}) collective-permute-start(bf16[256,512]{1,0:T(8,128)(2,1)S(1)} %join.1.a_ref.kv_ref), channel_id=1, source_target_pairs={{0,4},{4,0},{8,12},{12,8},{16,20},{20,16},{24,28},{28,24},{1,5},{5... | collective-permute-start | bytes 786440 | tf_op jit(solution)/shard_map/ppermute | solution.py:37
  14.2 0.0 collective-permute-done.2.core_ref
  14.2 0.0 copy-start
  14.2 2.6 %copy-done = bf16[512,5376]{1,0:T(8,128)(2,1)S(1)} copy-done((bf16[512,5376]{1,0:T(8,128)(2,1)S(1)}, bf16[512,5376]{1,0:T(8,128)(2,1)}, u32[]{:S(2)}) %copy-start) | copy-done | bytes 5505048
  16.8 0.0 copy-start.5
  16.8 1.1 %copy-done.5 = bf16[64,5376]{1,0:T(8,128)(2,1)S(1)} copy-done((bf16[64,5376]{1,0:T(8,128)(2,1)S(1)}, bf16[64,5376]{1,0:T(8,128)(2,1)}, u32[]{:S(2)}) %copy-start.5) | copy-done | bytes 688152
  17.9 0.0 slice-start
  17.9 1.9 %near_back.1.near_ref.dn_ref = bf16[128,512]{1,0:T(8,128)(2,1)S(1)} custom-call(bf16[64,5376]{1,0:T(8,128)(2,1)S(1)} %copy-done.5, bf16[64,5376]{1,0:T(8,128)(2,1)S(1)} %collective-permute-done.2.core_ref, bf16[512,5376]{1,0:T(8,128)(2,1)S(1)} %copy-done), custom_call_target="tpu_custom_call" | custom-call | flops 10000000000 | bytes 1 | tf_op jit(solution)/shard_map/near_back/pallas_call | solution.py:325
  19.8 0.0 slice-start.1
  19.8 0.0 collective-permute-done.r1_ref
  19.8 0.6 collective-permute-start.3
  20.4 4.4 %collective-permute-done.1.a_ref.b_ref.r2_ref.qf_ref = bf16[256,512]{1,0:T(8,128)(2,1)S(1)} collective-permute-done((bf16[256,512]{1,0:T(8,128)(2,1)S(1)}, bf16[256,512]{1,0:T(8,128)(2,1)S(1)}, u32[]{:S(2)}, u32[]{:S(2)}) %collective-permute-start.1) | collective-permute-done | bytes 262176 | tf_op jit(solution)/shard_map/ppermute | solution.py:48
  24.8 0.0 collective-permute-done.6.y_ref
  24.8 0.0 collective-permute-start.7
  24.8 0.0 copy-start.2
  24.8 1.6 %collective-permute-start.5 = (bf16[256,512]{1,0:T(8,128)(2,1)S(1)}, bf16[256,512]{1,0:T(8,128)(2,1)S(1)}, u32[]{:S(2)}, u32[]{:S(2)}) collective-permute-start(bf16[256,512]{1,0:T(8,128)(2,1)S(1)} %pick.1), channel_id=1, source_target_pairs={{0,4},{4,0},{8,12},{12,8},{16,20},{20,16},{24,28},{28,24},{1,5},{5... | collective-permute-start | bytes 786440 | tf_op jit(solution)/shard_map/ppermute | solution.py:37
  26.4 1.0 %collective-permute-done.3.x1_ref = bf16[256,512]{1,0:T(8,128)(2,1)S(1)} collective-permute-done((bf16[256,512]{1,0:T(8,128)(2,1)S(1)}, bf16[256,512]{1,0:T(8,128)(2,1)S(1)}, u32[]{:S(2)}, u32[]{:S(2)}) %collective-permute-start.3) | collective-permute-done | bytes 262176 | tf_op jit(solution)/shard_map/ppermute | solution.py:37
  27.4 0.0 collective-permute-done.7.yc_ref
  27.4 0.0 slice-done
  27.4 0.0 slice-done.1
  27.4 1.9 %far_back.1 = (bf16[128,512]{1,0:T(8,128)(2,1)S(1)}, bf16[256,256]{1,0:T(8,128)(2,1)S(1)}) custom-call(bf16[64,5376]{1,0:T(8,128)(2,1)S(1)} %collective-permute-done.6.y_ref, bf16[64,5376]{1,0:T(8,128)(2,1)S(1)} %collective-permute-done.7.yc_ref, bf16[512,5376]{1,0:T(8,128)(2,1)S(1)} %bitcast.1, bf16[128,512]{1,0:T(8,128)(2,1)S(1)} %near_back.1.near_ref.dn_ref), custom_call_target="tpu_custom_call" | custom-call | flops 10000000000 | bytes 1 | tf_op jit(solution)/shard_map/far_back/pallas_call | solution.py:325
  29.3 5.5 %collective-permute-start.8 = (bf16[256,256]{1,0:T(8,128)(2,1)S(1)}, bf16[256,256]{1,0:T(8,128)(2,1)S(1)}, u32[]{:S(2)}, u32[]{:S(2)}) collective-permute-start(bf16[256,256]{1,0:T(8,128)(2,1)S(1)} %get-tuple-element.44), channel_id=1, source_target_pairs={{0,16},{4,20},{8,24},{12,28},{16,0},{20,4},{24,8},{28,12},{1,17},{... | collective-permute-start | bytes 393224 | tf_op jit(solution)/shard_map/ppermute | solution.py:48
  34.8 0.0 collective-permute-done.4.p0_ref
  34.8 0.0 copy-done.2
  34.8 2.0 %attend_early.1 = (f32[2,4,256,512]{3,2,1,0:T(8,128)S(1)}, f32[8,512]{1,0:T(8,128)S(1)}, f32[2,128,512]{2,1,0:T(8,128)S(1)}) custom-call(bf16[256,512]{1,0:T(8,128)(2,1)S(1)} %copy-done.2, bf16[256,512]{1,0:T(8,128)(2,1)S(1)} %join.1.a_ref.kv_ref, bf16[256,512]{1,0:T(8,128)(2,1)S(1)} %collective-permute-done.r1_ref, ...), custom_call_target="tpu_custom_call" | custom-call | flops 1 | bytes 1 | tf_op jit(solution)/shard_map/attend_early/pallas_call | solution.py:325
  36.8 0.0 collective-permute-done.5.x2_ref.qx_ref
  36.8 1.4 %attend.1 = (bf16[256,512]{1,0:T(8,128)(2,1)S(1)}, bf16[2,5,256,512]{3,2,1,0:T(8,128)(2,1)S(1)}, f32[8,512]{1,0:T(8,128)S(1)}, bf16[304,256]{1,0:T(8,128)(2,1)S(1)}) custom-call(bf16[256,512]{1,0:T(8,128)(2,1)S(1)} %copy-done.2, bf16[256,512]{1,0:T(8,128)(2,1)S(1)} %collective-permute-done.4.p0_ref, ...), custom_call_target="tpu_custom_call" | custom-call | flops 1 | bytes 1 | tf_op jit(solution)/shard_map/attend/pallas_call | solution.py:325
  38.3 1.6 %project.1 = (bf16[64,5376]{1,0:T(8,128)(2,1)S(1)}, bf16[64,5376]{1,0:T(8,128)(2,1)S(1)}, bf16[64,5376]{1,0:T(8,128)(2,1)S(1)}, bf16[64,5376]{1,0:T(8,128)(2,1)S(1)}) custom-call(bf16[256,512]{1,0:T(8,128)(2,1)S(1)} %get-tuple-element.50.o_ref, bf16[512,5376]{1,0:T(8,128)(2,1)S(1)} %bitcast.1), custom_call_target="tpu_custom_call" | custom-call | flops 1 | bytes 1 | tf_op jit(solution)/shard_map/project/pallas_call | solution.py:325
  39.9 0.0 collective-permute-done.8.a_ref.af_ref
  39.9 0.1 collective-permute-start.13
  40.0 0.8 %collective-permute-start.9 = (bf16[304,256]{1,0:T(8,128)(2,1)S(1)}, bf16[304,256]{1,0:T(8,128)(2,1)S(1)}, u32[]{:S(2)}, u32[]{:S(2)}) collective-permute-start(bf16[304,256]{1,0:T(8,128)(2,1)S(1)} %get-tuple-element.47), channel_id=1, source_target_pairs={{0,16},{4,20},{8,24},{12,28},{16,0},{20,4},{24,8},{28,12},{1,17},{... | collective-permute-start | bytes 466952 | tf_op jit(solution)/shard_map/ppermute | solution.py:48
  40.8 0.6 across_grad.1
  41.3 2.4 %collective-permute-start.11 = (bf16[256,512]{1,0:T(8,128)(2,1)S(1)}, bf16[256,512]{1,0:T(8,128)(2,1)S(1)}, u32[]{:S(2)}, u32[]{:S(2)}) collective-permute-start(bf16[256,512]{1,0:T(8,128)(2,1)S(1)} %across_grad.1), channel_id=1, source_target_pairs={{0,4},{4,0},{8,12},{12,8},{16,20},{20,16},{24,28},{28,24},{1,5},{5... | collective-permute-start | bytes 786440 | tf_op jit(solution)/shard_map/ppermute | solution.py:37
  43.8 0.0 collective-permute-done.13.refs_1_
  43.8 0.2 far_sum.1
  43.9 0.6 collective-permute-start.15
  44.5 0.0 collective-permute-start.14
  44.5 3.4 %attend_grad.1 = (bf16[256,512]{1,0:T(8,128)(2,1)}, f32[256,512]{1,0:T(8,128)S(1)}, bf16[256,512]{1,0:T(8,128)(2,1)S(1)}, bf16[256,512]{1,0:T(8,128)(2,1)S(1)}) custom-call(bf16[256,512]{1,0:T(8,128)(2,1)S(1)} %copy-done.2, bf16[256,512]{1,0:T(8,128)(2,1)S(1)} %join.1.a_ref.kv_ref, bf16[256,512]{1,0:T(8,128)(2,1)S(1)} %collective-permute-done.r1_ref, ...), custom_call_target="tpu_custom_call" | custom-call | flops 10000000000 | bytes 1 | tf_op jit(solution)/shard_map/attend_grad/pallas_call | solution.py:325
  47.9 2.7 %collective-permute-done.9.b_ref.bf_ref = bf16[304,256]{1,0:T(8,128)(2,1)S(1)} collective-permute-done((bf16[304,256]{1,0:T(8,128)(2,1)S(1)}, bf16[304,256]{1,0:T(8,128)(2,1)S(1)}, u32[]{:S(2)}, u32[]{:S(2)}) %collective-permute-start.9) | collective-permute-done | bytes 155680 | tf_op jit(solution)/shard_map/ppermute | solution.py:48
  50.6 1.5 %collective-permute-start.10 = (bf16[304,512]{1,0:T(8,128)(2,1)S(1)}, bf16[304,512]{1,0:T(8,128)(2,1)S(1)}, u32[]{:S(2)}, u32[]{:S(2)}) collective-permute-start(bf16[304,512]{1,0:T(8,128)(2,1)S(1)} %pair.1), channel_id=1, source_target_pairs={{0,4},{4,0},{8,12},{12,8},{16,20},{20,16},{24,28},{28,24},{1,5},{5... | collective-permute-start | bytes 933896 | tf_op jit(solution)/shard_map/ppermute | solution.py:37
  52.2 0.0 collective-permute-done.11.refs_1_
  52.2 0.1 hop_sum.1
  52.2 1.3 %collective-permute-start.12 = (bf16[256,512]{1,0:T(8,128)(2,1)S(1)}, bf16[256,512]{1,0:T(8,128)(2,1)S(1)}, u32[]{:S(2)}, u32[]{:S(2)}) collective-permute-start(bf16[256,512]{1,0:T(8,128)(2,1)S(1)} %hop_sum.1), channel_id=1, source_target_pairs={{8,0},{12,4},{16,8},{20,12},{24,16},{28,20},{9,1},{13,5},{17,9},{2... | collective-permute-start | bytes 786440 | tf_op jit(solution)/shard_map/ppermute | solution.py:32
  53.5 6.5 %collective-permute-done.10.px_ref.pair_ref = bf16[304,512]{1,0:T(8,128)(2,1)S(1)} collective-permute-done((bf16[304,512]{1,0:T(8,128)(2,1)S(1)}, bf16[304,512]{1,0:T(8,128)(2,1)S(1)}, u32[]{:S(2)}, u32[]{:S(2)}) %collective-permute-start.10) | collective-permute-done | bytes 311328 | tf_op jit(solution)/shard_map/ppermute | solution.py:37
  60.0 1.5 %far_grad.1.far_ref = f32[256,512]{1,0:T(8,128)S(1)} custom-call(bf16[256,512]{1,0:T(8,128)(2,1)S(1)} %join.1.a_ref.kv_ref, bf16[256,512]{1,0:T(8,128)(2,1)S(1)} %collective-permute-done.1.a_ref.b_ref.r2_ref.qf_ref, bf16[256,256]{1,0:T(8,128)(2,1)S(1)} %collective-permute-done.8.a_ref.af_ref, bf16[304,256]{1,0:T(8,128)(2,1)S(1)} %collective-permute-done.9.b_ref.bf_ref, ...), custom_call_target="tpu_custom_call" | custom-call | flops 100000000 | bytes 1 | tf_op jit(solution)/shard_map/far_grad/pallas_call | solution.py:325
  61.5 0.6 %collective-permute-done.12.hop_ref = bf16[256,512]{1,0:T(8,128)(2,1)S(1)} collective-permute-done((bf16[256,512]{1,0:T(8,128)(2,1)S(1)}, bf16[256,512]{1,0:T(8,128)(2,1)S(1)}, u32[]{:S(2)}, u32[]{:S(2)}) %collective-permute-start.12) | collective-permute-done | bytes 262176 | tf_op jit(solution)/shard_map/ppermute | solution.py:32
  62.1 0.0 collective-permute-done.14.core_ref
  62.1 0.0 collective-permute-done.15.y_ref
  62.1 1.2 %closing.1 = (bf16[256,256]{1,0:T(8,128)(2,1)}, bf16[256,256]{1,0:T(8,128)(2,1)}, bf16[64,5376]{1,0:T(8,128)(2,1)}) custom-call(f32[256,512]{1,0:T(8,128)S(1)} %get-tuple-element.46.own_ref, f32[256,512]{1,0:T(8,128)S(1)} %far_grad.1.far_ref, bf16[256,512]{1,0:T(8,128)(2,1)S(1)} %collective-permute-done.12.hop_ref, ...), custom_call_target="tpu_custom_call" | custom-call | flops 1 | bytes 1 | tf_op jit(solution)/shard_map/closing/pallas_call | solution.py:325
  (5 shorter events, 0.1 us)
Async XLA Ops:
  0.6 13.6 %collective-permute-start.2 = (bf16[64,5376]{1,0:T(8,128)(2,1)}, bf16[64,5376]{1,0:T(8,128)(2,1)S(1)}, u32[]{:S(2)}, u32[]{:S(2)}) collective-permute-start(bf16[64,5376]{1,0:T(8,128)(2,1)} %own_ref.1), channel_id=1, source_target_pairs={{0,1},{1,0},{2,3},{3,2},{4,5},{5,4},{6,7},{7,6},{8,9},{9,8},{10,11... | collective-permute-start | bytes 2064392 | tf_op jit(solution)/shard_map/ppermute | solution.py:37
  1.1 23.6 %collective-permute-start.6 = (bf16[64,5376]{1,0:T(8,128)(2,1)}, bf16[64,5376]{1,0:T(8,128)(2,1)S(1)}, u32[]{:S(2)}, u32[]{:S(2)}) collective-permute-start(bf16[64,5376]{1,0:T(8,128)(2,1)} %own_ref.1), channel_id=1, source_target_pairs={{0,2},{1,3},{2,0},{3,1},{4,6},{5,7},{6,4},{7,5},{8,10},{9,11},{10,... | collective-permute-start | bytes 2064392 | tf_op jit(solution)/shard_map/ppermute | solution.py:37
  3.7 0.9 %copy-start.3 = (bf16[256,256]{1,0:T(8,128)(2,1)S(1)}, bf16[256,256]{1,0:T(8,128)(2,1)}, u32[]{:S(2)}) copy-start(bf16[256,256]{1,0:T(8,128)(2,1)} %k_ref.1) | copy-start | bytes 393220
  4.6 0.9 %copy-start.4 = (bf16[256,256]{1,0:T(8,128)(2,1)S(1)}, bf16[256,256]{1,0:T(8,128)(2,1)}, u32[]{:S(2)}) copy-start(bf16[256,256]{1,0:T(8,128)(2,1)} %v_ref.1) | copy-start | bytes 393220
  5.6 14.2 %collective-permute-start = (bf16[256,512]{1,0:T(8,128)(2,1)S(1)}, bf16[256,512]{1,0:T(8,128)(2,1)S(1)}, u32[]{:S(2)}, u32[]{:S(2)}) collective-permute-start(bf16[256,512]{1,0:T(8,128)(2,1)S(1)} %join.1.a_ref.kv_ref), channel_id=1, source_target_pairs={{0,8},{4,12},{8,16},{12,20},{16,24},{20,28},{1,9},{5,13},{9,17},{1... | collective-permute-start | bytes 786440 | tf_op jit(solution)/shard_map/ppermute | solution.py:32
  9.1 1.0 %copy-start.1 = (bf16[256,512]{1,0:T(8,128)(2,1)S(1)}, bf16[256,512]{1,0:T(8,128)(2,1)}, u32[]{:S(2)}) copy-start(bf16[256,512]{1,0:T(8,128)(2,1)} %q_ref.7) | copy-start | bytes 786436
  10.1 14.7 %collective-permute-start.1 = (bf16[256,512]{1,0:T(8,128)(2,1)S(1)}, bf16[256,512]{1,0:T(8,128)(2,1)S(1)}, u32[]{:S(2)}, u32[]{:S(2)}) collective-permute-start(bf16[256,512]{1,0:T(8,128)(2,1)S(1)} %far_sent.1), channel_id=1, source_target_pairs={{0,16},{4,20},{8,24},{12,28},{16,0},{20,4},{24,8},{28,12},{1,17},{... | collective-permute-start | bytes 786440 | tf_op jit(solution)/shard_map/ppermute | solution.py:48
  12.7 22.1 %collective-permute-start.4 = (bf16[256,512]{1,0:T(8,128)(2,1)S(1)}, bf16[256,512]{1,0:T(8,128)(2,1)S(1)}, u32[]{:S(2)}, u32[]{:S(2)}) collective-permute-start(bf16[256,512]{1,0:T(8,128)(2,1)S(1)} %join.1.a_ref.kv_ref), channel_id=1, source_target_pairs={{0,4},{4,0},{8,12},{12,8},{16,20},{20,16},{24,28},{28,24},{1,5},{5... | collective-permute-start | bytes 786440 | tf_op jit(solution)/shard_map/ppermute | solution.py:37
  14.2 2.6 %copy-start = (bf16[512,5376]{1,0:T(8,128)(2,1)S(1)}, bf16[512,5376]{1,0:T(8,128)(2,1)}, u32[]{:S(2)}) copy-start(bf16[512,5376]{1,0:T(8,128)(2,1)} %w_ref.5) | copy-start | bytes 16515076
  16.8 1.1 %copy-start.5 = (bf16[64,5376]{1,0:T(8,128)(2,1)S(1)}, bf16[64,5376]{1,0:T(8,128)(2,1)}, u32[]{:S(2)}) copy-start(bf16[64,5376]{1,0:T(8,128)(2,1)} %own_ref.1) | copy-start | bytes 2064388
  17.9 9.5 %slice-start = ((s8[5505024]{0:T(1024)(128)(4,1)}), s8[4194304]{0:T(1024)(128)(4,1)S(1)}, s32[]{:S(2)}) async-start(s8[5505024]{0:T(1024)(128)(4,1)} %bitcast), calls=%async_computation | async-start | bytes 8388608
  19.8 7.6 %slice-start.1 = ((s8[5505024]{0:T(1024)(128)(4,1)}), s8[1310720]{0:T(1024)(128)(4,1)S(1)}, s32[]{:S(2)}) async-start(s8[5505024]{0:T(1024)(128)(4,1)} %bitcast), calls=%async_computation.1 | async-start | bytes 2621440
  19.8 7.6 %collective-permute-start.3 = (bf16[256,512]{1,0:T(8,128)(2,1)S(1)}, bf16[256,512]{1,0:T(8,128)(2,1)S(1)}, u32[]{:S(2)}, u32[]{:S(2)}) collective-permute-start(bf16[256,512]{1,0:T(8,128)(2,1)S(1)} %collective-permute-done.r1_ref), channel_id=1, source_target_pairs={{0,4},{4,0},{8,12},{12,8},{16,20},{20,16},{24,28},{28,24},{1,5},{5... | collective-permute-start | bytes 786440 | tf_op jit(solution)/shard_map/ppermute | solution.py:37
  24.8 2.6 %collective-permute-start.7 = (bf16[64,5376]{1,0:T(8,128)(2,1)S(1)}, bf16[64,5376]{1,0:T(8,128)(2,1)S(1)}, u32[]{:S(2)}, u32[]{:S(2)}) collective-permute-start(bf16[64,5376]{1,0:T(8,128)(2,1)S(1)} %collective-permute-done.6.y_ref), channel_id=1, source_target_pairs={{0,1},{1,0},{2,3},{3,2},{4,5},{5,4},{6,7},{7,6},{8,9},{9,8},{10,11... | collective-permute-start | bytes 2064392 | tf_op jit(solution)/shard_map/ppermute | solution.py:37
  24.8 10.0 %copy-start.2 = (bf16[256,512]{1,0:T(8,128)(2,1)S(1)}, bf16[256,512]{1,0:T(8,128)(2,1)}, u32[]{:S(2)}) copy-start(bf16[256,512]{1,0:T(8,128)(2,1)} %q_ref.7) | copy-start | bytes 786436
  24.8 12.0 %collective-permute-start.5 = (bf16[256,512]{1,0:T(8,128)(2,1)S(1)}, bf16[256,512]{1,0:T(8,128)(2,1)S(1)}, u32[]{:S(2)}, u32[]{:S(2)}) collective-permute-start(bf16[256,512]{1,0:T(8,128)(2,1)S(1)} %pick.1), channel_id=1, source_target_pairs={{0,4},{4,0},{8,12},{12,8},{16,20},{20,16},{24,28},{28,24},{1,5},{5... | collective-permute-start | bytes 786440 | tf_op jit(solution)/shard_map/ppermute | solution.py:37
  29.3 10.6 %collective-permute-start.8 = (bf16[256,256]{1,0:T(8,128)(2,1)S(1)}, bf16[256,256]{1,0:T(8,128)(2,1)S(1)}, u32[]{:S(2)}, u32[]{:S(2)}) collective-permute-start(bf16[256,256]{1,0:T(8,128)(2,1)S(1)} %get-tuple-element.44), channel_id=1, source_target_pairs={{0,16},{4,20},{8,24},{12,28},{16,0},{20,4},{24,8},{28,12},{1,17},{... | collective-permute-start | bytes 393224 | tf_op jit(solution)/shard_map/ppermute | solution.py:48
  39.9 3.9 %collective-permute-start.13 = (bf16[64,5376]{1,0:T(8,128)(2,1)S(1)}, bf16[64,5376]{1,0:T(8,128)(2,1)S(1)}, u32[]{:S(2)}, u32[]{:S(2)}) collective-permute-start(bf16[64,5376]{1,0:T(8,128)(2,1)S(1)} %get-tuple-element.56), channel_id=1, source_target_pairs={{0,1},{1,0},{2,3},{3,2},{4,5},{5,4},{6,7},{7,6},{8,9},{9,8},{10,11... | collective-permute-start | bytes 2064392 | tf_op jit(solution)/shard_map/ppermute | solution.py:37
  40.0 10.6 %collective-permute-start.9 = (bf16[304,256]{1,0:T(8,128)(2,1)S(1)}, bf16[304,256]{1,0:T(8,128)(2,1)S(1)}, u32[]{:S(2)}, u32[]{:S(2)}) collective-permute-start(bf16[304,256]{1,0:T(8,128)(2,1)S(1)} %get-tuple-element.47), channel_id=1, source_target_pairs={{0,16},{4,20},{8,24},{12,28},{16,0},{20,4},{24,8},{28,12},{1,17},{... | collective-permute-start | bytes 466952 | tf_op jit(solution)/shard_map/ppermute | solution.py:48
  41.3 10.8 %collective-permute-start.11 = (bf16[256,512]{1,0:T(8,128)(2,1)S(1)}, bf16[256,512]{1,0:T(8,128)(2,1)S(1)}, u32[]{:S(2)}, u32[]{:S(2)}) collective-permute-start(bf16[256,512]{1,0:T(8,128)(2,1)S(1)} %across_grad.1), channel_id=1, source_target_pairs={{0,4},{4,0},{8,12},{12,8},{16,20},{20,16},{24,28},{28,24},{1,5},{5... | collective-permute-start | bytes 786440 | tf_op jit(solution)/shard_map/ppermute | solution.py:37
  43.9 18.2 %collective-permute-start.15 = (bf16[64,5376]{1,0:T(8,128)(2,1)S(1)}, bf16[64,5376]{1,0:T(8,128)(2,1)S(1)}, u32[]{:S(2)}, u32[]{:S(2)}) collective-permute-start(bf16[64,5376]{1,0:T(8,128)(2,1)S(1)} %far_sum.1), channel_id=1, source_target_pairs={{0,2},{1,3},{2,0},{3,1},{4,6},{5,7},{6,4},{7,5},{8,10},{9,11},{10,... | collective-permute-start | bytes 2064392 | tf_op jit(solution)/shard_map/ppermute | solution.py:37
  44.5 17.6 %collective-permute-start.14 = (bf16[64,5376]{1,0:T(8,128)(2,1)S(1)}, bf16[64,5376]{1,0:T(8,128)(2,1)S(1)}, u32[]{:S(2)}, u32[]{:S(2)}) collective-permute-start(bf16[64,5376]{1,0:T(8,128)(2,1)S(1)} %get-tuple-element.57), channel_id=1, source_target_pairs={{0,1},{1,0},{2,3},{3,2},{4,5},{5,4},{6,7},{7,6},{8,9},{9,8},{10,11... | collective-permute-start | bytes 2064392 | tf_op jit(solution)/shard_map/ppermute | solution.py:37
  50.6 9.4 %collective-permute-start.10 = (bf16[304,512]{1,0:T(8,128)(2,1)S(1)}, bf16[304,512]{1,0:T(8,128)(2,1)S(1)}, u32[]{:S(2)}, u32[]{:S(2)}) collective-permute-start(bf16[304,512]{1,0:T(8,128)(2,1)S(1)} %pair.1), channel_id=1, source_target_pairs={{0,4},{4,0},{8,12},{12,8},{16,20},{20,16},{24,28},{28,24},{1,5},{5... | collective-permute-start | bytes 933896 | tf_op jit(solution)/shard_map/ppermute | solution.py:37
  52.2 9.9 %collective-permute-start.12 = (bf16[256,512]{1,0:T(8,128)(2,1)S(1)}, bf16[256,512]{1,0:T(8,128)(2,1)S(1)}, u32[]{:S(2)}, u32[]{:S(2)}) collective-permute-start(bf16[256,512]{1,0:T(8,128)(2,1)S(1)} %hop_sum.1), channel_id=1, source_target_pairs={{8,0},{12,4},{16,8},{20,12},{24,16},{28,20},{9,1},{13,5},{17,9},{2... | collective-permute-start | bytes 786440 | tf_op jit(solution)/shard_map/ppermute | solution.py:32

commit v11 on v10

--- a/solution.py
+++ b/solution.py
@@ -350,8 +350,8 @@
     og_yc = swapped(gate(og_y, r2, grad_near), "head", 1)
     first = jax.ShapeDtypeStruct((tok, q_cols // 2), BF16)
     second = jax.ShapeDtypeStruct((tok + 3 * PACK, q_cols // 2), BF16)
-    grad_far, sent_first = call(far_back_kernel, "far_back", (half_grad, first), [], gate(og_y, x1), og_yc, out_weight, grad_near,
-                                cost=LARGE)
+    grad_far, sent_first = call(far_back_kernel, "far_back", (half_grad, first), [], og_y, og_yc, out_weight, grad_near,
+                                cost=SMALL)
 
     def down(value):
         return far_swapped(*[lambda: value] * 2)[1]
@@ -368,6 +368,7 @@
         ),
         [],
         queries, kv, gate(r1, p0), r2, x1,
+        cost=SMALL,
     )
     attended, probs, stats, sent_second = call(
         forward_kernel,
@@ -381,13 +382,13 @@
         [],
         queries, p0, x2, *early, grad_near, grad_far,
     )
+    t_x = call(across_kernel, "across_grad", block, [], queries, x1, probs, stats, grad_near, grad_far)
+    d1 = swapped(t_x, "seq", 1)
     far_second = down(sent_second)
     near_own, near_core, far_own, far_core = call(
-        project_kernel, "project", (rows,) * 4, [], attended, out_weight
+        project_kernel, "project", (rows,) * 4, [], gate(attended, t_x), out_weight
     )
     sent = swapped(gate(far_core, far_first), "head", 1)
-    t_x = call(across_kernel, "across_grad", block, [], queries, x1, probs, stats, grad_near, gate(grad_far, far_core))
-    d1 = swapped(t_x, "seq", 1)
     far_sum = call(sum_kernel, "far_sum", rows, [], far_own, sent)
     from_y = swapped(far_sum, "head", 2)
 

time: 63.6 us -> 61.8 us (0.972)
  starting transfers between devices: 25.1 us -> 21.8 us
  waiting for transfers between devices: 15.2 us -> 16.6 us
    ppermute x11, starting transfers between devices: 11.4 us -> 9.55 us  [swapped(): return lax.ppermute(value, axis, [(i, i ^ bit) for i in range(count)])]
    ppermute x3, starting transfers between devices: 8.91 us -> 7.49 us  [far_swapped(): lax.ppermute(lower() if lower is upper else jnp.where(side == r, lower(),...]
    ppermute x11, waiting for transfers between devices: 7.52 us -> 8.68 us  [swapped(): return lax.ppermute(value, axis, [(i, i ^ bit) for i in range(count)])]
    ppermute x3, waiting for transfers between devices: 7.07 us -> 7.96 us  [far_swapped(): lax.ppermute(lower() if lower is upper else jnp.where(side == r, lower(),...]
  transfers between devices with their start and end apart: 16 -> 16, of which waited for: 5 -> 5; matrix products, arithmetic and copies ran while one was open for 0% -> 0% of each run, Pallas kernels for 23% -> 24%
where the time goes in v11:
time: 61.8 us; the launch traced here: 61.5 us
  starting transfers between devices  21.8 us (35%)
  waiting for transfers between devices  16.6 us (27%)
  Pallas kernels  15.8 us (26%)
  local copies, waits for them, and re-layouts  6.43 us (10%)
  between operations  0.81 us (1%)
    pallas_call x15, Pallas kernels, call(): pl.pallas_call(kernel, out_shape=outs, in_specs=[VMEM] * len(operands), o...  15.8 us
    ppermute x11, starting transfers between devices, swapped(): return lax.ppermute(value, axis, [(i, i ^ bit) for i in range(count)])  9.55 us
    ppermute x11, waiting for transfers between devices, swapped(): return lax.ppermute(value, axis, [(i, i ^ bit) for i in range(count)])  8.68 us
    ppermute x3, waiting for transfers between devices, far_swapped(): lax.ppermute(lower() if lower is upper else jnp.where(side == r, lower(),...  7.96 us
    ppermute x3, starting transfers between devices, far_swapped(): lax.ppermute(lower() if lower is upper else jnp.where(side == r, lower(),...  7.49 us
    unnamed x16, local copies, waits for them, and re-layouts  6.43 us
    ppermute x2, starting transfers between devices, shifted(): lax.ppermute(value, 'seq', [(i, i + steps) for i in range(first, last)])  4.79 us
  transfers between devices with their start and end apart: 16, of which 5 were waited for; matrix products, arithmetic and copies ran while one was open for 0% of the time, Pallas kernels for 24%

profile of v11, /device:TPU:0, one launch (start us, length us, event | category | flops | bytes accessed | tf_op | source)
XLA Modules:
  0.0 61.5 jit_solution(2474537296804019394)
XLA Ops:
  0.6 0.5 collective-permute-start.2
  1.1 2.6 %collective-permute-start.6 = (bf16[64,5376]{1,0:T(8,128)(2,1)}, bf16[64,5376]{1,0:T(8,128)(2,1)S(1)}, u32[]{:S(2)}, u32[]{:S(2)}) collective-permute-start(bf16[64,5376]{1,0:T(8,128)(2,1)} %own_ref.1), channel_id=1, source_target_pairs={{0,2},{1,3},{2,0},{3,1},{4,6},{5,7},{6,4},{7,5},{8,10},{9,11},{10,... | collective-permute-start | bytes 2064392 | tf_op jit(solution)/shard_map/ppermute | solution.py:37
  3.7 0.0 copy-start.3
  3.7 0.9 %copy-done.3 = bf16[256,256]{1,0:T(8,128)(2,1)S(1)} copy-done((bf16[256,256]{1,0:T(8,128)(2,1)S(1)}, bf16[256,256]{1,0:T(8,128)(2,1)}, u32[]{:S(2)}) %copy-start.3) | copy-done | bytes 131096
  4.6 0.0 copy-start.4
  4.7 0.9 %copy-done.4 = bf16[256,256]{1,0:T(8,128)(2,1)S(1)} copy-done((bf16[256,256]{1,0:T(8,128)(2,1)S(1)}, bf16[256,256]{1,0:T(8,128)(2,1)}, u32[]{:S(2)}) %copy-start.4) | copy-done | bytes 131096
  5.6 3.5 %collective-permute-start = (bf16[256,512]{1,0:T(8,128)(2,1)S(1)}, bf16[256,512]{1,0:T(8,128)(2,1)S(1)}, u32[]{:S(2)}, u32[]{:S(2)}) collective-permute-start(bf16[256,512]{1,0:T(8,128)(2,1)S(1)} %join.1.a_ref.kv_ref), channel_id=1, source_target_pairs={{0,8},{4,12},{8,16},{12,20},{16,24},{20,28},{1,9},{5,13},{9,17},{1... | collective-permute-start | bytes 786440 | tf_op jit(solution)/shard_map/ppermute | solution.py:32
  9.1 0.0 copy-start.1
  9.1 0.9 %copy-done.1 = bf16[256,512]{1,0:T(8,128)(2,1)S(1)} copy-done((bf16[256,512]{1,0:T(8,128)(2,1)S(1)}, bf16[256,512]{1,0:T(8,128)(2,1)}, u32[]{:S(2)}) %copy-start.1) | copy-done | bytes 262168
  10.1 2.6 %collective-permute-start.1 = (bf16[256,512]{1,0:T(8,128)(2,1)S(1)}, bf16[256,512]{1,0:T(8,128)(2,1)S(1)}, u32[]{:S(2)}, u32[]{:S(2)}) collective-permute-start(bf16[256,512]{1,0:T(8,128)(2,1)S(1)} %far_sent.1), channel_id=1, source_target_pairs={{0,16},{4,20},{8,24},{12,28},{16,0},{20,4},{24,8},{28,12},{1,17},{... | collective-permute-start | bytes 786440 | tf_op jit(solution)/shard_map/ppermute | solution.py:48
  12.7 1.5 %collective-permute-start.4 = (bf16[256,512]{1,0:T(8,128)(2,1)S(1)}, bf16[256,512]{1,0:T(8,128)(2,1)S(1)}, u32[]{:S(2)}, u32[]{:S(2)}) collective-permute-start(bf16[256,512]{1,0:T(8,128)(2,1)S(1)} %join.1.a_ref.kv_ref), channel_id=1, source_target_pairs={{0,4},{4,0},{8,12},{12,8},{16,20},{20,16},{24,28},{28,24},{1,5},{5... | collective-permute-start | bytes 786440 | tf_op jit(solution)/shard_map/ppermute | solution.py:37
  14.2 0.0 collective-permute-done.2.core_ref
  14.2 0.0 copy-start
  14.2 2.6 %copy-done = bf16[512,5376]{1,0:T(8,128)(2,1)S(1)} copy-done((bf16[512,5376]{1,0:T(8,128)(2,1)S(1)}, bf16[512,5376]{1,0:T(8,128)(2,1)}, u32[]{:S(2)}) %copy-start) | copy-done | bytes 5505048
  16.8 0.0 copy-start.5
  16.8 1.1 %copy-done.5 = bf16[64,5376]{1,0:T(8,128)(2,1)S(1)} copy-done((bf16[64,5376]{1,0:T(8,128)(2,1)S(1)}, bf16[64,5376]{1,0:T(8,128)(2,1)}, u32[]{:S(2)}) %copy-start.5) | copy-done | bytes 688152
  17.9 0.0 slice-start
  17.9 1.9 %near_back.1.near_ref.dn_ref = bf16[128,512]{1,0:T(8,128)(2,1)S(1)} custom-call(bf16[64,5376]{1,0:T(8,128)(2,1)S(1)} %copy-done.5, bf16[64,5376]{1,0:T(8,128)(2,1)S(1)} %collective-permute-done.2.core_ref, bf16[512,5376]{1,0:T(8,128)(2,1)S(1)} %copy-done), custom_call_target="tpu_custom_call" | custom-call | flops 10000000000 | bytes 1 | tf_op jit(solution)/shard_map/near_back/pallas_call | solution.py:325
  19.8 0.0 slice-start.1
  19.8 0.0 collective-permute-done.r1_ref
  19.8 0.6 collective-permute-start.3
  20.4 4.4 %collective-permute-done.1.a_ref.b_ref.r2_ref.qf_ref = bf16[256,512]{1,0:T(8,128)(2,1)S(1)} collective-permute-done((bf16[256,512]{1,0:T(8,128)(2,1)S(1)}, bf16[256,512]{1,0:T(8,128)(2,1)S(1)}, u32[]{:S(2)}, u32[]{:S(2)}) %collective-permute-start.1) | collective-permute-done | bytes 262176 | tf_op jit(solution)/shard_map/ppermute | solution.py:48
  24.8 0.0 collective-permute-done.6.y_ref
  24.8 0.0 collective-permute-start.7
  24.8 0.0 copy-start.2
  24.8 1.6 %collective-permute-start.5 = (bf16[256,512]{1,0:T(8,128)(2,1)S(1)}, bf16[256,512]{1,0:T(8,128)(2,1)S(1)}, u32[]{:S(2)}, u32[]{:S(2)}) collective-permute-start(bf16[256,512]{1,0:T(8,128)(2,1)S(1)} %pick.1), channel_id=1, source_target_pairs={{0,4},{4,0},{8,12},{12,8},{16,20},{20,16},{24,28},{28,24},{1,5},{5... | collective-permute-start | bytes 786440 | tf_op jit(solution)/shard_map/ppermute | solution.py:37
  26.4 0.5 collective-permute-done.7.yc_ref
  26.9 0.0 slice-done
  26.9 0.0 slice-done.1
  26.9 1.9 %far_back.1 = (bf16[128,512]{1,0:T(8,128)(2,1)S(1)}, bf16[256,256]{1,0:T(8,128)(2,1)S(1)}) custom-call(bf16[64,5376]{1,0:T(8,128)(2,1)S(1)} %collective-permute-done.6.y_ref, bf16[64,5376]{1,0:T(8,128)(2,1)S(1)} %collective-permute-done.7.yc_ref, bf16[512,5376]{1,0:T(8,128)(2,1)S(1)} %bitcast.1, bf16[128,512]{1,0:T(8,128)(2,1)S(1)} %near_back.1.near_ref.dn_ref), custom_call_target="tpu_custom_call" | custom-call | flops 1 | bytes 1 | tf_op jit(solution)/shard_map/far_back/pallas_call | solution.py:325
  28.8 1.6 %collective-permute-start.8 = (bf16[256,256]{1,0:T(8,128)(2,1)S(1)}, bf16[256,256]{1,0:T(8,128)(2,1)S(1)}, u32[]{:S(2)}, u32[]{:S(2)}) collective-permute-start(bf16[256,256]{1,0:T(8,128)(2,1)S(1)} %get-tuple-element.42), channel_id=1, source_target_pairs={{0,16},{4,20},{8,24},{12,28},{16,0},{20,4},{24,8},{28,12},{1,17},{... | collective-permute-start | bytes 393224 | tf_op jit(solution)/shard_map/ppermute | solution.py:48
  30.4 0.0 collective-permute-done.4.p0_ref
  30.4 0.0 collective-permute-done.3.x1_ref
  30.4 0.0 copy-done.2
  30.4 2.0 %attend_early.1 = (f32[2,4,256,512]{3,2,1,0:T(8,128)S(1)}, f32[8,512]{1,0:T(8,128)S(1)}, f32[2,128,512]{2,1,0:T(8,128)S(1)}) custom-call(bf16[256,512]{1,0:T(8,128)(2,1)S(1)} %copy-done.2, bf16[256,512]{1,0:T(8,128)(2,1)S(1)} %join.1.a_ref.kv_ref, bf16[256,512]{1,0:T(8,128)(2,1)S(1)} %collective-permute-done.r1_ref, ...), custom_call_target="tpu_custom_call" | custom-call | flops 1 | bytes 1 | tf_op jit(solution)/shard_map/attend_early/pallas_call | solution.py:325
  32.5 1.1 %collective-permute-done.5.x2_ref.qx_ref = bf16[256,512]{1,0:T(8,128)(2,1)S(1)} collective-permute-done((bf16[256,512]{1,0:T(8,128)(2,1)S(1)}, bf16[256,512]{1,0:T(8,128)(2,1)S(1)}, u32[]{:S(2)}, u32[]{:S(2)}) %collective-permute-start.5) | collective-permute-done | bytes 262176 | tf_op jit(solution)/shard_map/ppermute | solution.py:37
  33.6 1.5 %attend.1 = (bf16[256,512]{1,0:T(8,128)(2,1)S(1)}, bf16[2,5,256,512]{3,2,1,0:T(8,128)(2,1)S(1)}, f32[8,512]{1,0:T(8,128)S(1)}, bf16[304,256]{1,0:T(8,128)(2,1)S(1)}) custom-call(bf16[256,512]{1,0:T(8,128)(2,1)S(1)} %copy-done.2, bf16[256,512]{1,0:T(8,128)(2,1)S(1)} %collective-permute-done.4.p0_ref, ...), custom_call_target="tpu_custom_call" | custom-call | flops 1 | bytes 1 | tf_op jit(solution)/shard_map/attend/pallas_call | solution.py:325
  35.1 0.6 across_grad.1
  35.6 1.6 %project.1 = (bf16[64,5376]{1,0:T(8,128)(2,1)S(1)}, bf16[64,5376]{1,0:T(8,128)(2,1)S(1)}, bf16[64,5376]{1,0:T(8,128)(2,1)S(1)}, bf16[64,5376]{1,0:T(8,128)(2,1)S(1)}) custom-call(bf16[256,512]{1,0:T(8,128)(2,1)S(1)} %get-tuple-element.49.o_ref, bf16[512,5376]{1,0:T(8,128)(2,1)S(1)} %bitcast.1), custom_call_target="tpu_custom_call" | custom-call | flops 1 | bytes 1 | tf_op jit(solution)/shard_map/project/pallas_call | solution.py:325
  37.2 0.0 collective-permute-done.8.a_ref.af_ref
  37.3 0.1 collective-permute-start.13
  37.3 1.6 %collective-permute-start.11 = (bf16[256,512]{1,0:T(8,128)(2,1)S(1)}, bf16[256,512]{1,0:T(8,128)(2,1)S(1)}, u32[]{:S(2)}, u32[]{:S(2)}) collective-permute-start(bf16[256,512]{1,0:T(8,128)(2,1)S(1)} %across_grad.1), channel_id=1, source_target_pairs={{0,4},{4,0},{8,12},{12,8},{16,20},{20,16},{24,28},{28,24},{1,5},{5... | collective-permute-start | bytes 786440 | tf_op jit(solution)/shard_map/ppermute | solution.py:37
  38.9 3.2 %collective-permute-start.9 = (bf16[304,256]{1,0:T(8,128)(2,1)S(1)}, bf16[304,256]{1,0:T(8,128)(2,1)S(1)}, u32[]{:S(2)}, u32[]{:S(2)}) collective-permute-start(bf16[304,256]{1,0:T(8,128)(2,1)S(1)} %get-tuple-element.45), channel_id=1, source_target_pairs={{0,16},{4,20},{8,24},{12,28},{16,0},{20,4},{24,8},{28,12},{1,17},{... | collective-permute-start | bytes 466952 | tf_op jit(solution)/shard_map/ppermute | solution.py:48
  42.1 0.0 collective-permute-done.13.refs_1_
  42.1 0.2 far_sum.1
  42.3 0.6 collective-permute-start.15
  42.8 0.0 collective-permute-start.14
  42.8 3.4 %attend_grad.1 = (bf16[256,512]{1,0:T(8,128)(2,1)}, f32[256,512]{1,0:T(8,128)S(1)}, bf16[256,512]{1,0:T(8,128)(2,1)S(1)}, bf16[256,512]{1,0:T(8,128)(2,1)S(1)}) custom-call(bf16[256,512]{1,0:T(8,128)(2,1)S(1)} %copy-done.2, bf16[256,512]{1,0:T(8,128)(2,1)S(1)} %join.1.a_ref.kv_ref, bf16[256,512]{1,0:T(8,128)(2,1)S(1)} %collective-permute-done.r1_ref, ...), custom_call_target="tpu_custom_call" | custom-call | flops 10000000000 | bytes 1 | tf_op jit(solution)/shard_map/attend_grad/pallas_call | solution.py:325
  46.2 3.6 %collective-permute-done.9.b_ref.bf_ref = bf16[304,256]{1,0:T(8,128)(2,1)S(1)} collective-permute-done((bf16[304,256]{1,0:T(8,128)(2,1)S(1)}, bf16[304,256]{1,0:T(8,128)(2,1)S(1)}, u32[]{:S(2)}, u32[]{:S(2)}) %collective-permute-start.9) | collective-permute-done | bytes 155680 | tf_op jit(solution)/shard_map/ppermute | solution.py:48
  49.8 0.6 collective-permute-start.10
  50.4 0.0 collective-permute-done.11.refs_1_
  50.4 0.1 hop_sum.1
  50.5 1.3 %collective-permute-start.12 = (bf16[256,512]{1,0:T(8,128)(2,1)S(1)}, bf16[256,512]{1,0:T(8,128)(2,1)S(1)}, u32[]{:S(2)}, u32[]{:S(2)}) collective-permute-start(bf16[256,512]{1,0:T(8,128)(2,1)S(1)} %hop_sum.1), channel_id=1, source_target_pairs={{8,0},{12,4},{16,8},{20,12},{24,16},{28,20},{9,1},{13,5},{17,9},{2... | collective-permute-start | bytes 786440 | tf_op jit(solution)/shard_map/ppermute | solution.py:32
  51.8 7.0 %collective-permute-done.10.px_ref.pair_ref = bf16[304,512]{1,0:T(8,128)(2,1)S(1)} collective-permute-done((bf16[304,512]{1,0:T(8,128)(2,1)S(1)}, bf16[304,512]{1,0:T(8,128)(2,1)S(1)}, u32[]{:S(2)}, u32[]{:S(2)}) %collective-permute-start.10) | collective-permute-done | bytes 311328 | tf_op jit(solution)/shard_map/ppermute | solution.py:37
  58.8 1.5 %far_grad.1.far_ref = f32[256,512]{1,0:T(8,128)S(1)} custom-call(bf16[256,512]{1,0:T(8,128)(2,1)S(1)} %join.1.a_ref.kv_ref, bf16[256,512]{1,0:T(8,128)(2,1)S(1)} %collective-permute-done.1.a_ref.b_ref.r2_ref.qf_ref, bf16[256,256]{1,0:T(8,128)(2,1)S(1)} %collective-permute-done.8.a_ref.af_ref, bf16[304,256]{1,0:T(8,128)(2,1)S(1)} %collective-permute-done.9.b_ref.bf_ref, ...), custom_call_target="tpu_custom_call" | custom-call | flops 100000000 | bytes 1 | tf_op jit(solution)/shard_map/far_grad/pallas_call | solution.py:325
  60.3 0.0 collective-permute-done.12.hop_ref
  60.3 0.0 collective-permute-done.14.core_ref
  60.3 0.0 collective-permute-done.15.y_ref
  60.3 1.2 %closing.1 = (bf16[256,256]{1,0:T(8,128)(2,1)}, bf16[256,256]{1,0:T(8,128)(2,1)}, bf16[64,5376]{1,0:T(8,128)(2,1)}) custom-call(f32[256,512]{1,0:T(8,128)S(1)} %get-tuple-element.44.own_ref, f32[256,512]{1,0:T(8,128)S(1)} %far_grad.1.far_ref, bf16[256,512]{1,0:T(8,128)(2,1)S(1)} %collective-permute-done.12.hop_ref, ...), custom_call_target="tpu_custom_call" | custom-call | flops 1 | bytes 1 | tf_op jit(solution)/shard_map/closing/pallas_call | solution.py:325
  (5 shorter events, 0.1 us)
Async XLA Ops:
  0.6 13.6 %collective-permute-start.2 = (bf16[64,5376]{1,0:T(8,128)(2,1)}, bf16[64,5376]{1,0:T(8,128)(2,1)S(1)}, u32[]{:S(2)}, u32[]{:S(2)}) collective-permute-start(bf16[64,5376]{1,0:T(8,128)(2,1)} %own_ref.1), channel_id=1, source_target_pairs={{0,1},{1,0},{2,3},{3,2},{4,5},{5,4},{6,7},{7,6},{8,9},{9,8},{10,11... | collective-permute-start | bytes 2064392 | tf_op jit(solution)/shard_map/ppermute | solution.py:37
  1.1 23.6 %collective-permute-start.6 = (bf16[64,5376]{1,0:T(8,128)(2,1)}, bf16[64,5376]{1,0:T(8,128)(2,1)S(1)}, u32[]{:S(2)}, u32[]{:S(2)}) collective-permute-start(bf16[64,5376]{1,0:T(8,128)(2,1)} %own_ref.1), channel_id=1, source_target_pairs={{0,2},{1,3},{2,0},{3,1},{4,6},{5,7},{6,4},{7,5},{8,10},{9,11},{10,... | collective-permute-start | bytes 2064392 | tf_op jit(solution)/shard_map/ppermute | solution.py:37
  3.7 0.9 %copy-start.3 = (bf16[256,256]{1,0:T(8,128)(2,1)S(1)}, bf16[256,256]{1,0:T(8,128)(2,1)}, u32[]{:S(2)}) copy-start(bf16[256,256]{1,0:T(8,128)(2,1)} %k_ref.1) | copy-start | bytes 393220
  4.6 0.9 %copy-start.4 = (bf16[256,256]{1,0:T(8,128)(2,1)S(1)}, bf16[256,256]{1,0:T(8,128)(2,1)}, u32[]{:S(2)}) copy-start(bf16[256,256]{1,0:T(8,128)(2,1)} %v_ref.1) | copy-start | bytes 393220
  5.6 14.2 %collective-permute-start = (bf16[256,512]{1,0:T(8,128)(2,1)S(1)}, bf16[256,512]{1,0:T(8,128)(2,1)S(1)}, u32[]{:S(2)}, u32[]{:S(2)}) collective-permute-start(bf16[256,512]{1,0:T(8,128)(2,1)S(1)} %join.1.a_ref.kv_ref), channel_id=1, source_target_pairs={{0,8},{4,12},{8,16},{12,20},{16,24},{20,28},{1,9},{5,13},{9,17},{1... | collective-permute-start | bytes 786440 | tf_op jit(solution)/shard_map/ppermute | solution.py:32
  9.1 1.0 %copy-start.1 = (bf16[256,512]{1,0:T(8,128)(2,1)S(1)}, bf16[256,512]{1,0:T(8,128)(2,1)}, u32[]{:S(2)}) copy-start(bf16[256,512]{1,0:T(8,128)(2,1)} %q_ref.7) | copy-start | bytes 786436
  10.1 14.7 %collective-permute-start.1 = (bf16[256,512]{1,0:T(8,128)(2,1)S(1)}, bf16[256,512]{1,0:T(8,128)(2,1)S(1)}, u32[]{:S(2)}, u32[]{:S(2)}) collective-permute-start(bf16[256,512]{1,0:T(8,128)(2,1)S(1)} %far_sent.1), channel_id=1, source_target_pairs={{0,16},{4,20},{8,24},{12,28},{16,0},{20,4},{24,8},{28,12},{1,17},{... | collective-permute-start | bytes 786440 | tf_op jit(solution)/shard_map/ppermute | solution.py:48
  12.7 17.7 %collective-permute-start.4 = (bf16[256,512]{1,0:T(8,128)(2,1)S(1)}, bf16[256,512]{1,0:T(8,128)(2,1)S(1)}, u32[]{:S(2)}, u32[]{:S(2)}) collective-permute-start(bf16[256,512]{1,0:T(8,128)(2,1)S(1)} %join.1.a_ref.kv_ref), channel_id=1, source_target_pairs={{0,4},{4,0},{8,12},{12,8},{16,20},{20,16},{24,28},{28,24},{1,5},{5... | collective-permute-start | bytes 786440 | tf_op jit(solution)/shard_map/ppermute | solution.py:37
  14.2 2.6 %copy-start = (bf16[512,5376]{1,0:T(8,128)(2,1)S(1)}, bf16[512,5376]{1,0:T(8,128)(2,1)}, u32[]{:S(2)}) copy-start(bf16[512,5376]{1,0:T(8,128)(2,1)} %w_ref.5) | copy-start | bytes 16515076
  16.8 1.1 %copy-start.5 = (bf16[64,5376]{1,0:T(8,128)(2,1)S(1)}, bf16[64,5376]{1,0:T(8,128)(2,1)}, u32[]{:S(2)}) copy-start(bf16[64,5376]{1,0:T(8,128)(2,1)} %own_ref.1) | copy-start | bytes 2064388
  17.9 9.0 %slice-start = ((s8[5505024]{0:T(1024)(128)(4,1)}), s8[4194304]{0:T(1024)(128)(4,1)S(1)}, s32[]{:S(2)}) async-start(s8[5505024]{0:T(1024)(128)(4,1)} %bitcast), calls=%async_computation | async-start | bytes 8388608
  19.8 7.1 %slice-start.1 = ((s8[5505024]{0:T(1024)(128)(4,1)}), s8[1310720]{0:T(1024)(128)(4,1)S(1)}, s32[]{:S(2)}) async-start(s8[5505024]{0:T(1024)(128)(4,1)} %bitcast), calls=%async_computation.1 | async-start | bytes 2621440
  19.8 10.7 %collective-permute-start.3 = (bf16[256,512]{1,0:T(8,128)(2,1)S(1)}, bf16[256,512]{1,0:T(8,128)(2,1)S(1)}, u32[]{:S(2)}, u32[]{:S(2)}) collective-permute-start(bf16[256,512]{1,0:T(8,128)(2,1)S(1)} %collective-permute-done.r1_ref), channel_id=1, source_target_pairs={{0,4},{4,0},{8,12},{12,8},{16,20},{20,16},{24,28},{28,24},{1,5},{5... | collective-permute-start | bytes 786440 | tf_op jit(solution)/shard_map/ppermute | solution.py:37
  24.8 2.1 %collective-permute-start.7 = (bf16[64,5376]{1,0:T(8,128)(2,1)S(1)}, bf16[64,5376]{1,0:T(8,128)(2,1)S(1)}, u32[]{:S(2)}, u32[]{:S(2)}) collective-permute-start(bf16[64,5376]{1,0:T(8,128)(2,1)S(1)} %collective-permute-done.6.y_ref), channel_id=1, source_target_pairs={{0,1},{1,0},{2,3},{3,2},{4,5},{5,4},{6,7},{7,6},{8,9},{9,8},{10,11... | collective-permute-start | bytes 2064392 | tf_op jit(solution)/shard_map/ppermute | solution.py:37
  24.8 5.6 %copy-start.2 = (bf16[256,512]{1,0:T(8,128)(2,1)S(1)}, bf16[256,512]{1,0:T(8,128)(2,1)}, u32[]{:S(2)}) copy-start(bf16[256,512]{1,0:T(8,128)(2,1)} %q_ref.7) | copy-start | bytes 786436
  24.8 8.8 %collective-permute-start.5 = (bf16[256,512]{1,0:T(8,128)(2,1)S(1)}, bf16[256,512]{1,0:T(8,128)(2,1)S(1)}, u32[]{:S(2)}, u32[]{:S(2)}) collective-permute-start(bf16[256,512]{1,0:T(8,128)(2,1)S(1)} %pick.1), channel_id=1, source_target_pairs={{0,4},{4,0},{8,12},{12,8},{16,20},{20,16},{24,28},{28,24},{1,5},{5... | collective-permute-start | bytes 786440 | tf_op jit(solution)/shard_map/ppermute | solution.py:37
  28.8 8.5 %collective-permute-start.8 = (bf16[256,256]{1,0:T(8,128)(2,1)S(1)}, bf16[256,256]{1,0:T(8,128)(2,1)S(1)}, u32[]{:S(2)}, u32[]{:S(2)}) collective-permute-start(bf16[256,256]{1,0:T(8,128)(2,1)S(1)} %get-tuple-element.42), channel_id=1, source_target_pairs={{0,16},{4,20},{8,24},{12,28},{16,0},{20,4},{24,8},{28,12},{1,17},{... | collective-permute-start | bytes 393224 | tf_op jit(solution)/shard_map/ppermute | solution.py:48
  37.3 4.9 %collective-permute-start.13 = (bf16[64,5376]{1,0:T(8,128)(2,1)S(1)}, bf16[64,5376]{1,0:T(8,128)(2,1)S(1)}, u32[]{:S(2)}, u32[]{:S(2)}) collective-permute-start(bf16[64,5376]{1,0:T(8,128)(2,1)S(1)} %get-tuple-element.54), channel_id=1, source_target_pairs={{0,1},{1,0},{2,3},{3,2},{4,5},{5,4},{6,7},{7,6},{8,9},{9,8},{10,11... | collective-permute-start | bytes 2064392 | tf_op jit(solution)/shard_map/ppermute | solution.py:37
  37.3 13.1 %collective-permute-start.11 = (bf16[256,512]{1,0:T(8,128)(2,1)S(1)}, bf16[256,512]{1,0:T(8,128)(2,1)S(1)}, u32[]{:S(2)}, u32[]{:S(2)}) collective-permute-start(bf16[256,512]{1,0:T(8,128)(2,1)S(1)} %across_grad.1), channel_id=1, source_target_pairs={{0,4},{4,0},{8,12},{12,8},{16,20},{20,16},{24,28},{28,24},{1,5},{5... | collective-permute-start | bytes 786440 | tf_op jit(solution)/shard_map/ppermute | solution.py:37
  38.9 10.9 %collective-permute-start.9 = (bf16[304,256]{1,0:T(8,128)(2,1)S(1)}, bf16[304,256]{1,0:T(8,128)(2,1)S(1)}, u32[]{:S(2)}, u32[]{:S(2)}) collective-permute-start(bf16[304,256]{1,0:T(8,128)(2,1)S(1)} %get-tuple-element.45), channel_id=1, source_target_pairs={{0,16},{4,20},{8,24},{12,28},{16,0},{20,4},{24,8},{28,12},{1,17},{... | collective-permute-start | bytes 466952 | tf_op jit(solution)/shard_map/ppermute | solution.py:48
  42.3 18.0 %collective-permute-start.15 = (bf16[64,5376]{1,0:T(8,128)(2,1)S(1)}, bf16[64,5376]{1,0:T(8,128)(2,1)S(1)}, u32[]{:S(2)}, u32[]{:S(2)}) collective-permute-start(bf16[64,5376]{1,0:T(8,128)(2,1)S(1)} %far_sum.1), channel_id=1, source_target_pairs={{0,2},{1,3},{2,0},{3,1},{4,6},{5,7},{6,4},{7,5},{8,10},{9,11},{10,... | collective-permute-start | bytes 2064392 | tf_op jit(solution)/shard_map/ppermute | solution.py:37
  42.8 17.5 %collective-permute-start.14 = (bf16[64,5376]{1,0:T(8,128)(2,1)S(1)}, bf16[64,5376]{1,0:T(8,128)(2,1)S(1)}, u32[]{:S(2)}, u32[]{:S(2)}) collective-permute-start(bf16[64,5376]{1,0:T(8,128)(2,1)S(1)} %get-tuple-element.55), channel_id=1, source_target_pairs={{0,1},{1,0},{2,3},{3,2},{4,5},{5,4},{6,7},{7,6},{8,9},{9,8},{10,11... | collective-permute-start | bytes 2064392 | tf_op jit(solution)/shard_map/ppermute | solution.py:37
  49.8 9.0 %collective-permute-start.10 = (bf16[304,512]{1,0:T(8,128)(2,1)S(1)}, bf16[304,512]{1,0:T(8,128)(2,1)S(1)}, u32[]{:S(2)}, u32[]{:S(2)}) collective-permute-start(bf16[304,512]{1,0:T(8,128)(2,1)S(1)} %pair.1), channel_id=1, source_target_pairs={{0,4},{4,0},{8,12},{12,8},{16,20},{20,16},{24,28},{28,24},{1,5},{5... | collective-permute-start | bytes 933896 | tf_op jit(solution)/shard_map/ppermute | solution.py:37
  50.5 9.8 %collective-permute-start.12 = (bf16[256,512]{1,0:T(8,128)(2,1)S(1)}, bf16[256,512]{1,0:T(8,128)(2,1)S(1)}, u32[]{:S(2)}, u32[]{:S(2)}) collective-permute-start(bf16[256,512]{1,0:T(8,128)(2,1)S(1)} %hop_sum.1), channel_id=1, source_target_pairs={{8,0},{12,4},{16,8},{20,12},{24,16},{28,20},{9,1},{13,5},{17,9},{2... | collective-permute-start | bytes 786440 | tf_op jit(solution)/shard_map/ppermute | solution.py:32

commit v12 on v11

--- a/solution.py
+++ b/solution.py
@@ -169,14 +169,20 @@
         o_ref[:, low + HEAD_SIZE : low + 2 * HEAD_SIZE] = out[tok:]
     spare = jnp.zeros((stat_ref.shape[0] - len(stats), 2 * tok), F32)
     stat_ref[...] = jnp.concatenate(stats + [spare], 0)
-    half = d_rel.shape[1] // 2
+    width = second_ref.shape[1]
     packed = jnp.concatenate([st[:, :tok] for st in stats] + [st[:, tok:] for st in stats], 0)
     packed = jnp.concatenate([packed, jnp.zeros((PACK - packed.shape[0], tok), F32)], 0)
-    second_ref[:tok, :] = d_rel[:, half:]
+    second_ref[:tok, :] = d_rel[:, d_rel.shape[1] - width :]
     for part in range(3):
         rounded = packed.astype(BF16)
-        second_ref[tok + part * PACK : tok + (part + 1) * PACK, :] = rounded
+        for c, rows in enumerate(part_rows(part, tok, width)):
+            second_ref[rows, :] = rounded[:, c * width : (c + 1) * width]
         packed = packed - rounded.astype(F32)
+
+
+def part_rows(part, tok, width):
+    pieces = tok // width
+    return [slice(tok + (part * pieces + c) * PACK, tok + (part * pieces + c + 1) * PACK) for c in range(pieces)]
 
 
 def project_kernel(o_ref, w_ref, *part_refs):
@@ -250,19 +256,23 @@
             dq_ref[rows, low + HEAD_SIZE : low + 2 * HEAD_SIZE] = dq[tok + r * size : tok + (r + 1) * size]
 
 
-def unpacked(second_ref, tok, kv_heads):
-    parts = [second_ref[tok + i * PACK : tok + (i + 1) * PACK, :tok].astype(F32) for i in range(3)]
+def unpacked(ref, tok, width, kv_heads):
+    parts = [
+        jnp.concatenate([ref[rows, :width] for rows in part_rows(part, tok, width)], 1).astype(F32) for part in range(3)
+    ]
     packed = parts[0] + (parts[1] + parts[2])
     count = 2 * kv_heads
     return [jnp.concatenate([packed[i : i + 1], packed[count + i : count + i + 1]], 1) for i in range(count)]
 
 
 def pair_kernel(t_ref, a_ref, b_ref, out_ref):
-    tok, half = a_ref.shape
+    tok, width = a_ref.shape[0], b_ref.shape[1]
     odd = lax.rem(lax.axis_index("seq"), 2) == 1
     out_ref[:tok, :] = jnp.where(odd, t_ref[...], jnp.concatenate([a_ref[...], b_ref[:tok, :]], 1))
-    out_ref[tok:, :half] = b_ref[tok:, :]
-    out_ref[tok:, half:] = jnp.zeros((b_ref.shape[0] - tok, half), BF16)
+    for part in range(3):
+        (into,) = part_rows(part, tok, tok)
+        out_ref[into, :tok] = jnp.concatenate([b_ref[rows, :] for rows in part_rows(part, tok, width)], 1)
+    out_ref[tok:, tok:] = jnp.zeros((out_ref.shape[0] - tok, out_ref.shape[1] - tok), BF16)
 
 
 def far_kernel(kv_ref, qf_ref, af_ref, bf_ref, qx_ref, px_ref, t_ref):
@@ -274,8 +284,8 @@
     straight = jnp.logical_and(jnp.logical_not(causal_mask(tok, head)), seq + FAR < count)
     across = jnp.logical_and(lax.rem(seq, 2) == 1, seq + FAR - 1 < count)
     sources = [
-        (own_order(qf_ref, head), jnp.concatenate([af_ref[...], bf_ref[:tok, :]], 1), unpacked(bf_ref, tok, kv_heads), straight),
-        (own_order(qx_ref, head), px_ref[:tok, :], unpacked(px_ref, tok, kv_heads), across),
+        (own_order(qf_ref, head), jnp.concatenate([af_ref[...], bf_ref[:tok, :]], 1), unpacked(bf_ref, tok, bf_ref.shape[1], kv_heads), straight),
+        (own_order(qx_ref, head), px_ref[:tok, :], unpacked(px_ref, tok, tok, kv_heads), across),
     ]
     scale = LOGIT_SCALE * LOG2E
     for g in range(kv_heads):
@@ -348,8 +358,9 @@
     x1 = swapped(gate(r1, grad_near), "seq", 1)
     x2 = swapped(call(functools.partial(either_kernel, is_odd), "pick", block, [], r2, q_far, cost=LARGE), "seq", 1)
     og_yc = swapped(gate(og_y, r2, grad_near), "head", 1)
-    first = jax.ShapeDtypeStruct((tok, q_cols // 2), BF16)
-    second = jax.ShapeDtypeStruct((tok + 3 * PACK, q_cols // 2), BF16)
+    rest = q_cols // 4
+    first = jax.ShapeDtypeStruct((tok, q_cols - rest), BF16)
+    second = jax.ShapeDtypeStruct((tok + 3 * PACK * (tok // rest), rest), BF16)
     grad_far, sent_first = call(far_back_kernel, "far_back", (half_grad, first), [], og_y, og_yc, out_weight, grad_near,
                                 cost=SMALL)
 
@@ -384,13 +395,13 @@
     )
     t_x = call(across_kernel, "across_grad", block, [], queries, x1, probs, stats, grad_near, grad_far)
     d1 = swapped(t_x, "seq", 1)
-    far_second = down(sent_second)
     near_own, near_core, far_own, far_core = call(
         project_kernel, "project", (rows,) * 4, [], gate(attended, t_x), out_weight
     )
     sent = swapped(gate(far_core, far_first), "head", 1)
     far_sum = call(sum_kernel, "far_sum", rows, [], far_own, sent)
     from_y = swapped(far_sum, "head", 2)
+    far_second = down(gate(sent_second, far_sum))
 
     query_gradient, t_own, t_1, t_z = call(
         backward_kernel,
@@ -401,7 +412,7 @@
         cost=LARGE,
     )
     e1 = shifted(call(sum_kernel, "hop_sum", block, [], t_1, d1), -2)
-    pair = jax.ShapeDtypeStruct((second.shape[0], q_cols), BF16)
+    pair = jax.ShapeDtypeStruct((tok + 3 * PACK, q_cols), BF16)
     pair = swapped(call(pair_kernel, "pair", pair, [], t_z, far_first, far_second), "seq", 1)
     from_core = swapped(gate(near_core, far_sum), "head", 1)
     t_far = call(far_kernel, "far_grad", wide_block, [],

time: 61.8 us -> 63.6 us (1.029)
  waiting for transfers between devices: 16.6 us -> 21 us
  starting transfers between devices: 21.8 us -> 19.2 us
    ppermute x3, waiting for transfers between devices: 7.96 us -> 11.7 us  [far_swapped(): lax.ppermute(lower() if lower is upper else jnp.where(side == r, lower(),...]
    ppermute x3, starting transfers between devices: 7.49 us -> 4.28 us  [far_swapped(): lax.ppermute(lower() if lower is upper else jnp.where(side == r, lower(),...]
  transfers between devices with their start and end apart: 16 -> 16, of which waited for: 5 -> 8; matrix products, arithmetic and copies ran while one was open for 0% -> 0% of each run, Pallas kernels for 24% -> 23%
where the time goes in v12:
time: 63.6 us; the launch traced here: 63.2 us
  waiting for transfers between devices  21 us (33%)
  starting transfers between devices  19.2 us (30%)
  Pallas kernels  15.8 us (25%)
  local copies, waits for them, and re-layouts  6.43 us (10%)
  between operations  0.77 us (1%)
    pallas_call x15, Pallas kernels, call(): pl.pallas_call(kernel, out_shape=outs, in_specs=[VMEM] * len(operands), o...  15.8 us
    ppermute x3, waiting for transfers between devices, far_swapped(): lax.ppermute(lower() if lower is upper else jnp.where(side == r, lower(),...  11.7 us
    ppermute x11, starting transfers between devices, swapped(): return lax.ppermute(value, axis, [(i, i ^ bit) for i in range(count)])  10.1 us
    ppermute x11, waiting for transfers between devices, swapped(): return lax.ppermute(value, axis, [(i, i ^ bit) for i in range(count)])  8.97 us
    unnamed x16, local copies, waits for them, and re-layouts  6.43 us
    ppermute x2, starting transfers between devices, shifted(): lax.ppermute(value, 'seq', [(i, i + steps) for i in range(first, last)])  4.79 us
    ppermute x3, starting transfers between devices, far_swapped(): lax.ppermute(lower() if lower is upper else jnp.where(side == r, lower(),...  4.28 us
  transfers between devices with their start and end apart: 16, of which 8 were waited for; matrix products, arithmetic and copies ran while one was open for 0% of the time, Pallas kernels for 23%

profile of v12, /device:TPU:0, one launch (start us, length us, event | category | flops | bytes accessed | tf_op | source)
XLA Modules:
  0.0 63.2 jit_solution(8920309662388171332)
XLA Ops:
  0.6 0.5 collective-permute-start.2
  1.1 2.6 %collective-permute-start.6 = (bf16[64,5376]{1,0:T(8,128)(2,1)}, bf16[64,5376]{1,0:T(8,128)(2,1)S(1)}, u32[]{:S(2)}, u32[]{:S(2)}) collective-permute-start(bf16[64,5376]{1,0:T(8,128)(2,1)} %own_ref.1), channel_id=1, source_target_pairs={{0,2},{1,3},{2,0},{3,1},{4,6},{5,7},{6,4},{7,5},{8,10},{9,11},{10,... | collective-permute-start | bytes 2064392 | tf_op jit(solution)/shard_map/ppermute | solution.py:37
  3.7 0.0 copy-start.3
  3.7 0.9 %copy-done.3 = bf16[256,256]{1,0:T(8,128)(2,1)S(1)} copy-done((bf16[256,256]{1,0:T(8,128)(2,1)S(1)}, bf16[256,256]{1,0:T(8,128)(2,1)}, u32[]{:S(2)}) %copy-start.3) | copy-done | bytes 131096
  4.6 0.0 copy-start.4
  4.7 0.9 %copy-done.4 = bf16[256,256]{1,0:T(8,128)(2,1)S(1)} copy-done((bf16[256,256]{1,0:T(8,128)(2,1)S(1)}, bf16[256,256]{1,0:T(8,128)(2,1)}, u32[]{:S(2)}) %copy-start.4) | copy-done | bytes 131096
  5.6 3.5 %collective-permute-start = (bf16[256,512]{1,0:T(8,128)(2,1)S(1)}, bf16[256,512]{1,0:T(8,128)(2,1)S(1)}, u32[]{:S(2)}, u32[]{:S(2)}) collective-permute-start(bf16[256,512]{1,0:T(8,128)(2,1)S(1)} %join.1.a_ref.kv_ref), channel_id=1, source_target_pairs={{0,8},{4,12},{8,16},{12,20},{16,24},{20,28},{1,9},{5,13},{9,17},{1... | collective-permute-start | bytes 786440 | tf_op jit(solution)/shard_map/ppermute | solution.py:32
  9.1 0.0 copy-start.1
  9.1 0.9 %copy-done.1 = bf16[256,512]{1,0:T(8,128)(2,1)S(1)} copy-done((bf16[256,512]{1,0:T(8,128)(2,1)S(1)}, bf16[256,512]{1,0:T(8,128)(2,1)}, u32[]{:S(2)}) %copy-start.1) | copy-done | bytes 262168
  10.1 2.6 %collective-permute-start.1 = (bf16[256,512]{1,0:T(8,128)(2,1)S(1)}, bf16[256,512]{1,0:T(8,128)(2,1)S(1)}, u32[]{:S(2)}, u32[]{:S(2)}) collective-permute-start(bf16[256,512]{1,0:T(8,128)(2,1)S(1)} %far_sent.1), channel_id=1, source_target_pairs={{0,16},{4,20},{8,24},{12,28},{16,0},{20,4},{24,8},{28,12},{1,17},{... | collective-permute-start | bytes 786440 | tf_op jit(solution)/shard_map/ppermute | solution.py:48
  12.7 1.5 %collective-permute-start.4 = (bf16[256,512]{1,0:T(8,128)(2,1)S(1)}, bf16[256,512]{1,0:T(8,128)(2,1)S(1)}, u32[]{:S(2)}, u32[]{:S(2)}) collective-permute-start(bf16[256,512]{1,0:T(8,128)(2,1)S(1)} %join.1.a_ref.kv_ref), channel_id=1, source_target_pairs={{0,4},{4,0},{8,12},{12,8},{16,20},{20,16},{24,28},{28,24},{1,5},{5... | collective-permute-start | bytes 786440 | tf_op jit(solution)/shard_map/ppermute | solution.py:37
  14.2 0.0 collective-permute-done.2.core_ref
  14.2 0.0 copy-start
  14.2 2.6 %copy-done = bf16[512,5376]{1,0:T(8,128)(2,1)S(1)} copy-done((bf16[512,5376]{1,0:T(8,128)(2,1)S(1)}, bf16[512,5376]{1,0:T(8,128)(2,1)}, u32[]{:S(2)}) %copy-start) | copy-done | bytes 5505048
  16.8 0.0 copy-start.5
  16.8 1.1 %copy-done.5 = bf16[64,5376]{1,0:T(8,128)(2,1)S(1)} copy-done((bf16[64,5376]{1,0:T(8,128)(2,1)S(1)}, bf16[64,5376]{1,0:T(8,128)(2,1)}, u32[]{:S(2)}) %copy-start.5) | copy-done | bytes 688152
  17.9 0.0 slice-start
  17.9 1.9 %near_back.1.near_ref.dn_ref = bf16[128,512]{1,0:T(8,128)(2,1)S(1)} custom-call(bf16[64,5376]{1,0:T(8,128)(2,1)S(1)} %copy-done.5, bf16[64,5376]{1,0:T(8,128)(2,1)S(1)} %collective-permute-done.2.core_ref, bf16[512,5376]{1,0:T(8,128)(2,1)S(1)} %copy-done), custom_call_target="tpu_custom_call" | custom-call | flops 10000000000 | bytes 1 | tf_op jit(solution)/shard_map/near_back/pallas_call | solution.py:335
  19.8 0.0 slice-start.1
  19.8 0.0 collective-permute-done.r1_ref
  19.8 0.6 collective-permute-start.3
  20.4 4.4 %collective-permute-done.1.a_ref.b_ref.r2_ref.qf_ref = bf16[256,512]{1,0:T(8,128)(2,1)S(1)} collective-permute-done((bf16[256,512]{1,0:T(8,128)(2,1)S(1)}, bf16[256,512]{1,0:T(8,128)(2,1)S(1)}, u32[]{:S(2)}, u32[]{:S(2)}) %collective-permute-start.1) | collective-permute-done | bytes 262176 | tf_op jit(solution)/shard_map/ppermute | solution.py:48
  24.8 0.0 collective-permute-done.6.y_ref
  24.8 0.0 collective-permute-start.7
  24.8 0.0 copy-start.2
  24.8 1.6 %collective-permute-start.5 = (bf16[256,512]{1,0:T(8,128)(2,1)S(1)}, bf16[256,512]{1,0:T(8,128)(2,1)S(1)}, u32[]{:S(2)}, u32[]{:S(2)}) collective-permute-start(bf16[256,512]{1,0:T(8,128)(2,1)S(1)} %pick.1), channel_id=1, source_target_pairs={{0,4},{4,0},{8,12},{12,8},{16,20},{20,16},{24,28},{28,24},{1,5},{5... | collective-permute-start | bytes 786440 | tf_op jit(solution)/shard_map/ppermute | solution.py:37
  26.4 0.5 collective-permute-done.7.yc_ref
  26.9 0.0 slice-done
  26.9 0.0 slice-done.1
  26.9 1.9 %far_back.1 = (bf16[128,512]{1,0:T(8,128)(2,1)S(1)}, bf16[256,384]{1,0:T(8,128)(2,1)S(1)}) custom-call(bf16[64,5376]{1,0:T(8,128)(2,1)S(1)} %collective-permute-done.6.y_ref, bf16[64,5376]{1,0:T(8,128)(2,1)S(1)} %collective-permute-done.7.yc_ref, bf16[512,5376]{1,0:T(8,128)(2,1)S(1)} %bitcast.1, bf16[128,512]{1,0:T(8,128)(2,1)S(1)} %near_back.1.near_ref.dn_ref), custom_call_target="tpu_custom_call" | custom-call | flops 1 | bytes 1 | tf_op jit(solution)/shard_map/far_back/pallas_call | solution.py:335
  28.8 1.6 %collective-permute-start.8 = (bf16[256,384]{1,0:T(8,128)(2,1)S(1)}, bf16[256,384]{1,0:T(8,128)(2,1)S(1)}, u32[]{:S(2)}, u32[]{:S(2)}) collective-permute-start(bf16[256,384]{1,0:T(8,128)(2,1)S(1)} %get-tuple-element.43), channel_id=1, source_target_pairs={{0,16},{4,20},{8,24},{12,28},{16,0},{20,4},{24,8},{28,12},{1,17},{... | collective-permute-start | bytes 589832 | tf_op jit(solution)/shard_map/ppermute | solution.py:48
  30.4 0.0 collective-permute-done.4.p0_ref
  30.4 0.0 collective-permute-done.3.x1_ref
  30.4 0.0 copy-done.2
  30.4 2.0 %attend_early.1 = (f32[2,4,256,512]{3,2,1,0:T(8,128)S(1)}, f32[8,512]{1,0:T(8,128)S(1)}, f32[2,128,512]{2,1,0:T(8,128)S(1)}) custom-call(bf16[256,512]{1,0:T(8,128)(2,1)S(1)} %copy-done.2, bf16[256,512]{1,0:T(8,128)(2,1)S(1)} %join.1.a_ref.kv_ref, bf16[256,512]{1,0:T(8,128)(2,1)S(1)} %collective-permute-done.r1_ref, ...), custom_call_target="tpu_custom_call" | custom-call | flops 1 | bytes 1 | tf_op jit(solution)/shard_map/attend_early/pallas_call | solution.py:335
  32.5 1.1 %collective-permute-done.5.x2_ref.qx_ref = bf16[256,512]{1,0:T(8,128)(2,1)S(1)} collective-permute-done((bf16[256,512]{1,0:T(8,128)(2,1)S(1)}, bf16[256,512]{1,0:T(8,128)(2,1)S(1)}, u32[]{:S(2)}, u32[]{:S(2)}) %collective-permute-start.5) | collective-permute-done | bytes 262176 | tf_op jit(solution)/shard_map/ppermute | solution.py:37
  33.6 1.5 %attend.1 = (bf16[256,512]{1,0:T(8,128)(2,1)S(1)}, bf16[2,5,256,512]{3,2,1,0:T(8,128)(2,1)S(1)}, f32[8,512]{1,0:T(8,128)S(1)}, bf16[352,128]{1,0:T(8,128)(2,1)S(1)}) custom-call(bf16[256,512]{1,0:T(8,128)(2,1)S(1)} %copy-done.2, bf16[256,512]{1,0:T(8,128)(2,1)S(1)} %collective-permute-done.4.p0_ref, ...), custom_call_target="tpu_custom_call" | custom-call | flops 1 | bytes 1 | tf_op jit(solution)/shard_map/attend/pallas_call | solution.py:335
  35.1 0.6 across_grad.1
  35.6 1.6 %project.1 = (bf16[64,5376]{1,0:T(8,128)(2,1)S(1)}, bf16[64,5376]{1,0:T(8,128)(2,1)S(1)}, bf16[64,5376]{1,0:T(8,128)(2,1)S(1)}, bf16[64,5376]{1,0:T(8,128)(2,1)S(1)}) custom-call(bf16[256,512]{1,0:T(8,128)(2,1)S(1)} %get-tuple-element.48.o_ref, bf16[512,5376]{1,0:T(8,128)(2,1)S(1)} %bitcast.1), custom_call_target="tpu_custom_call" | custom-call | flops 1 | bytes 1 | tf_op jit(solution)/shard_map/project/pallas_call | solution.py:335
  37.2 3.7 %collective-permute-done.8.a_ref.af_ref = bf16[256,384]{1,0:T(8,128)(2,1)S(1)} collective-permute-done((bf16[256,384]{1,0:T(8,128)(2,1)S(1)}, bf16[256,384]{1,0:T(8,128)(2,1)S(1)}, u32[]{:S(2)}, u32[]{:S(2)}) %collective-permute-start.8) | collective-permute-done | bytes 196640 | tf_op jit(solution)/shard_map/ppermute | solution.py:48
  40.9 0.0 collective-permute-start.9
  40.9 1.5 %collective-permute-start.12 = (bf16[256,512]{1,0:T(8,128)(2,1)S(1)}, bf16[256,512]{1,0:T(8,128)(2,1)S(1)}, u32[]{:S(2)}, u32[]{:S(2)}) collective-permute-start(bf16[256,512]{1,0:T(8,128)(2,1)S(1)} %across_grad.1), channel_id=1, source_target_pairs={{0,4},{4,0},{8,12},{12,8},{16,20},{20,16},{24,28},{28,24},{1,5},{5... | collective-permute-start | bytes 786440 | tf_op jit(solution)/shard_map/ppermute | solution.py:37
  42.4 0.7 %collective-permute-done.9.refs_1_ = bf16[64,5376]{1,0:T(8,128)(2,1)S(1)} collective-permute-done((bf16[64,5376]{1,0:T(8,128)(2,1)S(1)}, bf16[64,5376]{1,0:T(8,128)(2,1)S(1)}, u32[]{:S(2)}, u32[]{:S(2)}) %collective-permute-start.9) | collective-permute-done | bytes 688160 | tf_op jit(solution)/shard_map/ppermute | solution.py:37
  43.1 0.2 far_sum.1
  43.2 0.6 collective-permute-start.15
  43.8 0.0 collective-permute-start.10
  43.8 0.0 collective-permute-start.14
  43.8 3.4 %attend_grad.1 = (bf16[256,512]{1,0:T(8,128)(2,1)}, f32[256,512]{1,0:T(8,128)S(1)}, bf16[256,512]{1,0:T(8,128)(2,1)S(1)}, bf16[256,512]{1,0:T(8,128)(2,1)S(1)}) custom-call(bf16[256,512]{1,0:T(8,128)(2,1)S(1)} %copy-done.2, bf16[256,512]{1,0:T(8,128)(2,1)S(1)} %join.1.a_ref.kv_ref, bf16[256,512]{1,0:T(8,128)(2,1)S(1)} %collective-permute-done.r1_ref, ...), custom_call_target="tpu_custom_call" | custom-call | flops 10000000000 | bytes 1 | tf_op jit(solution)/shard_map/attend_grad/pallas_call | solution.py:335
  47.2 3.7 %collective-permute-done.10.b_ref.bf_ref = bf16[352,128]{1,0:T(8,128)(2,1)S(1)} collective-permute-done((bf16[352,128]{1,0:T(8,128)(2,1)S(1)}, bf16[352,128]{1,0:T(8,128)(2,1)S(1)}, u32[]{:S(2)}, u32[]{:S(2)}) %collective-permute-start.10) | collective-permute-done | bytes 90144 | tf_op jit(solution)/shard_map/ppermute | solution.py:48
  50.9 1.3 %collective-permute-start.11 = (bf16[304,512]{1,0:T(8,128)(2,1)S(1)}, bf16[304,512]{1,0:T(8,128)(2,1)S(1)}, u32[]{:S(2)}, u32[]{:S(2)}) collective-permute-start(bf16[304,512]{1,0:T(8,128)(2,1)S(1)} %pair.1), channel_id=1, source_target_pairs={{0,4},{4,0},{8,12},{12,8},{16,20},{20,16},{24,28},{28,24},{1,5},{5... | collective-permute-start | bytes 933896 | tf_op jit(solution)/shard_map/ppermute | solution.py:37
  52.2 0.0 collective-permute-done.12.refs_1_
  52.2 0.1 hop_sum.1
  52.2 1.3 %collective-permute-start.13 = (bf16[256,512]{1,0:T(8,128)(2,1)S(1)}, bf16[256,512]{1,0:T(8,128)(2,1)S(1)}, u32[]{:S(2)}, u32[]{:S(2)}) collective-permute-start(bf16[256,512]{1,0:T(8,128)(2,1)S(1)} %hop_sum.1), channel_id=1, source_target_pairs={{8,0},{12,4},{16,8},{20,12},{24,16},{28,20},{9,1},{13,5},{17,9},{2... | collective-permute-start | bytes 786440 | tf_op jit(solution)/shard_map/ppermute | solution.py:32
  53.5 6.7 %collective-permute-done.11.px_ref.pair_ref = bf16[304,512]{1,0:T(8,128)(2,1)S(1)} collective-permute-done((bf16[304,512]{1,0:T(8,128)(2,1)S(1)}, bf16[304,512]{1,0:T(8,128)(2,1)S(1)}, u32[]{:S(2)}, u32[]{:S(2)}) %collective-permute-start.11) | collective-permute-done | bytes 311328 | tf_op jit(solution)/shard_map/ppermute | solution.py:37
  60.2 1.5 %far_grad.1.far_ref = f32[256,512]{1,0:T(8,128)S(1)} custom-call(bf16[256,512]{1,0:T(8,128)(2,1)S(1)} %join.1.a_ref.kv_ref, bf16[256,512]{1,0:T(8,128)(2,1)S(1)} %collective-permute-done.1.a_ref.b_ref.r2_ref.qf_ref, bf16[256,384]{1,0:T(8,128)(2,1)S(1)} %collective-permute-done.8.a_ref.af_ref, bf16[352,128]{1,0:T(8,128)(2,1)S(1)} %collective-permute-done.10.b_ref.bf_ref, ...), custom_call_target="tpu_custom_call" | custom-call | flops 100000000 | bytes 1 | tf_op jit(solution)/shard_map/far_grad/pallas_call | solution.py:335
  61.7 0.3 collective-permute-done.13.hop_ref
  62.0 0.0 collective-permute-done.14.core_ref
  62.0 0.0 collective-permute-done.15.y_ref
  62.1 1.2 %closing.1 = (bf16[256,256]{1,0:T(8,128)(2,1)}, bf16[256,256]{1,0:T(8,128)(2,1)}, bf16[64,5376]{1,0:T(8,128)(2,1)}) custom-call(f32[256,512]{1,0:T(8,128)S(1)} %get-tuple-element.45.own_ref, f32[256,512]{1,0:T(8,128)S(1)} %far_grad.1.far_ref, bf16[256,512]{1,0:T(8,128)(2,1)S(1)} %collective-permute-done.13.hop_ref, ...), custom_call_target="tpu_custom_call" | custom-call | flops 1 | bytes 1 | tf_op jit(solution)/shard_map/closing/pallas_call | solution.py:335
  (5 shorter events, 0.1 us)
Async XLA Ops:
  0.6 13.6 %collective-permute-start.2 = (bf16[64,5376]{1,0:T(8,128)(2,1)}, bf16[64,5376]{1,0:T(8,128)(2,1)S(1)}, u32[]{:S(2)}, u32[]{:S(2)}) collective-permute-start(bf16[64,5376]{1,0:T(8,128)(2,1)} %own_ref.1), channel_id=1, source_target_pairs={{0,1},{1,0},{2,3},{3,2},{4,5},{5,4},{6,7},{7,6},{8,9},{9,8},{10,11... | collective-permute-start | bytes 2064392 | tf_op jit(solution)/shard_map/ppermute | solution.py:37
  1.1 23.6 %collective-permute-start.6 = (bf16[64,5376]{1,0:T(8,128)(2,1)}, bf16[64,5376]{1,0:T(8,128)(2,1)S(1)}, u32[]{:S(2)}, u32[]{:S(2)}) collective-permute-start(bf16[64,5376]{1,0:T(8,128)(2,1)} %own_ref.1), channel_id=1, source_target_pairs={{0,2},{1,3},{2,0},{3,1},{4,6},{5,7},{6,4},{7,5},{8,10},{9,11},{10,... | collective-permute-start | bytes 2064392 | tf_op jit(solution)/shard_map/ppermute | solution.py:37
  3.7 0.9 %copy-start.3 = (bf16[256,256]{1,0:T(8,128)(2,1)S(1)}, bf16[256,256]{1,0:T(8,128)(2,1)}, u32[]{:S(2)}) copy-start(bf16[256,256]{1,0:T(8,128)(2,1)} %k_ref.1) | copy-start | bytes 393220
  4.6 0.9 %copy-start.4 = (bf16[256,256]{1,0:T(8,128)(2,1)S(1)}, bf16[256,256]{1,0:T(8,128)(2,1)}, u32[]{:S(2)}) copy-start(bf16[256,256]{1,0:T(8,128)(2,1)} %v_ref.1) | copy-start | bytes 393220
  5.6 14.2 %collective-permute-start = (bf16[256,512]{1,0:T(8,128)(2,1)S(1)}, bf16[256,512]{1,0:T(8,128)(2,1)S(1)}, u32[]{:S(2)}, u32[]{:S(2)}) collective-permute-start(bf16[256,512]{1,0:T(8,128)(2,1)S(1)} %join.1.a_ref.kv_ref), channel_id=1, source_target_pairs={{0,8},{4,12},{8,16},{12,20},{16,24},{20,28},{1,9},{5,13},{9,17},{1... | collective-permute-start | bytes 786440 | tf_op jit(solution)/shard_map/ppermute | solution.py:32
  9.1 1.0 %copy-start.1 = (bf16[256,512]{1,0:T(8,128)(2,1)S(1)}, bf16[256,512]{1,0:T(8,128)(2,1)}, u32[]{:S(2)}) copy-start(bf16[256,512]{1,0:T(8,128)(2,1)} %q_ref.7) | copy-start | bytes 786436
  10.1 14.7 %collective-permute-start.1 = (bf16[256,512]{1,0:T(8,128)(2,1)S(1)}, bf16[256,512]{1,0:T(8,128)(2,1)S(1)}, u32[]{:S(2)}, u32[]{:S(2)}) collective-permute-start(bf16[256,512]{1,0:T(8,128)(2,1)S(1)} %far_sent.1), channel_id=1, source_target_pairs={{0,16},{4,20},{8,24},{12,28},{16,0},{20,4},{24,8},{28,12},{1,17},{... | collective-permute-start | bytes 786440 | tf_op jit(solution)/shard_map/ppermute | solution.py:48
  12.7 17.7 %collective-permute-start.4 = (bf16[256,512]{1,0:T(8,128)(2,1)S(1)}, bf16[256,512]{1,0:T(8,128)(2,1)S(1)}, u32[]{:S(2)}, u32[]{:S(2)}) collective-permute-start(bf16[256,512]{1,0:T(8,128)(2,1)S(1)} %join.1.a_ref.kv_ref), channel_id=1, source_target_pairs={{0,4},{4,0},{8,12},{12,8},{16,20},{20,16},{24,28},{28,24},{1,5},{5... | collective-permute-start | bytes 786440 | tf_op jit(solution)/shard_map/ppermute | solution.py:37
  14.2 2.6 %copy-start = (bf16[512,5376]{1,0:T(8,128)(2,1)S(1)}, bf16[512,5376]{1,0:T(8,128)(2,1)}, u32[]{:S(2)}) copy-start(bf16[512,5376]{1,0:T(8,128)(2,1)} %w_ref.5) | copy-start | bytes 16515076
  16.8 1.1 %copy-start.5 = (bf16[64,5376]{1,0:T(8,128)(2,1)S(1)}, bf16[64,5376]{1,0:T(8,128)(2,1)}, u32[]{:S(2)}) copy-start(bf16[64,5376]{1,0:T(8,128)(2,1)} %own_ref.1) | copy-start | bytes 2064388
  17.9 9.0 %slice-start = ((s8[5505024]{0:T(1024)(128)(4,1)}), s8[4194304]{0:T(1024)(128)(4,1)S(1)}, s32[]{:S(2)}) async-start(s8[5505024]{0:T(1024)(128)(4,1)} %bitcast), calls=%async_computation | async-start | bytes 8388608
  19.8 7.1 %slice-start.1 = ((s8[5505024]{0:T(1024)(128)(4,1)}), s8[1310720]{0:T(1024)(128)(4,1)S(1)}, s32[]{:S(2)}) async-start(s8[5505024]{0:T(1024)(128)(4,1)} %bitcast), calls=%async_computation.1 | async-start | bytes 2621440
  19.8 10.7 %collective-permute-start.3 = (bf16[256,512]{1,0:T(8,128)(2,1)S(1)}, bf16[256,512]{1,0:T(8,128)(2,1)S(1)}, u32[]{:S(2)}, u32[]{:S(2)}) collective-permute-start(bf16[256,512]{1,0:T(8,128)(2,1)S(1)} %collective-permute-done.r1_ref), channel_id=1, source_target_pairs={{0,4},{4,0},{8,12},{12,8},{16,20},{20,16},{24,28},{28,24},{1,5},{5... | collective-permute-start | bytes 786440 | tf_op jit(solution)/shard_map/ppermute | solution.py:37
  24.8 2.1 %collective-permute-start.7 = (bf16[64,5376]{1,0:T(8,128)(2,1)S(1)}, bf16[64,5376]{1,0:T(8,128)(2,1)S(1)}, u32[]{:S(2)}, u32[]{:S(2)}) collective-permute-start(bf16[64,5376]{1,0:T(8,128)(2,1)S(1)} %collective-permute-done.6.y_ref), channel_id=1, source_target_pairs={{0,1},{1,0},{2,3},{3,2},{4,5},{5,4},{6,7},{7,6},{8,9},{9,8},{10,11... | collective-permute-start | bytes 2064392 | tf_op jit(solution)/shard_map/ppermute | solution.py:37
  24.8 5.6 %copy-start.2 = (bf16[256,512]{1,0:T(8,128)(2,1)S(1)}, bf16[256,512]{1,0:T(8,128)(2,1)}, u32[]{:S(2)}) copy-start(bf16[256,512]{1,0:T(8,128)(2,1)} %q_ref.7) | copy-start | bytes 786436
  24.8 8.8 %collective-permute-start.5 = (bf16[256,512]{1,0:T(8,128)(2,1)S(1)}, bf16[256,512]{1,0:T(8,128)(2,1)S(1)}, u32[]{:S(2)}, u32[]{:S(2)}) collective-permute-start(bf16[256,512]{1,0:T(8,128)(2,1)S(1)} %pick.1), channel_id=1, source_target_pairs={{0,4},{4,0},{8,12},{12,8},{16,20},{20,16},{24,28},{28,24},{1,5},{5... | collective-permute-start | bytes 786440 | tf_op jit(solution)/shard_map/ppermute | solution.py:37
  28.8 12.1 %collective-permute-start.8 = (bf16[256,384]{1,0:T(8,128)(2,1)S(1)}, bf16[256,384]{1,0:T(8,128)(2,1)S(1)}, u32[]{:S(2)}, u32[]{:S(2)}) collective-permute-start(bf16[256,384]{1,0:T(8,128)(2,1)S(1)} %get-tuple-element.43), channel_id=1, source_target_pairs={{0,16},{4,20},{8,24},{12,28},{16,0},{20,4},{24,8},{28,12},{1,17},{... | collective-permute-start | bytes 589832 | tf_op jit(solution)/shard_map/ppermute | solution.py:48
  40.9 2.1 %collective-permute-start.9 = (bf16[64,5376]{1,0:T(8,128)(2,1)S(1)}, bf16[64,5376]{1,0:T(8,128)(2,1)S(1)}, u32[]{:S(2)}, u32[]{:S(2)}) collective-permute-start(bf16[64,5376]{1,0:T(8,128)(2,1)S(1)} %get-tuple-element.51), channel_id=1, source_target_pairs={{0,1},{1,0},{2,3},{3,2},{4,5},{5,4},{6,7},{7,6},{8,9},{9,8},{10,11... | collective-permute-start | bytes 2064392 | tf_op jit(solution)/shard_map/ppermute | solution.py:37
  40.9 11.3 %collective-permute-start.12 = (bf16[256,512]{1,0:T(8,128)(2,1)S(1)}, bf16[256,512]{1,0:T(8,128)(2,1)S(1)}, u32[]{:S(2)}, u32[]{:S(2)}) collective-permute-start(bf16[256,512]{1,0:T(8,128)(2,1)S(1)} %across_grad.1), channel_id=1, source_target_pairs={{0,4},{4,0},{8,12},{12,8},{16,20},{20,16},{24,28},{28,24},{1,5},{5... | collective-permute-start | bytes 786440 | tf_op jit(solution)/shard_map/ppermute | solution.py:37
  43.2 18.8 %collective-permute-start.15 = (bf16[64,5376]{1,0:T(8,128)(2,1)S(1)}, bf16[64,5376]{1,0:T(8,128)(2,1)S(1)}, u32[]{:S(2)}, u32[]{:S(2)}) collective-permute-start(bf16[64,5376]{1,0:T(8,128)(2,1)S(1)} %far_sum.1), channel_id=1, source_target_pairs={{0,2},{1,3},{2,0},{3,1},{4,6},{5,7},{6,4},{7,5},{8,10},{9,11},{10,... | collective-permute-start | bytes 2064392 | tf_op jit(solution)/shard_map/ppermute | solution.py:37
  43.8 7.0 %collective-permute-start.10 = (bf16[352,128]{1,0:T(8,128)(2,1)S(1)}, bf16[352,128]{1,0:T(8,128)(2,1)S(1)}, u32[]{:S(2)}, u32[]{:S(2)}) collective-permute-start(bf16[352,128]{1,0:T(8,128)(2,1)S(1)} %get-tuple-element.52), channel_id=1, source_target_pairs={{0,16},{4,20},{8,24},{12,28},{16,0},{20,4},{24,8},{28,12},{1,17},{... | collective-permute-start | bytes 270344 | tf_op jit(solution)/shard_map/ppermute | solution.py:48
  43.8 18.2 %collective-permute-start.14 = (bf16[64,5376]{1,0:T(8,128)(2,1)S(1)}, bf16[64,5376]{1,0:T(8,128)(2,1)S(1)}, u32[]{:S(2)}, u32[]{:S(2)}) collective-permute-start(bf16[64,5376]{1,0:T(8,128)(2,1)S(1)} %get-tuple-element.57), channel_id=1, source_target_pairs={{0,1},{1,0},{2,3},{3,2},{4,5},{5,4},{6,7},{7,6},{8,9},{9,8},{10,11... | collective-permute-start | bytes 2064392 | tf_op jit(solution)/shard_map/ppermute | solution.py:37
  50.9 9.3 %collective-permute-start.11 = (bf16[304,512]{1,0:T(8,128)(2,1)S(1)}, bf16[304,512]{1,0:T(8,128)(2,1)S(1)}, u32[]{:S(2)}, u32[]{:S(2)}) collective-permute-start(bf16[304,512]{1,0:T(8,128)(2,1)S(1)} %pair.1), channel_id=1, source_target_pairs={{0,4},{4,0},{8,12},{12,8},{16,20},{20,16},{24,28},{28,24},{1,5},{5... | collective-permute-start | bytes 933896 | tf_op jit(solution)/shard_map/ppermute | solution.py:37
  52.2 9.8 %collective-permute-start.13 = (bf16[256,512]{1,0:T(8,128)(2,1)S(1)}, bf16[256,512]{1,0:T(8,128)(2,1)S(1)}, u32[]{:S(2)}, u32[]{:S(2)}) collective-permute-start(bf16[256,512]{1,0:T(8,128)(2,1)S(1)} %hop_sum.1), channel_id=1, source_target_pairs={{8,0},{12,4},{16,8},{20,12},{24,16},{28,20},{9,1},{13,5},{17,9},{2... | collective-permute-start | bytes 786440 | tf_op jit(solution)/shard_map/ppermute | solution.py:32

commit v13 on v11

--- a/solution.py
+++ b/solution.py
@@ -384,13 +384,13 @@
     )
     t_x = call(across_kernel, "across_grad", block, [], queries, x1, probs, stats, grad_near, grad_far)
     d1 = swapped(t_x, "seq", 1)
-    far_second = down(sent_second)
     near_own, near_core, far_own, far_core = call(
         project_kernel, "project", (rows,) * 4, [], gate(attended, t_x), out_weight
     )
     sent = swapped(gate(far_core, far_first), "head", 1)
     far_sum = call(sum_kernel, "far_sum", rows, [], far_own, sent)
     from_y = swapped(far_sum, "head", 2)
+    far_second = down(gate(sent_second, far_sum))
 
     query_gradient, t_own, t_1, t_z = call(
         backward_kernel,

time: 61.8 us -> 62.8 us (1.016)
  starting transfers between devices: 21.8 us -> 22.8 us
    ppermute x11, waiting for transfers between devices: 8.68 us -> 6.26 us  [swapped(): return lax.ppermute(value, axis, [(i, i ^ bit) for i in range(count)])]
    ppermute x2, waiting for transfers between devices: 0.01 us -> 2.02 us  [shifted(): lax.ppermute(value, 'seq', [(i, i + steps) for i in range(first, last)])]
    ppermute x11, starting transfers between devices: 9.55 us -> 10.5 us  [swapped(): return lax.ppermute(value, axis, [(i, i ^ bit) for i in range(count)])]
  transfers between devices with their start and end apart: 16 -> 16, of which waited for: 5 -> 7; matrix products, arithmetic and copies ran while one was open for 0% -> 0% of each run, Pallas kernels for 24% -> 23%
where the time goes in v13:
time: 62.8 us; the launch traced here: 62.5 us
  starting transfers between devices  22.8 us (36%)
  waiting for transfers between devices  16.7 us (27%)
  Pallas kernels  15.8 us (25%)
  local copies, waits for them, and re-layouts  6.43 us (10%)
  between operations  0.79 us (1%)
    pallas_call x15, Pallas kernels, call(): pl.pallas_call(kernel, out_shape=outs, in_specs=[VMEM] * len(operands), o...  15.8 us
    ppermute x11, starting transfers between devices, swapped(): return lax.ppermute(value, axis, [(i, i ^ bit) for i in range(count)])  10.5 us
    ppermute x3, waiting for transfers between devices, far_swapped(): lax.ppermute(lower() if lower is upper else jnp.where(side == r, lower(),...  8.38 us
    ppermute x3, starting transfers between devices, far_swapped(): lax.ppermute(lower() if lower is upper else jnp.where(side == r, lower(),...  7.5 us
    unnamed x16, local copies, waits for them, and re-layouts  6.43 us
    ppermute x11, waiting for transfers between devices, swapped(): return lax.ppermute(value, axis, [(i, i ^ bit) for i in range(count)])  6.26 us
    ppermute x2, starting transfers between devices, shifted(): lax.ppermute(value, 'seq', [(i, i + steps) for i in range(first, last)])  4.79 us
    ppermute x2, waiting for transfers between devices, shifted(): lax.ppermute(value, 'seq', [(i, i + steps) for i in range(first, last)])  2.02 us
  transfers between devices with their start and end apart: 16, of which 7 were waited for; matrix products, arithmetic and copies ran while one was open for 0% of the time, Pallas kernels for 23%

profile of v13, /device:TPU:0, one launch (start us, length us, event | category | flops | bytes accessed | tf_op | source)
XLA Modules:
  0.0 62.5 jit_solution(9422605667744798764)
XLA Ops:
  0.6 0.5 collective-permute-start.2
  1.1 2.6 %collective-permute-start.6 = (bf16[64,5376]{1,0:T(8,128)(2,1)}, bf16[64,5376]{1,0:T(8,128)(2,1)S(1)}, u32[]{:S(2)}, u32[]{:S(2)}) collective-permute-start(bf16[64,5376]{1,0:T(8,128)(2,1)} %own_ref.1), channel_id=1, source_target_pairs={{0,2},{1,3},{2,0},{3,1},{4,6},{5,7},{6,4},{7,5},{8,10},{9,11},{10,... | collective-permute-start | bytes 2064392 | tf_op jit(solution)/shard_map/ppermute | solution.py:37
  3.7 0.0 copy-start.3
  3.7 0.9 %copy-done.3 = bf16[256,256]{1,0:T(8,128)(2,1)S(1)} copy-done((bf16[256,256]{1,0:T(8,128)(2,1)S(1)}, bf16[256,256]{1,0:T(8,128)(2,1)}, u32[]{:S(2)}) %copy-start.3) | copy-done | bytes 131096
  4.6 0.0 copy-start.4
  4.7 0.9 %copy-done.4 = bf16[256,256]{1,0:T(8,128)(2,1)S(1)} copy-done((bf16[256,256]{1,0:T(8,128)(2,1)S(1)}, bf16[256,256]{1,0:T(8,128)(2,1)}, u32[]{:S(2)}) %copy-start.4) | copy-done | bytes 131096
  5.6 3.5 %collective-permute-start = (bf16[256,512]{1,0:T(8,128)(2,1)S(1)}, bf16[256,512]{1,0:T(8,128)(2,1)S(1)}, u32[]{:S(2)}, u32[]{:S(2)}) collective-permute-start(bf16[256,512]{1,0:T(8,128)(2,1)S(1)} %join.1.a_ref.kv_ref), channel_id=1, source_target_pairs={{0,8},{4,12},{8,16},{12,20},{16,24},{20,28},{1,9},{5,13},{9,17},{1... | collective-permute-start | bytes 786440 | tf_op jit(solution)/shard_map/ppermute | solution.py:32
  9.1 0.0 copy-start.1
  9.1 0.9 %copy-done.1 = bf16[256,512]{1,0:T(8,128)(2,1)S(1)} copy-done((bf16[256,512]{1,0:T(8,128)(2,1)S(1)}, bf16[256,512]{1,0:T(8,128)(2,1)}, u32[]{:S(2)}) %copy-start.1) | copy-done | bytes 262168
  10.1 2.6 %collective-permute-start.1 = (bf16[256,512]{1,0:T(8,128)(2,1)S(1)}, bf16[256,512]{1,0:T(8,128)(2,1)S(1)}, u32[]{:S(2)}, u32[]{:S(2)}) collective-permute-start(bf16[256,512]{1,0:T(8,128)(2,1)S(1)} %far_sent.1), channel_id=1, source_target_pairs={{0,16},{4,20},{8,24},{12,28},{16,0},{20,4},{24,8},{28,12},{1,17},{... | collective-permute-start | bytes 786440 | tf_op jit(solution)/shard_map/ppermute | solution.py:48
  12.7 1.5 %collective-permute-start.4 = (bf16[256,512]{1,0:T(8,128)(2,1)S(1)}, bf16[256,512]{1,0:T(8,128)(2,1)S(1)}, u32[]{:S(2)}, u32[]{:S(2)}) collective-permute-start(bf16[256,512]{1,0:T(8,128)(2,1)S(1)} %join.1.a_ref.kv_ref), channel_id=1, source_target_pairs={{0,4},{4,0},{8,12},{12,8},{16,20},{20,16},{24,28},{28,24},{1,5},{5... | collective-permute-start | bytes 786440 | tf_op jit(solution)/shard_map/ppermute | solution.py:37
  14.2 0.0 collective-permute-done.2.core_ref
  14.2 0.0 copy-start
  14.2 2.6 %copy-done = bf16[512,5376]{1,0:T(8,128)(2,1)S(1)} copy-done((bf16[512,5376]{1,0:T(8,128)(2,1)S(1)}, bf16[512,5376]{1,0:T(8,128)(2,1)}, u32[]{:S(2)}) %copy-start) | copy-done | bytes 5505048
  16.8 0.0 copy-start.5
  16.8 1.1 %copy-done.5 = bf16[64,5376]{1,0:T(8,128)(2,1)S(1)} copy-done((bf16[64,5376]{1,0:T(8,128)(2,1)S(1)}, bf16[64,5376]{1,0:T(8,128)(2,1)}, u32[]{:S(2)}) %copy-start.5) | copy-done | bytes 688152
  17.9 0.0 slice-start
  17.9 1.9 %near_back.1.near_ref.dn_ref = bf16[128,512]{1,0:T(8,128)(2,1)S(1)} custom-call(bf16[64,5376]{1,0:T(8,128)(2,1)S(1)} %copy-done.5, bf16[64,5376]{1,0:T(8,128)(2,1)S(1)} %collective-permute-done.2.core_ref, bf16[512,5376]{1,0:T(8,128)(2,1)S(1)} %copy-done), custom_call_target="tpu_custom_call" | custom-call | flops 10000000000 | bytes 1 | tf_op jit(solution)/shard_map/near_back/pallas_call | solution.py:325
  19.8 0.0 slice-start.1
  19.8 0.0 collective-permute-done.r1_ref
  19.8 0.6 collective-permute-start.3
  20.4 4.4 %collective-permute-done.1.a_ref.b_ref.r2_ref.qf_ref = bf16[256,512]{1,0:T(8,128)(2,1)S(1)} collective-permute-done((bf16[256,512]{1,0:T(8,128)(2,1)S(1)}, bf16[256,512]{1,0:T(8,128)(2,1)S(1)}, u32[]{:S(2)}, u32[]{:S(2)}) %collective-permute-start.1) | collective-permute-done | bytes 262176 | tf_op jit(solution)/shard_map/ppermute | solution.py:48
  24.8 0.0 collective-permute-done.6.y_ref
  24.8 0.0 collective-permute-start.7
  24.8 0.0 copy-start.2
  24.8 1.6 %collective-permute-start.5 = (bf16[256,512]{1,0:T(8,128)(2,1)S(1)}, bf16[256,512]{1,0:T(8,128)(2,1)S(1)}, u32[]{:S(2)}, u32[]{:S(2)}) collective-permute-start(bf16[256,512]{1,0:T(8,128)(2,1)S(1)} %pick.1), channel_id=1, source_target_pairs={{0,4},{4,0},{8,12},{12,8},{16,20},{20,16},{24,28},{28,24},{1,5},{5... | collective-permute-start | bytes 786440 | tf_op jit(solution)/shard_map/ppermute | solution.py:37
  26.4 0.5 collective-permute-done.7.yc_ref
  26.9 0.0 slice-done
  26.9 0.0 slice-done.1
  26.9 1.9 %far_back.1 = (bf16[128,512]{1,0:T(8,128)(2,1)S(1)}, bf16[256,256]{1,0:T(8,128)(2,1)S(1)}) custom-call(bf16[64,5376]{1,0:T(8,128)(2,1)S(1)} %collective-permute-done.6.y_ref, bf16[64,5376]{1,0:T(8,128)(2,1)S(1)} %collective-permute-done.7.yc_ref, bf16[512,5376]{1,0:T(8,128)(2,1)S(1)} %bitcast.1, bf16[128,512]{1,0:T(8,128)(2,1)S(1)} %near_back.1.near_ref.dn_ref), custom_call_target="tpu_custom_call" | custom-call | flops 1 | bytes 1 | tf_op jit(solution)/shard_map/far_back/pallas_call | solution.py:325
  28.8 1.6 %collective-permute-start.8 = (bf16[256,256]{1,0:T(8,128)(2,1)S(1)}, bf16[256,256]{1,0:T(8,128)(2,1)S(1)}, u32[]{:S(2)}, u32[]{:S(2)}) collective-permute-start(bf16[256,256]{1,0:T(8,128)(2,1)S(1)} %get-tuple-element.43), channel_id=1, source_target_pairs={{0,16},{4,20},{8,24},{12,28},{16,0},{20,4},{24,8},{28,12},{1,17},{... | collective-permute-start | bytes 393224 | tf_op jit(solution)/shard_map/ppermute | solution.py:48
  30.4 0.0 collective-permute-done.4.p0_ref
  30.4 0.0 collective-permute-done.3.x1_ref
  30.4 0.0 copy-done.2
  30.4 2.0 %attend_early.1 = (f32[2,4,256,512]{3,2,1,0:T(8,128)S(1)}, f32[8,512]{1,0:T(8,128)S(1)}, f32[2,128,512]{2,1,0:T(8,128)S(1)}) custom-call(bf16[256,512]{1,0:T(8,128)(2,1)S(1)} %copy-done.2, bf16[256,512]{1,0:T(8,128)(2,1)S(1)} %join.1.a_ref.kv_ref, bf16[256,512]{1,0:T(8,128)(2,1)S(1)} %collective-permute-done.r1_ref, ...), custom_call_target="tpu_custom_call" | custom-call | flops 1 | bytes 1 | tf_op jit(solution)/shard_map/attend_early/pallas_call | solution.py:325
  32.5 1.1 %collective-permute-done.5.x2_ref.qx_ref = bf16[256,512]{1,0:T(8,128)(2,1)S(1)} collective-permute-done((bf16[256,512]{1,0:T(8,128)(2,1)S(1)}, bf16[256,512]{1,0:T(8,128)(2,1)S(1)}, u32[]{:S(2)}, u32[]{:S(2)}) %collective-permute-start.5) | collective-permute-done | bytes 262176 | tf_op jit(solution)/shard_map/ppermute | solution.py:37
  33.6 1.5 %attend.1 = (bf16[256,512]{1,0:T(8,128)(2,1)S(1)}, bf16[2,5,256,512]{3,2,1,0:T(8,128)(2,1)S(1)}, f32[8,512]{1,0:T(8,128)S(1)}, bf16[304,256]{1,0:T(8,128)(2,1)S(1)}) custom-call(bf16[256,512]{1,0:T(8,128)(2,1)S(1)} %copy-done.2, bf16[256,512]{1,0:T(8,128)(2,1)S(1)} %collective-permute-done.4.p0_ref, ...), custom_call_target="tpu_custom_call" | custom-call | flops 1 | bytes 1 | tf_op jit(solution)/shard_map/attend/pallas_call | solution.py:325
  35.1 0.6 across_grad.1
  35.6 1.6 %project.1 = (bf16[64,5376]{1,0:T(8,128)(2,1)S(1)}, bf16[64,5376]{1,0:T(8,128)(2,1)S(1)}, bf16[64,5376]{1,0:T(8,128)(2,1)S(1)}, bf16[64,5376]{1,0:T(8,128)(2,1)S(1)}) custom-call(bf16[256,512]{1,0:T(8,128)(2,1)S(1)} %get-tuple-element.48.o_ref, bf16[512,5376]{1,0:T(8,128)(2,1)S(1)} %bitcast.1), custom_call_target="tpu_custom_call" | custom-call | flops 1 | bytes 1 | tf_op jit(solution)/shard_map/project/pallas_call | solution.py:325
  37.2 0.0 collective-permute-done.8.a_ref.af_ref
  37.3 0.1 collective-permute-start.9
  37.3 1.6 %collective-permute-start.12 = (bf16[256,512]{1,0:T(8,128)(2,1)S(1)}, bf16[256,512]{1,0:T(8,128)(2,1)S(1)}, u32[]{:S(2)}, u32[]{:S(2)}) collective-permute-start(bf16[256,512]{1,0:T(8,128)(2,1)S(1)} %across_grad.1), channel_id=1, source_target_pairs={{0,4},{4,0},{8,12},{12,8},{16,20},{20,16},{24,28},{28,24},{1,5},{5... | collective-permute-start | bytes 786440 | tf_op jit(solution)/shard_map/ppermute | solution.py:37
  38.9 0.6 collective-permute-done.9.refs_1_
  39.5 0.2 far_sum.1
  39.6 0.6 collective-permute-start.15
  40.2 3.2 %collective-permute-start.10 = (bf16[304,256]{1,0:T(8,128)(2,1)S(1)}, bf16[304,256]{1,0:T(8,128)(2,1)S(1)}, u32[]{:S(2)}, u32[]{:S(2)}) collective-permute-start(bf16[304,256]{1,0:T(8,128)(2,1)S(1)} %get-tuple-element.52), channel_id=1, source_target_pairs={{0,16},{4,20},{8,24},{12,28},{16,0},{20,4},{24,8},{28,12},{1,17},{... | collective-permute-start | bytes 466952 | tf_op jit(solution)/shard_map/ppermute | solution.py:48
  43.4 0.0 collective-permute-start.14
  43.4 3.4 %attend_grad.1 = (bf16[256,512]{1,0:T(8,128)(2,1)}, f32[256,512]{1,0:T(8,128)S(1)}, bf16[256,512]{1,0:T(8,128)(2,1)S(1)}, bf16[256,512]{1,0:T(8,128)(2,1)S(1)}) custom-call(bf16[256,512]{1,0:T(8,128)(2,1)S(1)} %copy-done.2, bf16[256,512]{1,0:T(8,128)(2,1)S(1)} %join.1.a_ref.kv_ref, bf16[256,512]{1,0:T(8,128)(2,1)S(1)} %collective-permute-done.r1_ref, ...), custom_call_target="tpu_custom_call" | custom-call | flops 10000000000 | bytes 1 | tf_op jit(solution)/shard_map/attend_grad/pallas_call | solution.py:325
  46.8 4.0 %collective-permute-done.10.b_ref.bf_ref = bf16[304,256]{1,0:T(8,128)(2,1)S(1)} collective-permute-done((bf16[304,256]{1,0:T(8,128)(2,1)S(1)}, bf16[304,256]{1,0:T(8,128)(2,1)S(1)}, u32[]{:S(2)}, u32[]{:S(2)}) %collective-permute-start.10) | collective-permute-done | bytes 155680 | tf_op jit(solution)/shard_map/ppermute | solution.py:48
  50.8 1.6 %collective-permute-start.11 = (bf16[304,512]{1,0:T(8,128)(2,1)S(1)}, bf16[304,512]{1,0:T(8,128)(2,1)S(1)}, u32[]{:S(2)}, u32[]{:S(2)}) collective-permute-start(bf16[304,512]{1,0:T(8,128)(2,1)S(1)} %pair.1), channel_id=1, source_target_pairs={{0,4},{4,0},{8,12},{12,8},{16,20},{20,16},{24,28},{28,24},{1,5},{5... | collective-permute-start | bytes 933896 | tf_op jit(solution)/shard_map/ppermute | solution.py:37
  52.4 0.0 collective-permute-done.12.refs_1_
  52.4 0.1 hop_sum.1
  52.5 1.3 %collective-permute-start.13 = (bf16[256,512]{1,0:T(8,128)(2,1)S(1)}, bf16[256,512]{1,0:T(8,128)(2,1)S(1)}, u32[]{:S(2)}, u32[]{:S(2)}) collective-permute-start(bf16[256,512]{1,0:T(8,128)(2,1)S(1)} %hop_sum.1), channel_id=1, source_target_pairs={{8,0},{12,4},{16,8},{20,12},{24,16},{28,20},{9,1},{13,5},{17,9},{2... | collective-permute-start | bytes 786440 | tf_op jit(solution)/shard_map/ppermute | solution.py:32
  53.8 4.0 %collective-permute-done.11.px_ref.pair_ref = bf16[304,512]{1,0:T(8,128)(2,1)S(1)} collective-permute-done((bf16[304,512]{1,0:T(8,128)(2,1)S(1)}, bf16[304,512]{1,0:T(8,128)(2,1)S(1)}, u32[]{:S(2)}, u32[]{:S(2)}) %collective-permute-start.11) | collective-permute-done | bytes 311328 | tf_op jit(solution)/shard_map/ppermute | solution.py:37
  57.8 1.5 %far_grad.1.far_ref = f32[256,512]{1,0:T(8,128)S(1)} custom-call(bf16[256,512]{1,0:T(8,128)(2,1)S(1)} %join.1.a_ref.kv_ref, bf16[256,512]{1,0:T(8,128)(2,1)S(1)} %collective-permute-done.1.a_ref.b_ref.r2_ref.qf_ref, bf16[256,256]{1,0:T(8,128)(2,1)S(1)} %collective-permute-done.8.a_ref.af_ref, bf16[304,256]{1,0:T(8,128)(2,1)S(1)} %collective-permute-done.10.b_ref.bf_ref, ...), custom_call_target="tpu_custom_call" | custom-call | flops 100000000 | bytes 1 | tf_op jit(solution)/shard_map/far_grad/pallas_call | solution.py:325
  59.3 2.0 %collective-permute-done.13.hop_ref = bf16[256,512]{1,0:T(8,128)(2,1)S(1)} collective-permute-done((bf16[256,512]{1,0:T(8,128)(2,1)S(1)}, bf16[256,512]{1,0:T(8,128)(2,1)S(1)}, u32[]{:S(2)}, u32[]{:S(2)}) %collective-permute-start.13) | collective-permute-done | bytes 262176 | tf_op jit(solution)/shard_map/ppermute | solution.py:32
  61.3 0.0 collective-permute-done.14.core_ref
  61.3 0.0 collective-permute-done.15.y_ref
  61.3 1.2 %closing.1 = (bf16[256,256]{1,0:T(8,128)(2,1)}, bf16[256,256]{1,0:T(8,128)(2,1)}, bf16[64,5376]{1,0:T(8,128)(2,1)}) custom-call(f32[256,512]{1,0:T(8,128)S(1)} %get-tuple-element.45.own_ref, f32[256,512]{1,0:T(8,128)S(1)} %far_grad.1.far_ref, bf16[256,512]{1,0:T(8,128)(2,1)S(1)} %collective-permute-done.13.hop_ref, ...), custom_call_target="tpu_custom_call" | custom-call | flops 1 | bytes 1 | tf_op jit(solution)/shard_map/closing/pallas_call | solution.py:325
  (5 shorter events, 0.1 us)
Async XLA Ops:
  0.6 13.6 %collective-permute-start.2 = (bf16[64,5376]{1,0:T(8,128)(2,1)}, bf16[64,5376]{1,0:T(8,128)(2,1)S(1)}, u32[]{:S(2)}, u32[]{:S(2)}) collective-permute-start(bf16[64,5376]{1,0:T(8,128)(2,1)} %own_ref.1), channel_id=1, source_target_pairs={{0,1},{1,0},{2,3},{3,2},{4,5},{5,4},{6,7},{7,6},{8,9},{9,8},{10,11... | collective-permute-start | bytes 2064392 | tf_op jit(solution)/shard_map/ppermute | solution.py:37
  1.1 23.6 %collective-permute-start.6 = (bf16[64,5376]{1,0:T(8,128)(2,1)}, bf16[64,5376]{1,0:T(8,128)(2,1)S(1)}, u32[]{:S(2)}, u32[]{:S(2)}) collective-permute-start(bf16[64,5376]{1,0:T(8,128)(2,1)} %own_ref.1), channel_id=1, source_target_pairs={{0,2},{1,3},{2,0},{3,1},{4,6},{5,7},{6,4},{7,5},{8,10},{9,11},{10,... | collective-permute-start | bytes 2064392 | tf_op jit(solution)/shard_map/ppermute | solution.py:37
  3.7 0.9 %copy-start.3 = (bf16[256,256]{1,0:T(8,128)(2,1)S(1)}, bf16[256,256]{1,0:T(8,128)(2,1)}, u32[]{:S(2)}) copy-start(bf16[256,256]{1,0:T(8,128)(2,1)} %k_ref.1) | copy-start | bytes 393220
  4.6 0.9 %copy-start.4 = (bf16[256,256]{1,0:T(8,128)(2,1)S(1)}, bf16[256,256]{1,0:T(8,128)(2,1)}, u32[]{:S(2)}) copy-start(bf16[256,256]{1,0:T(8,128)(2,1)} %v_ref.1) | copy-start | bytes 393220
  5.6 14.2 %collective-permute-start = (bf16[256,512]{1,0:T(8,128)(2,1)S(1)}, bf16[256,512]{1,0:T(8,128)(2,1)S(1)}, u32[]{:S(2)}, u32[]{:S(2)}) collective-permute-start(bf16[256,512]{1,0:T(8,128)(2,1)S(1)} %join.1.a_ref.kv_ref), channel_id=1, source_target_pairs={{0,8},{4,12},{8,16},{12,20},{16,24},{20,28},{1,9},{5,13},{9,17},{1... | collective-permute-start | bytes 786440 | tf_op jit(solution)/shard_map/ppermute | solution.py:32
  9.1 1.0 %copy-start.1 = (bf16[256,512]{1,0:T(8,128)(2,1)S(1)}, bf16[256,512]{1,0:T(8,128)(2,1)}, u32[]{:S(2)}) copy-start(bf16[256,512]{1,0:T(8,128)(2,1)} %q_ref.7) | copy-start | bytes 786436
  10.1 14.7 %collective-permute-start.1 = (bf16[256,512]{1,0:T(8,128)(2,1)S(1)}, bf16[256,512]{1,0:T(8,128)(2,1)S(1)}, u32[]{:S(2)}, u32[]{:S(2)}) collective-permute-start(bf16[256,512]{1,0:T(8,128)(2,1)S(1)} %far_sent.1), channel_id=1, source_target_pairs={{0,16},{4,20},{8,24},{12,28},{16,0},{20,4},{24,8},{28,12},{1,17},{... | collective-permute-start | bytes 786440 | tf_op jit(solution)/shard_map/ppermute | solution.py:48
  12.7 17.7 %collective-permute-start.4 = (bf16[256,512]{1,0:T(8,128)(2,1)S(1)}, bf16[256,512]{1,0:T(8,128)(2,1)S(1)}, u32[]{:S(2)}, u32[]{:S(2)}) collective-permute-start(bf16[256,512]{1,0:T(8,128)(2,1)S(1)} %join.1.a_ref.kv_ref), channel_id=1, source_target_pairs={{0,4},{4,0},{8,12},{12,8},{16,20},{20,16},{24,28},{28,24},{1,5},{5... | collective-permute-start | bytes 786440 | tf_op jit(solution)/shard_map/ppermute | solution.py:37
  14.2 2.6 %copy-start = (bf16[512,5376]{1,0:T(8,128)(2,1)S(1)}, bf16[512,5376]{1,0:T(8,128)(2,1)}, u32[]{:S(2)}) copy-start(bf16[512,5376]{1,0:T(8,128)(2,1)} %w_ref.5) | copy-start | bytes 16515076
  16.8 1.1 %copy-start.5 = (bf16[64,5376]{1,0:T(8,128)(2,1)S(1)}, bf16[64,5376]{1,0:T(8,128)(2,1)}, u32[]{:S(2)}) copy-start(bf16[64,5376]{1,0:T(8,128)(2,1)} %own_ref.1) | copy-start | bytes 2064388
  17.9 9.0 %slice-start = ((s8[5505024]{0:T(1024)(128)(4,1)}), s8[4194304]{0:T(1024)(128)(4,1)S(1)}, s32[]{:S(2)}) async-start(s8[5505024]{0:T(1024)(128)(4,1)} %bitcast), calls=%async_computation | async-start | bytes 8388608
  19.8 7.1 %slice-start.1 = ((s8[5505024]{0:T(1024)(128)(4,1)}), s8[1310720]{0:T(1024)(128)(4,1)S(1)}, s32[]{:S(2)}) async-start(s8[5505024]{0:T(1024)(128)(4,1)} %bitcast), calls=%async_computation.1 | async-start | bytes 2621440
  19.8 10.7 %collective-permute-start.3 = (bf16[256,512]{1,0:T(8,128)(2,1)S(1)}, bf16[256,512]{1,0:T(8,128)(2,1)S(1)}, u32[]{:S(2)}, u32[]{:S(2)}) collective-permute-start(bf16[256,512]{1,0:T(8,128)(2,1)S(1)} %collective-permute-done.r1_ref), channel_id=1, source_target_pairs={{0,4},{4,0},{8,12},{12,8},{16,20},{20,16},{24,28},{28,24},{1,5},{5... | collective-permute-start | bytes 786440 | tf_op jit(solution)/shard_map/ppermute | solution.py:37
  24.8 2.1 %collective-permute-start.7 = (bf16[64,5376]{1,0:T(8,128)(2,1)S(1)}, bf16[64,5376]{1,0:T(8,128)(2,1)S(1)}, u32[]{:S(2)}, u32[]{:S(2)}) collective-permute-start(bf16[64,5376]{1,0:T(8,128)(2,1)S(1)} %collective-permute-done.6.y_ref), channel_id=1, source_target_pairs={{0,1},{1,0},{2,3},{3,2},{4,5},{5,4},{6,7},{7,6},{8,9},{9,8},{10,11... | collective-permute-start | bytes 2064392 | tf_op jit(solution)/shard_map/ppermute | solution.py:37
  24.8 5.6 %copy-start.2 = (bf16[256,512]{1,0:T(8,128)(2,1)S(1)}, bf16[256,512]{1,0:T(8,128)(2,1)}, u32[]{:S(2)}) copy-start(bf16[256,512]{1,0:T(8,128)(2,1)} %q_ref.7) | copy-start | bytes 786436
  24.8 8.8 %collective-permute-start.5 = (bf16[256,512]{1,0:T(8,128)(2,1)S(1)}, bf16[256,512]{1,0:T(8,128)(2,1)S(1)}, u32[]{:S(2)}, u32[]{:S(2)}) collective-permute-start(bf16[256,512]{1,0:T(8,128)(2,1)S(1)} %pick.1), channel_id=1, source_target_pairs={{0,4},{4,0},{8,12},{12,8},{16,20},{20,16},{24,28},{28,24},{1,5},{5... | collective-permute-start | bytes 786440 | tf_op jit(solution)/shard_map/ppermute | solution.py:37
  28.8 8.5 %collective-permute-start.8 = (bf16[256,256]{1,0:T(8,128)(2,1)S(1)}, bf16[256,256]{1,0:T(8,128)(2,1)S(1)}, u32[]{:S(2)}, u32[]{:S(2)}) collective-permute-start(bf16[256,256]{1,0:T(8,128)(2,1)S(1)} %get-tuple-element.43), channel_id=1, source_target_pairs={{0,16},{4,20},{8,24},{12,28},{16,0},{20,4},{24,8},{28,12},{1,17},{... | collective-permute-start | bytes 393224 | tf_op jit(solution)/shard_map/ppermute | solution.py:48
  37.3 2.2 %collective-permute-start.9 = (bf16[64,5376]{1,0:T(8,128)(2,1)S(1)}, bf16[64,5376]{1,0:T(8,128)(2,1)S(1)}, u32[]{:S(2)}, u32[]{:S(2)}) collective-permute-start(bf16[64,5376]{1,0:T(8,128)(2,1)S(1)} %get-tuple-element.51), channel_id=1, source_target_pairs={{0,1},{1,0},{2,3},{3,2},{4,5},{5,4},{6,7},{7,6},{8,9},{9,8},{10,11... | collective-permute-start | bytes 2064392 | tf_op jit(solution)/shard_map/ppermute | solution.py:37
  37.3 15.1 %collective-permute-start.12 = (bf16[256,512]{1,0:T(8,128)(2,1)S(1)}, bf16[256,512]{1,0:T(8,128)(2,1)S(1)}, u32[]{:S(2)}, u32[]{:S(2)}) collective-permute-start(bf16[256,512]{1,0:T(8,128)(2,1)S(1)} %across_grad.1), channel_id=1, source_target_pairs={{0,4},{4,0},{8,12},{12,8},{16,20},{20,16},{24,28},{28,24},{1,5},{5... | collective-permute-start | bytes 786440 | tf_op jit(solution)/shard_map/ppermute | solution.py:37
  39.6 21.7 %collective-permute-start.15 = (bf16[64,5376]{1,0:T(8,128)(2,1)S(1)}, bf16[64,5376]{1,0:T(8,128)(2,1)S(1)}, u32[]{:S(2)}, u32[]{:S(2)}) collective-permute-start(bf16[64,5376]{1,0:T(8,128)(2,1)S(1)} %far_sum.1), channel_id=1, source_target_pairs={{0,2},{1,3},{2,0},{3,1},{4,6},{5,7},{6,4},{7,5},{8,10},{9,11},{10,... | collective-permute-start | bytes 2064392 | tf_op jit(solution)/shard_map/ppermute | solution.py:37
  40.2 10.6 %collective-permute-start.10 = (bf16[304,256]{1,0:T(8,128)(2,1)S(1)}, bf16[304,256]{1,0:T(8,128)(2,1)S(1)}, u32[]{:S(2)}, u32[]{:S(2)}) collective-permute-start(bf16[304,256]{1,0:T(8,128)(2,1)S(1)} %get-tuple-element.52), channel_id=1, source_target_pairs={{0,16},{4,20},{8,24},{12,28},{16,0},{20,4},{24,8},{28,12},{1,17},{... | collective-permute-start | bytes 466952 | tf_op jit(solution)/shard_map/ppermute | solution.py:48
  43.4 17.9 %collective-permute-start.14 = (bf16[64,5376]{1,0:T(8,128)(2,1)S(1)}, bf16[64,5376]{1,0:T(8,128)(2,1)S(1)}, u32[]{:S(2)}, u32[]{:S(2)}) collective-permute-start(bf16[64,5376]{1,0:T(8,128)(2,1)S(1)} %get-tuple-element.57), channel_id=1, source_target_pairs={{0,1},{1,0},{2,3},{3,2},{4,5},{5,4},{6,7},{7,6},{8,9},{9,8},{10,11... | collective-permute-start | bytes 2064392 | tf_op jit(solution)/shard_map/ppermute | solution.py:37
  50.8 7.0 %collective-permute-start.11 = (bf16[304,512]{1,0:T(8,128)(2,1)S(1)}, bf16[304,512]{1,0:T(8,128)(2,1)S(1)}, u32[]{:S(2)}, u32[]{:S(2)}) collective-permute-start(bf16[304,512]{1,0:T(8,128)(2,1)S(1)} %pair.1), channel_id=1, source_target_pairs={{0,4},{4,0},{8,12},{12,8},{16,20},{20,16},{24,28},{28,24},{1,5},{5... | collective-permute-start | bytes 933896 | tf_op jit(solution)/shard_map/ppermute | solution.py:37
  52.5 8.8 %collective-permute-start.13 = (bf16[256,512]{1,0:T(8,128)(2,1)S(1)}, bf16[256,512]{1,0:T(8,128)(2,1)S(1)}, u32[]{:S(2)}, u32[]{:S(2)}) collective-permute-start(bf16[256,512]{1,0:T(8,128)(2,1)S(1)} %hop_sum.1), channel_id=1, source_target_pairs={{8,0},{12,4},{16,8},{20,12},{24,16},{28,20},{9,1},{13,5},{17,9},{2... | collective-permute-start | bytes 786440 | tf_op jit(solution)/shard_map/ppermute | solution.py:32

commit v14 on v10

--- a/solution.py
+++ b/solution.py
@@ -350,8 +350,8 @@
     og_yc = swapped(gate(og_y, r2, grad_near), "head", 1)
     first = jax.ShapeDtypeStruct((tok, q_cols // 2), BF16)
     second = jax.ShapeDtypeStruct((tok + 3 * PACK, q_cols // 2), BF16)
-    grad_far, sent_first = call(far_back_kernel, "far_back", (half_grad, first), [], gate(og_y, x1), og_yc, out_weight, grad_near,
-                                cost=LARGE)
+    grad_far, sent_first = call(far_back_kernel, "far_back", (half_grad, first), [], og_y, og_yc, out_weight, grad_near,
+                                cost=SMALL)
 
     def down(value):
         return far_swapped(*[lambda: value] * 2)[1]
@@ -368,6 +368,7 @@
         ),
         [],
         queries, kv, gate(r1, p0), r2, x1,
+        cost=SMALL,
     )
     attended, probs, stats, sent_second = call(
         forward_kernel,

time: 63.6 us -> 61.5 us (0.967)
  starting transfers between devices: 25.1 us -> 22.9 us
    ppermute x3, starting transfers between devices: 8.91 us -> 7.56 us  [far_swapped(): lax.ppermute(lower() if lower is upper else jnp.where(side == r, lower(),...]
    ppermute x3, waiting for transfers between devices: 7.07 us -> 6.09 us  [far_swapped(): lax.ppermute(lower() if lower is upper else jnp.where(side == r, lower(),...]
    ppermute x11, starting transfers between devices: 11.4 us -> 10.5 us  [swapped(): return lax.ppermute(value, axis, [(i, i ^ bit) for i in range(count)])]
    ppermute x2, waiting for transfers between devices: 0.64 us -> 1.31 us  [shifted(): lax.ppermute(value, 'seq', [(i, i + steps) for i in range(first, last)])]
  transfers between devices with their start and end apart: 16 -> 16, of which waited for: 5 -> 6; matrix products, arithmetic and copies ran while one was open for 0% -> 0% of each run, Pallas kernels for 23% -> 24%
where the time goes in v14:
time: 61.5 us; the launch traced here: 61.2 us
  starting transfers between devices  22.9 us (37%)
  Pallas kernels  15.8 us (26%)
  waiting for transfers between devices  15.3 us (25%)
  local copies, waits for them, and re-layouts  6.43 us (10%)
  between operations  0.79 us (1%)
    pallas_call x15, Pallas kernels, call(): pl.pallas_call(kernel, out_shape=outs, in_specs=[VMEM] * len(operands), o...  15.8 us
    ppermute x11, starting transfers between devices, swapped(): return lax.ppermute(value, axis, [(i, i ^ bit) for i in range(count)])  10.5 us
    ppermute x11, waiting for transfers between devices, swapped(): return lax.ppermute(value, axis, [(i, i ^ bit) for i in range(count)])  7.91 us
    ppermute x3, starting transfers between devices, far_swapped(): lax.ppermute(lower() if lower is upper else jnp.where(side == r, lower(),...  7.56 us
    unnamed x16, local copies, waits for them, and re-layouts  6.43 us
    ppermute x3, waiting for transfers between devices, far_swapped(): lax.ppermute(lower() if lower is upper else jnp.where(side == r, lower(),...  6.09 us
    ppermute x2, starting transfers between devices, shifted(): lax.ppermute(value, 'seq', [(i, i + steps) for i in range(first, last)])  4.79 us
    ppermute x2, waiting for transfers between devices, shifted(): lax.ppermute(value, 'seq', [(i, i + steps) for i in range(first, last)])  1.31 us
  transfers between devices with their start and end apart: 16, of which 6 were waited for; matrix products, arithmetic and copies ran while one was open for 0% of the time, Pallas kernels for 24%

profile of v14, /device:TPU:0, one launch (start us, length us, event | category | flops | bytes accessed | tf_op | source)
XLA Modules:
  0.0 61.2 jit_solution(17853712016111806984)
XLA Ops:
  0.6 0.5 collective-permute-start.2
  1.1 2.6 %collective-permute-start.6 = (bf16[64,5376]{1,0:T(8,128)(2,1)}, bf16[64,5376]{1,0:T(8,128)(2,1)S(1)}, u32[]{:S(2)}, u32[]{:S(2)}) collective-permute-start(bf16[64,5376]{1,0:T(8,128)(2,1)} %own_ref.1), channel_id=1, source_target_pairs={{0,2},{1,3},{2,0},{3,1},{4,6},{5,7},{6,4},{7,5},{8,10},{9,11},{10,... | collective-permute-start | bytes 2064392 | tf_op jit(solution)/shard_map/ppermute | solution.py:37
  3.7 0.0 copy-start.3
  3.7 0.9 %copy-done.3 = bf16[256,256]{1,0:T(8,128)(2,1)S(1)} copy-done((bf16[256,256]{1,0:T(8,128)(2,1)S(1)}, bf16[256,256]{1,0:T(8,128)(2,1)}, u32[]{:S(2)}) %copy-start.3) | copy-done | bytes 131096
  4.6 0.0 copy-start.4
  4.7 0.9 %copy-done.4 = bf16[256,256]{1,0:T(8,128)(2,1)S(1)} copy-done((bf16[256,256]{1,0:T(8,128)(2,1)S(1)}, bf16[256,256]{1,0:T(8,128)(2,1)}, u32[]{:S(2)}) %copy-start.4) | copy-done | bytes 131096
  5.6 3.5 %collective-permute-start = (bf16[256,512]{1,0:T(8,128)(2,1)S(1)}, bf16[256,512]{1,0:T(8,128)(2,1)S(1)}, u32[]{:S(2)}, u32[]{:S(2)}) collective-permute-start(bf16[256,512]{1,0:T(8,128)(2,1)S(1)} %join.1.a_ref.kv_ref), channel_id=1, source_target_pairs={{0,8},{4,12},{8,16},{12,20},{16,24},{20,28},{1,9},{5,13},{9,17},{1... | collective-permute-start | bytes 786440 | tf_op jit(solution)/shard_map/ppermute | solution.py:32
  9.1 0.0 copy-start.1
  9.1 0.9 %copy-done.1 = bf16[256,512]{1,0:T(8,128)(2,1)S(1)} copy-done((bf16[256,512]{1,0:T(8,128)(2,1)S(1)}, bf16[256,512]{1,0:T(8,128)(2,1)}, u32[]{:S(2)}) %copy-start.1) | copy-done | bytes 262168
  10.1 2.6 %collective-permute-start.1 = (bf16[256,512]{1,0:T(8,128)(2,1)S(1)}, bf16[256,512]{1,0:T(8,128)(2,1)S(1)}, u32[]{:S(2)}, u32[]{:S(2)}) collective-permute-start(bf16[256,512]{1,0:T(8,128)(2,1)S(1)} %far_sent.1), channel_id=1, source_target_pairs={{0,16},{4,20},{8,24},{12,28},{16,0},{20,4},{24,8},{28,12},{1,17},{... | collective-permute-start | bytes 786440 | tf_op jit(solution)/shard_map/ppermute | solution.py:48
  12.7 1.5 %collective-permute-start.4 = (bf16[256,512]{1,0:T(8,128)(2,1)S(1)}, bf16[256,512]{1,0:T(8,128)(2,1)S(1)}, u32[]{:S(2)}, u32[]{:S(2)}) collective-permute-start(bf16[256,512]{1,0:T(8,128)(2,1)S(1)} %join.1.a_ref.kv_ref), channel_id=1, source_target_pairs={{0,4},{4,0},{8,12},{12,8},{16,20},{20,16},{24,28},{28,24},{1,5},{5... | collective-permute-start | bytes 786440 | tf_op jit(solution)/shard_map/ppermute | solution.py:37
  14.2 0.0 collective-permute-done.2.core_ref
  14.2 0.0 copy-start
  14.2 2.6 %copy-done = bf16[512,5376]{1,0:T(8,128)(2,1)S(1)} copy-done((bf16[512,5376]{1,0:T(8,128)(2,1)S(1)}, bf16[512,5376]{1,0:T(8,128)(2,1)}, u32[]{:S(2)}) %copy-start) | copy-done | bytes 5505048
  16.8 0.0 copy-start.5
  16.8 1.1 %copy-done.5 = bf16[64,5376]{1,0:T(8,128)(2,1)S(1)} copy-done((bf16[64,5376]{1,0:T(8,128)(2,1)S(1)}, bf16[64,5376]{1,0:T(8,128)(2,1)}, u32[]{:S(2)}) %copy-start.5) | copy-done | bytes 688152
  17.9 0.0 slice-start
  17.9 1.9 %near_back.1.near_ref.dn_ref = bf16[128,512]{1,0:T(8,128)(2,1)S(1)} custom-call(bf16[64,5376]{1,0:T(8,128)(2,1)S(1)} %copy-done.5, bf16[64,5376]{1,0:T(8,128)(2,1)S(1)} %collective-permute-done.2.core_ref, bf16[512,5376]{1,0:T(8,128)(2,1)S(1)} %copy-done), custom_call_target="tpu_custom_call" | custom-call | flops 10000000000 | bytes 1 | tf_op jit(solution)/shard_map/near_back/pallas_call | solution.py:325
  19.8 0.0 slice-start.1
  19.8 0.0 collective-permute-done.r1_ref
  19.8 0.6 collective-permute-start.3
  20.4 4.4 %collective-permute-done.1.a_ref.b_ref.r2_ref.qf_ref = bf16[256,512]{1,0:T(8,128)(2,1)S(1)} collective-permute-done((bf16[256,512]{1,0:T(8,128)(2,1)S(1)}, bf16[256,512]{1,0:T(8,128)(2,1)S(1)}, u32[]{:S(2)}, u32[]{:S(2)}) %collective-permute-start.1) | collective-permute-done | bytes 262176 | tf_op jit(solution)/shard_map/ppermute | solution.py:48
  24.8 0.0 collective-permute-done.6.y_ref
  24.8 0.0 collective-permute-start.7
  24.8 0.0 copy-start.2
  24.8 1.6 %collective-permute-start.5 = (bf16[256,512]{1,0:T(8,128)(2,1)S(1)}, bf16[256,512]{1,0:T(8,128)(2,1)S(1)}, u32[]{:S(2)}, u32[]{:S(2)}) collective-permute-start(bf16[256,512]{1,0:T(8,128)(2,1)S(1)} %pick.1), channel_id=1, source_target_pairs={{0,4},{4,0},{8,12},{12,8},{16,20},{20,16},{24,28},{28,24},{1,5},{5... | collective-permute-start | bytes 786440 | tf_op jit(solution)/shard_map/ppermute | solution.py:37
  26.4 0.5 collective-permute-done.7.yc_ref
  26.9 0.0 slice-done
  26.9 0.0 slice-done.1
  26.9 1.9 %far_back.1 = (bf16[128,512]{1,0:T(8,128)(2,1)S(1)}, bf16[256,256]{1,0:T(8,128)(2,1)S(1)}) custom-call(bf16[64,5376]{1,0:T(8,128)(2,1)S(1)} %collective-permute-done.6.y_ref, bf16[64,5376]{1,0:T(8,128)(2,1)S(1)} %collective-permute-done.7.yc_ref, bf16[512,5376]{1,0:T(8,128)(2,1)S(1)} %bitcast.1, bf16[128,512]{1,0:T(8,128)(2,1)S(1)} %near_back.1.near_ref.dn_ref), custom_call_target="tpu_custom_call" | custom-call | flops 1 | bytes 1 | tf_op jit(solution)/shard_map/far_back/pallas_call | solution.py:325
  28.8 1.6 %collective-permute-start.8 = (bf16[256,256]{1,0:T(8,128)(2,1)S(1)}, bf16[256,256]{1,0:T(8,128)(2,1)S(1)}, u32[]{:S(2)}, u32[]{:S(2)}) collective-permute-start(bf16[256,256]{1,0:T(8,128)(2,1)S(1)} %get-tuple-element.42), channel_id=1, source_target_pairs={{0,16},{4,20},{8,24},{12,28},{16,0},{20,4},{24,8},{28,12},{1,17},{... | collective-permute-start | bytes 393224 | tf_op jit(solution)/shard_map/ppermute | solution.py:48
  30.4 0.0 collective-permute-done.4.p0_ref
  30.4 0.0 collective-permute-done.3.x1_ref
  30.4 0.0 copy-done.2
  30.4 2.0 %attend_early.1 = (f32[2,4,256,512]{3,2,1,0:T(8,128)S(1)}, f32[8,512]{1,0:T(8,128)S(1)}, f32[2,128,512]{2,1,0:T(8,128)S(1)}) custom-call(bf16[256,512]{1,0:T(8,128)(2,1)S(1)} %copy-done.2, bf16[256,512]{1,0:T(8,128)(2,1)S(1)} %join.1.a_ref.kv_ref, bf16[256,512]{1,0:T(8,128)(2,1)S(1)} %collective-permute-done.r1_ref, ...), custom_call_target="tpu_custom_call" | custom-call | flops 1 | bytes 1 | tf_op jit(solution)/shard_map/attend_early/pallas_call | solution.py:325
  32.5 1.1 %collective-permute-done.5.x2_ref.qx_ref = bf16[256,512]{1,0:T(8,128)(2,1)S(1)} collective-permute-done((bf16[256,512]{1,0:T(8,128)(2,1)S(1)}, bf16[256,512]{1,0:T(8,128)(2,1)S(1)}, u32[]{:S(2)}, u32[]{:S(2)}) %collective-permute-start.5) | collective-permute-done | bytes 262176 | tf_op jit(solution)/shard_map/ppermute | solution.py:37
  33.6 1.5 %attend.1 = (bf16[256,512]{1,0:T(8,128)(2,1)S(1)}, bf16[2,5,256,512]{3,2,1,0:T(8,128)(2,1)S(1)}, f32[8,512]{1,0:T(8,128)S(1)}, bf16[304,256]{1,0:T(8,128)(2,1)S(1)}) custom-call(bf16[256,512]{1,0:T(8,128)(2,1)S(1)} %copy-done.2, bf16[256,512]{1,0:T(8,128)(2,1)S(1)} %collective-permute-done.4.p0_ref, ...), custom_call_target="tpu_custom_call" | custom-call | flops 1 | bytes 1 | tf_op jit(solution)/shard_map/attend/pallas_call | solution.py:325
  35.1 1.6 %project.1 = (bf16[64,5376]{1,0:T(8,128)(2,1)S(1)}, bf16[64,5376]{1,0:T(8,128)(2,1)S(1)}, bf16[64,5376]{1,0:T(8,128)(2,1)S(1)}, bf16[64,5376]{1,0:T(8,128)(2,1)S(1)}) custom-call(bf16[256,512]{1,0:T(8,128)(2,1)S(1)} %get-tuple-element.48.o_ref, bf16[512,5376]{1,0:T(8,128)(2,1)S(1)} %bitcast.1), custom_call_target="tpu_custom_call" | custom-call | flops 1 | bytes 1 | tf_op jit(solution)/shard_map/project/pallas_call | solution.py:325
  36.7 0.0 collective-permute-done.8.a_ref.af_ref
  36.7 0.1 collective-permute-start.13
  36.7 3.3 %collective-permute-start.9 = (bf16[304,256]{1,0:T(8,128)(2,1)S(1)}, bf16[304,256]{1,0:T(8,128)(2,1)S(1)}, u32[]{:S(2)}, u32[]{:S(2)}) collective-permute-start(bf16[304,256]{1,0:T(8,128)(2,1)S(1)} %get-tuple-element.45), channel_id=1, source_target_pairs={{0,16},{4,20},{8,24},{12,28},{16,0},{20,4},{24,8},{28,12},{1,17},{... | collective-permute-start | bytes 466952 | tf_op jit(solution)/shard_map/ppermute | solution.py:48
  40.0 0.6 across_grad.1
  40.6 1.6 %collective-permute-start.11 = (bf16[256,512]{1,0:T(8,128)(2,1)S(1)}, bf16[256,512]{1,0:T(8,128)(2,1)S(1)}, u32[]{:S(2)}, u32[]{:S(2)}) collective-permute-start(bf16[256,512]{1,0:T(8,128)(2,1)S(1)} %across_grad.1), channel_id=1, source_target_pairs={{0,4},{4,0},{8,12},{12,8},{16,20},{20,16},{24,28},{28,24},{1,5},{5... | collective-permute-start | bytes 786440 | tf_op jit(solution)/shard_map/ppermute | solution.py:37
  42.2 0.0 collective-permute-done.13.refs_1_
  42.2 0.2 far_sum.1
  42.3 0.6 collective-permute-start.15
  42.9 0.0 collective-permute-start.14
  42.9 3.4 %attend_grad.1 = (bf16[256,512]{1,0:T(8,128)(2,1)}, f32[256,512]{1,0:T(8,128)S(1)}, bf16[256,512]{1,0:T(8,128)(2,1)S(1)}, bf16[256,512]{1,0:T(8,128)(2,1)S(1)}) custom-call(bf16[256,512]{1,0:T(8,128)(2,1)S(1)} %copy-done.2, bf16[256,512]{1,0:T(8,128)(2,1)S(1)} %join.1.a_ref.kv_ref, bf16[256,512]{1,0:T(8,128)(2,1)S(1)} %collective-permute-done.r1_ref, ...), custom_call_target="tpu_custom_call" | custom-call | flops 10000000000 | bytes 1 | tf_op jit(solution)/shard_map/attend_grad/pallas_call | solution.py:325
  46.3 1.7 %collective-permute-done.9.b_ref.bf_ref = bf16[304,256]{1,0:T(8,128)(2,1)S(1)} collective-permute-done((bf16[304,256]{1,0:T(8,128)(2,1)S(1)}, bf16[304,256]{1,0:T(8,128)(2,1)S(1)}, u32[]{:S(2)}, u32[]{:S(2)}) %collective-permute-start.9) | collective-permute-done | bytes 155680 | tf_op jit(solution)/shard_map/ppermute | solution.py:48
  48.0 1.6 %collective-permute-start.10 = (bf16[304,512]{1,0:T(8,128)(2,1)S(1)}, bf16[304,512]{1,0:T(8,128)(2,1)S(1)}, u32[]{:S(2)}, u32[]{:S(2)}) collective-permute-start(bf16[304,512]{1,0:T(8,128)(2,1)S(1)} %pair.1), channel_id=1, source_target_pairs={{0,4},{4,0},{8,12},{12,8},{16,20},{20,16},{24,28},{28,24},{1,5},{5... | collective-permute-start | bytes 933896 | tf_op jit(solution)/shard_map/ppermute | solution.py:37
  49.6 0.0 collective-permute-done.11.refs_1_
  49.6 0.1 hop_sum.1
  49.7 1.3 %collective-permute-start.12 = (bf16[256,512]{1,0:T(8,128)(2,1)S(1)}, bf16[256,512]{1,0:T(8,128)(2,1)S(1)}, u32[]{:S(2)}, u32[]{:S(2)}) collective-permute-start(bf16[256,512]{1,0:T(8,128)(2,1)S(1)} %hop_sum.1), channel_id=1, source_target_pairs={{8,0},{12,4},{16,8},{20,12},{24,16},{28,20},{9,1},{13,5},{17,9},{2... | collective-permute-start | bytes 786440 | tf_op jit(solution)/shard_map/ppermute | solution.py:32
  51.0 6.3 %collective-permute-done.10.px_ref.pair_ref = bf16[304,512]{1,0:T(8,128)(2,1)S(1)} collective-permute-done((bf16[304,512]{1,0:T(8,128)(2,1)S(1)}, bf16[304,512]{1,0:T(8,128)(2,1)S(1)}, u32[]{:S(2)}, u32[]{:S(2)}) %collective-permute-start.10) | collective-permute-done | bytes 311328 | tf_op jit(solution)/shard_map/ppermute | solution.py:37
  57.2 1.5 %far_grad.1.far_ref = f32[256,512]{1,0:T(8,128)S(1)} custom-call(bf16[256,512]{1,0:T(8,128)(2,1)S(1)} %join.1.a_ref.kv_ref, bf16[256,512]{1,0:T(8,128)(2,1)S(1)} %collective-permute-done.1.a_ref.b_ref.r2_ref.qf_ref, bf16[256,256]{1,0:T(8,128)(2,1)S(1)} %collective-permute-done.8.a_ref.af_ref, bf16[304,256]{1,0:T(8,128)(2,1)S(1)} %collective-permute-done.9.b_ref.bf_ref, ...), custom_call_target="tpu_custom_call" | custom-call | flops 100000000 | bytes 1 | tf_op jit(solution)/shard_map/far_grad/pallas_call | solution.py:325
  58.7 1.3 %collective-permute-done.12.hop_ref = bf16[256,512]{1,0:T(8,128)(2,1)S(1)} collective-permute-done((bf16[256,512]{1,0:T(8,128)(2,1)S(1)}, bf16[256,512]{1,0:T(8,128)(2,1)S(1)}, u32[]{:S(2)}, u32[]{:S(2)}) %collective-permute-start.12) | collective-permute-done | bytes 262176 | tf_op jit(solution)/shard_map/ppermute | solution.py:32
  60.0 0.0 collective-permute-done.14.core_ref
  60.0 0.0 collective-permute-done.15.y_ref
  60.0 1.2 %closing.1 = (bf16[256,256]{1,0:T(8,128)(2,1)}, bf16[256,256]{1,0:T(8,128)(2,1)}, bf16[64,5376]{1,0:T(8,128)(2,1)}) custom-call(f32[256,512]{1,0:T(8,128)S(1)} %get-tuple-element.44.own_ref, f32[256,512]{1,0:T(8,128)S(1)} %far_grad.1.far_ref, bf16[256,512]{1,0:T(8,128)(2,1)S(1)} %collective-permute-done.12.hop_ref, ...), custom_call_target="tpu_custom_call" | custom-call | flops 1 | bytes 1 | tf_op jit(solution)/shard_map/closing/pallas_call | solution.py:325
  (5 shorter events, 0.1 us)
Async XLA Ops:
  0.6 13.6 %collective-permute-start.2 = (bf16[64,5376]{1,0:T(8,128)(2,1)}, bf16[64,5376]{1,0:T(8,128)(2,1)S(1)}, u32[]{:S(2)}, u32[]{:S(2)}) collective-permute-start(bf16[64,5376]{1,0:T(8,128)(2,1)} %own_ref.1), channel_id=1, source_target_pairs={{0,1},{1,0},{2,3},{3,2},{4,5},{5,4},{6,7},{7,6},{8,9},{9,8},{10,11... | collective-permute-start | bytes 2064392 | tf_op jit(solution)/shard_map/ppermute | solution.py:37
  1.1 23.6 %collective-permute-start.6 = (bf16[64,5376]{1,0:T(8,128)(2,1)}, bf16[64,5376]{1,0:T(8,128)(2,1)S(1)}, u32[]{:S(2)}, u32[]{:S(2)}) collective-permute-start(bf16[64,5376]{1,0:T(8,128)(2,1)} %own_ref.1), channel_id=1, source_target_pairs={{0,2},{1,3},{2,0},{3,1},{4,6},{5,7},{6,4},{7,5},{8,10},{9,11},{10,... | collective-permute-start | bytes 2064392 | tf_op jit(solution)/shard_map/ppermute | solution.py:37
  3.7 0.9 %copy-start.3 = (bf16[256,256]{1,0:T(8,128)(2,1)S(1)}, bf16[256,256]{1,0:T(8,128)(2,1)}, u32[]{:S(2)}) copy-start(bf16[256,256]{1,0:T(8,128)(2,1)} %k_ref.1) | copy-start | bytes 393220
  4.6 0.9 %copy-start.4 = (bf16[256,256]{1,0:T(8,128)(2,1)S(1)}, bf16[256,256]{1,0:T(8,128)(2,1)}, u32[]{:S(2)}) copy-start(bf16[256,256]{1,0:T(8,128)(2,1)} %v_ref.1) | copy-start | bytes 393220
  5.6 14.2 %collective-permute-start = (bf16[256,512]{1,0:T(8,128)(2,1)S(1)}, bf16[256,512]{1,0:T(8,128)(2,1)S(1)}, u32[]{:S(2)}, u32[]{:S(2)}) collective-permute-start(bf16[256,512]{1,0:T(8,128)(2,1)S(1)} %join.1.a_ref.kv_ref), channel_id=1, source_target_pairs={{0,8},{4,12},{8,16},{12,20},{16,24},{20,28},{1,9},{5,13},{9,17},{1... | collective-permute-start | bytes 786440 | tf_op jit(solution)/shard_map/ppermute | solution.py:32
  9.1 1.0 %copy-start.1 = (bf16[256,512]{1,0:T(8,128)(2,1)S(1)}, bf16[256,512]{1,0:T(8,128)(2,1)}, u32[]{:S(2)}) copy-start(bf16[256,512]{1,0:T(8,128)(2,1)} %q_ref.7) | copy-start | bytes 786436
  10.1 14.7 %collective-permute-start.1 = (bf16[256,512]{1,0:T(8,128)(2,1)S(1)}, bf16[256,512]{1,0:T(8,128)(2,1)S(1)}, u32[]{:S(2)}, u32[]{:S(2)}) collective-permute-start(bf16[256,512]{1,0:T(8,128)(2,1)S(1)} %far_sent.1), channel_id=1, source_target_pairs={{0,16},{4,20},{8,24},{12,28},{16,0},{20,4},{24,8},{28,12},{1,17},{... | collective-permute-start | bytes 786440 | tf_op jit(solution)/shard_map/ppermute | solution.py:48
  12.7 17.7 %collective-permute-start.4 = (bf16[256,512]{1,0:T(8,128)(2,1)S(1)}, bf16[256,512]{1,0:T(8,128)(2,1)S(1)}, u32[]{:S(2)}, u32[]{:S(2)}) collective-permute-start(bf16[256,512]{1,0:T(8,128)(2,1)S(1)} %join.1.a_ref.kv_ref), channel_id=1, source_target_pairs={{0,4},{4,0},{8,12},{12,8},{16,20},{20,16},{24,28},{28,24},{1,5},{5... | collective-permute-start | bytes 786440 | tf_op jit(solution)/shard_map/ppermute | solution.py:37
  14.2 2.6 %copy-start = (bf16[512,5376]{1,0:T(8,128)(2,1)S(1)}, bf16[512,5376]{1,0:T(8,128)(2,1)}, u32[]{:S(2)}) copy-start(bf16[512,5376]{1,0:T(8,128)(2,1)} %w_ref.5) | copy-start | bytes 16515076
  16.8 1.1 %copy-start.5 = (bf16[64,5376]{1,0:T(8,128)(2,1)S(1)}, bf16[64,5376]{1,0:T(8,128)(2,1)}, u32[]{:S(2)}) copy-start(bf16[64,5376]{1,0:T(8,128)(2,1)} %own_ref.1) | copy-start | bytes 2064388
  17.9 9.0 %slice-start = ((s8[5505024]{0:T(1024)(128)(4,1)}), s8[4194304]{0:T(1024)(128)(4,1)S(1)}, s32[]{:S(2)}) async-start(s8[5505024]{0:T(1024)(128)(4,1)} %bitcast), calls=%async_computation | async-start | bytes 8388608
  19.8 7.1 %slice-start.1 = ((s8[5505024]{0:T(1024)(128)(4,1)}), s8[1310720]{0:T(1024)(128)(4,1)S(1)}, s32[]{:S(2)}) async-start(s8[5505024]{0:T(1024)(128)(4,1)} %bitcast), calls=%async_computation.1 | async-start | bytes 2621440
  19.8 10.7 %collective-permute-start.3 = (bf16[256,512]{1,0:T(8,128)(2,1)S(1)}, bf16[256,512]{1,0:T(8,128)(2,1)S(1)}, u32[]{:S(2)}, u32[]{:S(2)}) collective-permute-start(bf16[256,512]{1,0:T(8,128)(2,1)S(1)} %collective-permute-done.r1_ref), channel_id=1, source_target_pairs={{0,4},{4,0},{8,12},{12,8},{16,20},{20,16},{24,28},{28,24},{1,5},{5... | collective-permute-start | bytes 786440 | tf_op jit(solution)/shard_map/ppermute | solution.py:37
  24.8 2.1 %collective-permute-start.7 = (bf16[64,5376]{1,0:T(8,128)(2,1)S(1)}, bf16[64,5376]{1,0:T(8,128)(2,1)S(1)}, u32[]{:S(2)}, u32[]{:S(2)}) collective-permute-start(bf16[64,5376]{1,0:T(8,128)(2,1)S(1)} %collective-permute-done.6.y_ref), channel_id=1, source_target_pairs={{0,1},{1,0},{2,3},{3,2},{4,5},{5,4},{6,7},{7,6},{8,9},{9,8},{10,11... | collective-permute-start | bytes 2064392 | tf_op jit(solution)/shard_map/ppermute | solution.py:37
  24.8 5.6 %copy-start.2 = (bf16[256,512]{1,0:T(8,128)(2,1)S(1)}, bf16[256,512]{1,0:T(8,128)(2,1)}, u32[]{:S(2)}) copy-start(bf16[256,512]{1,0:T(8,128)(2,1)} %q_ref.7) | copy-start | bytes 786436
  24.8 8.8 %collective-permute-start.5 = (bf16[256,512]{1,0:T(8,128)(2,1)S(1)}, bf16[256,512]{1,0:T(8,128)(2,1)S(1)}, u32[]{:S(2)}, u32[]{:S(2)}) collective-permute-start(bf16[256,512]{1,0:T(8,128)(2,1)S(1)} %pick.1), channel_id=1, source_target_pairs={{0,4},{4,0},{8,12},{12,8},{16,20},{20,16},{24,28},{28,24},{1,5},{5... | collective-permute-start | bytes 786440 | tf_op jit(solution)/shard_map/ppermute | solution.py:37
  28.8 7.9 %collective-permute-start.8 = (bf16[256,256]{1,0:T(8,128)(2,1)S(1)}, bf16[256,256]{1,0:T(8,128)(2,1)S(1)}, u32[]{:S(2)}, u32[]{:S(2)}) collective-permute-start(bf16[256,256]{1,0:T(8,128)(2,1)S(1)} %get-tuple-element.42), channel_id=1, source_target_pairs={{0,16},{4,20},{8,24},{12,28},{16,0},{20,4},{24,8},{28,12},{1,17},{... | collective-permute-start | bytes 393224 | tf_op jit(solution)/shard_map/ppermute | solution.py:48
  36.7 5.5 %collective-permute-start.13 = (bf16[64,5376]{1,0:T(8,128)(2,1)S(1)}, bf16[64,5376]{1,0:T(8,128)(2,1)S(1)}, u32[]{:S(2)}, u32[]{:S(2)}) collective-permute-start(bf16[64,5376]{1,0:T(8,128)(2,1)S(1)} %get-tuple-element.54), channel_id=1, source_target_pairs={{0,1},{1,0},{2,3},{3,2},{4,5},{5,4},{6,7},{7,6},{8,9},{9,8},{10,11... | collective-permute-start | bytes 2064392 | tf_op jit(solution)/shard_map/ppermute | solution.py:37
  36.7 11.2 %collective-permute-start.9 = (bf16[304,256]{1,0:T(8,128)(2,1)S(1)}, bf16[304,256]{1,0:T(8,128)(2,1)S(1)}, u32[]{:S(2)}, u32[]{:S(2)}) collective-permute-start(bf16[304,256]{1,0:T(8,128)(2,1)S(1)} %get-tuple-element.45), channel_id=1, source_target_pairs={{0,16},{4,20},{8,24},{12,28},{16,0},{20,4},{24,8},{28,12},{1,17},{... | collective-permute-start | bytes 466952 | tf_op jit(solution)/shard_map/ppermute | solution.py:48
  40.6 9.0 %collective-permute-start.11 = (bf16[256,512]{1,0:T(8,128)(2,1)S(1)}, bf16[256,512]{1,0:T(8,128)(2,1)S(1)}, u32[]{:S(2)}, u32[]{:S(2)}) collective-permute-start(bf16[256,512]{1,0:T(8,128)(2,1)S(1)} %across_grad.1), channel_id=1, source_target_pairs={{0,4},{4,0},{8,12},{12,8},{16,20},{20,16},{24,28},{28,24},{1,5},{5... | collective-permute-start | bytes 786440 | tf_op jit(solution)/shard_map/ppermute | solution.py:37
  42.3 17.7 %collective-permute-start.15 = (bf16[64,5376]{1,0:T(8,128)(2,1)S(1)}, bf16[64,5376]{1,0:T(8,128)(2,1)S(1)}, u32[]{:S(2)}, u32[]{:S(2)}) collective-permute-start(bf16[64,5376]{1,0:T(8,128)(2,1)S(1)} %far_sum.1), channel_id=1, source_target_pairs={{0,2},{1,3},{2,0},{3,1},{4,6},{5,7},{6,4},{7,5},{8,10},{9,11},{10,... | collective-permute-start | bytes 2064392 | tf_op jit(solution)/shard_map/ppermute | solution.py:37
  42.9 17.1 %collective-permute-start.14 = (bf16[64,5376]{1,0:T(8,128)(2,1)S(1)}, bf16[64,5376]{1,0:T(8,128)(2,1)S(1)}, u32[]{:S(2)}, u32[]{:S(2)}) collective-permute-start(bf16[64,5376]{1,0:T(8,128)(2,1)S(1)} %get-tuple-element.55), channel_id=1, source_target_pairs={{0,1},{1,0},{2,3},{3,2},{4,5},{5,4},{6,7},{7,6},{8,9},{9,8},{10,11... | collective-permute-start | bytes 2064392 | tf_op jit(solution)/shard_map/ppermute | solution.py:37
  48.0 9.2 %collective-permute-start.10 = (bf16[304,512]{1,0:T(8,128)(2,1)S(1)}, bf16[304,512]{1,0:T(8,128)(2,1)S(1)}, u32[]{:S(2)}, u32[]{:S(2)}) collective-permute-start(bf16[304,512]{1,0:T(8,128)(2,1)S(1)} %pair.1), channel_id=1, source_target_pairs={{0,4},{4,0},{8,12},{12,8},{16,20},{20,16},{24,28},{28,24},{1,5},{5... | collective-permute-start | bytes 933896 | tf_op jit(solution)/shard_map/ppermute | solution.py:37
  49.7 10.3 %collective-permute-start.12 = (bf16[256,512]{1,0:T(8,128)(2,1)S(1)}, bf16[256,512]{1,0:T(8,128)(2,1)S(1)}, u32[]{:S(2)}, u32[]{:S(2)}) collective-permute-start(bf16[256,512]{1,0:T(8,128)(2,1)S(1)} %hop_sum.1), channel_id=1, source_target_pairs={{8,0},{12,4},{16,8},{20,12},{24,16},{28,20},{9,1},{13,5},{17,9},{2... | collective-permute-start | bytes 786440 | tf_op jit(solution)/shard_map/ppermute | solution.py:32

commit v15 on v14

--- a/solution.py
+++ b/solution.py
@@ -12,7 +12,7 @@
 LOGIT_SCALE = 168.0 ** (-0.5)
 LOG2E = 1.4426950408889634
 NEG = -1e30
-PACK = 16
+PACK = 8
 FAR = 4
 F32 = jnp.float32
 BF16 = jnp.bfloat16
@@ -171,7 +171,6 @@
     stat_ref[...] = jnp.concatenate(stats + [spare], 0)
     half = d_rel.shape[1] // 2
     packed = jnp.concatenate([st[:, :tok] for st in stats] + [st[:, tok:] for st in stats], 0)
-    packed = jnp.concatenate([packed, jnp.zeros((PACK - packed.shape[0], tok), F32)], 0)
     second_ref[:tok, :] = d_rel[:, half:]
     for part in range(3):
         rounded = packed.astype(BF16)

time: 61.5 us -> 61.5 us (level)
    ppermute x2, waiting for transfers between devices: 1.31 us -> 2.35 us  [shifted(): lax.ppermute(value, 'seq', [(i, i + steps) for i in range(first, last)])]
where the time goes in v15:
time: 61.5 us; the launch traced here: 61.2 us
  starting transfers between devices  22.9 us (37%)
  Pallas kernels  15.9 us (26%)
  waiting for transfers between devices  15.3 us (25%)
  local copies, waits for them, and re-layouts  6.43 us (10%)
  between operations  0.79 us (1%)
    pallas_call x15, Pallas kernels, call(): pl.pallas_call(kernel, out_shape=outs, in_specs=[VMEM] * len(operands), o...  15.9 us
    ppermute x11, starting transfers between devices, swapped(): return lax.ppermute(value, axis, [(i, i ^ bit) for i in range(count)])  10.5 us
    ppermute x3, starting transfers between devices, far_swapped(): lax.ppermute(lower() if lower is upper else jnp.where(side == r, lower(),...  7.57 us
    ppermute x11, waiting for transfers between devices, swapped(): return lax.ppermute(value, axis, [(i, i ^ bit) for i in range(count)])  7.37 us
    unnamed x16, local copies, waits for them, and re-layouts  6.43 us
    ppermute x3, waiting for transfers between devices, far_swapped(): lax.ppermute(lower() if lower is upper else jnp.where(side == r, lower(),...  5.56 us
    ppermute x2, starting transfers between devices, shifted(): lax.ppermute(value, 'seq', [(i, i + steps) for i in range(first, last)])  4.79 us
    ppermute x2, waiting for transfers between devices, shifted(): lax.ppermute(value, 'seq', [(i, i + steps) for i in range(first, last)])  2.35 us
  transfers between devices with their start and end apart: 16, of which 6 were waited for; matrix products, arithmetic and copies ran while one was open for 0% of the time, Pallas kernels for 24%

profile of v15, /device:TPU:0, one launch (start us, length us, event | category | flops | bytes accessed | tf_op | source)
XLA Modules:
  0.0 61.2 jit_solution(7027727215296860874)
XLA Ops:
  0.6 0.5 collective-permute-start.2
  1.1 2.6 %collective-permute-start.6 = (bf16[64,5376]{1,0:T(8,128)(2,1)}, bf16[64,5376]{1,0:T(8,128)(2,1)S(1)}, u32[]{:S(2)}, u32[]{:S(2)}) collective-permute-start(bf16[64,5376]{1,0:T(8,128)(2,1)} %own_ref.1), channel_id=1, source_target_pairs={{0,2},{1,3},{2,0},{3,1},{4,6},{5,7},{6,4},{7,5},{8,10},{9,11},{10,... | collective-permute-start | bytes 2064392 | tf_op jit(solution)/shard_map/ppermute | solution.py:37
  3.7 0.0 copy-start.3
  3.7 0.9 %copy-done.3 = bf16[256,256]{1,0:T(8,128)(2,1)S(1)} copy-done((bf16[256,256]{1,0:T(8,128)(2,1)S(1)}, bf16[256,256]{1,0:T(8,128)(2,1)}, u32[]{:S(2)}) %copy-start.3) | copy-done | bytes 131096
  4.6 0.0 copy-start.4
  4.7 0.9 %copy-done.4 = bf16[256,256]{1,0:T(8,128)(2,1)S(1)} copy-done((bf16[256,256]{1,0:T(8,128)(2,1)S(1)}, bf16[256,256]{1,0:T(8,128)(2,1)}, u32[]{:S(2)}) %copy-start.4) | copy-done | bytes 131096
  5.6 3.5 %collective-permute-start = (bf16[256,512]{1,0:T(8,128)(2,1)S(1)}, bf16[256,512]{1,0:T(8,128)(2,1)S(1)}, u32[]{:S(2)}, u32[]{:S(2)}) collective-permute-start(bf16[256,512]{1,0:T(8,128)(2,1)S(1)} %join.1.a_ref.kv_ref), channel_id=1, source_target_pairs={{0,8},{4,12},{8,16},{12,20},{16,24},{20,28},{1,9},{5,13},{9,17},{1... | collective-permute-start | bytes 786440 | tf_op jit(solution)/shard_map/ppermute | solution.py:32
  9.1 0.0 copy-start.1
  9.1 0.9 %copy-done.1 = bf16[256,512]{1,0:T(8,128)(2,1)S(1)} copy-done((bf16[256,512]{1,0:T(8,128)(2,1)S(1)}, bf16[256,512]{1,0:T(8,128)(2,1)}, u32[]{:S(2)}) %copy-start.1) | copy-done | bytes 262168
  10.1 2.6 %collective-permute-start.1 = (bf16[256,512]{1,0:T(8,128)(2,1)S(1)}, bf16[256,512]{1,0:T(8,128)(2,1)S(1)}, u32[]{:S(2)}, u32[]{:S(2)}) collective-permute-start(bf16[256,512]{1,0:T(8,128)(2,1)S(1)} %far_sent.1), channel_id=1, source_target_pairs={{0,16},{4,20},{8,24},{12,28},{16,0},{20,4},{24,8},{28,12},{1,17},{... | collective-permute-start | bytes 786440 | tf_op jit(solution)/shard_map/ppermute | solution.py:48
  12.7 1.5 %collective-permute-start.4 = (bf16[256,512]{1,0:T(8,128)(2,1)S(1)}, bf16[256,512]{1,0:T(8,128)(2,1)S(1)}, u32[]{:S(2)}, u32[]{:S(2)}) collective-permute-start(bf16[256,512]{1,0:T(8,128)(2,1)S(1)} %join.1.a_ref.kv_ref), channel_id=1, source_target_pairs={{0,4},{4,0},{8,12},{12,8},{16,20},{20,16},{24,28},{28,24},{1,5},{5... | collective-permute-start | bytes 786440 | tf_op jit(solution)/shard_map/ppermute | solution.py:37
  14.2 0.0 collective-permute-done.2.core_ref
  14.2 0.0 copy-start
  14.2 2.6 %copy-done = bf16[512,5376]{1,0:T(8,128)(2,1)S(1)} copy-done((bf16[512,5376]{1,0:T(8,128)(2,1)S(1)}, bf16[512,5376]{1,0:T(8,128)(2,1)}, u32[]{:S(2)}) %copy-start) | copy-done | bytes 5505048
  16.8 0.0 copy-start.5
  16.8 1.1 %copy-done.5 = bf16[64,5376]{1,0:T(8,128)(2,1)S(1)} copy-done((bf16[64,5376]{1,0:T(8,128)(2,1)S(1)}, bf16[64,5376]{1,0:T(8,128)(2,1)}, u32[]{:S(2)}) %copy-start.5) | copy-done | bytes 688152
  17.9 0.0 slice-start
  17.9 1.9 %near_back.1.near_ref.dn_ref = bf16[128,512]{1,0:T(8,128)(2,1)S(1)} custom-call(bf16[64,5376]{1,0:T(8,128)(2,1)S(1)} %copy-done.5, bf16[64,5376]{1,0:T(8,128)(2,1)S(1)} %collective-permute-done.2.core_ref, bf16[512,5376]{1,0:T(8,128)(2,1)S(1)} %copy-done), custom_call_target="tpu_custom_call" | custom-call | flops 10000000000 | bytes 1 | tf_op jit(solution)/shard_map/near_back/pallas_call | solution.py:324
  19.8 0.0 slice-start.1
  19.8 0.0 collective-permute-done.r1_ref
  19.8 0.6 collective-permute-start.3
  20.4 4.4 %collective-permute-done.1.a_ref.b_ref.r2_ref.qf_ref = bf16[256,512]{1,0:T(8,128)(2,1)S(1)} collective-permute-done((bf16[256,512]{1,0:T(8,128)(2,1)S(1)}, bf16[256,512]{1,0:T(8,128)(2,1)S(1)}, u32[]{:S(2)}, u32[]{:S(2)}) %collective-permute-start.1) | collective-permute-done | bytes 262176 | tf_op jit(solution)/shard_map/ppermute | solution.py:48
  24.8 0.0 collective-permute-done.6.y_ref
  24.8 0.0 collective-permute-start.7
  24.8 0.0 copy-start.2
  24.8 1.6 %collective-permute-start.5 = (bf16[256,512]{1,0:T(8,128)(2,1)S(1)}, bf16[256,512]{1,0:T(8,128)(2,1)S(1)}, u32[]{:S(2)}, u32[]{:S(2)}) collective-permute-start(bf16[256,512]{1,0:T(8,128)(2,1)S(1)} %pick.1), channel_id=1, source_target_pairs={{0,4},{4,0},{8,12},{12,8},{16,20},{20,16},{24,28},{28,24},{1,5},{5... | collective-permute-start | bytes 786440 | tf_op jit(solution)/shard_map/ppermute | solution.py:37
  26.4 0.5 collective-permute-done.7.yc_ref
  26.9 0.0 slice-done
  26.9 0.0 slice-done.1
  26.9 1.9 %far_back.1 = (bf16[128,512]{1,0:T(8,128)(2,1)S(1)}, bf16[256,256]{1,0:T(8,128)(2,1)S(1)}) custom-call(bf16[64,5376]{1,0:T(8,128)(2,1)S(1)} %collective-permute-done.6.y_ref, bf16[64,5376]{1,0:T(8,128)(2,1)S(1)} %collective-permute-done.7.yc_ref, bf16[512,5376]{1,0:T(8,128)(2,1)S(1)} %bitcast.1, bf16[128,512]{1,0:T(8,128)(2,1)S(1)} %near_back.1.near_ref.dn_ref), custom_call_target="tpu_custom_call" | custom-call | flops 1 | bytes 1 | tf_op jit(solution)/shard_map/far_back/pallas_call | solution.py:324
  28.8 1.6 %collective-permute-start.8 = (bf16[256,256]{1,0:T(8,128)(2,1)S(1)}, bf16[256,256]{1,0:T(8,128)(2,1)S(1)}, u32[]{:S(2)}, u32[]{:S(2)}) collective-permute-start(bf16[256,256]{1,0:T(8,128)(2,1)S(1)} %get-tuple-element.42), channel_id=1, source_target_pairs={{0,16},{4,20},{8,24},{12,28},{16,0},{20,4},{24,8},{28,12},{1,17},{... | collective-permute-start | bytes 393224 | tf_op jit(solution)/shard_map/ppermute | solution.py:48
  30.4 0.0 collective-permute-done.4.p0_ref
  30.4 0.0 collective-permute-done.3.x1_ref
  30.4 0.0 copy-done.2
  30.4 2.1 %attend_early.1 = (f32[2,4,256,512]{3,2,1,0:T(8,128)S(1)}, f32[8,512]{1,0:T(8,128)S(1)}, f32[2,128,512]{2,1,0:T(8,128)S(1)}) custom-call(bf16[256,512]{1,0:T(8,128)(2,1)S(1)} %copy-done.2, bf16[256,512]{1,0:T(8,128)(2,1)S(1)} %join.1.a_ref.kv_ref, bf16[256,512]{1,0:T(8,128)(2,1)S(1)} %collective-permute-done.r1_ref, ...), custom_call_target="tpu_custom_call" | custom-call | flops 1 | bytes 1 | tf_op jit(solution)/shard_map/attend_early/pallas_call | solution.py:324
  32.5 1.1 %collective-permute-done.5.x2_ref.qx_ref = bf16[256,512]{1,0:T(8,128)(2,1)S(1)} collective-permute-done((bf16[256,512]{1,0:T(8,128)(2,1)S(1)}, bf16[256,512]{1,0:T(8,128)(2,1)S(1)}, u32[]{:S(2)}, u32[]{:S(2)}) %collective-permute-start.5) | collective-permute-done | bytes 262176 | tf_op jit(solution)/shard_map/ppermute | solution.py:37
  33.6 1.4 %attend.1 = (bf16[256,512]{1,0:T(8,128)(2,1)S(1)}, bf16[2,5,256,512]{3,2,1,0:T(8,128)(2,1)S(1)}, f32[8,512]{1,0:T(8,128)S(1)}, bf16[280,256]{1,0:T(8,128)(2,1)S(1)}) custom-call(bf16[256,512]{1,0:T(8,128)(2,1)S(1)} %copy-done.2, bf16[256,512]{1,0:T(8,128)(2,1)S(1)} %collective-permute-done.4.p0_ref, ...), custom_call_target="tpu_custom_call" | custom-call | flops 1 | bytes 1 | tf_op jit(solution)/shard_map/attend/pallas_call | solution.py:324
  35.0 1.6 %project.1 = (bf16[64,5376]{1,0:T(8,128)(2,1)S(1)}, bf16[64,5376]{1,0:T(8,128)(2,1)S(1)}, bf16[64,5376]{1,0:T(8,128)(2,1)S(1)}, bf16[64,5376]{1,0:T(8,128)(2,1)S(1)}) custom-call(bf16[256,512]{1,0:T(8,128)(2,1)S(1)} %get-tuple-element.48.o_ref, bf16[512,5376]{1,0:T(8,128)(2,1)S(1)} %bitcast.1), custom_call_target="tpu_custom_call" | custom-call | flops 1 | bytes 1 | tf_op jit(solution)/shard_map/project/pallas_call | solution.py:324
  36.7 0.0 collective-permute-done.8.a_ref.af_ref
  36.7 0.1 collective-permute-start.13
  36.7 3.3 %collective-permute-start.9 = (bf16[280,256]{1,0:T(8,128)(2,1)S(1)}, bf16[280,256]{1,0:T(8,128)(2,1)S(1)}, u32[]{:S(2)}, u32[]{:S(2)}) collective-permute-start(bf16[280,256]{1,0:T(8,128)(2,1)S(1)} %get-tuple-element.45), channel_id=1, source_target_pairs={{0,16},{4,20},{8,24},{12,28},{16,0},{20,4},{24,8},{28,12},{1,17},{... | collective-permute-start | bytes 430088 | tf_op jit(solution)/shard_map/ppermute | solution.py:48
  40.0 0.6 across_grad.1
  40.6 1.5 %collective-permute-start.11 = (bf16[256,512]{1,0:T(8,128)(2,1)S(1)}, bf16[256,512]{1,0:T(8,128)(2,1)S(1)}, u32[]{:S(2)}, u32[]{:S(2)}) collective-permute-start(bf16[256,512]{1,0:T(8,128)(2,1)S(1)} %across_grad.1), channel_id=1, source_target_pairs={{0,4},{4,0},{8,12},{12,8},{16,20},{20,16},{24,28},{28,24},{1,5},{5... | collective-permute-start | bytes 786440 | tf_op jit(solution)/shard_map/ppermute | solution.py:37
  42.2 0.0 collective-permute-done.13.refs_1_
  42.2 0.2 far_sum.1
  42.3 0.6 collective-permute-start.15
  42.9 0.0 collective-permute-start.14
  42.9 3.4 %attend_grad.1 = (bf16[256,512]{1,0:T(8,128)(2,1)}, f32[256,512]{1,0:T(8,128)S(1)}, bf16[256,512]{1,0:T(8,128)(2,1)S(1)}, bf16[256,512]{1,0:T(8,128)(2,1)S(1)}) custom-call(bf16[256,512]{1,0:T(8,128)(2,1)S(1)} %copy-done.2, bf16[256,512]{1,0:T(8,128)(2,1)S(1)} %join.1.a_ref.kv_ref, bf16[256,512]{1,0:T(8,128)(2,1)S(1)} %collective-permute-done.r1_ref, ...), custom_call_target="tpu_custom_call" | custom-call | flops 10000000000 | bytes 1 | tf_op jit(solution)/shard_map/attend_grad/pallas_call | solution.py:324
  46.3 1.2 %collective-permute-done.9.b_ref.bf_ref = bf16[280,256]{1,0:T(8,128)(2,1)S(1)} collective-permute-done((bf16[280,256]{1,0:T(8,128)(2,1)S(1)}, bf16[280,256]{1,0:T(8,128)(2,1)S(1)}, u32[]{:S(2)}, u32[]{:S(2)}) %collective-permute-start.9) | collective-permute-done | bytes 143392 | tf_op jit(solution)/shard_map/ppermute | solution.py:48
  47.5 1.6 %collective-permute-start.10 = (bf16[280,512]{1,0:T(8,128)(2,1)S(1)}, bf16[280,512]{1,0:T(8,128)(2,1)S(1)}, u32[]{:S(2)}, u32[]{:S(2)}) collective-permute-start(bf16[280,512]{1,0:T(8,128)(2,1)S(1)} %pair.1), channel_id=1, source_target_pairs={{0,4},{4,0},{8,12},{12,8},{16,20},{20,16},{24,28},{28,24},{1,5},{5... | collective-permute-start | bytes 860168 | tf_op jit(solution)/shard_map/ppermute | solution.py:37
  49.0 0.0 collective-permute-done.11.refs_1_
  49.0 0.1 hop_sum.1
  49.1 1.3 %collective-permute-start.12 = (bf16[256,512]{1,0:T(8,128)(2,1)S(1)}, bf16[256,512]{1,0:T(8,128)(2,1)S(1)}, u32[]{:S(2)}, u32[]{:S(2)}) collective-permute-start(bf16[256,512]{1,0:T(8,128)(2,1)S(1)} %hop_sum.1), channel_id=1, source_target_pairs={{8,0},{12,4},{16,8},{20,12},{24,16},{28,20},{9,1},{13,5},{17,9},{2... | collective-permute-start | bytes 786440 | tf_op jit(solution)/shard_map/ppermute | solution.py:32
  50.4 5.7 %collective-permute-done.10.px_ref.pair_ref = bf16[280,512]{1,0:T(8,128)(2,1)S(1)} collective-permute-done((bf16[280,512]{1,0:T(8,128)(2,1)S(1)}, bf16[280,512]{1,0:T(8,128)(2,1)S(1)}, u32[]{:S(2)}, u32[]{:S(2)}) %collective-permute-start.10) | collective-permute-done | bytes 286752 | tf_op jit(solution)/shard_map/ppermute | solution.py:37
  56.1 1.5 %far_grad.1.far_ref = f32[256,512]{1,0:T(8,128)S(1)} custom-call(bf16[256,512]{1,0:T(8,128)(2,1)S(1)} %join.1.a_ref.kv_ref, bf16[256,512]{1,0:T(8,128)(2,1)S(1)} %collective-permute-done.1.a_ref.b_ref.r2_ref.qf_ref, bf16[256,256]{1,0:T(8,128)(2,1)S(1)} %collective-permute-done.8.a_ref.af_ref, bf16[280,256]{1,0:T(8,128)(2,1)S(1)} %collective-permute-done.9.b_ref.bf_ref, ...), custom_call_target="tpu_custom_call" | custom-call | flops 100000000 | bytes 1 | tf_op jit(solution)/shard_map/far_grad/pallas_call | solution.py:324
  57.6 2.3 %collective-permute-done.12.hop_ref = bf16[256,512]{1,0:T(8,128)(2,1)S(1)} collective-permute-done((bf16[256,512]{1,0:T(8,128)(2,1)S(1)}, bf16[256,512]{1,0:T(8,128)(2,1)S(1)}, u32[]{:S(2)}, u32[]{:S(2)}) %collective-permute-start.12) | collective-permute-done | bytes 262176 | tf_op jit(solution)/shard_map/ppermute | solution.py:32
  60.0 0.0 collective-permute-done.14.core_ref
  60.0 0.0 collective-permute-done.15.y_ref
  60.0 1.2 %closing.1 = (bf16[256,256]{1,0:T(8,128)(2,1)}, bf16[256,256]{1,0:T(8,128)(2,1)}, bf16[64,5376]{1,0:T(8,128)(2,1)}) custom-call(f32[256,512]{1,0:T(8,128)S(1)} %get-tuple-element.44.own_ref, f32[256,512]{1,0:T(8,128)S(1)} %far_grad.1.far_ref, bf16[256,512]{1,0:T(8,128)(2,1)S(1)} %collective-permute-done.12.hop_ref, ...), custom_call_target="tpu_custom_call" | custom-call | flops 1 | bytes 1 | tf_op jit(solution)/shard_map/closing/pallas_call | solution.py:324
  (5 shorter events, 0.1 us)
Async XLA Ops:
  0.6 13.6 %collective-permute-start.2 = (bf16[64,5376]{1,0:T(8,128)(2,1)}, bf16[64,5376]{1,0:T(8,128)(2,1)S(1)}, u32[]{:S(2)}, u32[]{:S(2)}) collective-permute-start(bf16[64,5376]{1,0:T(8,128)(2,1)} %own_ref.1), channel_id=1, source_target_pairs={{0,1},{1,0},{2,3},{3,2},{4,5},{5,4},{6,7},{7,6},{8,9},{9,8},{10,11... | collective-permute-start | bytes 2064392 | tf_op jit(solution)/shard_map/ppermute | solution.py:37
  1.1 23.6 %collective-permute-start.6 = (bf16[64,5376]{1,0:T(8,128)(2,1)}, bf16[64,5376]{1,0:T(8,128)(2,1)S(1)}, u32[]{:S(2)}, u32[]{:S(2)}) collective-permute-start(bf16[64,5376]{1,0:T(8,128)(2,1)} %own_ref.1), channel_id=1, source_target_pairs={{0,2},{1,3},{2,0},{3,1},{4,6},{5,7},{6,4},{7,5},{8,10},{9,11},{10,... | collective-permute-start | bytes 2064392 | tf_op jit(solution)/shard_map/ppermute | solution.py:37
  3.7 0.9 %copy-start.3 = (bf16[256,256]{1,0:T(8,128)(2,1)S(1)}, bf16[256,256]{1,0:T(8,128)(2,1)}, u32[]{:S(2)}) copy-start(bf16[256,256]{1,0:T(8,128)(2,1)} %k_ref.1) | copy-start | bytes 393220
  4.6 0.9 %copy-start.4 = (bf16[256,256]{1,0:T(8,128)(2,1)S(1)}, bf16[256,256]{1,0:T(8,128)(2,1)}, u32[]{:S(2)}) copy-start(bf16[256,256]{1,0:T(8,128)(2,1)} %v_ref.1) | copy-start | bytes 393220
  5.6 14.2 %collective-permute-start = (bf16[256,512]{1,0:T(8,128)(2,1)S(1)}, bf16[256,512]{1,0:T(8,128)(2,1)S(1)}, u32[]{:S(2)}, u32[]{:S(2)}) collective-permute-start(bf16[256,512]{1,0:T(8,128)(2,1)S(1)} %join.1.a_ref.kv_ref), channel_id=1, source_target_pairs={{0,8},{4,12},{8,16},{12,20},{16,24},{20,28},{1,9},{5,13},{9,17},{1... | collective-permute-start | bytes 786440 | tf_op jit(solution)/shard_map/ppermute | solution.py:32
  9.1 1.0 %copy-start.1 = (bf16[256,512]{1,0:T(8,128)(2,1)S(1)}, bf16[256,512]{1,0:T(8,128)(2,1)}, u32[]{:S(2)}) copy-start(bf16[256,512]{1,0:T(8,128)(2,1)} %q_ref.7) | copy-start | bytes 786436
  10.1 14.7 %collective-permute-start.1 = (bf16[256,512]{1,0:T(8,128)(2,1)S(1)}, bf16[256,512]{1,0:T(8,128)(2,1)S(1)}, u32[]{:S(2)}, u32[]{:S(2)}) collective-permute-start(bf16[256,512]{1,0:T(8,128)(2,1)S(1)} %far_sent.1), channel_id=1, source_target_pairs={{0,16},{4,20},{8,24},{12,28},{16,0},{20,4},{24,8},{28,12},{1,17},{... | collective-permute-start | bytes 786440 | tf_op jit(solution)/shard_map/ppermute | solution.py:48
  12.7 17.7 %collective-permute-start.4 = (bf16[256,512]{1,0:T(8,128)(2,1)S(1)}, bf16[256,512]{1,0:T(8,128)(2,1)S(1)}, u32[]{:S(2)}, u32[]{:S(2)}) collective-permute-start(bf16[256,512]{1,0:T(8,128)(2,1)S(1)} %join.1.a_ref.kv_ref), channel_id=1, source_target_pairs={{0,4},{4,0},{8,12},{12,8},{16,20},{20,16},{24,28},{28,24},{1,5},{5... | collective-permute-start | bytes 786440 | tf_op jit(solution)/shard_map/ppermute | solution.py:37
  14.2 2.6 %copy-start = (bf16[512,5376]{1,0:T(8,128)(2,1)S(1)}, bf16[512,5376]{1,0:T(8,128)(2,1)}, u32[]{:S(2)}) copy-start(bf16[512,5376]{1,0:T(8,128)(2,1)} %w_ref.5) | copy-start | bytes 16515076
  16.8 1.1 %copy-start.5 = (bf16[64,5376]{1,0:T(8,128)(2,1)S(1)}, bf16[64,5376]{1,0:T(8,128)(2,1)}, u32[]{:S(2)}) copy-start(bf16[64,5376]{1,0:T(8,128)(2,1)} %own_ref.1) | copy-start | bytes 2064388
  17.9 9.0 %slice-start = ((s8[5505024]{0:T(1024)(128)(4,1)}), s8[4194304]{0:T(1024)(128)(4,1)S(1)}, s32[]{:S(2)}) async-start(s8[5505024]{0:T(1024)(128)(4,1)} %bitcast), calls=%async_computation | async-start | bytes 8388608
  19.8 7.1 %slice-start.1 = ((s8[5505024]{0:T(1024)(128)(4,1)}), s8[1310720]{0:T(1024)(128)(4,1)S(1)}, s32[]{:S(2)}) async-start(s8[5505024]{0:T(1024)(128)(4,1)} %bitcast), calls=%async_computation.1 | async-start | bytes 2621440
  19.8 10.7 %collective-permute-start.3 = (bf16[256,512]{1,0:T(8,128)(2,1)S(1)}, bf16[256,512]{1,0:T(8,128)(2,1)S(1)}, u32[]{:S(2)}, u32[]{:S(2)}) collective-permute-start(bf16[256,512]{1,0:T(8,128)(2,1)S(1)} %collective-permute-done.r1_ref), channel_id=1, source_target_pairs={{0,4},{4,0},{8,12},{12,8},{16,20},{20,16},{24,28},{28,24},{1,5},{5... | collective-permute-start | bytes 786440 | tf_op jit(solution)/shard_map/ppermute | solution.py:37
  24.8 2.1 %collective-permute-start.7 = (bf16[64,5376]{1,0:T(8,128)(2,1)S(1)}, bf16[64,5376]{1,0:T(8,128)(2,1)S(1)}, u32[]{:S(2)}, u32[]{:S(2)}) collective-permute-start(bf16[64,5376]{1,0:T(8,128)(2,1)S(1)} %collective-permute-done.6.y_ref), channel_id=1, source_target_pairs={{0,1},{1,0},{2,3},{3,2},{4,5},{5,4},{6,7},{7,6},{8,9},{9,8},{10,11... | collective-permute-start | bytes 2064392 | tf_op jit(solution)/shard_map/ppermute | solution.py:37
  24.8 5.6 %copy-start.2 = (bf16[256,512]{1,0:T(8,128)(2,1)S(1)}, bf16[256,512]{1,0:T(8,128)(2,1)}, u32[]{:S(2)}) copy-start(bf16[256,512]{1,0:T(8,128)(2,1)} %q_ref.7) | copy-start | bytes 786436
  24.8 8.8 %collective-permute-start.5 = (bf16[256,512]{1,0:T(8,128)(2,1)S(1)}, bf16[256,512]{1,0:T(8,128)(2,1)S(1)}, u32[]{:S(2)}, u32[]{:S(2)}) collective-permute-start(bf16[256,512]{1,0:T(8,128)(2,1)S(1)} %pick.1), channel_id=1, source_target_pairs={{0,4},{4,0},{8,12},{12,8},{16,20},{20,16},{24,28},{28,24},{1,5},{5... | collective-permute-start | bytes 786440 | tf_op jit(solution)/shard_map/ppermute | solution.py:37
  28.8 7.9 %collective-permute-start.8 = (bf16[256,256]{1,0:T(8,128)(2,1)S(1)}, bf16[256,256]{1,0:T(8,128)(2,1)S(1)}, u32[]{:S(2)}, u32[]{:S(2)}) collective-permute-start(bf16[256,256]{1,0:T(8,128)(2,1)S(1)} %get-tuple-element.42), channel_id=1, source_target_pairs={{0,16},{4,20},{8,24},{12,28},{16,0},{20,4},{24,8},{28,12},{1,17},{... | collective-permute-start | bytes 393224 | tf_op jit(solution)/shard_map/ppermute | solution.py:48
  36.7 5.5 %collective-permute-start.13 = (bf16[64,5376]{1,0:T(8,128)(2,1)S(1)}, bf16[64,5376]{1,0:T(8,128)(2,1)S(1)}, u32[]{:S(2)}, u32[]{:S(2)}) collective-permute-start(bf16[64,5376]{1,0:T(8,128)(2,1)S(1)} %get-tuple-element.54), channel_id=1, source_target_pairs={{0,1},{1,0},{2,3},{3,2},{4,5},{5,4},{6,7},{7,6},{8,9},{9,8},{10,11... | collective-permute-start | bytes 2064392 | tf_op jit(solution)/shard_map/ppermute | solution.py:37
  36.7 10.7 %collective-permute-start.9 = (bf16[280,256]{1,0:T(8,128)(2,1)S(1)}, bf16[280,256]{1,0:T(8,128)(2,1)S(1)}, u32[]{:S(2)}, u32[]{:S(2)}) collective-permute-start(bf16[280,256]{1,0:T(8,128)(2,1)S(1)} %get-tuple-element.45), channel_id=1, source_target_pairs={{0,16},{4,20},{8,24},{12,28},{16,0},{20,4},{24,8},{28,12},{1,17},{... | collective-permute-start | bytes 430088 | tf_op jit(solution)/shard_map/ppermute | solution.py:48
  40.6 8.4 %collective-permute-start.11 = (bf16[256,512]{1,0:T(8,128)(2,1)S(1)}, bf16[256,512]{1,0:T(8,128)(2,1)S(1)}, u32[]{:S(2)}, u32[]{:S(2)}) collective-permute-start(bf16[256,512]{1,0:T(8,128)(2,1)S(1)} %across_grad.1), channel_id=1, source_target_pairs={{0,4},{4,0},{8,12},{12,8},{16,20},{20,16},{24,28},{28,24},{1,5},{5... | collective-permute-start | bytes 786440 | tf_op jit(solution)/shard_map/ppermute | solution.py:37
  42.3 17.7 %collective-permute-start.15 = (bf16[64,5376]{1,0:T(8,128)(2,1)S(1)}, bf16[64,5376]{1,0:T(8,128)(2,1)S(1)}, u32[]{:S(2)}, u32[]{:S(2)}) collective-permute-start(bf16[64,5376]{1,0:T(8,128)(2,1)S(1)} %far_sum.1), channel_id=1, source_target_pairs={{0,2},{1,3},{2,0},{3,1},{4,6},{5,7},{6,4},{7,5},{8,10},{9,11},{10,... | collective-permute-start | bytes 2064392 | tf_op jit(solution)/shard_map/ppermute | solution.py:37
  42.9 17.1 %collective-permute-start.14 = (bf16[64,5376]{1,0:T(8,128)(2,1)S(1)}, bf16[64,5376]{1,0:T(8,128)(2,1)S(1)}, u32[]{:S(2)}, u32[]{:S(2)}) collective-permute-start(bf16[64,5376]{1,0:T(8,128)(2,1)S(1)} %get-tuple-element.55), channel_id=1, source_target_pairs={{0,1},{1,0},{2,3},{3,2},{4,5},{5,4},{6,7},{7,6},{8,9},{9,8},{10,11... | collective-permute-start | bytes 2064392 | tf_op jit(solution)/shard_map/ppermute | solution.py:37
  47.5 8.7 %collective-permute-start.10 = (bf16[280,512]{1,0:T(8,128)(2,1)S(1)}, bf16[280,512]{1,0:T(8,128)(2,1)S(1)}, u32[]{:S(2)}, u32[]{:S(2)}) collective-permute-start(bf16[280,512]{1,0:T(8,128)(2,1)S(1)} %pair.1), channel_id=1, source_target_pairs={{0,4},{4,0},{8,12},{12,8},{16,20},{20,16},{24,28},{28,24},{1,5},{5... | collective-permute-start | bytes 860168 | tf_op jit(solution)/shard_map/ppermute | solution.py:37
  49.1 10.9 %collective-permute-start.12 = (bf16[256,512]{1,0:T(8,128)(2,1)S(1)}, bf16[256,512]{1,0:T(8,128)(2,1)S(1)}, u32[]{:S(2)}, u32[]{:S(2)}) collective-permute-start(bf16[256,512]{1,0:T(8,128)(2,1)S(1)} %hop_sum.1), channel_id=1, source_target_pairs={{8,0},{12,4},{16,8},{20,12},{24,16},{28,20},{9,1},{13,5},{17,9},{2... | collective-permute-start | bytes 786440 | tf_op jit(solution)/shard_map/ppermute | solution.py:32
